TPU v7x, 32 devices: a whole 2x2x4 slice. The times are simulated.
32 devices in a mesh: seq: 16 (over z, x, core), heads: 2 (over y).
Axes of the slice: x: 2, y: 2, z: 4, core: 2. Of those that a mesh axis runs over, the one named last changes fastest.
Arguments:
- frames: float32 [16384, 768], P('seq'), may hold values from -6 to 6
- cotangent: float32 [16384, 768], P('seq'), may hold values from -6 to 6
- lengths: int32 [64], replicated, may hold values from 1 to 1536, 16384 in all
- kernel: float32 [768, 48, 128], P('heads', None, 'seq'), may hold values from -0.078125 to 0.078125
- kernel_moment: float32 [768, 48, 128], P('heads', None, 'seq'), may hold values from -224 to 224
- kernel_average: float32 [768, 48, 128], P('heads', None, 'seq'), may hold values from -0.078125 to 0.078125
- project: float32 [768, 3, 768], P('seq', None, 'heads'), may hold values from -0.21875 to 0.21875
- project_moment: float32 [768, 3, 768], P('seq', None, 'heads'), may hold values from -224 to 224
- project_average: float32 [768, 3, 768], P('seq', None, 'heads'), may hold values from -0.21875 to 0.21875
- combine: float32 [768, 768], P('heads', 'seq'), may hold values from -0.875 to 0.875
- combine_moment: float32 [768, 768], P('heads', 'seq'), may hold values from -224 to 224
- combine_average: float32 [768, 768], P('heads', 'seq'), may hold values from -0.875 to 0.875
- expand: float32 [768, 3072], P('seq', 'heads'), may hold values from -0.21875 to 0.21875
- expand_moment: float32 [768, 3072], P('seq', 'heads'), may hold values from -224 to 224
- expand_average: float32 [768, 3072], P('seq', 'heads'), may hold values from -0.21875 to 0.21875
- shrink: float32 [3072, 768], P('heads', 'seq'), may hold values from -0.109375 to 0.109375
- shrink_moment: float32 [3072, 768], P('heads', 'seq'), may hold values from -224 to 224
- shrink_average: float32 [3072, 768], P('heads', 'seq'), may hold values from -0.109375 to 0.109375
- unitbias: float32 [3072], P(('heads', 'seq')), may hold values from -3 to 3
- unitbias_moment: float32 [3072], P(('heads', 'seq')), may hold values from -224 to 224
- unitbias_average: float32 [3072], P(('heads', 'seq')), may hold values from -3 to 3
- chanbias: float32 [3, 768], P(None, ('heads', 'seq')), may hold values from -3 to 3
- chanbias_moment: float32 [3, 768], P(None, ('heads', 'seq')), may hold values from -224 to 224
- chanbias_average: float32 [3, 768], P(None, ('heads', 'seq')), may hold values from -3 to 3
- outbias: float32 [2, 768], P(None, 'seq'), may hold values from -3 to 3
- outbias_moment: float32 [2, 768], P(None, 'seq'), may hold values from -224 to 224
- outbias_average: float32 [2, 768], P(None, 'seq'), may hold values from -3 to 3
- normparams: float32 [3, 2, 768], P(None, None, 'seq'), may hold values from -1.2 to 1.3, as said below
- normparams_moment: float32 [3, 2, 768], P(None, None, 'seq'), may hold values from -224 to 224
- normparams_average: float32 [3, 2, 768], P(None, None, 'seq'), may hold values from -1.2 to 1.3, as said below
Outputs:
- layer_out: float32 [16384, 768], P('seq')
- frames_grad: float32 [16384, 768], P('seq')
- kernel_grad: float32 [768, 48, 128], P('heads', None, 'seq')
- kernel_next: float32 [768, 48, 128], P('heads', None, 'seq')
- kernel_newmoment: float32 [768, 48, 128], P('heads', None, 'seq')
- kernel_newaverage: float32 [768, 48, 128], P('heads', None, 'seq')
- kernel_bfloat: bfloat16 [768, 48, 128], P('heads', None, 'seq')
- project_grad: float32 [768, 3, 768], P('seq', None, 'heads')
- project_next: float32 [768, 3, 768], P('seq', None, 'heads')
- project_newmoment: float32 [768, 3, 768], P('seq', None, 'heads')
- project_newaverage: float32 [768, 3, 768], P('seq', None, 'heads')
- project_bfloat: bfloat16 [768, 3, 768], P('seq', None, 'heads')
- combine_grad: float32 [768, 768], P('heads', 'seq')
- combine_next: float32 [768, 768], P('heads', 'seq')
- combine_newmoment: float32 [768, 768], P('heads', 'seq')
- combine_newaverage: float32 [768, 768], P('heads', 'seq')
- combine_bfloat: bfloat16 [768, 768], P('heads', 'seq')
- expand_grad: float32 [768, 3072], P('seq', 'heads')
- expand_next: float32 [768, 3072], P('seq', 'heads')
- expand_newmoment: float32 [768, 3072], P('seq', 'heads')
- expand_newaverage: float32 [768, 3072], P('seq', 'heads')
- expand_bfloat: bfloat16 [768, 3072], P('seq', 'heads')
- shrink_grad: float32 [3072, 768], P('heads', 'seq')
- shrink_next: float32 [3072, 768], P('heads', 'seq')
- shrink_newmoment: float32 [3072, 768], P('heads', 'seq')
- shrink_newaverage: float32 [3072, 768], P('heads', 'seq')
- shrink_bfloat: bfloat16 [3072, 768], P('heads', 'seq')
- unitbias_grad: float32 [3072], P(('heads', 'seq'))
- unitbias_next: float32 [3072], P(('heads', 'seq'))
- unitbias_newmoment: float32 [3072], P(('heads', 'seq'))
- unitbias_newaverage: float32 [3072], P(('heads', 'seq'))
- unitbias_bfloat: bfloat16 [3072], P(('heads', 'seq'))
- chanbias_grad: float32 [3, 768], P(None, ('heads', 'seq'))
- chanbias_next: float32 [3, 768], P(None, ('heads', 'seq'))
- chanbias_newmoment: float32 [3, 768], P(None, ('heads', 'seq'))
- chanbias_newaverage: float32 [3, 768], P(None, ('heads', 'seq'))
- chanbias_bfloat: bfloat16 [3, 768], P(None, ('heads', 'seq'))
- outbias_grad: float32 [2, 768], P(None, 'seq')
- outbias_next: float32 [2, 768], P(None, 'seq')
- outbias_newmoment: float32 [2, 768], P(None, 'seq')
- outbias_newaverage: float32 [2, 768], P(None, 'seq')
- outbias_bfloat: bfloat16 [2, 768], P(None, 'seq')
- normparams_grad: float32 [3, 2, 768], P(None, None, 'seq')
- normparams_next: float32 [3, 2, 768], P(None, None, 'seq')
- normparams_newmoment: float32 [3, 2, 768], P(None, None, 'seq')
- normparams_newaverage: float32 [3, 2, 768], P(None, None, 'seq')
- normparams_bfloat: bfloat16 [3, 2, 768], P(None, None, 'seq')
Inputs may be any that keep to these rules, and one draw needn't show every extreme that they name: lengths sum to 16384; the longest is exactly 1536. `normparams`: entry [n, 0] holds norm n's gains, entry [n, 1] its shifts. `normparams_average`: entry [n, 0] holds gains, entry [n, 1] shifts.
All inputs are finite; a program needn't handle non-finite values.
Results may differ from a plain program's by a relative error of at most 0.015.
Values may be sent and summed in bfloat16 or wider, within the bound.
No kernel may reach another device: no remote copies, remote signals or barrier semaphores. Data moves between devices by JAX's collectives and lax.ppermute only.
A program may use at most 512 MiB of HBM per device.

v0:
```python
import jax
import jax.numpy as jnp
from jax import lax
from jax.sharding import PartitionSpec as P

HEAD = 64


EPSILON = 1e-05
NEGATIVE = -1e30
tap_group = 16


def padded_2(cells, sides, width):
    for axis, dim in sides:
        count = lax.axis_size(axis)
        ends = count - 1
        head = lax.slice_in_dim(cells, 0, width, axis=dim)
        tail = lax.slice_in_dim(cells, cells.shape[dim] - width, cells.shape[dim], axis=dim)
        cells = jnp.concatenate(
            [
                lax.ppermute(tail, axis, [(i, (i + 1) % count) for i in range(ends)]),
                cells,
                lax.ppermute(head, axis, [((i + 1) % count, i) for i in range(ends)]),
            ],
            axis=dim,
        )
    return cells


def passed_along(block, axis, distance):
    devices = range(lax.axis_size(axis))
    route = [(i - distance, i) for i in devices if i - distance in devices]
    return lax.ppermute(block, axis, route)


def layer_norm(values, gain, shift):
    centered = values - jnp.mean(values, axis=-1, keepdims=True)
    scale = lax.rsqrt(jnp.mean(centered * centered, axis=-1, keepdims=True) + EPSILON)
    return centered * scale * gain + shift


def gelu_exact(values):
    return jax.nn.gelu(values, approximate=False)


def segment_of(positions, ends, total):
    counted = jnp.sum((ends[None, :] <= positions[:, None]).astype(jnp.int32), axis=1)
    before = (positions < 0).astype(jnp.int32)
    inside = (positions >= 0) & (positions < total)
    return jnp.where(inside, counted, -1 - before)


def tap_valid(pad_seg, row_seg, start, count, rows):
    return jnp.stack([pad_seg[start + j : start + j + rows] == row_seg for j in range(count)])


def tap_window(padded, valid, start, count, rows, groups, ingroup):
    pieces = jnp.stack([padded[start + j : start + j + rows] for j in range(count)])
    window = jnp.where(valid[:, :, None], pieces, jnp.zeros((), padded.dtype))
    return window.reshape(count, rows, groups, ingroup)


def shares_rows(row_seg, key_seg):
    inside = key_seg >= 0
    lowest = jnp.min(jnp.where(inside, key_seg, jnp.int32(1 << 30)))
    highest = jnp.max(jnp.where(inside, key_seg, jnp.int32(-3)))
    return (highest >= row_seg[0]) & (lowest <= row_seg[-1])


def score_rows(queries, keys, row_seg, key_seg):
    raw = jnp.einsum("thd,khd->htk", queries, keys, preferred_element_type=jnp.float32)
    same = row_seg[:, None] == key_seg[None, :]
    return jnp.where(same[None], raw, NEGATIVE)


def nesterov(weight, grad, moment, average, rate):
    moment_new = 0.5 * moment + grad
    weight_new = weight - rate * (grad + 0.5 * moment_new)
    average_new = 0.5 * average + 0.5 * weight_new
    return (grad, weight_new, moment_new, average_new, weight_new.astype(jnp.bfloat16))


def body(
    frames,
    cotangent,
    lengths,
    kernel,
    kernel_moment,
    kernel_average,
    project,
    project_moment,
    project_average,
    combine,
    combine_moment,
    combine_average,
    expand,
    expand_moment,
    expand_average,
    shrink,
    shrink_moment,
    shrink_average,
    unitbias,
    unitbias_moment,
    unitbias_average,
    chanbias,
    chanbias_moment,
    chanbias_average,
    outbias,
    outbias_moment,
    outbias_average,
    normparams,
    normparams_moment,
    normparams_average,
):
    half_type = jnp.bfloat16
    full_type = jnp.float32
    rows = frames.shape[0]
    width = frames.shape[1]
    total = lax.axis_size("seq") * rows
    first = lax.axis_index("seq") * rows
    w_kernel, w_project, w_combine, w_expand, w_shrink, w_unit, w_chan, w_out, w_norm = (
        lax.all_gather(kernel.astype(half_type), "seq", axis=2, tiled=True),
        lax.all_gather(project.astype(half_type), "seq", axis=0, tiled=True),
        lax.all_gather(combine.astype(half_type), "seq", axis=1, tiled=True),
        lax.all_gather(expand.astype(half_type), "seq", axis=0, tiled=True),
        lax.all_gather(shrink.astype(half_type), "seq", axis=1, tiled=True),
        lax.all_gather(unitbias.astype(half_type), "seq", axis=0, tiled=True),
        lax.all_gather(chanbias.astype(half_type), "seq", axis=1, tiled=True),
        lax.all_gather(outbias.astype(half_type), "seq", axis=1, tiled=True),
        lax.all_gather(normparams.astype(half_type), "seq", axis=2, tiled=True),
    )
    b_unit = w_unit.astype(full_type)
    b_chan = w_chan.astype(full_type)
    b_out = w_out.astype(full_type)
    norms = w_norm.astype(full_type)
    half = w_combine.shape[0]
    ingroup = w_kernel.shape[1]
    taps = w_kernel.shape[2]
    groups = half // ingroup
    reach_taps = taps // 2
    heads_local = half // HEAD
    hidden_full = w_expand.shape[1] * lax.axis_size("heads")
    ends = jnp.cumsum(lengths)
    row_seg = segment_of(first + jnp.arange(rows, dtype=jnp.int32), ends, total)
    channel_start = lax.axis_index("heads") * half
    conv_input = lax.dynamic_slice_in_dim(frames, channel_start, half, 1).astype(half_type)
    padded = padded_2(conv_input, (("seq", 0),), reach_taps)
    pad_seg = segment_of(first - reach_taps + jnp.arange(rows + taps, dtype=jnp.int32), ends, total)
    kernel4 = w_kernel.reshape(groups, ingroup, ingroup, taps)
    conv = jnp.zeros((rows, groups, ingroup), full_type)
    for start in range(0, taps, tap_group):
        valid = tap_valid(pad_seg, row_seg, start, tap_group, rows)
        window = tap_window(padded, valid, start, tap_group, rows, groups, ingroup)
        conv = conv + jnp.einsum(
            "jtgi,goij->tgo",
            window,
            kernel4[..., start : start + tap_group],
            preferred_element_type=full_type,
        )
    pre = conv.reshape(rows, half) + b_chan[0]
    spread_part = gelu_exact(pre).astype(half_type)
    spread = lax.all_gather(spread_part, "heads", axis=1, tiled=True)
    h1, norm0_back = jax.vjp(
        layer_norm, frames + spread.astype(full_type), norms[0, 0], norms[0, 1]
    )
    scale = HEAD ** (-0.5)
    h1_half = h1.astype(half_type)
    proj = jnp.einsum("td,dcf->tcf", h1_half, w_project, preferred_element_type=full_type)
    queries = ((proj[:, 0] + b_chan[1]) * scale).astype(half_type).reshape(rows, heads_local, HEAD)
    keys = proj[:, 1].astype(half_type).reshape(rows, heads_local, HEAD)
    values = (proj[:, 2] + b_chan[2]).astype(half_type).reshape(rows, heads_local, HEAD)
    key_blocks = [(keys, values, row_seg, 0)]
    for shift_by in (1, -1, 2, -2):
        far_keys, far_values = passed_along((keys, values), "seq", shift_by)
        far_seg = segment_of(
            first - shift_by * rows + jnp.arange(rows, dtype=jnp.int32), ends, total
        )
        key_blocks.append((far_keys, far_values, far_seg, shift_by))
    running_top = jnp.full((heads_local, rows), NEGATIVE, full_type)
    running_mass = jnp.zeros((heads_local, rows), full_type)
    for block_keys, block_values, key_seg, shift_by in key_blocks:

        def grow_mass(block_keys=block_keys, key_seg=key_seg, top=running_top, mass=running_mass):
            raw = score_rows(queries, block_keys, row_seg, key_seg)
            new_top = jnp.maximum(top, jnp.max(raw, axis=-1))
            new_mass = mass * jnp.exp(top - new_top) + jnp.sum(
                jnp.exp(raw - new_top[..., None]), axis=-1
            )
            return (new_top, new_mass)

        def keep_mass(top=running_top, mass=running_mass):
            return (top, mass)

        running_top, running_mass = lax.cond(shares_rows(row_seg, key_seg), grow_mass, keep_mass)
    lse = running_top + jnp.log(running_mass)
    mixed = jnp.zeros((rows, heads_local, HEAD), full_type)
    for block_keys, block_values, key_seg, shift_by in key_blocks:

        def weigh_values(block_keys=block_keys, block_values=block_values, key_seg=key_seg):
            raw = score_rows(queries, block_keys, row_seg, key_seg)
            probs = jnp.exp(raw - lse[..., None]).astype(half_type)
            return jnp.einsum("htk,khd->thd", probs, block_values, preferred_element_type=full_type)

        def no_values():
            return jnp.zeros((rows, heads_local, HEAD), full_type)

        mixed = mixed + lax.cond(shares_rows(row_seg, key_seg), weigh_values, no_values)
    attended = mixed.reshape(rows, half).astype(half_type)
    branch = lax.psum(
        jnp.dot(attended, w_combine, preferred_element_type=full_type).astype(jnp.bfloat16), "heads"
    ).astype(jnp.float32)
    h2, norm1_back = jax.vjp(layer_norm, h1 + branch + b_out[0], norms[1, 0], norms[1, 1])
    h2_half = h2.astype(half_type)
    inner = jnp.dot(h2_half, w_expand, preferred_element_type=full_type) + b_unit
    hidden, gelu_inner_back = jax.vjp(gelu_exact, inner)
    hidden_half = hidden.astype(half_type)
    outer = lax.psum(
        jnp.dot(hidden_half, w_shrink, preferred_element_type=full_type).astype(jnp.bfloat16),
        "heads",
    ).astype(jnp.float32)
    layer_out, norm2_back = jax.vjp(layer_norm, h2 + outer + b_out[1], norms[2, 0], norms[2, 1])
    dx3, gain2_grad, shift2_grad = norm2_back(cotangent)
    outer_bias_grad = jnp.sum(dx3, axis=0)
    d_out = dx3.astype(half_type)
    shrink_grad = jnp.einsum("tf,td->fd", hidden_half, d_out, preferred_element_type=full_type)
    d_hidden = jnp.einsum("td,fd->tf", d_out, w_shrink, preferred_element_type=full_type)
    d_inner = gelu_inner_back(d_hidden)[0]
    unit_grad = jnp.sum(d_inner, axis=0)
    d_inner_half = d_inner.astype(half_type)
    expand_grad = jnp.einsum("td,tf->df", h2_half, d_inner_half, preferred_element_type=full_type)
    dh2_part = jnp.einsum("tf,df->td", d_inner_half, w_expand, preferred_element_type=full_type)
    dh2 = dx3 + lax.psum(dh2_part.astype(jnp.bfloat16), "heads").astype(jnp.float32)
    dx2, gain1_grad, shift1_grad = norm1_back(dh2)
    branch_bias_grad = jnp.sum(dx2, axis=0)
    d_branch = dx2.astype(half_type)
    combine_grad = jnp.einsum("tc,td->cd", attended, d_branch, preferred_element_type=full_type)
    d_att = jnp.einsum("td,cd->tc", d_branch, w_combine, preferred_element_type=full_type).astype(
        half_type
    )
    d_att = d_att.reshape(rows, heads_local, HEAD)
    delta = jnp.transpose(jnp.sum(d_att.astype(full_type) * mixed, axis=-1))
    d_queries = jnp.zeros((rows, heads_local, HEAD), full_type)
    d_keys = jnp.zeros((rows, heads_local, HEAD), full_type)
    d_values = jnp.zeros((rows, heads_local, HEAD), full_type)
    for block_keys, block_values, key_seg, shift_by in key_blocks:

        def back_block(block_keys=block_keys, block_values=block_values, key_seg=key_seg):
            raw = score_rows(queries, block_keys, row_seg, key_seg)
            probs = jnp.exp(raw - lse[..., None])
            probs_half = probs.astype(half_type)
            d_probs = jnp.einsum(
                "thd,khd->htk", d_att, block_values, preferred_element_type=full_type
            )
            d_score = (probs * (d_probs - delta[..., None])).astype(half_type)
            query_part = jnp.einsum(
                "htk,khd->thd", d_score, block_keys, preferred_element_type=full_type
            )
            key_part = jnp.einsum(
                "htk,thd->khd", d_score, queries, preferred_element_type=full_type
            )
            value_part = jnp.einsum(
                "htk,thd->khd", probs_half, d_att, preferred_element_type=full_type
            )
            return (query_part, key_part, value_part)

        def no_block():
            empty = jnp.zeros((rows, heads_local, HEAD), full_type)
            return (empty, empty, empty)

        query_part, key_part, value_part = lax.cond(
            shares_rows(row_seg, key_seg), back_block, no_block
        )
        d_queries = d_queries + query_part
        if shift_by == 0:
            d_keys = key_part
            d_values = value_part
        else:
            back_keys, back_values = (
                passed_along(key_part.astype(jnp.bfloat16), "seq", -shift_by).astype(
                    key_part.dtype
                ),
                passed_along(value_part.astype(jnp.bfloat16), "seq", -shift_by).astype(
                    value_part.dtype
                ),
            )
            d_keys = d_keys + back_keys
            d_values = d_values + back_values
    dq_half = d_queries.reshape(rows, half).astype(half_type) * scale
    dk_half = d_keys.reshape(rows, half).astype(half_type)
    dv_half = d_values.reshape(rows, half).astype(half_type)
    stacked = jnp.stack([dq_half, dk_half, dv_half], axis=1)
    project_grad = jnp.einsum("td,tcf->dcf", h1_half, stacked, preferred_element_type=full_type)
    query_bias_grad = jnp.sum(dq_half.astype(full_type), axis=0)
    value_bias_grad = jnp.sum(dv_half.astype(full_type), axis=0)
    dh1_part = jnp.einsum("tcf,dcf->td", stacked, w_project, preferred_element_type=full_type)
    dh1 = dx2 + lax.psum(dh1_part.astype(jnp.bfloat16), "heads").astype(jnp.float32)
    dx1, gain0_grad, shift0_grad = norm0_back(dh1)
    d_spread = lax.dynamic_slice_in_dim(dx1, channel_start, half, 1)
    gelu_pre_back = jax.vjp(gelu_exact, pre)[1]
    d_conv = gelu_pre_back(d_spread)[0]
    conv_bias_grad = jnp.sum(d_conv, axis=0)
    d_conv_half = d_conv.astype(half_type).reshape(rows, groups, ingroup)
    kernel_parts = []
    d_padded = jnp.zeros((rows + taps, half), full_type)
    for start in range(0, taps, tap_group):
        valid = tap_valid(pad_seg, row_seg, start, tap_group, rows)
        window = tap_window(padded, valid, start, tap_group, rows, groups, ingroup)
        kernel_parts.append(
            jnp.einsum("jtgi,tgo->goij", window, d_conv_half, preferred_element_type=full_type)
        )
        spread_back = jnp.einsum(
            "tgo,goij->jtgi",
            d_conv_half,
            kernel4[..., start : start + tap_group],
            preferred_element_type=full_type,
        )
        spread_back = jnp.where(valid[:, :, None], spread_back.reshape(tap_group, rows, half), 0.0)
        for offset in range(tap_group):
            d_padded = d_padded.at[start + offset : start + offset + rows].add(spread_back[offset])
    kernel_grad = jnp.concatenate(kernel_parts, axis=3).reshape(half, ingroup, taps)
    d_input = d_padded[reach_taps : reach_taps + rows]
    rim_pairs = ((1, d_padded[rows + reach_taps :]), (-1, d_padded[:reach_taps]))
    for shift_by, rim in rim_pairs:
        arrived = passed_along(rim.astype(jnp.bfloat16), "seq", shift_by).astype(rim.dtype)
        if shift_by == 1:
            d_input = d_input.at[:reach_taps].add(arrived)
        else:
            d_input = d_input.at[rows - reach_taps :].add(arrived)
    frames_grad = dx1 + lax.all_gather(
        d_input.astype(jnp.bfloat16), "heads", axis=1, tiled=True
    ).astype(d_input.dtype)
    chan_grad = jnp.stack([conv_bias_grad, query_bias_grad, value_bias_grad])
    out_grad = jnp.stack([branch_bias_grad, outer_bias_grad])
    norm_grad = jnp.stack(
        [
            jnp.stack([gain0_grad, shift0_grad]),
            jnp.stack([gain1_grad, shift1_grad]),
            jnp.stack([gain2_grad, shift2_grad]),
        ]
    )
    (
        kernel_sum,
        project_sum,
        combine_sum,
        expand_sum,
        shrink_sum,
        unit_sum,
        chan_sum,
        out_sum,
        norm_sum,
    ) = (
        lax.psum_scatter(kernel_grad, "seq", scatter_dimension=2, tiled=True),
        lax.psum_scatter(project_grad, "seq", scatter_dimension=0, tiled=True),
        lax.psum_scatter(combine_grad, "seq", scatter_dimension=1, tiled=True),
        lax.psum_scatter(expand_grad, "seq", scatter_dimension=0, tiled=True),
        lax.psum_scatter(shrink_grad, "seq", scatter_dimension=1, tiled=True),
        lax.psum_scatter(unit_grad, "seq", scatter_dimension=0, tiled=True),
        lax.psum_scatter(chan_grad, "seq", scatter_dimension=1, tiled=True),
        lax.psum_scatter(out_grad, "seq", scatter_dimension=1, tiled=True),
        lax.psum_scatter(norm_grad, "seq", scatter_dimension=2, tiled=True),
    )
    root = total**0.5
    small_rate = 0.1 / root
    unit_rate = 0.5 / root
    kernel_out = nesterov(
        kernel, kernel_sum, kernel_moment, kernel_average, (ingroup * taps) ** (-0.5) / root
    )
    project_out = nesterov(
        project, project_sum, project_moment, project_average, width ** (-0.5) / root
    )
    combine_out = nesterov(
        combine, combine_sum, combine_moment, combine_average, (width // 16) ** (-0.5) / root
    )
    expand_out = nesterov(expand, expand_sum, expand_moment, expand_average, width ** (-0.5) / root)
    shrink_out = nesterov(
        shrink, shrink_sum, shrink_moment, shrink_average, hidden_full ** (-0.5) / root
    )
    unit_out = nesterov(unitbias, unit_sum, unitbias_moment, unitbias_average, unit_rate)
    chan_out = nesterov(chanbias, chan_sum, chanbias_moment, chanbias_average, small_rate)
    outb_out = nesterov(outbias, out_sum, outbias_moment, outbias_average, small_rate)
    norm_out = nesterov(normparams, norm_sum, normparams_moment, normparams_average, small_rate)
    return (
        layer_out,
        frames_grad,
        kernel_out[0],
        kernel_out[1],
        kernel_out[2],
        kernel_out[3],
        kernel_out[4],
        project_out[0],
        project_out[1],
        project_out[2],
        project_out[3],
        project_out[4],
        combine_out[0],
        combine_out[1],
        combine_out[2],
        combine_out[3],
        combine_out[4],
        expand_out[0],
        expand_out[1],
        expand_out[2],
        expand_out[3],
        expand_out[4],
        shrink_out[0],
        shrink_out[1],
        shrink_out[2],
        shrink_out[3],
        shrink_out[4],
        unit_out[0],
        unit_out[1],
        unit_out[2],
        unit_out[3],
        unit_out[4],
        chan_out[0],
        chan_out[1],
        chan_out[2],
        chan_out[3],
        chan_out[4],
        outb_out[0],
        outb_out[1],
        outb_out[2],
        outb_out[3],
        outb_out[4],
        norm_out[0],
        norm_out[1],
        norm_out[2],
        norm_out[3],
        norm_out[4],
    )


def solution(mesh):
    return jax.shard_map(
        body,
        mesh=mesh,
        in_specs=(
            P("seq", None),
            P("seq", None),
            P(),
            P("heads", None, "seq"),
            P("heads", None, "seq"),
            P("heads", None, "seq"),
            P("seq", None, "heads"),
            P("seq", None, "heads"),
            P("seq", None, "heads"),
            P("heads", "seq"),
            P("heads", "seq"),
            P("heads", "seq"),
            P("seq", "heads"),
            P("seq", "heads"),
            P("seq", "heads"),
            P("heads", "seq"),
            P("heads", "seq"),
            P("heads", "seq"),
            P(("heads", "seq")),
            P(("heads", "seq")),
            P(("heads", "seq")),
            P(None, ("heads", "seq")),
            P(None, ("heads", "seq")),
            P(None, ("heads", "seq")),
            P(None, "seq"),
            P(None, "seq"),
            P(None, "seq"),
            P(None, None, "seq"),
            P(None, None, "seq"),
            P(None, None, "seq"),
        ),
        out_specs=(
            P("seq", None),
            P("seq", None),
            P("heads", None, "seq"),
            P("heads", None, "seq"),
            P("heads", None, "seq"),
            P("heads", None, "seq"),
            P("heads", None, "seq"),
            P("seq", None, "heads"),
            P("seq", None, "heads"),
            P("seq", None, "heads"),
            P("seq", None, "heads"),
            P("seq", None, "heads"),
            P("heads", "seq"),
            P("heads", "seq"),
            P("heads", "seq"),
            P("heads", "seq"),
            P("heads", "seq"),
            P("seq", "heads"),
            P("seq", "heads"),
            P("seq", "heads"),
            P("seq", "heads"),
            P("seq", "heads"),
            P("heads", "seq"),
            P("heads", "seq"),
            P("heads", "seq"),
            P("heads", "seq"),
            P("heads", "seq"),
            P(("heads", "seq")),
            P(("heads", "seq")),
            P(("heads", "seq")),
            P(("heads", "seq")),
            P(("heads", "seq")),
            P(None, ("heads", "seq")),
            P(None, ("heads", "seq")),
            P(None, ("heads", "seq")),
            P(None, ("heads", "seq")),
            P(None, ("heads", "seq")),
            P(None, "seq"),
            P(None, "seq"),
            P(None, "seq"),
            P(None, "seq"),
            P(None, "seq"),
            P(None, None, "seq"),
            P(None, None, "seq"),
            P(None, None, "seq"),
            P(None, None, "seq"),
            P(None, None, "seq"),
        ),
        check_vma=False,
    )
```

profile of v0, /device:TPU:0, one launch (start us, length us, event | category | flops | bytes accessed | tf_op | source)
XLA Modules:
  0.0 3429.2 jit_solution(15483977664293872958)
XLA Ops:
  19.2 23.1 all-gather
  273.9 18.5 all_gather.36
  315.9 21.2 all-gather.13.cloned.1.call-done
  362.1 43.2 %collective-permute-start.8 = (bf16[1024,6,64]{0,2,1:T(8,128)(2,1)}, bf16[1024,6,64]{0,2,1:T(8,128)(2,1)}, u32[]{:S(2)}, u32[]{:S(2)}) collective-permute-start(bf16[1024,6,64]{0,2,1:T(8,128)(2,1)} %add_convert_fusion.5), channel_id=1, source_target_pairs={{0,4},{2,6},{4,8},{6,10},{8,12},{10,14},{12,16},{14,18},{16,20},{1... | collective-permute-start | bytes 2359304 | tf_op jit(solution)/shard_map/ppermute | solution.py:34
  428.3 35.5 %all_gather.38 = bf16[384,768]{0,1:T(8,128)(2,1)} all-gather(bf16[384,48]{0,1:T(8,128)(2,1)S(1)} %convert_element_type.392), channel_id=1, replica_groups=mesh['seq'=16,'heads'=2] {'seq'}, dimensions={1}, use_global_device_ids=true | all-gather | bytes 626688 | tf_op jit(solution)/shard_map/all_gather | solution.py:125
  464.0 24.3 conditional.15
  488.3 24.2 conditional.17
  512.5 25.5 conditional.19
  553.8 20.0 conditional.22
  598.1 52.3 %all-gather.1 = bf16[16,48,2]{1,2,0:T(2,128)(2,1)S(1)} all-gather(bf16[1,48,2]{1,2,0:T(2,128)(2,1)S(1)} %convert_bitcast_fusion.1), channel_id=1, replica_groups=mesh['seq'=16,'heads'=2] {'seq'}, dimensions={0}, use_global_device_ids=true | all-gather | bytes 3264 | tf_op jit(solution)/shard_map/all_gather | solution.py:130
  652.1 30.2 all-reduce.1
  688.1 37.3 %all-gather.15.cloned.1.call-done = bf16[768,1536]{1,0:T(8,128)(2,1)} async-done(((bf16[48,1536]{1,0:T(8,128)(2,1)}), bf16[768,1536]{1,0:T(8,128)(2,1)}) %all-gather.15.cloned.1.call-update) | async-done | bytes 2359312 | tf_op jit(solution)/shard_map/all_gather | solution.py:126
  725.4 19.8 multiply_convert_fusion.5
  745.2 24.3 all-gather.17.cloned.1.call-done
  776.2 50.2 %all-reduce.12.cloned.1.call-done = bf16[1024,768]{1,0:T(8,128)(2,1)} async-done(((bf16[1024,768]{1,0:T(8,128)(2,1)}), bf16[1024,768]{1,0:T(8,128)(2,1)}) %all-reduce.12.cloned.1.call-update) | async-done | bytes 1572880 | tf_op jit(solution)/shard_map/psum | solution.py:218
  850.6 51.6 %all-reduce.14.cloned.1.call-done = bf16[1024,768]{1,0:T(8,128)(2,1)} async-done(((bf16[1024,768]{1,0:T(8,128)(2,1)}), bf16[1024,768]{1,0:T(8,128)(2,1)}) %all-reduce.14.cloned.1.call-update) | async-done | bytes 1572880 | tf_op jit(solution)/shard_map/psum | solution.py:233
  912.2 58.1 %conditional.29 = (f32[1024,6,64]{0,2,1:T(8,128)}, f32[1024,6,64]{0,2,1:T(8,128)S(1)}, f32[1024,6,64]{0,2,1:T(8,128)}) conditional(s32[]{:T(128)} %convert_element_type.379, () %tuple.664, (s32[1024]{0:T(1024)S(1)}, s32[1024]{0:T(1024)S(1)}, bf16[1024,6,64]{0,2,1:T(8,128)(2,1)S(1)}, bf16[1024,6,64]{0,2,1:T(8,128)(2,1)}, f32[6,1024]{1,0:T(8,128)S(1)}, ...), branch_computations={%region_69.70_spmd, %region_70.71_spmd} | conditional | flops 4077912064 | bytes 141377696 | solution.py:271
  991.1 57.9 %conditional.27 = (f32[1024,6,64]{0,2,1:T(8,128)}, f32[1024,6,64]{0,2,1:T(8,128)}, f32[1024,6,64]{0,2,1:T(8,128)}) conditional(s32[]{:T(128)} %convert_element_type.385, () %tuple.660, (s32[1024]{0:T(1024)S(1)}, s32[1024]{0:T(1024)S(1)}, bf16[1024,6,64]{0,2,1:T(8,128)(2,1)S(1)}, bf16[1024,6,64]{0,2,1:T(8,128)(2,1)S(1)}, f32[6,1024]{1,0:T(8,128)S(1)}, ...), branch_computations={%region_65.66_spmd, %region_66.67_spmd} | conditional | flops 4077912064 | bytes 134037584 | solution.py:271
  1071.7 52.4 %collective-permute-start.13 = (bf16[1024,6,64]{0,2,1:T(8,128)(2,1)}, bf16[1024,6,64]{0,2,1:T(8,128)(2,1)}, u32[]{:S(2)}, u32[]{:S(2)}) collective-permute-start(bf16[1024,6,64]{0,2,1:T(8,128)(2,1)} %convert_element_type.419), channel_id=1, source_target_pairs={{0,4},{2,6},{4,8},{6,10},{8,12},{10,14},{12,16},{14,18},{16,20},{1... | collective-permute-start | bytes 2359304 | tf_op jit(solution)/shard_map/ppermute | solution.py:34
  1131.4 57.5 %conditional.25 = (f32[1024,6,64]{0,2,1:T(8,128)}, f32[1024,6,64]{0,2,1:T(8,128)S(1)}, f32[1024,6,64]{0,2,1:T(8,128)}) conditional(s32[]{:T(128)} %convert_element_type.372, () %tuple.656, (s32[1024]{0:T(1024)S(1)}, bf16[1024,6,64]{0,2,1:T(8,128)(2,1)S(1)}, bf16[1024,6,64]{0,2,1:T(8,128)(2,1)}, f32[6,1024]{1,0:T(8,128)S(1)}, ...), branch_computations={%region_61.62_spmd, %region_62.63_spmd} | conditional | flops 4077912064 | bytes 135082080 | solution.py:271
  1231.6 50.4 %all-reduce.16.cloned.1.call-done = bf16[1024,768]{1,0:T(8,128)(2,1)} async-done(((bf16[1024,768]{1,0:T(8,128)(2,1)}), bf16[1024,768]{1,0:T(8,128)(2,1)}) %all-reduce.16.cloned.1.call-update) | async-done | bytes 1572880 | tf_op jit(solution)/shard_map/psum | solution.py:297
  1304.8 17.8 copy.563
  1322.5 24.7 copy.564
  1498.1 17.9 copy.566
  1516.0 24.6 copy.567
  1540.6 17.5 broadcast_select_fusion.6
  1702.2 17.7 copy.569
  1719.9 24.6 copy.570
  1744.5 17.5 broadcast_select_fusion.5
  1906.3 17.7 copy.572
  1924.0 24.6 copy.573
  1948.7 17.5 broadcast_select_fusion.4
  2110.2 17.7 copy.575
  2127.9 24.6 copy.576
  2152.6 17.9 broadcast_select_fusion.3
  2314.5 17.7 copy.578
  2332.2 24.6 copy.579
  2356.8 17.5 broadcast_select_fusion.2
  2518.6 17.7 copy.581
  2536.3 24.6 copy.582
  2560.9 17.5 broadcast_select_fusion.1
  2721.6 17.7 copy.584
  2739.3 24.6 copy.585
  2764.0 17.5 broadcast_select_fusion
  3127.6 46.3 %concatenate.405 = f32[8,48,48,128]{3,2,1,0:T(8,128)} concatenate(f32[8,48,48,16]{3,2,1,0:T(8,128)} %copy.594, f32[8,48,48,16]{3,2,1,0:T(8,128)} %copy.595, f32[8,48,48,16]{3,2,1,0:T(8,128)} %copy.596, f32[8,48,48,16]{3,2,1,0:T(8,128)} %copy.597, f32[8,48,48,16]{3,2,1,0:T(8,128)} %copy.598, f32[8,48,48,16]{3,2,1,0:T(8,128)} %copy.599, f32[8,48,48,16]{3,2,1,0:T(8,128)} %copy.600, ...), dimensions={3} | concatenate | bytes 18874368 | tf_op jit(solution)/shard_map/concatenate | solution.py:321
  3188.3 63.6 %all-reduce.4 = (f32[1536]{0:T(1024)S(1)}, f32[3,384]{1,0:T(4,128)S(1)}) all-reduce(f32[1536]{0:T(1024)S(1)} %copy-done.172, f32[3,384]{1,0:T(4,128)S(1)} %pad_maximum_fusion.6), channel_id=7, replica_groups=mesh['seq'=16,'heads'=2] {'seq'}, use_global_device_ids=true, to_apply=%region_80.81.clone | all-reduce | flops 2688 | bytes 21504
  3267.5 34.3 %reduce-scatter.15.cloned.1.call-done = f32[48,3,384]{2,0,1:T(8,128)} async-done(((f32[768,3,384]{2,0,1:T(8,128)}), f32[48,3,384]{2,0,1:T(8,128)}) %reduce-scatter.15.cloned.1.call-update) | async-done | bytes 221200 | tf_op jit(solution)/shard_map/reduce_scatter | solution.py:354
  3304.3 111.8 %reduce-scatter.13.cloned.1.call-done = f32[384,48,8]{0,1,2:T(8,128)} async-done(((f32[384,48,128]{0,1,2:T(8,128)}), f32[384,48,8]{0,1,2:T(8,128)}) %reduce-scatter.13.cloned.1.call-update) | async-done | bytes 589840 | tf_op jit(solution)/shard_map/reduce_scatter | solution.py:353
  (1271 shorter events, 2194.7 us)
Async XLA Ops:
  7.2 182.1 %all-gather.9.cloned.1.call-start = ((), (), s32[]{:S(2)}) async-start(), calls=%async_computation.7 | async-start | bytes 5013504 | tf_op jit(solution)/shard_map/all_gather | solution.py:123
  9.2 303.4 %all-gather.11.cloned.1.call-start = ((), (), s32[]{:S(2)}) async-start(), calls=%async_computation.8 | async-start | bytes 2359296 | tf_op jit(solution)/shard_map/all_gather | solution.py:163
  11.2 34.9 %collective-permute-start.1 = (bf16[64,384]{0,1:T(8,128)(2,1)S(1)}, bf16[64,384]{0,1:T(8,128)(2,1)S(1)}, u32[]{:S(2)}, u32[]{:S(2)}) collective-permute-start(bf16[64,384]{0,1:T(8,128)(2,1)S(1)} %get-tuple-element.2529), channel_id=1, source_target_pairs={{2,0},{4,2},{6,4},{8,6},{10,8},{12,10},{14,12},{16,14},{18,16},{20... | collective-permute-start | bytes 147464 | tf_op jit(solution)/shard_map/ppermute | solution.py:24
  12.5 40.9 %collective-permute-start = (bf16[64,384]{0,1:T(8,128)(2,1)S(1)}, bf16[64,384]{0,1:T(8,128)(2,1)S(1)}, u32[]{:S(2)}, u32[]{:S(2)}) collective-permute-start(bf16[64,384]{0,1:T(8,128)(2,1)S(1)} %get-tuple-element.2528), channel_id=1, source_target_pairs={{0,2},{2,4},{4,6},{6,8},{8,10},{10,12},{12,14},{14,16},{16,18},{18... | collective-permute-start | bytes 147464 | tf_op jit(solution)/shard_map/ppermute | solution.py:22
  45.5 178.7 %copy-start.116 = (pred[16,1024]{1,0:T(8,128)(4,1)}, pred[16,1024]{1,0:T(8,128)(4,1)S(1)}, u32[]{:S(2)}) copy-start(pred[16,1024]{1,0:T(8,128)(4,1)S(1)} %stack.1260) | copy-start | bytes 49156
  45.7 185.9 %copy-start.119 = (pred[16,1024]{1,0:T(8,128)(4,1)}, pred[16,1024]{1,0:T(8,128)(4,1)S(1)}, u32[]{:S(2)}) copy-start(pred[16,1024]{1,0:T(8,128)(4,1)S(1)} %stack.1226) | copy-start | bytes 49156
  45.8 192.9 %copy-start.122 = (pred[16,1024]{1,0:T(8,128)(4,1)}, pred[16,1024]{1,0:T(8,128)(4,1)S(1)}, u32[]{:S(2)}) copy-start(pred[16,1024]{1,0:T(8,128)(4,1)S(1)} %stack.1192) | copy-start | bytes 49156
  45.9 199.9 %copy-start.127 = (pred[16,1024]{1,0:T(8,128)(4,1)}, pred[16,1024]{1,0:T(8,128)(4,1)S(1)}, u32[]{:S(2)}) copy-start(pred[16,1024]{1,0:T(8,128)(4,1)S(1)} %stack.1158) | copy-start | bytes 49156
  46.1 207.0 %copy-start.125 = (pred[16,1024]{1,0:T(8,128)(4,1)}, pred[16,1024]{1,0:T(8,128)(4,1)S(1)}, u32[]{:S(2)}) copy-start(pred[16,1024]{1,0:T(8,128)(4,1)S(1)} %stack.1396) | copy-start | bytes 49156
  269.1 68.0 %all-gather.13.cloned.1.call-start = ((), (), s32[]{:S(2)}) async-start(), calls=%async_computation.9 | async-start | bytes 1880064 | tf_op jit(solution)/shard_map/all_gather | solution.py:124
  269.9 412.5 %all-reduce.10.cloned.1.call-start = ((), (), s32[]{:S(2)}) async-start(), calls=%async_computation.10 | async-start | bytes 3145728 | tf_op jit(solution)/shard_map/psum | solution.py:210
  293.4 258.8 %copy-start.105 = (s32[1024]{0:T(1024)}, s32[1024]{0:T(1024)S(1)}, u32[]{:S(2)}) copy-start(s32[1024]{0:T(1024)S(1)} %get-tuple-element.2371) | copy-start | bytes 12292
  296.7 257.2 %copy-start.101 = (s32[1024]{0:T(1024)}, s32[1024]{0:T(1024)S(1)}, u32[]{:S(2)}) copy-start(s32[1024]{0:T(1024)S(1)} %get-tuple-element.2370) | copy-start | bytes 12292
  342.2 19.9 collective-permute-start.2
  344.4 60.9 %collective-permute-start.3 = (bf16[1024,6,64]{0,2,1:T(8,128)(2,1)}, bf16[1024,6,64]{0,2,1:T(8,128)(2,1)S(1)}, u32[]{:S(2)}, u32[]{:S(2)}) collective-permute-start(bf16[1024,6,64]{0,2,1:T(8,128)(2,1)} %bitcast.175), channel_id=1, source_target_pairs={{2,0},{4,2},{6,4},{8,6},{10,8},{12,10},{14,12},{16,14},{18,16},{20... | collective-permute-start | bytes 2359304 | tf_op jit(solution)/shard_map/ppermute | solution.py:34
  345.7 71.8 %collective-permute-start.4 = (bf16[1024,6,64]{0,2,1:T(8,128)(2,1)}, bf16[1024,6,64]{0,2,1:T(8,128)(2,1)S(1)}, u32[]{:S(2)}, u32[]{:S(2)}) collective-permute-start(bf16[1024,6,64]{0,2,1:T(8,128)(2,1)} %bitcast.175), channel_id=1, source_target_pairs={{0,4},{2,6},{4,8},{6,10},{8,12},{10,14},{12,16},{14,18},{16,20},{1... | collective-permute-start | bytes 2359304 | tf_op jit(solution)/shard_map/ppermute | solution.py:34
  351.0 235.2 %copy-start.103 = (s32[1024]{0:T(1024)}, s32[1024]{0:T(1024)S(1)}, u32[]{:S(2)}) copy-start(s32[1024]{0:T(1024)S(1)} %get-tuple-element.2369) | copy-start | bytes 12292
  356.3 156.2 %collective-permute-start.5 = (bf16[1024,6,64]{0,2,1:T(8,128)(2,1)}, bf16[1024,6,64]{0,2,1:T(8,128)(2,1)}, u32[]{:S(2)}, u32[]{:S(2)}) collective-permute-start(bf16[1024,6,64]{0,2,1:T(8,128)(2,1)} %bitcast.175), channel_id=1, source_target_pairs={{4,0},{6,2},{8,4},{10,6},{12,8},{14,10},{16,12},{18,14},{20,16},{2... | collective-permute-start | bytes 2359304 | tf_op jit(solution)/shard_map/ppermute | solution.py:34
  360.8 178.1 %collective-permute-start.9 = (bf16[1024,6,64]{0,2,1:T(8,128)(2,1)}, bf16[1024,6,64]{0,2,1:T(8,128)(2,1)}, u32[]{:S(2)}, u32[]{:S(2)}) collective-permute-start(bf16[1024,6,64]{0,2,1:T(8,128)(2,1)} %add_convert_fusion.5), channel_id=1, source_target_pairs={{4,0},{6,2},{8,4},{10,6},{12,8},{14,10},{16,12},{18,14},{20,16},{2... | collective-permute-start | bytes 2359304 | tf_op jit(solution)/shard_map/ppermute | solution.py:34
  362.1 224.2 %copy-start.15 = (bf16[1024,6,64]{0,2,1:T(8,128)(2,1)}, bf16[1024,6,64]{0,2,1:T(8,128)(2,1)S(1)}, u32[]{:S(2)}) copy-start(bf16[1024,6,64]{0,2,1:T(8,128)(2,1)S(1)} %collective-permute-done.2) | copy-start | bytes 2359300
  362.1 190.2 %collective-permute-start.8 = (bf16[1024,6,64]{0,2,1:T(8,128)(2,1)}, bf16[1024,6,64]{0,2,1:T(8,128)(2,1)}, u32[]{:S(2)}, u32[]{:S(2)}) collective-permute-start(bf16[1024,6,64]{0,2,1:T(8,128)(2,1)} %add_convert_fusion.5), channel_id=1, source_target_pairs={{0,4},{2,6},{4,8},{6,10},{8,12},{10,14},{12,16},{14,18},{16,20},{1... | collective-permute-start | bytes 2359304 | tf_op jit(solution)/shard_map/ppermute | solution.py:34
  405.3 148.5 %collective-permute-start.7 = (bf16[1024,6,64]{0,2,1:T(8,128)(2,1)}, bf16[1024,6,64]{0,2,1:T(8,128)(2,1)}, u32[]{:S(2)}, u32[]{:S(2)}) collective-permute-start(bf16[1024,6,64]{0,2,1:T(8,128)(2,1)} %add_convert_fusion.5), channel_id=1, source_target_pairs={{2,0},{4,2},{6,4},{8,6},{10,8},{12,10},{14,12},{16,14},{18,16},{20... | collective-permute-start | bytes 2359304 | tf_op jit(solution)/shard_map/ppermute | solution.py:34
  417.4 168.8 %collective-permute-start.6 = (bf16[1024,6,64]{0,2,1:T(8,128)(2,1)}, bf16[1024,6,64]{0,2,1:T(8,128)(2,1)}, u32[]{:S(2)}, u32[]{:S(2)}) collective-permute-start(bf16[1024,6,64]{0,2,1:T(8,128)(2,1)} %add_convert_fusion.5), channel_id=1, source_target_pairs={{0,2},{2,4},{4,6},{6,8},{8,10},{10,12},{12,14},{14,16},{16,18},{18... | collective-permute-start | bytes 2359304 | tf_op jit(solution)/shard_map/ppermute | solution.py:34
  596.4 129.0 %all-gather.15.cloned.1.call-start = ((), (), s32[]{:S(2)}) async-start(), calls=%async_computation.11 | async-start | bytes 2506752 | tf_op jit(solution)/shard_map/all_gather | solution.py:126
  597.2 172.3 %all-gather.17.cloned.1.call-start = ((), (), s32[]{:S(2)}) async-start(), calls=%async_computation.12 | async-start | bytes 2506752 | tf_op jit(solution)/shard_map/all_gather | solution.py:127
  598.0 228.4 %all-reduce.12.cloned.1.call-start = ((), (), s32[]{:S(2)}) async-start(), calls=%async_computation.13 | async-start | bytes 3145728 | tf_op jit(solution)/shard_map/psum | solution.py:218
  685.9 221.2 %copy-start.85 = (f32[1024]{0:T(1024)}, f32[1024]{0:T(1024)S(1)}, u32[]{:S(2)}) copy-start(f32[1024]{0:T(1024)S(1)} %broadcast_multiply_fusion.1) | copy-start | bytes 12292
  688.1 219.1 %copy-start.99 = (f32[1024]{0:T(1024)}, f32[1024]{0:T(1024)S(1)}, u32[]{:S(2)}) copy-start(f32[1024]{0:T(1024)S(1)} %fusion.444) | copy-start | bytes 12292
  775.9 126.3 %all-reduce.14.cloned.1.call-start = ((), (), s32[]{:S(2)}) async-start(), calls=%async_computation.14 | async-start | bytes 3145728 | tf_op jit(solution)/shard_map/psum | solution.py:233
  850.6 431.4 %all-reduce.16.cloned.1.call-start = ((), (), s32[]{:S(2)}) async-start(), calls=%async_computation.15 | async-start | bytes 3145728 | tf_op jit(solution)/shard_map/psum | solution.py:297
  972.7 216.2 %collective-permute-start.17 = (bf16[1024,6,64]{0,2,1:T(8,128)(2,1)}, bf16[1024,6,64]{0,2,1:T(8,128)(2,1)}, u32[]{:S(2)}, u32[]{:S(2)}) collective-permute-start(bf16[1024,6,64]{0,2,1:T(8,128)(2,1)} %convert_element_type.429), channel_id=1, source_target_pairs={{0,4},{2,6},{4,8},{6,10},{8,12},{10,14},{12,16},{14,18},{16,20},{1... | collective-permute-start | bytes 2359304 | tf_op jit(solution)/shard_map/ppermute | solution.py:34
  989.8 200.5 %collective-permute-start.16 = (bf16[1024,6,64]{0,2,1:T(8,128)(2,1)}, bf16[1024,6,64]{0,2,1:T(8,128)(2,1)}, u32[]{:S(2)}, u32[]{:S(2)}) collective-permute-start(bf16[1024,6,64]{0,2,1:T(8,128)(2,1)} %convert_element_type.427), channel_id=1, source_target_pairs={{4,0},{6,2},{8,4},{10,6},{12,8},{14,10},{16,12},{18,14},{20,16},{2... | collective-permute-start | bytes 2359304 | tf_op jit(solution)/shard_map/ppermute | solution.py:34
  1051.5 140.9 %collective-permute-start.15 = (bf16[1024,6,64]{0,2,1:T(8,128)(2,1)}, bf16[1024,6,64]{0,2,1:T(8,128)(2,1)}, u32[]{:S(2)}, u32[]{:S(2)}) collective-permute-start(bf16[1024,6,64]{0,2,1:T(8,128)(2,1)} %convert_element_type.425), channel_id=1, source_target_pairs={{0,2},{2,4},{4,6},{6,8},{8,10},{10,12},{12,14},{14,16},{16,18},{18... | collective-permute-start | bytes 2359304 | tf_op jit(solution)/shard_map/ppermute | solution.py:34
  1069.4 129.4 %collective-permute-start.14 = (bf16[1024,6,64]{0,2,1:T(8,128)(2,1)}, bf16[1024,6,64]{0,2,1:T(8,128)(2,1)}, u32[]{:S(2)}, u32[]{:S(2)}) collective-permute-start(bf16[1024,6,64]{0,2,1:T(8,128)(2,1)} %convert_element_type.423), channel_id=1, source_target_pairs={{2,0},{4,2},{6,4},{8,6},{10,8},{12,10},{14,12},{16,14},{18,16},{20... | collective-permute-start | bytes 2359304 | tf_op jit(solution)/shard_map/ppermute | solution.py:34
  1071.7 132.0 %collective-permute-start.13 = (bf16[1024,6,64]{0,2,1:T(8,128)(2,1)}, bf16[1024,6,64]{0,2,1:T(8,128)(2,1)}, u32[]{:S(2)}, u32[]{:S(2)}) collective-permute-start(bf16[1024,6,64]{0,2,1:T(8,128)(2,1)} %convert_element_type.419), channel_id=1, source_target_pairs={{0,4},{2,6},{4,8},{6,10},{8,12},{10,14},{12,16},{14,18},{16,20},{1... | collective-permute-start | bytes 2359304 | tf_op jit(solution)/shard_map/ppermute | solution.py:34
  1188.9 20.2 collective-permute-start.12
  1190.2 18.9 collective-permute-start.11
  1192.5 16.6 collective-permute-start.10
  1217.5 1968.6 %reduce-scatter.17.cloned.1.call-start = ((), (), s32[]{:S(2)}) async-start(), calls=%async_computation.19 | async-start | bytes 1253376 | tf_op jit(solution)/shard_map/reduce_scatter | solution.py:355
  1230.9 2023.4 %reduce-scatter.23.cloned.1.call-start = ((), (), s32[]{:S(2)}) async-start(), calls=%async_computation.22 | async-start | bytes 417792
  2921.7 8.4 collective-permute-start.18
  2923.4 7.3 collective-permute-start.19
  2925.7 330.5 %reduce-scatter.25.cloned.1.call-start = ((), (), s32[]{:S(2)}) async-start(), calls=%async_computation.23 | async-start | bytes 417792
  2930.0 328.4 %all-gather.19.cloned.1.call-start = ((), (), s32[]{:S(2)}) async-start(), calls=%async_computation.16 | async-start | bytes 2359296 | tf_op jit(solution)/shard_map/all_gather | solution.py:330
  2934.6 327.4 %reduce-scatter.19.cloned.1.call-start = ((), (), s32[]{:S(2)}) async-start(), calls=%async_computation.20 | async-start | bytes 5013504 | tf_op jit(solution)/shard_map/reduce_scatter | solution.py:356
  2942.7 322.1 %reduce-scatter.21.cloned.1.call-start = ((), (), s32[]{:S(2)}) async-start(), calls=%async_computation.21 | async-start | bytes 5013504 | tf_op jit(solution)/shard_map/reduce_scatter | solution.py:357
  2951.3 350.5 %reduce-scatter.15.cloned.1.call-start = ((), (), s32[]{:S(2)}) async-start(), calls=%async_computation.18 | async-start | bytes 3760128 | tf_op jit(solution)/shard_map/reduce_scatter | solution.py:354
  2959.1 457.0 %reduce-scatter.13.cloned.1.call-start = ((), (), s32[]{:S(2)}) async-start(), calls=%async_computation.17 | async-start | bytes 10027008 | tf_op jit(solution)/shard_map/reduce_scatter | solution.py:353
  (190 other events, 4599.1 us)
Sparse Core Ops, SparseCore 0:
  10.9 56.0 all-gather.8
  269.2 24.5 all-gather.10
  296.7 40.3 all-gather.12
  596.5 83.5 all-reduce.9
  683.0 42.3 all-gather.14
  728.4 41.0 all-gather.16
  776.0 50.2 all-reduce.11
  850.7 51.4 all-reduce.13
  1217.6 64.3 all-reduce.15
  1286.0 58.0 reduce-scatter.16
  2925.9 58.1 reduce-scatter.22
  2988.4 54.5 reduce-scatter.24
  3044.5 26.2 all-gather.18
  3075.1 75.5 reduce-scatter.18
  3155.4 74.8 reduce-scatter.20
  3234.7 67.0 reduce-scatter.14
  3305.7 110.3 reduce-scatter.12
where the time goes:
time: 3420 us; the launch traced here: 3430 us
  local copies, waits for them, and re-layouts  1380 us (40%)
  other arithmetic  661 us (19%)
  matrix products  567 us (17%)
  waiting for transfers between devices  398 us (12%)
  blocking collectives  223 us (7%)
  starting transfers between devices  139 us (4%)
  between operations  34.7 us (1%)
    scatter-add x113, local copies, waits for them, and re-layouts, body(): d_padded.at[start + offset:start + offset + rows].add(spread_back[offset])  732 us
    add x112, other arithmetic, body(): d_padded.at[start + offset:start + offset + rows].add(spread_back[offset])  307 us
    reshape x8, local copies, waits for them, and re-layouts, body(): spread_back.reshape(tap_group, rows, half)  197 us
    transpose x8, local copies, waits for them, and re-layouts, body(): jnp.einsum('tgo,goij->jtgi', d_conv_half, kernel4[..., start:start + tap_...  142 us
    ppermute x18, starting transfers between devices, passed_along(): return lax.ppermute(block, axis, route)  134 us
    select_n x8, other arithmetic, body(): jnp.where(valid[:, :, None], spread_back.reshape(tap_group, rows, half),...  132 us
    unnamed x522, local copies, waits for them, and re-layouts  130 us
    reduce_scatter x1, waiting for transfers between devices, body(): lax.psum_scatter(kernel_grad, 'seq', scatter_dimension=2, tiled=True)  112 us
  transfers between devices with their start and end apart: 37, of which 10 were waited for; matrix products, arithmetic and copies ran while one was open for 69% of the time, Pallas kernels for 0%

commit v1 on v0

v1 whole, which is shorter than its diff:
```python
import functools

import jax
import jax.numpy as jnp
from jax import lax
from jax.experimental import pallas as pl
from jax.experimental.pallas import tpu as pltpu
from jax.sharding import PartitionSpec as P

HEAD = 64
EPSILON = 1e-05

bf16, f32, i32 = jnp.bfloat16, jnp.float32, jnp.int32
CG, TAPS, GROUPS, HALO = 48, 128, 8, 64
ROWS, WIN, HALF = 1024, 1152, 384
CM, XM = 272, 304
NQ = 33
LCAP = 1408
PJ = 134
VLIM = 58 << 20


def iota(shape, dim):
    return lax.broadcasted_iota(i32, shape, dim)


def block_plan(starts, ends, first):
    w0 = first - HALO
    b = jnp.clip(starts - w0, 0, WIN)
    e = jnp.clip(ends - w0, 0, WIN)
    nblk = (e - b + 3) // 4
    n = starts.shape[0]
    before = jnp.arange(n)[None, :] < jnp.arange(n)[:, None]
    bs = jnp.sum(jnp.where(before, nblk[None, :], 0), axis=1).astype(i32)
    bs = bs + (jnp.clip(-w0, 0, WIN) + 3) // 4
    w = jnp.arange(WIN, dtype=i32)
    inside = (b[None, :] <= w[:, None]) & (w[:, None] < e[None, :])
    p = jnp.sum(jnp.where(inside, 4 * bs - b + w[:, None] + 1, 0), axis=1).astype(i32) - 1
    m = jnp.arange(LCAP, dtype=i32)
    hit = (bs[None, :] <= m[:, None]) & (m[:, None] < (bs + nblk)[None, :])
    bseg = jnp.sum(jnp.where(hit, jnp.arange(1, n + 1, dtype=i32)[None, :], 0), axis=1).astype(i32) - 1
    chunks = jnp.maximum((p[HALO + ROWS - 1] // 4 - 16) // CM + 1, 1)
    return (
        jnp.reshape(chunks, (1,)).astype(i32),
        jnp.broadcast_to(p[None, :], (8, WIN)),
        jnp.broadcast_to(p[:, None], (WIN, 128)),
        jnp.broadcast_to(bseg[:, None], (LCAP, 128)),
    )


def select_pair(h, rows, base):
    lane = iota((rows, 256), 1)
    src = CG * (2 * h + (lane >> 7)) + (lane & 63) - base
    ok = ((lane & 63) < CG) & (iota((rows, 256), 0) == src)
    return jnp.where(ok, 1.0, 0.0).astype(bf16)


def build_selector(s_ref, prow, c, first, rows):
    for t in range(4):
        pos = 4 * (iota((rows, prow.shape[1]), 0) + (CM * c + first)) + t
        s_ref[t] = jnp.where(pos == prow, 1.0, 0.0).astype(bf16)


def build_blocks(s_ref, dup, rows):
    y = [
        jnp.dot(s_ref[t], dup, preferred_element_type=f32).astype(bf16) for t in range(4)
    ]
    low = iota((rows, 128), 1) < 64
    out = []
    for g in range(2):
        tiles = [v[:, 128 * g : 128 * g + 128] for v in y]
        out.append(
            jnp.concatenate(
                [jnp.where(low, tiles[0], tiles[1]), jnp.where(low, tiles[2], tiles[3])], axis=1
            )
        )
    return out


def build_taps(k_ref, sel, p_ref, base_tile):
    p_ref[...] = jnp.zeros_like(p_ref)
    step = 16
    for j0 in range(0, TAPS, step):
        part = k_ref[pl.ds(j0, step), :, pl.ds(pl.multiple_of(base_tile * 128, 128), 256)]
        d = jnp.dot(part.reshape(step * CG, 256), sel, preferred_element_type=f32)
        d = d.astype(bf16).reshape(step, CG, 256)
        for g in range(2):
            p_ref[g, pl.ds(j0 + 2, step), 0:CG, 0:64] = d[:, :, 128 * g : 128 * g + 64]
            p_ref[g, pl.ds(j0 + 3, step), 0:CG, 64:128] = d[:, :, 128 * g + 64 : 128 * g + 128]


def conv_kernel(
    back, chunks_ref, prow_ref, pcol_ref, bseg_ref, x_ref, k_ref, out_ref, s_ref, mask_ref, p_ref, xb_ref
):
    h = pl.program_id(0)
    base_tile = h // 2
    chunks = chunks_ref[0]

    @pl.when(h == 0)
    def _():
        out_ref[...] = jnp.zeros_like(out_ref)

    sel = select_pair(h, 256, 128 * base_tile)
    build_taps(k_ref, sel, p_ref, base_tile)
    lanes = pl.ds(pl.multiple_of(base_tile * 128, 128), 256)
    dup = jnp.dot(x_ref[:, lanes], sel, preferred_element_type=f32).astype(bf16)

    def chunk(c, carry):
        @pl.when((h == 0) | (chunks > 1))
        def _():
            build_selector(s_ref, prow_ref[0:1, :], c, 0, XM)
            seg = bseg_ref[pl.ds(pl.multiple_of(CM * c, 16), XM), :]
            for q in range(NQ):
                same = seg[q : q + CM] == seg[16 : 16 + CM]
                mask_ref[q] = jnp.where(same, 1.0, 0.0).astype(bf16)

        xb = build_blocks(s_ref, dup, XM)
        for g in range(2):
            xb_ref[g] = xb[g]
        pcol = pcol_ref[pl.ds(HALO, ROWS), :]
        local = (pcol >> 2) - (16 + CM * c)
        place = jnp.where(
            jnp.concatenate([local] * 3, axis=1)[:, :CM] == iota((ROWS, CM), 1), 1.0, 0.0
        ).astype(bf16)
        phase = pcol & 3
        hi = iota((ROWS, 128), 1) >> 6
        pick = jnp.concatenate([phase == hi, phase == hi + 2], axis=1)
        total = jnp.zeros((ROWS, 256), f32)
        for g in range(2):
            acc = jnp.zeros((CM, 256), f32)
            for q in range(NQ):
                m = mask_ref[q]
                xs = xb_ref[g, q : q + CM, :] * jnp.concatenate([m, m], axis=1)
                if back:
                    a, b = 130 - 4 * q, 128 - 4 * q
                else:
                    a, b = 4 * q + 2, 4 * q
                w = jnp.concatenate(
                    [
                        p_ref[g, a : a + 4].reshape(256, 128),
                        p_ref[g, b : b + 4].reshape(256, 128),
                    ],
                    axis=1,
                )
                dims = (((1,), (1 if back else 0,)), ((), ()))
                acc = acc + lax.dot_general(xs, w, dims, preferred_element_type=f32)
            y = jnp.dot(place, acc.astype(bf16), preferred_element_type=f32)
            y = jnp.where(pick, y, 0.0).astype(bf16)
            lane = iota((256, 256), 1)
            row = iota((256, 256), 0) & 63
            fold = (row < CG) & (lane == CG * (2 * h + g) - 128 * base_tile + row)
            total = total + jnp.dot(
                y, jnp.where(fold, 1.0, 0.0).astype(bf16), preferred_element_type=f32
            )
        out_ref[:, lanes] += total
        return carry

    lax.fori_loop(0, chunks, chunk, 0)


def smem():
    return pl.BlockSpec(memory_space=pltpu.SMEM)


def whole(shape):
    return pl.BlockSpec(shape, lambda h: (0,) * len(shape))


def conv(plan, window, taps, back):
    chunks, prow, pcol, bseg = plan
    return pl.pallas_call(
        functools.partial(conv_kernel, back),
        grid=(4,),
        out_shape=jax.ShapeDtypeStruct((ROWS, HALF), f32),
        in_specs=[
            smem(),
            whole((8, WIN)),
            whole((WIN, 128)),
            whole((LCAP, 128)),
            whole((WIN, HALF)),
            whole((TAPS, CG, HALF)),
        ],
        out_specs=whole((ROWS, HALF)),
        scratch_shapes=[
            pltpu.VMEM((4, XM, WIN), bf16),
            pltpu.VMEM((NQ, CM, 128), bf16),
            pltpu.VMEM((2, PJ, 64, 128), bf16),
            pltpu.VMEM((2, XM, 256), bf16),
        ],
        compiler_params=pltpu.CompilerParams(vmem_limit_bytes=VLIM),
        cost_estimate=pl.CostEstimate(flops=30_000_000_000, bytes_accessed=9_000_000, transcendentals=0),
        name="conv_back" if back else "conv_forward",
    )(chunks, prow, pcol, bseg, window, taps)


def tap_grad_kernel(
    chunks_ref, prow_ref, bseg_ref, x_ref, d_ref, out_ref, s_ref, sd_ref, mask_ref, xt_ref, dp_ref, acc_ref
):
    h = pl.program_id(0)
    base_tile = h // 2
    chunks = chunks_ref[0]

    @pl.when(h == 0)
    def _():
        out_ref[...] = jnp.zeros_like(out_ref)
        dp_ref[...] = jnp.zeros_like(dp_ref)

    acc_ref[...] = jnp.zeros_like(acc_ref)
    sel = select_pair(h, 256, 128 * base_tile)
    lanes = pl.ds(pl.multiple_of(base_tile * 128, 128), 256)
    xdup = jnp.dot(x_ref[:, lanes], sel, preferred_element_type=f32).astype(bf16)
    ddup = jnp.dot(d_ref[:, lanes], sel, preferred_element_type=f32).astype(bf16)

    def chunk(c, carry):
        @pl.when((h == 0) | (chunks > 1))
        def _():
            build_selector(s_ref, prow_ref[0:1, :], c, 0, XM)
            build_selector(sd_ref, prow_ref[0:1, HALO : HALO + ROWS], c, 16, CM)
            seg = bseg_ref[pl.ds(pl.multiple_of(CM * c, 16), XM), :]
            none = jnp.full((32, 128), -7, i32)
            own = jnp.concatenate([none, seg[16 : 16 + CM], none], axis=0)
            for q in range(NQ):
                same = seg == own[32 - q : 32 - q + XM]
                mask_ref[q] = jnp.where(same, 1.0, 0.0).astype(bf16)

        xb = build_blocks(s_ref, xdup, XM)
        db = build_blocks(sd_ref, ddup, CM)
        for g in range(2):
            xt_ref[g] = xb[g].T
            dp_ref[g, 32 : 32 + CM, :] = db[g]
        for g in range(2):
            for q in range(NQ):
                m = mask_ref[q]
                ds = dp_ref[g, 32 - q : 32 - q + XM, :] * jnp.concatenate([m, m], axis=1)
                part = jnp.dot(xt_ref[g], ds, preferred_element_type=f32)
                acc_ref[g, 4 * q + 2 : 4 * q + 6] += part[:, 0:128].reshape(4, 64, 128)
                acc_ref[g, 4 * q : 4 * q + 4] += part[:, 128:256].reshape(4, 64, 128)
        return carry

    lax.fori_loop(0, chunks, chunk, 0)
    low = iota((1, 1, 128), 2) < 64
    row = iota((128, 256), 0)
    lane = iota((128, 256), 1)
    src = CG * (2 * h + (row >> 6)) + (row & 63) - 128 * base_tile
    back = jnp.where(((row & 63) < CG) & (lane == src), 1.0, 0.0).astype(bf16)
    step = 16
    for j0 in range(0, TAPS, step):
        now = [acc_ref[g, j0 + 2 : j0 + 2 + step, 0:CG, :] for g in range(2)]
        nxt = [acc_ref[g, j0 + 3 : j0 + 3 + step, 0:CG, :] for g in range(2)]
        here = jnp.where(low, now[0], nxt[1]).reshape(step * CG, 128)
        far = jnp.where(low, now[1], nxt[0]).reshape(step * CG, 128)
        both = (here + pltpu.roll(far, 64, 1)).astype(bf16)
        o = jnp.dot(both, back, preferred_element_type=f32).astype(bf16).reshape(step, CG, 256)
        out_ref[j0 : j0 + step, :, lanes] += o


def tap_grad(plan, window, d_conv):
    chunks, prow, pcol, bseg = plan
    return pl.pallas_call(
        tap_grad_kernel,
        grid=(4,),
        out_shape=jax.ShapeDtypeStruct((TAPS, CG, HALF), bf16),
        in_specs=[
            smem(),
            whole((8, WIN)),
            whole((LCAP, 128)),
            whole((WIN, HALF)),
            whole((ROWS, HALF)),
        ],
        out_specs=whole((TAPS, CG, HALF)),
        scratch_shapes=[
            pltpu.VMEM((4, XM, WIN), bf16),
            pltpu.VMEM((4, CM, ROWS), bf16),
            pltpu.VMEM((NQ, XM, 128), bf16),
            pltpu.VMEM((2, 256, XM), bf16),
            pltpu.VMEM((2, 32 + CM + 32, 256), bf16),
            pltpu.VMEM((2, PJ, 64, 128), f32),
        ],
        compiler_params=pltpu.CompilerParams(vmem_limit_bytes=VLIM),
        cost_estimate=pl.CostEstimate(flops=40_000_000_000, bytes_accessed=9_000_000, transcendentals=0),
        name="tap_gradient",
    )(chunks, prow, bseg, window, d_conv)
REACH = 1536
SPAN = ROWS + 2 * REACH
QT, KT = 256, 256
NEG = -1e30


def segment_count(ends, positions):
    return jnp.sum((ends[None, :] <= positions[:, None]).astype(i32), axis=1).astype(i32)

def attention_plan(starts, ends, first):
    w = first - REACH + jnp.arange(SPAN, dtype=i32)
    kseg = segment_count(ends, w)
    kseg = jnp.where(w < 0, -1, kseg)
    qseg = kseg[REACH : REACH + ROWS]
    edge = qseg.reshape(ROWS // QT, QT)
    n = jnp.arange(starts.shape[0], dtype=i32)
    head = jnp.sum(jnp.where(n[None] == edge[:, :1], starts[None], 0), axis=1) - (first - REACH)
    tail = jnp.sum(jnp.where(n[None] == edge[:, -1:], ends[None], 0), axis=1) - (first - REACH)
    lo = jnp.clip(head // KT, 0, SPAN // KT - 1)
    hi = jnp.clip((tail + KT - 1) // KT, 1, SPAN // KT)
    return (
        jnp.stack([lo, hi]).astype(i32),
        jnp.broadcast_to(qseg[None], (8, ROWS)),
        jnp.broadcast_to(kseg[:, None], (SPAN, 128)),
    )

def split_heads(a):
    low = iota(a.shape, 1) < 64
    zero = jnp.zeros((), a.dtype)
    return jnp.where(low, a, zero), jnp.where(low, zero, a)

def forward_kernel(range_ref, qseg_ref, kseg_ref, q_ref, k_ref, v_ref, o_ref, lse_ref, vt_ref, m_ref, l_ref, acc_ref):
    qi = pl.program_id(1)

    @pl.when(qi == 0)
    def _():
        def flip(t, carry):
            at = pl.ds(pl.multiple_of(t * KT, KT), KT)
            vt_ref[:, at] = v_ref[at, :].T
            return carry
        lax.fori_loop(range_ref[0, 0], range_ref[1, ROWS // QT - 1], flip, 0)

    qs = split_heads(q_ref[...])
    m_ref[...] = jnp.full_like(m_ref, NEG)
    l_ref[...] = jnp.zeros_like(l_ref)
    acc_ref[...] = jnp.zeros_like(acc_ref)

    def tile(t, carry):
        at = pl.ds(pl.multiple_of(t * KT, KT), KT)
        ks = kseg_ref[at, :]
        same = jnp.concatenate([ks] * (QT // 128), axis=1) == qseg_ref[0:1, :]
        k = k_ref[at, :]
        for e in range(2):
            s = lax.dot_general(k, qs[e], (((1,), (1,)), ((), ())), preferred_element_type=f32)
            s = jnp.where(same, s, NEG)
            m = m_ref[e : e + 1, :]
            new = jnp.maximum(m, jnp.max(s, axis=0, keepdims=True))
            p = jnp.exp(s - new)
            alpha = jnp.exp(m - new)
            l_ref[e : e + 1, :] = l_ref[e : e + 1, :] * alpha + jnp.sum(p, axis=0, keepdims=True)
            vt = vt_ref[64 * e : 64 * e + 64, at]
            acc_ref[e] = acc_ref[e] * alpha + jnp.dot(vt, p.astype(bf16), preferred_element_type=f32)
            m_ref[e : e + 1, :] = new
        return carry

    lax.fori_loop(range_ref[0, qi], range_ref[1, qi], tile, 0)
    o = jnp.concatenate([acc_ref[e] / l_ref[e : e + 1, :] for e in range(2)], axis=0)
    o_ref[...] = o.T
    lse_ref[0] = m_ref[...] + jnp.log(l_ref[...])


def attend(plan, q, kv):
    ranges, qseg, kseg = plan
    return pl.pallas_call(
        forward_kernel,
        grid=(HALF // 128, ROWS // QT),
        out_shape=(
            jax.ShapeDtypeStruct((ROWS, HALF), f32),
            jax.ShapeDtypeStruct((HALF // 128, 8, ROWS), f32),
        ),
        in_specs=[
            pl.BlockSpec(memory_space=pltpu.SMEM),
            pl.BlockSpec((8, QT), lambda h, i: (0, i)),
            pl.BlockSpec((SPAN, 128), lambda h, i: (0, 0)),
            pl.BlockSpec((QT, 128), lambda h, i: (i, h)),
            pl.BlockSpec((SPAN, 128), lambda h, i: (0, h)),
            pl.BlockSpec((SPAN, 128), lambda h, i: (0, h + HALF // 128)),
        ],
        out_specs=(
            pl.BlockSpec((QT, 128), lambda h, i: (i, h)),
            pl.BlockSpec((1, 8, QT), lambda h, i: (h, 0, i)),
        ),
        scratch_shapes=[
            pltpu.VMEM((128, SPAN), bf16),
            pltpu.VMEM((8, QT), f32),
            pltpu.VMEM((8, QT), f32),
            pltpu.VMEM((2, 64, QT), f32),
        ],
        compiler_params=pltpu.CompilerParams(vmem_limit_bytes=VLIM),
        cost_estimate=pl.CostEstimate(flops=20_000_000_000, bytes_accessed=12_000_000, transcendentals=0),
        name="attention_forward",
    )(ranges, qseg, kseg, q, kv, kv)


def backward_kernel(range_ref, qseg_ref, kseg_ref, q_ref, k_ref, v_ref, do_ref, o_ref, lse_ref,
                    dq_ref, dk_far_ref, dv_far_ref, dk_own_ref, dv_own_ref, kt_ref, dk_ref, dv_ref, dqt_ref):
    qi = pl.program_id(1)
    last = ROWS // QT - 1

    @pl.when(qi == 0)
    def _():
        dk_ref[...] = jnp.zeros_like(dk_ref)
        dv_ref[...] = jnp.zeros_like(dv_ref)
        def flip(t, carry):
            at = pl.ds(pl.multiple_of(t * KT, KT), KT)
            kt_ref[:, at] = k_ref[at, :].T
            return carry
        lax.fori_loop(range_ref[0, 0], range_ref[1, last], flip, 0)

    qs = split_heads(q_ref[...])
    dos = split_heads(do_ref[...])
    qcat = jnp.concatenate(qs, axis=0)
    docat = jnp.concatenate(dos, axis=0)
    dm = (do_ref[...].astype(f32) * o_ref[...]).T
    delta = [jnp.sum(dm[64 * e : 64 * e + 64], axis=0, keepdims=True) for e in range(2)]
    dqt_ref[...] = jnp.zeros_like(dqt_ref)

    def tile(t, carry):
        at = pl.ds(pl.multiple_of(t * KT, KT), KT)
        ks = kseg_ref[at, :]
        same = jnp.concatenate([ks] * (QT // 128), axis=1) == qseg_ref[0:1, :]
        k = k_ref[at, :]
        v = v_ref[at, :]
        ps, dss = [], []
        for e in range(2):
            dims = (((1,), (1,)), ((), ()))
            s = lax.dot_general(k, qs[e], dims, preferred_element_type=f32)
            p = jnp.exp(jnp.where(same, s - lse_ref[0, e : e + 1, :], NEG))
            dp = lax.dot_general(v, dos[e], dims, preferred_element_type=f32)
            ds = (p * (dp - delta[e])).astype(bf16)
            dqt_ref[e] += jnp.dot(kt_ref[64 * e : 64 * e + 64, at], ds, preferred_element_type=f32)
            ps.append(p.astype(bf16))
            dss.append(ds)
        dk_ref[at, :] += jnp.dot(jnp.concatenate(dss, axis=1), qcat, preferred_element_type=f32)
        dv_ref[at, :] += jnp.dot(jnp.concatenate(ps, axis=1), docat, preferred_element_type=f32)
        return carry

    lax.fori_loop(range_ref[0, qi], range_ref[1, qi], tile, 0)
    dq = jnp.concatenate([dqt_ref[0], dqt_ref[1]], axis=0).T
    dq_ref[...] = dq.astype(bf16) * jnp.asarray(0.125, bf16)

    @pl.when(qi == last)
    def _():
        for far, own, acc in ((dk_far_ref, dk_own_ref, dk_ref), (dv_far_ref, dv_own_ref, dv_ref)):
            far[0:REACH, :] = acc[0:REACH, :].astype(bf16)
            far[REACH : 2 * REACH, :] = acc[REACH + ROWS : SPAN, :].astype(bf16)
            own[...] = acc[REACH : REACH + ROWS, :]


def attend_back(plan, q, kv, d_att, mixed, lse):
    ranges, qseg, kseg = plan
    rowspec = pl.BlockSpec((QT, 128), lambda h, i: (i, h))
    span = pl.BlockSpec((SPAN, 128), lambda h, i: (0, h))
    span_v = pl.BlockSpec((SPAN, 128), lambda h, i: (0, h + HALF // 128))
    far = pl.BlockSpec((2 * REACH, 128), lambda h, i: (0, h))
    own = pl.BlockSpec((ROWS, 128), lambda h, i: (0, h))
    dq, dk_far, dv_far, dk_own, dv_own = pl.pallas_call(
        backward_kernel,
        grid=(HALF // 128, ROWS // QT),
        out_shape=(
            jax.ShapeDtypeStruct((ROWS, HALF), bf16),
            jax.ShapeDtypeStruct((2 * REACH, HALF), bf16),
            jax.ShapeDtypeStruct((2 * REACH, HALF), bf16),
            jax.ShapeDtypeStruct((ROWS, HALF), f32),
            jax.ShapeDtypeStruct((ROWS, HALF), f32),
        ),
        in_specs=[
            pl.BlockSpec(memory_space=pltpu.SMEM),
            pl.BlockSpec((8, QT), lambda h, i: (0, i)),
            pl.BlockSpec((SPAN, 128), lambda h, i: (0, 0)),
            rowspec, span, span_v, rowspec, rowspec,
            pl.BlockSpec((1, 8, QT), lambda h, i: (h, 0, i)),
        ],
        out_specs=(rowspec, far, far, own, own),
        scratch_shapes=[
            pltpu.VMEM((128, SPAN), bf16),
            pltpu.VMEM((SPAN, 128), f32),
            pltpu.VMEM((SPAN, 128), f32),
            pltpu.VMEM((2, 64, QT), f32),
        ],
        compiler_params=pltpu.CompilerParams(vmem_limit_bytes=VLIM),
        cost_estimate=pl.CostEstimate(flops=50_000_000_000, bytes_accessed=25_000_000, transcendentals=0),
        name="attention_backward",
    )(ranges, qseg, kseg, q, kv, kv, d_att, mixed, lse)
    return dq, jnp.concatenate([dk_far, dv_far], axis=1), jnp.concatenate([dk_own, dv_own], axis=1)


def exchange(part):
    return lax.ppermute(part, "heads", [(0, 1), (1, 0)])


def pair_sum(part):
    half = part.astype(bf16)
    return half.astype(f32) + exchange(half).astype(f32)


def side_by_side(own, other, index):
    return jnp.where(
        index == 0,
        jnp.concatenate([own, other], axis=1),
        jnp.concatenate([other, own], axis=1),
    )


def passed(block, distance):
    count = lax.axis_size("seq")
    route = [(i - distance, i) for i in range(count) if 0 <= i - distance < count]
    return lax.ppermute(block, "seq", route)


def layer_norm(values, gain, shift):
    centered = values - jnp.mean(values, axis=-1, keepdims=True)
    scale = lax.rsqrt(jnp.mean(centered * centered, axis=-1, keepdims=True) + EPSILON)
    return centered * scale * gain + shift


def gelu_exact(values):
    return jax.nn.gelu(values, approximate=False)


def nesterov(weight, grad, moment, average, rate):
    moment_new = 0.5 * moment + grad
    weight_new = weight - rate * (grad + 0.5 * moment_new)
    average_new = 0.5 * average + 0.5 * weight_new
    return (grad, weight_new, moment_new, average_new, weight_new.astype(bf16))


def dot(a, b, ca, cb):
    return lax.dot_general(a, b, (((ca,), (cb,)), ((), ())), preferred_element_type=f32)


def gathered(shard):
    return lax.all_gather(shard, "seq", axis=0, tiled=True)


def scattered(whole_sum):
    return lax.psum_scatter(whole_sum, "seq", scatter_dimension=0, tiled=True)


def body(
    frames,
    cotangent,
    lengths,
    kernel,
    kernel_moment,
    kernel_average,
    project,
    project_moment,
    project_average,
    combine,
    combine_moment,
    combine_average,
    expand,
    expand_moment,
    expand_average,
    shrink,
    shrink_moment,
    shrink_average,
    unitbias,
    unitbias_moment,
    unitbias_average,
    chanbias,
    chanbias_moment,
    chanbias_average,
    outbias,
    outbias_moment,
    outbias_average,
    normparams,
    normparams_moment,
    normparams_average,
):
    devices = lax.axis_size("seq")
    rows, width = frames.shape
    total = devices * rows
    first = lax.axis_index("seq") * rows
    index = lax.axis_index("heads")
    local = project.shape[0]
    hidden_units = expand.shape[1]

    w_kernel = gathered(jnp.transpose(kernel, (2, 1, 0)).astype(bf16))
    small = jnp.concatenate(
        [unitbias, chanbias.reshape(-1), outbias.reshape(-1), normparams.reshape(-1)]
    ).astype(bf16)
    w_small = gathered(small[None])
    w_first = gathered(
        jnp.concatenate(
            [project[:, 0], project[:, 1], project[:, 2], combine.T], axis=1
        ).astype(bf16)
    )
    w_second = gathered(jnp.concatenate([expand, shrink.T], axis=1).astype(bf16))
    cuts = [unitbias.size, chanbias.size, outbias.size, normparams.size]
    parts, at = [], 0
    for size in cuts:
        parts.append(w_small[:, at : at + size].astype(f32))
        at += size
    b_unit = parts[0].reshape(-1)
    b_chan = jnp.transpose(parts[1].reshape(devices, 3, -1), (1, 0, 2)).reshape(3, -1)
    b_out = jnp.transpose(parts[2].reshape(devices, 2, -1), (1, 0, 2)).reshape(2, -1)
    norms = jnp.transpose(parts[3].reshape(devices, 3, 2, -1), (1, 2, 0, 3)).reshape(3, 2, -1)

    count = lengths.shape[0]
    order = jnp.arange(count, dtype=i32)
    ends = jnp.sum(jnp.where(order[None, :] <= order[:, None], lengths[None, :], 0), axis=1).astype(i32)
    starts = ends - lengths
    plan = block_plan(starts, ends, first)
    reach = attention_plan(starts, ends, first)

    x_half = lax.dynamic_slice_in_dim(frames, index * HALF, HALF, 1).astype(bf16)
    window = jnp.concatenate(
        [passed(x_half[rows - HALO :], 1), x_half, passed(x_half[:HALO], -1)], axis=0
    )
    pre = conv(plan, window, w_kernel, False) + b_chan[0]
    spread_part = gelu_exact(pre).astype(bf16)
    spread = side_by_side(spread_part, exchange(spread_part), index)
    h1, norm0_back = jax.vjp(layer_norm, frames + spread.astype(f32), norms[0, 0], norms[0, 1])
    h1_half = h1.astype(bf16)
    proj = dot(h1_half, w_first[:, : 3 * HALF], 1, 0)
    scale = HEAD ** (-0.5)
    queries = ((proj[:, :HALF] + b_chan[1]) * scale).astype(bf16)
    keys = proj[:, HALF : 2 * HALF].astype(bf16)
    values = (proj[:, 2 * HALF :] + b_chan[2]).astype(bf16)
    both = jnp.concatenate([keys, values], axis=1)
    near = REACH - rows
    span = jnp.concatenate(
        [
            passed(both[rows - near :], 2),
            passed(both, 1),
            both,
            passed(both, -1),
            passed(both[:near], -2),
        ],
        axis=0,
    )
    mixed, lse = attend(reach, queries, span)
    attended = mixed.astype(bf16)
    w_combine = w_first[:, 3 * HALF :]
    branch = pair_sum(dot(attended, w_combine, 1, 1))
    h2, norm1_back = jax.vjp(layer_norm, h1 + branch + b_out[0], norms[1, 0], norms[1, 1])
    h2_half = h2.astype(bf16)
    w_expand = w_second[:, :hidden_units]
    w_shrink = w_second[:, hidden_units:]
    inner = dot(h2_half, w_expand, 1, 0) + b_unit
    hidden, gelu_inner_back = jax.vjp(gelu_exact, inner)
    hidden_half = hidden.astype(bf16)
    outer = pair_sum(dot(hidden_half, w_shrink, 1, 1))
    layer_out, norm2_back = jax.vjp(layer_norm, h2 + outer + b_out[1], norms[2, 0], norms[2, 1])
    dx3, gain2_grad, shift2_grad = norm2_back(cotangent)
    outer_bias_grad = jnp.sum(dx3, axis=0)
    d_out = dx3.astype(bf16)
    d_hidden = dot(d_out, w_shrink, 1, 0)
    d_inner = gelu_inner_back(d_hidden)[0]
    unit_grad = jnp.sum(d_inner, axis=0)
    d_inner_half = d_inner.astype(bf16)
    dh2 = dx3 + pair_sum(dot(d_inner_half, w_expand, 1, 1))
    second_sum = scattered(
        jnp.concatenate(
            [dot(h2_half, d_inner_half, 0, 0).astype(bf16), dot(d_out, hidden_half, 0, 0).astype(bf16)],
            axis=1,
        )
    ).astype(f32)
    dx2, gain1_grad, shift1_grad = norm1_back(dh2)
    branch_bias_grad = jnp.sum(dx2, axis=0)
    d_branch = dx2.astype(bf16)
    d_att = dot(d_branch, w_combine, 1, 0).astype(bf16)
    dq_half, far, own = attend_back(reach, queries, span, d_att, mixed, lse)
    d_both = own
    for distance, lo, hi, to in (
        (2, 0, near, rows - near),
        (1, near, REACH, 0),
        (-1, REACH, REACH + rows, 0),
        (-2, REACH + rows, 2 * REACH, 0),
    ):
        back = passed(far[lo:hi], -distance).astype(f32)
        pad = (to, rows - to - back.shape[0])
        d_both = d_both + jnp.pad(back, (pad, (0, 0)))
    d_both_half = d_both.astype(bf16)
    stacked = jnp.concatenate([dq_half, d_both_half], axis=1)
    query_bias_grad = jnp.sum(dq_half.astype(f32), axis=0)
    value_bias_grad = jnp.sum(d_both_half[:, HALF:].astype(f32), axis=0)
    dh1 = dx2 + pair_sum(dot(stacked, w_first[:, : 3 * HALF], 1, 1))
    first_sum = scattered(
        jnp.concatenate(
            [dot(h1_half, stacked, 0, 0).astype(bf16), dot(d_branch, attended, 0, 0).astype(bf16)],
            axis=1,
        )
    ).astype(f32)
    dx1, gain0_grad, shift0_grad = norm0_back(dh1)
    d_spread = lax.dynamic_slice_in_dim(dx1, index * HALF, HALF, 1)
    d_conv = jax.vjp(gelu_exact, pre)[1](d_spread)[0]
    conv_bias_grad = jnp.sum(d_conv, axis=0)
    d_conv_half = d_conv.astype(bf16)
    kernel_sum = scattered(tap_grad(plan, window, d_conv_half)).astype(f32)
    d_window = jnp.concatenate(
        [passed(d_conv_half[rows - HALO :], 1), d_conv_half, passed(d_conv_half[:HALO], -1)], axis=0
    )
    d_input = conv(plan, d_window, w_kernel, True).astype(bf16)
    frames_grad = dx1 + side_by_side(d_input, exchange(d_input), index).astype(f32)

    spread_out = lambda grad, lead: jnp.transpose(
        grad.reshape(lead, devices, -1), (1, 0, 2)
    ).reshape(devices, -1)
    small_sum = scattered(
        jnp.concatenate(
            [
                unit_grad.reshape(devices, -1),
                spread_out(jnp.stack([conv_bias_grad, query_bias_grad, value_bias_grad]), 3),
                spread_out(jnp.stack([branch_bias_grad, outer_bias_grad]), 2),
                spread_out(
                    jnp.stack(
                        [gain0_grad, shift0_grad, gain1_grad, shift1_grad, gain2_grad, shift2_grad]
                    ),
                    6,
                ),
            ],
            axis=1,
        )
    )[0]
    pieces, at = [], 0
    for size in cuts:
        pieces.append(small_sum[at : at + size])
        at += size
    unit_sum = pieces[0]
    chan_sum = pieces[1].reshape(chanbias.shape)
    out_sum = pieces[2].reshape(outbias.shape)
    norm_sum = pieces[3].reshape(normparams.shape)
    project_sum = jnp.stack([first_sum[:, HALF * i : HALF * (i + 1)] for i in range(3)], axis=1)

    root = total**0.5
    small_rate = 0.1 / root
    out = [layer_out, frames_grad]
    for weight, grad, moment, average, rate in (
        (kernel, jnp.transpose(kernel_sum, (2, 1, 0)), kernel_moment, kernel_average, (CG * TAPS) ** (-0.5) / root),
        (project, project_sum, project_moment, project_average, width ** (-0.5) / root),
        (combine, first_sum[:, 3 * HALF :].T, combine_moment, combine_average, (width // 16) ** (-0.5) / root),
        (expand, second_sum[:, :hidden_units], expand_moment, expand_average, width ** (-0.5) / root),
        (shrink, second_sum[:, hidden_units:].T, shrink_moment, shrink_average, (2 * hidden_units) ** (-0.5) / root),
        (unitbias, unit_sum, unitbias_moment, unitbias_average, 0.5 / root),
        (chanbias, chan_sum, chanbias_moment, chanbias_average, small_rate),
        (outbias, out_sum, outbias_moment, outbias_average, small_rate),
        (normparams, norm_sum, normparams_moment, normparams_average, small_rate),
    ):
        out.extend(nesterov(weight, grad, moment, average, rate))
    return tuple(out)


def solution(mesh):
    kernel_spec = P("heads", None, "seq")
    project_spec = P("seq", None, "heads")
    tall = P("heads", "seq")
    wide = P("seq", "heads")
    unit = P(("heads", "seq"))
    chan = P(None, ("heads", "seq"))
    outb = P(None, "seq")
    norm = P(None, None, "seq")
    weights = (kernel_spec, project_spec, tall, wide, tall, unit, chan, outb, norm)
    rows = P("seq", None)
    return jax.shard_map(
        body,
        mesh=mesh,
        in_specs=(rows, rows, P()) + tuple(s for s in weights for _ in range(3)),
        out_specs=(rows, rows) + tuple(s for s in weights for _ in range(5)),
        check_vma=False,
    )
```

time: 3420 us -> 851 us (0.25)
  local copies, waits for them, and re-layouts: 1380 us -> 37.9 us
  other arithmetic: 661 us -> 69.5 us
  matrix products: 567 us -> 64.1 us
  waiting for transfers between devices: 398 us -> 170 us
  Pallas kernels: 0 us -> 197 us
  blocking collectives: 223 us -> 165 us
    scatter-add x113 -> x0, local copies, waits for them, and re-layouts: 732 us -> none  [body(): d_padded.at[start + offset:start + offset + rows].add(spread_back[offset])]
    dot_general x57 -> x12, matrix products: 567 us -> 64.1 us  [dot(): lax.dot_general(a, b, (((ca,), (cb,)), ((), ())), preferred_element_type=...]
    add x121 -> x4, other arithmetic: 313 us -> 2.23 us  [the longest x1 2.14 us: body(): dx1 + side_by_side(d_input, exchange(d_input), index).astype(f32)]
    reshape x17 -> x10, local copies, waits for them, and re-layouts: 219 us -> 0.78 us  [the longest x3 0.24 us: body(): spread_out = lambda grad, lead: jnp.transpose(grad.reshape(lead, devices,...]
    transpose x16 -> x2, local copies, waits for them, and re-layouts: 199 us -> 0.16 us  [the longest x1 0.08 us: body(): jnp.transpose(parts[1].reshape(devices, 3, -1), (1, 0, 2)).reshape(3, -1)]
    pallas_call x0 -> x5, Pallas kernels: none -> 197 us  [the longest x2 86.3 us: conv(): pl.pallas_call(functools.partial(conv_kernel, back), grid=(4,), out_shape...]
    psum x4 -> x0, waiting for transfers between devices: 152 us -> none  [the longest x1 51.6 us: body(): lax.psum(dh2_part.astype(jnp.bfloat16), 'heads').astype(jnp.float32)]
    reduce_scatter x5 -> x3, waiting for transfers between devices: 146 us -> 0.02 us  [scattered(): return lax.psum_scatter(whole_sum, 'seq', scatter_dimension=0, tiled=True)]
  transfers between devices with their start and end apart: 37 -> 24, of which waited for: 10 -> 10; matrix products, arithmetic and copies ran while one was open for 69% -> 11% of each run, Pallas kernels for 0% -> 19%
where the time goes in v1:
time: 851 us; the launch traced here: 843 us
  Pallas kernels  197 us (23%)
  waiting for transfers between devices  170 us (20%)
  blocking collectives  165 us (19%)
  starting transfers between devices  122 us (14%)
  other arithmetic  69.5 us (8%)
  matrix products  64.1 us (8%)
  local copies, waits for them, and re-layouts  37.9 us (4%)
  between operations  18.7 us (2%)
    unnamed x1, blocking collectives  140 us
    ppermute x12, starting transfers between devices, passed(): return lax.ppermute(block, 'seq', route)  111 us
    ppermute x6, waiting for transfers between devices, exchange(): return lax.ppermute(part, 'heads', [(0, 1), (1, 0)])  91.8 us
    pallas_call x2, Pallas kernels, conv(): pl.pallas_call(functools.partial(conv_kernel, back), grid=(4,), out_shape...  86.3 us
    dot_general x12, matrix products, dot(): lax.dot_general(a, b, (((ca,), (cb,)), ((), ())), preferred_element_type=...  64.1 us
    ppermute x12, waiting for transfers between devices, passed(): return lax.ppermute(block, 'seq', route)  58.1 us
    pallas_call x1, Pallas kernels, tap_grad(): pl.pallas_call(tap_grad_kernel, grid=(4,), out_shape=jax.ShapeDtypeStruct...  40.7 us
    pallas_call x1, Pallas kernels, attend_back(): pl.pallas_call(backward_kernel, grid=(HALF // 128, ROWS // QT), out_shape...  37.9 us
  transfers between devices with their start and end apart: 24, of which 10 were waited for; matrix products, arithmetic and copies ran while one was open for 11% of the time, Pallas kernels for 19%

profile of v1, /device:TPU:0, one launch (start us, length us, event | category | flops | bytes accessed | tf_op | source)
XLA Modules:
  0.0 843.2 jit_solution(14020524443722951794)
XLA Ops:
  7.3 1.9 copy.149
  10.8 2.4 collective-permute-start
  17.3 25.2 %all-gather = bf16[16,1,552]{2,1,0:T(2,128)(2,1)S(1)} all-gather(bf16[1,1,552]{2,1,0:T(2,128)(2,1)S(1)} %maximum_bitcast_fusion.2), channel_id=1, replica_groups=mesh['seq'=16,'heads'=2] {'seq'}, dimensions={0}, use_global_device_ids=true | all-gather | bytes 18768 | tf_op jit(solution)/shard_map/all_gather | solution.py:525
  47.0 19.9 %all-gather.5.cloned.1.call-done.k_ref = bf16[128,48,384]{2,1,0:T(8,128)(2,1)} async-done(((bf16[8,48,384]{2,1,0:T(8,128)(2,1)}), bf16[128,48,384]{2,1,0:T(8,128)(2,1)}) %all-gather.5.cloned.1.call-update) | async-done | bytes 4718608 | tf_op jit(solution)/shard_map/all_gather | solution.py:525
  69.8 42.7 %conv_forward.1 = f32[1024,384]{1,0:T(8,128)} custom-call(s32[1]{0:T(128)} %bitcast.1.chunks_ref, s32[8,1152]{1,0:T(8,128)} %broadcast_in_dim.140.prow_ref, s32[1152,128]{1,0:T(8,128)} %broadcast_in_dim.141.pcol_ref, s32[1408,128]{1,0:T(8,128)} %broadcast_in_dim.144.bseg_ref, bf16[1152,384]{1,0:T(8,128)(2,1)} %pad_maximum_fusion.6.x_ref, ...), custom_call_target="tpu_custom_call" | custom-call | flops 30000001024 | bytes 9000000 | tf_op jit(solution)/shard_map/conv_forward/pallas_call | solution.py:171
  112.5 5.6 multiply_convert_fusion.1
  121.3 16.6 %collective-permute-done.2 = bf16[1024,384]{1,0:T(8,128)(2,1)} collective-permute-done((bf16[1024,384]{1,0:T(8,128)(2,1)S(1)}, bf16[1024,384]{1,0:T(8,128)(2,1)}, u32[]{:S(2)}, u32[]{:S(2)}) %collective-permute-start.2) | collective-permute-done | bytes 786464 | tf_op jit(solution)/shard_map/ppermute | solution.py:481
  137.9 3.4 fusion.81
  141.8 3.9 fusion.40
  148.4 2.5 collective-permute-start.4
  154.1 4.5 collective-permute-start.3
  160.9 49.8 %collective-permute-done.3 = bf16[512,768]{1,0:T(8,128)(2,1)S(1)} collective-permute-done((bf16[512,768]{1,0:T(8,128)(2,1)S(1)}, bf16[512,768]{1,0:T(8,128)(2,1)S(1)}, u32[]{:S(2)}, u32[]{:S(2)}) %collective-permute-start.3) | collective-permute-done | bytes 786464 | tf_op jit(solution)/shard_map/ppermute | solution.py:500
  212.6 2.6 copy-done.47
  215.2 2.9 broadcast_in_dim.151.kseg_ref
  218.7 31.6 %attention_forward.1 = (f32[1024,384]{1,0:T(8,128)}, f32[3,8,1024]{2,1,0:T(8,128)}) custom-call(s32[2,4]{1,0:T(2,128)} %pad_add_fusion.range_ref, s32[8,1024]{1,0:T(8,128)} %broadcast_in_dim.150.qseg_ref, s32[4096,128]{1,0:T(8,128)} %broadcast_in_dim.151.kseg_ref, bf16[1024,384]{1,0:T(8,128)(2,1)} %get-tuple-element.380.q_ref, bf16[4096,768]{1,0:T(8,128)(2,1)} %copy-done.47, ...), custom_call_target="tpu_custom_call" | custom-call | flops 20000000000 | bytes 12000000 | tf_op jit(solution)/shard_map/attention_forward/pallas_call | solution.py:356
  250.4 3.7 convolution_convert_fusion.3
  254.1 1.7 collective-permute-start.7
  256.1 18.7 %collective-permute-done.7 = bf16[1024,768]{1,0:T(8,128)(2,1)} collective-permute-done((bf16[1024,768]{1,0:T(8,128)(2,1)}, bf16[1024,768]{1,0:T(8,128)(2,1)}, u32[]{:S(2)}, u32[]{:S(2)}) %collective-permute-start.7) | collective-permute-done | bytes 1572896 | tf_op jit(solution)/shard_map/ppermute | solution.py:481
  274.8 3.2 fusion.80
  280.3 20.0 %multiply_convert_fusion = (bf16[1024,1536]{1,0:T(8,128)(2,1)S(1)}, f32[1024,1536]{1,0:T(8,128)}, f32[1024,1536]{1,0:T(8,128)}) fusion(f32[1536]{0:T(1024)S(1)} %reshape.518, bf16[768,3072]{1,0:T(8,128)(2,1)} %all-gather.9.cloned.1.call-done, f32[1024,768]{1,0:T(8,128)} %copy-done, f32[768]{0:T(1024)S(1)} %get-tuple-element.310, ...), kind=kOutput, calls=%fused_computation.3 | convolution fusion | flops 2523660288 | bytes 21254144 | tf_op jit(solution)/shard_map/dot_general | solution.py:521
  300.3 3.9 fusion.25
  304.2 1.8 collective-permute-start.8
  306.0 18.9 %collective-permute-done.8 = bf16[1024,768]{1,0:T(8,128)(2,1)} collective-permute-done((bf16[1024,768]{1,0:T(8,128)(2,1)}, bf16[1024,768]{1,0:T(8,128)(2,1)}, u32[]{:S(2)}, u32[]{:S(2)}) %collective-permute-start.8) | collective-permute-done | bytes 1572896 | tf_op jit(solution)/shard_map/ppermute | solution.py:481
  325.0 4.2 fusion.78
  332.7 2.7 fusion.77
  336.6 7.1 fusion.88
  343.7 2.6 fusion.22
  346.4 1.8 collective-permute-start.9
  348.2 18.7 %collective-permute-done.9 = bf16[1024,768]{1,0:T(8,128)(2,1)S(1)} collective-permute-done((bf16[1024,768]{1,0:T(8,128)(2,1)S(1)}, bf16[1024,768]{1,0:T(8,128)(2,1)S(1)}, u32[]{:S(2)}, u32[]{:S(2)}) %collective-permute-start.9) | collective-permute-done | bytes 1572896 | tf_op jit(solution)/shard_map/ppermute | solution.py:481
  366.9 2.2 multiply_reduce_fusion.1
  372.3 3.0 convolution_convert_fusion.5.do_ref
  375.2 37.9 %attention_backward.1 = (bf16[1024,384]{1,0:T(8,128)(2,1)}, bf16[3072,384]{1,0:T(8,128)(2,1)}, bf16[3072,384]{1,0:T(8,128)(2,1)}, f32[1024,384]{1,0:T(8,128)}, f32[1024,384]{1,0:T(8,128)}) custom-call(s32[2,4]{1,0:T(2,128)} %pad_add_fusion.range_ref, s32[8,1024]{1,0:T(8,128)} %broadcast_in_dim.150.qseg_ref, s32[4096,128]{1,0:T(8,128)} %broadcast_in_dim.151.kseg_ref, ...), custom_call_target="tpu_custom_call" | custom-call | flops 49999998976 | bytes 25000000 | tf_op jit(solution)/shard_map/attention_backward/pallas_call | solution.py:449
  413.2 2.1 constant_dynamic-update-slice_fusion.6
  417.8 35.7 %collective-permute-start.12 = (bf16[1024,768]{1,0:T(8,128)(2,1)S(1)}, bf16[1024,768]{1,0:T(8,128)(2,1)S(1)}, u32[]{:S(2)}, u32[]{:S(2)}) collective-permute-start(bf16[1024,768]{1,0:T(8,128)(2,1)S(1)} %get-tuple-element.378), channel_id=1, source_target_pairs={{0,2},{2,4},{4,6},{6,8},{8,10},{10,12},{12,14},{14,16},{16,18},{18... | collective-permute-start | bytes 4718600 | tf_op jit(solution)/shard_map/ppermute | solution.py:500
  455.2 56.6 %collective-permute-start.13 = (bf16[512,768]{1,0:T(8,128)(2,1)S(1)}, bf16[512,768]{1,0:T(8,128)(2,1)S(1)}, u32[]{:S(2)}, u32[]{:S(2)}) collective-permute-start(bf16[512,768]{1,0:T(8,128)(2,1)S(1)} %get-tuple-element.376), channel_id=1, source_target_pairs={{0,4},{2,6},{4,8},{6,10},{8,12},{10,14},{12,16},{14,18},{16,20},{1... | collective-permute-start | bytes 2359304 | tf_op jit(solution)/shard_map/ppermute | solution.py:500
  513.0 6.8 collective-permute-done.10
  522.5 2.6 convolution_convert_fusion.2
  527.4 5.7 convolution_convert_fusion.4
  534.8 4.4 convolution_convert_fusion
  539.5 6.0 convolution_convert_fusion.1
  545.5 2.7 pad_maximum_fusion
  551.4 2.4 collective-permute-done.14
  553.8 4.0 multiply_reduce_fusion.2
  564.0 139.5 %all-reduce.2 = f32[16,552]{1,0:T(8,128)S(1)} all-reduce(f32[16,552]{1,0:T(8,128)S(1)} %pad_maximum_fusion.11), channel_id=5, replica_groups=mesh['seq'=16,'heads'=2] {'seq'}, use_global_device_ids=true, to_apply=%region_34.35.clone | all-reduce | flops 8832 | bytes 70656
  710.2 40.7 %tap_gradient.1 = bf16[128,48,384]{2,1,0:T(8,128)(2,1)} custom-call(s32[1]{0:T(128)} %bitcast.1.chunks_ref, s32[8,1152]{1,0:T(8,128)} %broadcast_in_dim.140.prow_ref, s32[1408,128]{1,0:T(8,128)} %broadcast_in_dim.144.bseg_ref, bf16[1152,384]{1,0:T(8,128)(2,1)} %pad_maximum_fusion.6.x_ref, bf16[1024,384]{1,0:T(8,128)(2,1)} %copy-done.15), custom_call_target="tpu_custom_call" | custom-call | flops 40000000000 | bytes 9000000 | tf_op jit(solution)/shard_map/tap_gradient/pallas_call | solution.py:259
  753.5 43.6 %conv_back.1 = f32[1024,384]{1,0:T(8,128)} custom-call(s32[1]{0:T(128)} %bitcast.1.chunks_ref, s32[8,1152]{1,0:T(8,128)} %broadcast_in_dim.140.prow_ref, s32[1152,128]{1,0:T(8,128)} %broadcast_in_dim.141.pcol_ref, s32[1408,128]{1,0:T(8,128)} %broadcast_in_dim.144.bseg_ref, bf16[1152,384]{1,0:T(8,128)(2,1)} %pad_maximum_fusion.7.x_ref, ...), custom_call_target="tpu_custom_call" | custom-call | flops 30000001024 | bytes 9000000 | tf_op jit(solution)/shard_map/conv_back/pallas_call | solution.py:171
  802.4 16.5 %collective-permute-done.17 = bf16[1024,384]{1,0:T(8,128)(2,1)S(1)} collective-permute-done((bf16[1024,384]{1,0:T(8,128)(2,1)S(1)}, bf16[1024,384]{1,0:T(8,128)(2,1)S(1)}, u32[]{:S(2)}, u32[]{:S(2)}) %collective-permute-start.17) | collective-permute-done | bytes 786464 | tf_op jit(solution)/shard_map/ppermute | solution.py:481
  818.9 2.1 convert_add_fusion
  (366 shorter events, 85.4 us)
Async XLA Ops:
  7.3 59.7 %all-gather.5.cloned.1.call-start = ((), (), s32[]{:S(2)}) async-start(), calls=%async_computation.3 | async-start | bytes 5013504 | tf_op jit(solution)/shard_map/all_gather | solution.py:525
  9.2 132.5 %all-gather.7.cloned.1.call-start = ((), (), s32[]{:S(2)}) async-start(), calls=%async_computation.4 | async-start | bytes 2506752 | tf_op jit(solution)/shard_map/all_gather | solution.py:525
  10.8 35.2 %collective-permute-start = (bf16[64,384]{1,0:T(8,128)(2,1)S(1)}, bf16[64,384]{1,0:T(8,128)(2,1)S(1)}, u32[]{:S(2)}, u32[]{:S(2)}) collective-permute-start(bf16[64,384]{1,0:T(8,128)(2,1)S(1)} %get-tuple-element.389), channel_id=1, source_target_pairs={{0,2},{2,4},{4,6},{6,8},{8,10},{10,12},{12,14},{14,16},{16,18},{18... | collective-permute-start | bytes 147464 | tf_op jit(solution)/shard_map/ppermute | solution.py:500
  13.2 32.8 %collective-permute-start.1 = (bf16[64,384]{1,0:T(8,128)(2,1)S(1)}, bf16[64,384]{1,0:T(8,128)(2,1)S(1)}, u32[]{:S(2)}, u32[]{:S(2)}) collective-permute-start(bf16[64,384]{1,0:T(8,128)(2,1)S(1)} %get-tuple-element.390), channel_id=1, source_target_pairs={{2,0},{4,2},{6,4},{8,6},{10,8},{12,10},{14,12},{16,14},{18,16},{20... | collective-permute-start | bytes 147464 | tf_op jit(solution)/shard_map/ppermute | solution.py:500
  16.2 264.0 %all-gather.9.cloned.1.call-start = ((), (), s32[]{:S(2)}) async-start(), calls=%async_computation.5 | async-start | bytes 5013504 | tf_op jit(solution)/shard_map/all_gather | solution.py:525
  46.0 66.5 %copy-start.52 = (f32[384]{0:T(512)}, f32[384]{0:T(512)S(1)}, u32[]{:S(2)}) copy-start(f32[384]{0:T(512)S(1)} %add.403) | copy-start | bytes 4612
  118.1 19.8 %collective-permute-start.2 = (bf16[1024,384]{1,0:T(8,128)(2,1)S(1)}, bf16[1024,384]{1,0:T(8,128)(2,1)}, u32[]{:S(2)}, u32[]{:S(2)}) collective-permute-start(bf16[1024,384]{1,0:T(8,128)(2,1)S(1)} %get-tuple-element.367), channel_id=1, source_target_pairs={{0,1},{1,0},{2,3},{3,2},{4,5},{5,4},{6,7},{7,6},{8,9},{9,8},{10,11... | collective-permute-start | bytes 2359304 | tf_op jit(solution)/shard_map/ppermute | solution.py:481
  120.4 700.7 %reduce-scatter.6.cloned.1.call-start = ((), (), s32[]{:S(2)}) async-start(), calls=%async_computation.7 | async-start | bytes 2506752 | tf_op jit(solution)/shard_map/reduce_scatter | solution.py:529
  148.4 62.3 %collective-permute-start.4 = (bf16[1024,768]{1,0:T(8,128)(2,1)}, bf16[1024,768]{1,0:T(8,128)(2,1)}, u32[]{:S(2)}, u32[]{:S(2)}) collective-permute-start(bf16[1024,768]{1,0:T(8,128)(2,1)} %pad_maximum_fusion.3), channel_id=1, source_target_pairs={{0,2},{2,4},{4,6},{6,8},{8,10},{10,12},{12,14},{14,16},{16,18},{18... | collective-permute-start | bytes 4718600 | tf_op jit(solution)/shard_map/ppermute | solution.py:500
  151.1 61.3 %collective-permute-start.5 = (bf16[1024,768]{1,0:T(8,128)(2,1)}, bf16[1024,768]{1,0:T(8,128)(2,1)S(1)}, u32[]{:S(2)}, u32[]{:S(2)}) collective-permute-start(bf16[1024,768]{1,0:T(8,128)(2,1)} %pad_maximum_fusion.3), channel_id=1, source_target_pairs={{2,0},{4,2},{6,4},{8,6},{10,8},{12,10},{14,12},{16,14},{18,16},{20... | collective-permute-start | bytes 4718600 | tf_op jit(solution)/shard_map/ppermute | solution.py:500
  154.1 58.1 %copy-start.10 = (bf16[1024,384]{1,0:T(8,128)(2,1)S(1)}, bf16[1024,384]{1,0:T(8,128)(2,1)}, u32[]{:S(2)}) copy-start(bf16[1024,384]{1,0:T(8,128)(2,1)} %copy-done.9) | copy-start | bytes 2359300
  154.1 58.1 %copy-start.12 = (bf16[1024,384]{1,0:T(8,128)(2,1)S(1)}, bf16[1024,384]{1,0:T(8,128)(2,1)}, u32[]{:S(2)}) copy-start(bf16[1024,384]{1,0:T(8,128)(2,1)} %copy-done.11) | copy-start | bytes 2359300
  154.1 56.5 %collective-permute-start.3 = (bf16[512,768]{1,0:T(8,128)(2,1)S(1)}, bf16[512,768]{1,0:T(8,128)(2,1)S(1)}, u32[]{:S(2)}, u32[]{:S(2)}) collective-permute-start(bf16[512,768]{1,0:T(8,128)(2,1)S(1)} %get-tuple-element.385), channel_id=1, source_target_pairs={{0,4},{2,6},{4,8},{6,10},{8,12},{10,14},{12,16},{14,18},{16,20},{1... | collective-permute-start | bytes 2359304 | tf_op jit(solution)/shard_map/ppermute | solution.py:500
  158.9 53.5 %collective-permute-start.6 = (bf16[512,768]{1,0:T(8,128)(2,1)S(1)}, bf16[512,768]{1,0:T(8,128)(2,1)S(1)}, u32[]{:S(2)}, u32[]{:S(2)}) collective-permute-start(bf16[512,768]{1,0:T(8,128)(2,1)S(1)} %get-tuple-element.384), channel_id=1, source_target_pairs={{4,0},{6,2},{8,4},{10,6},{12,8},{14,10},{16,12},{18,14},{20,16},{2... | collective-permute-start | bytes 2359304 | tf_op jit(solution)/shard_map/ppermute | solution.py:500
  254.1 20.7 %collective-permute-start.7 = (bf16[1024,768]{1,0:T(8,128)(2,1)}, bf16[1024,768]{1,0:T(8,128)(2,1)}, u32[]{:S(2)}, u32[]{:S(2)}) collective-permute-start(bf16[1024,768]{1,0:T(8,128)(2,1)} %convolution_convert_fusion.3), channel_id=1, source_target_pairs={{0,1},{1,0},{2,3},{3,2},{4,5},{5,4},{6,7},{7,6},{8,9},{9,8},{10,11... | collective-permute-start | bytes 4718600 | tf_op jit(solution)/shard_map/ppermute | solution.py:481
  304.2 20.8 %collective-permute-start.8 = (bf16[1024,768]{1,0:T(8,128)(2,1)}, bf16[1024,768]{1,0:T(8,128)(2,1)}, u32[]{:S(2)}, u32[]{:S(2)}) collective-permute-start(bf16[1024,768]{1,0:T(8,128)(2,1)} %fusion.25), channel_id=1, source_target_pairs={{0,1},{1,0},{2,3},{3,2},{4,5},{5,4},{6,7},{7,6},{8,9},{9,8},{10,11... | collective-permute-start | bytes 4718600 | tf_op jit(solution)/shard_map/ppermute | solution.py:481
  346.4 20.5 %collective-permute-start.9 = (bf16[1024,768]{1,0:T(8,128)(2,1)S(1)}, bf16[1024,768]{1,0:T(8,128)(2,1)S(1)}, u32[]{:S(2)}, u32[]{:S(2)}) collective-permute-start(bf16[1024,768]{1,0:T(8,128)(2,1)S(1)} %fusion.22), channel_id=1, source_target_pairs={{0,1},{1,0},{2,3},{3,2},{4,5},{5,4},{6,7},{7,6},{8,9},{9,8},{10,11... | collective-permute-start | bytes 4718600 | tf_op jit(solution)/shard_map/ppermute | solution.py:481
  416.0 95.8 %copy-start.22 = (f32[1024,384]{1,0:T(8,128)S(1)}, f32[1024,384]{1,0:T(8,128)}, u32[]{:S(2)}) copy-start(f32[1024,384]{1,0:T(8,128)} %get-tuple-element.54.o_ref) | copy-start | bytes 4718596
  416.3 95.6 %copy-start.6 = (f32[1024,768]{1,0:T(8,128)S(1)}, f32[1024,768]{1,0:T(8,128)}, u32[]{:S(2)}) copy-start(f32[1024,768]{1,0:T(8,128)} %copy-done.5) | copy-start | bytes 9437188
  416.3 105.0 %collective-permute-start.11 = (bf16[1024,768]{1,0:T(8,128)(2,1)S(1)}, bf16[1024,768]{1,0:T(8,128)(2,1)S(1)}, u32[]{:S(2)}, u32[]{:S(2)}) collective-permute-start(bf16[1024,768]{1,0:T(8,128)(2,1)S(1)} %get-tuple-element.377), channel_id=1, source_target_pairs={{2,0},{4,2},{6,4},{8,6},{10,8},{12,10},{14,12},{16,14},{18,16},{20... | collective-permute-start | bytes 4718600 | tf_op jit(solution)/shard_map/ppermute | solution.py:500
  417.8 103.5 %collective-permute-start.12 = (bf16[1024,768]{1,0:T(8,128)(2,1)S(1)}, bf16[1024,768]{1,0:T(8,128)(2,1)S(1)}, u32[]{:S(2)}, u32[]{:S(2)}) collective-permute-start(bf16[1024,768]{1,0:T(8,128)(2,1)S(1)} %get-tuple-element.378), channel_id=1, source_target_pairs={{0,2},{2,4},{4,6},{6,8},{8,10},{10,12},{12,14},{14,16},{16,18},{18... | collective-permute-start | bytes 4718600 | tf_op jit(solution)/shard_map/ppermute | solution.py:500
  453.6 67.7 %copy-start.23 = (f32[1024,384]{1,0:T(8,128)S(1)}, f32[1024,384]{1,0:T(8,128)}, u32[]{:S(2)}) copy-start(f32[1024,384]{1,0:T(8,128)} %get-tuple-element.57) | copy-start | bytes 4718596
  453.6 67.7 %copy-start.24 = (f32[1024,384]{1,0:T(8,128)S(1)}, f32[1024,384]{1,0:T(8,128)}, u32[]{:S(2)}) copy-start(f32[1024,384]{1,0:T(8,128)} %get-tuple-element.58) | copy-start | bytes 4718596
  453.6 66.2 %collective-permute-start.10 = (bf16[512,768]{1,0:T(8,128)(2,1)S(1)}, bf16[512,768]{1,0:T(8,128)(2,1)S(1)}, u32[]{:S(2)}, u32[]{:S(2)}) collective-permute-start(bf16[512,768]{1,0:T(8,128)(2,1)S(1)} %get-tuple-element.375), channel_id=1, source_target_pairs={{4,0},{6,2},{8,4},{10,6},{12,8},{14,10},{16,12},{18,14},{20,16},{2... | collective-permute-start | bytes 2359304 | tf_op jit(solution)/shard_map/ppermute | solution.py:500
  455.2 66.1 %collective-permute-start.13 = (bf16[512,768]{1,0:T(8,128)(2,1)S(1)}, bf16[512,768]{1,0:T(8,128)(2,1)S(1)}, u32[]{:S(2)}, u32[]{:S(2)}) collective-permute-start(bf16[512,768]{1,0:T(8,128)(2,1)S(1)} %get-tuple-element.376), channel_id=1, source_target_pairs={{0,4},{2,6},{4,8},{6,10},{8,12},{10,14},{12,16},{14,18},{16,20},{1... | collective-permute-start | bytes 2359304 | tf_op jit(solution)/shard_map/ppermute | solution.py:500
  526.7 298.3 %reduce-scatter.8.cloned.1.call-start = ((), (), s32[]{:S(2)}) async-start(), calls=%async_computation.8 | async-start | bytes 5013504 | tf_op jit(solution)/shard_map/reduce_scatter | solution.py:529
  533.1 20.7 %collective-permute-start.14 = (bf16[1024,768]{1,0:T(8,128)(2,1)}, bf16[1024,768]{1,0:T(8,128)(2,1)}, u32[]{:S(2)}, u32[]{:S(2)}) collective-permute-start(bf16[1024,768]{1,0:T(8,128)(2,1)} %convolution_convert_fusion.4), channel_id=1, source_target_pairs={{0,1},{1,0},{2,3},{3,2},{4,5},{5,4},{6,7},{7,6},{8,9},{9,8},{10,11... | collective-permute-start | bytes 4718600 | tf_op jit(solution)/shard_map/ppermute | solution.py:481
  548.3 281.4 %reduce-scatter.4.cloned.1.call-start = ((), (), s32[]{:S(2)}) async-start(), calls=%async_computation.6 | async-start | bytes 5013504 | tf_op jit(solution)/shard_map/reduce_scatter | solution.py:529
  562.4 145.5 %copy-start.74 = (f32[96]{0:T(128)S(1)}, f32[96]{0:T(128)}, u32[]{:S(2)}) copy-start(f32[96]{0:T(128)} %param.48) | copy-start | bytes 1156
  562.4 145.5 %copy-start.75 = (f32[96]{0:T(128)S(1)}, f32[96]{0:T(128)}, u32[]{:S(2)}) copy-start(f32[96]{0:T(128)} %param.49) | copy-start | bytes 1156
  562.4 146.6 %copy-start.69 = (f32[2,48]{1,0:T(2,128)S(1)}, f32[2,48]{1,0:T(2,128)}, u32[]{:S(2)}) copy-start(f32[2,48]{1,0:T(2,128)} %param.54) | copy-start | bytes 1156
  562.4 146.6 %copy-start.70 = (f32[2,48]{1,0:T(2,128)S(1)}, f32[2,48]{1,0:T(2,128)}, u32[]{:S(2)}) copy-start(f32[2,48]{1,0:T(2,128)} %param.55) | copy-start | bytes 1156
  562.4 147.2 %copy-start.61 = (f32[3,24]{1,0:T(4,128)S(1)}, f32[3,24]{1,0:T(4,128)}, u32[]{:S(2)}) copy-start(f32[3,24]{1,0:T(4,128)} %param.51) | copy-start | bytes 868
  562.4 147.2 %copy-start.66 = (f32[3,24]{1,0:T(4,128)S(1)}, f32[3,24]{1,0:T(4,128)}, u32[]{:S(2)}) copy-start(f32[3,24]{1,0:T(4,128)} %param.52) | copy-start | bytes 868
  563.2 147.0 %copy-start.15 = (bf16[1024,384]{1,0:T(8,128)(2,1)}, bf16[1024,384]{1,0:T(8,128)(2,1)S(1)}, u32[]{:S(2)}) copy-start(bf16[1024,384]{1,0:T(8,128)(2,1)S(1)} %get-tuple-element.332.d_ref) | copy-start | bytes 2359300
  704.4 46.6 %copy-start.58 = (f32[3,24]{1,0:T(4,128)}, f32[3,24]{1,0:T(4,128)S(1)}, u32[]{:S(2)}) copy-start(f32[3,24]{1,0:T(4,128)S(1)} %reshape.513) | copy-start | bytes 868
  705.2 47.2 %collective-permute-start.15 = (bf16[64,384]{1,0:T(8,128)(2,1)S(1)}, bf16[64,384]{1,0:T(8,128)(2,1)S(1)}, u32[]{:S(2)}, u32[]{:S(2)}) collective-permute-start(bf16[64,384]{1,0:T(8,128)(2,1)S(1)} %get-tuple-element.387), channel_id=1, source_target_pairs={{0,2},{2,4},{4,6},{6,8},{8,10},{10,12},{12,14},{14,16},{16,18},{18... | collective-permute-start | bytes 147464 | tf_op jit(solution)/shard_map/ppermute | solution.py:500
  706.5 45.9 %collective-permute-start.16 = (bf16[64,384]{1,0:T(8,128)(2,1)S(1)}, bf16[64,384]{1,0:T(8,128)(2,1)S(1)}, u32[]{:S(2)}, u32[]{:S(2)}) collective-permute-start(bf16[64,384]{1,0:T(8,128)(2,1)S(1)} %get-tuple-element.388), channel_id=1, source_target_pairs={{2,0},{4,2},{6,4},{8,6},{10,8},{12,10},{14,12},{16,14},{18,16},{20... | collective-permute-start | bytes 147464 | tf_op jit(solution)/shard_map/ppermute | solution.py:500
  709.0 91.1 %copy-start.76 = (f32[96]{0:T(128)}, f32[96]{0:T(128)S(1)}, u32[]{:S(2)}) copy-start(f32[96]{0:T(128)S(1)} %get-tuple-element.328) | copy-start | bytes 1156
  710.2 90.4 %copy-start.59 = (f32[3,24]{1,0:T(4,128)}, f32[3,24]{1,0:T(4,128)S(1)}, u32[]{:S(2)}) copy-start(f32[3,24]{1,0:T(4,128)S(1)} %get-tuple-element.325) | copy-start | bytes 868
  752.4 48.8 %copy-start.56 = (f32[3,2,48]{2,1,0:T(2,128)}, f32[3,2,48]{2,1,0:T(2,128)S(1)}, u32[]{:S(2)}) copy-start(f32[3,2,48]{2,1,0:T(2,128)S(1)} %reshape.515) | copy-start | bytes 3460
  753.4 46.6 %copy-start.78 = (f32[96]{0:T(128)S(1)}, f32[96]{0:T(128)}, u32[]{:S(2)}) copy-start(f32[96]{0:T(128)} %param.50) | copy-start | bytes 1156
  753.4 47.2 %copy-start.65 = (f32[3,24]{1,0:T(4,128)S(1)}, f32[3,24]{1,0:T(4,128)}, u32[]{:S(2)}) copy-start(f32[3,24]{1,0:T(4,128)} %param.53) | copy-start | bytes 868
  753.4 47.7 %copy-start.55 = (f32[3,2,48]{2,1,0:T(2,128)S(1)}, f32[3,2,48]{2,1,0:T(2,128)}, u32[]{:S(2)}) copy-start(f32[3,2,48]{2,1,0:T(2,128)} %param.57) | copy-start | bytes 3460
  753.4 47.8 %copy-start.64 = (f32[3,2,48]{2,1,0:T(2,128)S(1)}, f32[3,2,48]{2,1,0:T(2,128)}, u32[]{:S(2)}) copy-start(f32[3,2,48]{2,1,0:T(2,128)} %param.58) | copy-start | bytes 3460
  753.4 48.3 %copy-start.63 = (f32[3,2,48]{2,1,0:T(2,128)S(1)}, f32[3,2,48]{2,1,0:T(2,128)}, u32[]{:S(2)}) copy-start(f32[3,2,48]{2,1,0:T(2,128)} %param.59) | copy-start | bytes 3460
  753.5 65.4 %copy-start.3 = (f32[1024,768]{1,0:T(8,128)S(1)}, f32[1024,768]{1,0:T(8,128)}, u32[]{:S(2)}) copy-start(f32[1024,768]{1,0:T(8,128)} %copy-done.2) | copy-start | bytes 9437188
  798.6 20.3 %collective-permute-start.17 = (bf16[1024,384]{1,0:T(8,128)(2,1)S(1)}, bf16[1024,384]{1,0:T(8,128)(2,1)S(1)}, u32[]{:S(2)}, u32[]{:S(2)}) collective-permute-start(bf16[1024,384]{1,0:T(8,128)(2,1)S(1)} %convert_element_type.207), channel_id=1, source_target_pairs={{0,1},{1,0},{2,3},{3,2},{4,5},{5,4},{6,7},{7,6},{8,9},{9,8},{10,11... | collective-permute-start | bytes 2359304 | tf_op jit(solution)/shard_map/ppermute | solution.py:481
  (63 other events, 556.3 us)
Sparse Core Ops, SparseCore 0:
  11.0 55.9 all-gather.4
  69.8 40.7 all-gather.6
  120.5 86.8 all-gather.8
  526.9 133.4 reduce-scatter.5
  664.5 75.9 reduce-scatter.7
  752.5 73.5 reduce-scatter.3

commit v2 on v1

--- a/solution.py
+++ b/solution.py
@@ -8,6 +8,7 @@
 from jax.sharding import PartitionSpec as P
 
 HEAD = 64
+PAIRS = 3
 EPSILON = 1e-05
 
 bf16, f32, i32 = jnp.bfloat16, jnp.float32, jnp.int32
@@ -17,6 +18,7 @@
 NQ = 33
 LCAP = 1408
 PJ = 134
+EXTRA = 16
 VLIM = 58 << 20
 
 
@@ -194,7 +196,7 @@
 
 
 def tap_grad_kernel(
-    chunks_ref, prow_ref, bseg_ref, x_ref, d_ref, out_ref, s_ref, sd_ref, mask_ref, xt_ref, dp_ref, acc_ref
+    chunks_ref, prow_ref, bseg_ref, x_ref, d_ref, small_ref, out_ref, s_ref, sd_ref, mask_ref, xt_ref, dp_ref, acc_ref
 ):
     h = pl.program_id(0)
     base_tile = h // 2
@@ -203,6 +205,7 @@
     @pl.when(h == 0)
     def _():
         out_ref[...] = jnp.zeros_like(out_ref)
+        out_ref[:, out_ref.shape[1] - EXTRA :, :] = small_ref[...]
         dp_ref[...] = jnp.zeros_like(dp_ref)
 
     acc_ref[...] = jnp.zeros_like(acc_ref)
@@ -238,6 +241,7 @@
         return carry
 
     lax.fori_loop(0, chunks, chunk, 0)
+    per = TAPS // out_ref.shape[0]
     low = iota((1, 1, 128), 2) < 64
     row = iota((128, 256), 0)
     lane = iota((128, 256), 1)
@@ -250,24 +254,28 @@
         here = jnp.where(low, now[0], nxt[1]).reshape(step * CG, 128)
         far = jnp.where(low, now[1], nxt[0]).reshape(step * CG, 128)
         both = (here + pltpu.roll(far, 64, 1)).astype(bf16)
-        o = jnp.dot(both, back, preferred_element_type=f32).astype(bf16).reshape(step, CG, 256)
-        out_ref[j0 : j0 + step, :, lanes] += o
-
-
-def tap_grad(plan, window, d_conv):
+        o = jnp.dot(both, back, preferred_element_type=f32).astype(bf16)
+        o = o.reshape(step // per, per * CG, 256)
+        out_ref[j0 // per : (j0 + step) // per, 0 : per * CG, lanes] += o
+
+
+def tap_grad(plan, window, d_conv, small):
     chunks, prow, pcol, bseg = plan
+    devices = small.shape[0]
+    shape = (devices, TAPS // devices * CG + EXTRA, HALF)
     return pl.pallas_call(
         tap_grad_kernel,
         grid=(4,),
-        out_shape=jax.ShapeDtypeStruct((TAPS, CG, HALF), bf16),
+        out_shape=jax.ShapeDtypeStruct(shape, bf16),
         in_specs=[
             smem(),
             whole((8, WIN)),
             whole((LCAP, 128)),
             whole((WIN, HALF)),
             whole((ROWS, HALF)),
+            whole(small.shape),
         ],
-        out_specs=whole((TAPS, CG, HALF)),
+        out_specs=whole(shape),
         scratch_shapes=[
             pltpu.VMEM((4, XM, WIN), bf16),
             pltpu.VMEM((4, CM, ROWS), bf16),
@@ -279,17 +287,18 @@
         compiler_params=pltpu.CompilerParams(vmem_limit_bytes=VLIM),
         cost_estimate=pl.CostEstimate(flops=40_000_000_000, bytes_accessed=9_000_000, transcendentals=0),
         name="tap_gradient",
-    )(chunks, prow, bseg, window, d_conv)
+    )(chunks, prow, bseg, window, d_conv, small)
 REACH = 1536
 SPAN = ROWS + 2 * REACH
-QT, KT = 256, 256
+QT, KT = 128, 1664
+NEAR = REACH - ROWS
 NEG = -1e30
 
 
 def segment_count(ends, positions):
     return jnp.sum((ends[None, :] <= positions[:, None]).astype(i32), axis=1).astype(i32)
 
-def attention_plan(starts, ends, first):
+def attention_plan(starts, ends, first, odd):
     w = first - REACH + jnp.arange(SPAN, dtype=i32)
     kseg = segment_count(ends, w)
     kseg = jnp.where(w < 0, -1, kseg)
@@ -298,10 +307,12 @@
     n = jnp.arange(starts.shape[0], dtype=i32)
     head = jnp.sum(jnp.where(n[None] == edge[:, :1], starts[None], 0), axis=1) - (first - REACH)
     tail = jnp.sum(jnp.where(n[None] == edge[:, -1:], ends[None], 0), axis=1) - (first - REACH)
-    lo = jnp.clip(head // KT, 0, SPAN // KT - 1)
-    hi = jnp.clip((tail + KT - 1) // KT, 1, SPAN // KT)
+    lo = jnp.clip(head // 128, 0, SPAN // 128)
+    hi = jnp.clip((tail + 127) // 128, 1, SPAN // 128)
+    tiles = jnp.maximum((hi - lo + KT // 128 - 1) // (KT // 128), 1)
+    lo = jnp.minimum(lo, SPAN // 128 - tiles * (KT // 128))
     return (
-        jnp.stack([lo, hi]).astype(i32),
+        jnp.stack([lo, tiles, jnp.full_like(lo, odd)]).astype(i32),
         jnp.broadcast_to(qseg[None], (8, ROWS)),
         jnp.broadcast_to(kseg[:, None], (SPAN, 128)),
     )
@@ -311,93 +322,117 @@
     zero = jnp.zeros((), a.dtype)
     return jnp.where(low, a, zero), jnp.where(low, zero, a)
 
-def forward_kernel(range_ref, qseg_ref, kseg_ref, q_ref, k_ref, v_ref, o_ref, lse_ref, vt_ref, m_ref, l_ref, acc_ref):
-    qi = pl.program_id(1)
+def spots(range_ref):
+    odd = range_ref[2, 0] == 1
+    right, end = REACH + ROWS, SPAN - NEAR
+    at = [
+        jnp.where(odd, NEAR, right),
+        jnp.where(odd, right, NEAR),
+        jnp.where(odd, end, 0),
+        jnp.where(odd, 0, end),
+    ]
+    return [pl.multiple_of(x, NEAR) for x in at]
+
+
+def fill_span(range_ref, span_ref, own, others):
+    span_ref[REACH : REACH + ROWS, :] = own[...]
+    for at, piece in zip(spots(range_ref), others):
+        span_ref[pl.ds(at, piece.shape[0]), :] = piece[...]
+
+
+def flip_span(src_ref, dst_ref, lane):
+    for at in range(0, SPAN, 512):
+        dst_ref[:, at : at + 512] = src_ref[at : at + 512, lane : lane + 128].T
+
+
+def same_segment(kseg_ref, qseg_ref, at):
+    ks = kseg_ref[at, :]
+    ks = jnp.concatenate([ks] * (QT // 128), axis=1) if QT > 128 else ks
+    return ks == qseg_ref[0:1, :]
+
+
+def forward_kernel(range_ref, qseg_ref, kseg_ref, q_ref, k0, k1, k2, k3, k4, o_ref, half_ref, lse_ref, span_ref, vt_ref):
+    qi = pl.program_id(0)
 
     @pl.when(qi == 0)
     def _():
-        def flip(t, carry):
-            at = pl.ds(pl.multiple_of(t * KT, KT), KT)
-            vt_ref[:, at] = v_ref[at, :].T
-            return carry
-        lax.fori_loop(range_ref[0, 0], range_ref[1, ROWS // QT - 1], flip, 0)
+        fill_span(range_ref, span_ref, k0, (k1, k2, k3, k4))
+        flip_span(span_ref, vt_ref, 128)
 
     qs = split_heads(q_ref[...])
-    m_ref[...] = jnp.full_like(m_ref, NEG)
-    l_ref[...] = jnp.zeros_like(l_ref)
-    acc_ref[...] = jnp.zeros_like(acc_ref)
+
+    first, count = range_ref[0, qi], range_ref[1, qi]
 
     def tile(t, carry):
-        at = pl.ds(pl.multiple_of(t * KT, KT), KT)
-        ks = kseg_ref[at, :]
-        same = jnp.concatenate([ks] * (QT // 128), axis=1) == qseg_ref[0:1, :]
-        k = k_ref[at, :]
+        at = pl.ds(pl.multiple_of((first + t * (KT // 128)) * 128, 128), KT)
+        same = same_segment(kseg_ref, qseg_ref, at)
+        k = span_ref[at, 0:128]
+        out = []
         for e in range(2):
+            m, l, acc = carry[e]
             s = lax.dot_general(k, qs[e], (((1,), (1,)), ((), ())), preferred_element_type=f32)
             s = jnp.where(same, s, NEG)
-            m = m_ref[e : e + 1, :]
             new = jnp.maximum(m, jnp.max(s, axis=0, keepdims=True))
             p = jnp.exp(s - new)
             alpha = jnp.exp(m - new)
-            l_ref[e : e + 1, :] = l_ref[e : e + 1, :] * alpha + jnp.sum(p, axis=0, keepdims=True)
+            l = l * alpha + jnp.sum(p, axis=0, keepdims=True)
             vt = vt_ref[64 * e : 64 * e + 64, at]
-            acc_ref[e] = acc_ref[e] * alpha + jnp.dot(vt, p.astype(bf16), preferred_element_type=f32)
-            m_ref[e : e + 1, :] = new
-        return carry
-
-    lax.fori_loop(range_ref[0, qi], range_ref[1, qi], tile, 0)
-    o = jnp.concatenate([acc_ref[e] / l_ref[e : e + 1, :] for e in range(2)], axis=0)
-    o_ref[...] = o.T
-    lse_ref[0] = m_ref[...] + jnp.log(l_ref[...])
-
-
-def attend(plan, q, kv):
+            acc = acc * alpha + jnp.dot(vt, p.astype(bf16), preferred_element_type=f32)
+            out.append((new, l, acc))
+        return tuple(out)
+
+    start = (jnp.full((1, QT), NEG, f32), jnp.zeros((1, QT), f32), jnp.zeros((64, QT), f32))
+    ends = lax.fori_loop(0, count, tile, (start, start))
+    o = jnp.concatenate([acc / l for _, l, acc in ends], axis=0).T
+    o_ref[...] = o
+    half_ref[...] = o.astype(bf16)
+    for e in range(2):
+        lse_ref[e : e + 1, :] = ends[e][0] + jnp.log(ends[e][1])
+
+
+def piece_specs(h):
+    return [pl.BlockSpec((n, 256), lambda i: (0, h)) for n in (ROWS, ROWS, ROWS, NEAR, NEAR)]
+
+
+def attend(plan, h, q, pieces):
     ranges, qseg, kseg = plan
     return pl.pallas_call(
         forward_kernel,
-        grid=(HALF // 128, ROWS // QT),
+        grid=(ROWS // QT,),
         out_shape=(
-            jax.ShapeDtypeStruct((ROWS, HALF), f32),
-            jax.ShapeDtypeStruct((HALF // 128, 8, ROWS), f32),
+            jax.ShapeDtypeStruct((ROWS, 128), f32),
+            jax.ShapeDtypeStruct((ROWS, 128), bf16),
+            jax.ShapeDtypeStruct((8, ROWS), f32),
         ),
         in_specs=[
             pl.BlockSpec(memory_space=pltpu.SMEM),
-            pl.BlockSpec((8, QT), lambda h, i: (0, i)),
-            pl.BlockSpec((SPAN, 128), lambda h, i: (0, 0)),
-            pl.BlockSpec((QT, 128), lambda h, i: (i, h)),
-            pl.BlockSpec((SPAN, 128), lambda h, i: (0, h)),
-            pl.BlockSpec((SPAN, 128), lambda h, i: (0, h + HALF // 128)),
-        ],
+            pl.BlockSpec((8, QT), lambda i: (0, i)),
+            pl.BlockSpec((SPAN, 128), lambda i: (0, 0)),
+            pl.BlockSpec((QT, 128), lambda i: (i, h)),
+        ]
+        + piece_specs(h),
         out_specs=(
-            pl.BlockSpec((QT, 128), lambda h, i: (i, h)),
-            pl.BlockSpec((1, 8, QT), lambda h, i: (h, 0, i)),
+            pl.BlockSpec((QT, 128), lambda i: (i, 0)),
+            pl.BlockSpec((QT, 128), lambda i: (i, 0)),
+            pl.BlockSpec((8, QT), lambda i: (0, i)),
         ),
-        scratch_shapes=[
-            pltpu.VMEM((128, SPAN), bf16),
-            pltpu.VMEM((8, QT), f32),
-            pltpu.VMEM((8, QT), f32),
-            pltpu.VMEM((2, 64, QT), f32),
-        ],
+        scratch_shapes=[pltpu.VMEM((SPAN, 256), bf16), pltpu.VMEM((128, SPAN), bf16)],
         compiler_params=pltpu.CompilerParams(vmem_limit_bytes=VLIM),
-        cost_estimate=pl.CostEstimate(flops=20_000_000_000, bytes_accessed=12_000_000, transcendentals=0),
+        cost_estimate=pl.CostEstimate(flops=8_000_000_000, bytes_accessed=8_000_000, transcendentals=0),
         name="attention_forward",
-    )(ranges, qseg, kseg, q, kv, kv)
-
-
-def backward_kernel(range_ref, qseg_ref, kseg_ref, q_ref, k_ref, v_ref, do_ref, o_ref, lse_ref,
-                    dq_ref, dk_far_ref, dv_far_ref, dk_own_ref, dv_own_ref, kt_ref, dk_ref, dv_ref, dqt_ref):
-    qi = pl.program_id(1)
+    )(ranges, qseg, kseg, q, *pieces)
+
+
+def backward_kernel(range_ref, qseg_ref, kseg_ref, q_ref, k0, k1, k2, k3, k4, do_ref, o_ref, lse_ref,
+                    dq_ref, own_ref, f1, f2, f3, f4, span_ref, kt_ref, dkv_ref):
+    qi = pl.program_id(0)
     last = ROWS // QT - 1
 
     @pl.when(qi == 0)
     def _():
-        dk_ref[...] = jnp.zeros_like(dk_ref)
-        dv_ref[...] = jnp.zeros_like(dv_ref)
-        def flip(t, carry):
-            at = pl.ds(pl.multiple_of(t * KT, KT), KT)
-            kt_ref[:, at] = k_ref[at, :].T
-            return carry
-        lax.fori_loop(range_ref[0, 0], range_ref[1, last], flip, 0)
+        dkv_ref[...] = jnp.zeros_like(dkv_ref)
+        fill_span(range_ref, span_ref, k0, (k1, k2, k3, k4))
+        flip_span(span_ref, kt_ref, 0)
 
     qs = split_heads(q_ref[...])
     dos = split_heads(do_ref[...])
@@ -405,76 +440,75 @@
     docat = jnp.concatenate(dos, axis=0)
     dm = (do_ref[...].astype(f32) * o_ref[...]).T
     delta = [jnp.sum(dm[64 * e : 64 * e + 64], axis=0, keepdims=True) for e in range(2)]
-    dqt_ref[...] = jnp.zeros_like(dqt_ref)
+
+    first, count = range_ref[0, qi], range_ref[1, qi]
 
     def tile(t, carry):
-        at = pl.ds(pl.multiple_of(t * KT, KT), KT)
-        ks = kseg_ref[at, :]
-        same = jnp.concatenate([ks] * (QT // 128), axis=1) == qseg_ref[0:1, :]
-        k = k_ref[at, :]
-        v = v_ref[at, :]
-        ps, dss = [], []
+        at = pl.ds(pl.multiple_of((first + t * (KT // 128)) * 128, 128), KT)
+        same = same_segment(kseg_ref, qseg_ref, at)
+        k = span_ref[at, 0:128]
+        v = span_ref[at, 128:256]
+        ps, dss, out = [], [], []
         for e in range(2):
             dims = (((1,), (1,)), ((), ()))
             s = lax.dot_general(k, qs[e], dims, preferred_element_type=f32)
-            p = jnp.exp(jnp.where(same, s - lse_ref[0, e : e + 1, :], NEG))
+            p = jnp.exp(jnp.where(same, s - lse_ref[e : e + 1, :], NEG))
             dp = lax.dot_general(v, dos[e], dims, preferred_element_type=f32)
             ds = (p * (dp - delta[e])).astype(bf16)
-            dqt_ref[e] += jnp.dot(kt_ref[64 * e : 64 * e + 64, at], ds, preferred_element_type=f32)
+            kt = kt_ref[64 * e : 64 * e + 64, at]
+            out.append(carry[e] + jnp.dot(kt, ds, preferred_element_type=f32))
             ps.append(p.astype(bf16))
             dss.append(ds)
-        dk_ref[at, :] += jnp.dot(jnp.concatenate(dss, axis=1), qcat, preferred_element_type=f32)
-        dv_ref[at, :] += jnp.dot(jnp.concatenate(ps, axis=1), docat, preferred_element_type=f32)
-        return carry
-
-    lax.fori_loop(range_ref[0, qi], range_ref[1, qi], tile, 0)
-    dq = jnp.concatenate([dqt_ref[0], dqt_ref[1]], axis=0).T
+        dkv_ref[at, 0:128] += jnp.dot(jnp.concatenate(dss, axis=1), qcat, preferred_element_type=f32)
+        dkv_ref[at, 128:256] += jnp.dot(jnp.concatenate(ps, axis=1), docat, preferred_element_type=f32)
+        return tuple(out)
+
+    zero = jnp.zeros((64, QT), f32)
+    dqt = lax.fori_loop(0, count, tile, (zero, zero))
+    dq = jnp.concatenate(dqt, axis=0).T
     dq_ref[...] = dq.astype(bf16) * jnp.asarray(0.125, bf16)
 
     @pl.when(qi == last)
     def _():
-        for far, own, acc in ((dk_far_ref, dk_own_ref, dk_ref), (dv_far_ref, dv_own_ref, dv_ref)):
-            far[0:REACH, :] = acc[0:REACH, :].astype(bf16)
-            far[REACH : 2 * REACH, :] = acc[REACH + ROWS : SPAN, :].astype(bf16)
-            own[...] = acc[REACH : REACH + ROWS, :]
-
-
-def attend_back(plan, q, kv, d_att, mixed, lse):
+        for at, far in zip(spots(range_ref), (f1, f2, f3, f4)):
+            far[...] = dkv_ref[pl.ds(at, far.shape[0]), :].astype(bf16)
+        own_ref[...] = dkv_ref[REACH : REACH + ROWS, :]
+
+
+def attend_back(plan, h, q, pieces, d_att, mixed, lse):
     ranges, qseg, kseg = plan
-    rowspec = pl.BlockSpec((QT, 128), lambda h, i: (i, h))
-    span = pl.BlockSpec((SPAN, 128), lambda h, i: (0, h))
-    span_v = pl.BlockSpec((SPAN, 128), lambda h, i: (0, h + HALF // 128))
-    far = pl.BlockSpec((2 * REACH, 128), lambda h, i: (0, h))
-    own = pl.BlockSpec((ROWS, 128), lambda h, i: (0, h))
-    dq, dk_far, dv_far, dk_own, dv_own = pl.pallas_call(
+    rowspec = pl.BlockSpec((QT, 128), lambda i: (i, 0))
+    colspec = pl.BlockSpec((QT, 128), lambda i: (i, h))
+    return pl.pallas_call(
         backward_kernel,
-        grid=(HALF // 128, ROWS // QT),
+        grid=(ROWS // QT,),
         out_shape=(
-            jax.ShapeDtypeStruct((ROWS, HALF), bf16),
-            jax.ShapeDtypeStruct((2 * REACH, HALF), bf16),
-            jax.ShapeDtypeStruct((2 * REACH, HALF), bf16),
-            jax.ShapeDtypeStruct((ROWS, HALF), f32),
-            jax.ShapeDtypeStruct((ROWS, HALF), f32),
-        ),
+            jax.ShapeDtypeStruct((ROWS, 128), bf16),
+            jax.ShapeDtypeStruct((ROWS, 256), f32),
+        )
+        + tuple(jax.ShapeDtypeStruct((n, 256), bf16) for n in (ROWS, ROWS, NEAR, NEAR)),
         in_specs=[
             pl.BlockSpec(memory_space=pltpu.SMEM),
-            pl.BlockSpec((8, QT), lambda h, i: (0, i)),
-            pl.BlockSpec((SPAN, 128), lambda h, i: (0, 0)),
-            rowspec, span, span_v, rowspec, rowspec,
-            pl.BlockSpec((1, 8, QT), lambda h, i: (h, 0, i)),
-        ],
-        out_specs=(rowspec, far, far, own, own),
+            pl.BlockSpec((8, QT), lambda i: (0, i)),
+            pl.BlockSpec((SPAN, 128), lambda i: (0, 0)),
+            colspec,
+        ]
+        + piece_specs(h)
+        + [colspec, rowspec, pl.BlockSpec((8, QT), lambda i: (0, i))],
+        out_specs=(
+            rowspec,
+            pl.BlockSpec((ROWS, 256), lambda i: (0, 0)),
+        )
+        + tuple(pl.BlockSpec((n, 256), lambda i: (0, 0)) for n in (ROWS, ROWS, NEAR, NEAR)),
         scratch_shapes=[
+            pltpu.VMEM((SPAN, 256), bf16),
             pltpu.VMEM((128, SPAN), bf16),
-            pltpu.VMEM((SPAN, 128), f32),
-            pltpu.VMEM((SPAN, 128), f32),
-            pltpu.VMEM((2, 64, QT), f32),
+            pltpu.VMEM((SPAN, 256), f32),
         ],
         compiler_params=pltpu.CompilerParams(vmem_limit_bytes=VLIM),
-        cost_estimate=pl.CostEstimate(flops=50_000_000_000, bytes_accessed=25_000_000, transcendentals=0),
+        cost_estimate=pl.CostEstimate(flops=8_000_000_000, bytes_accessed=12_000_000, transcendentals=0),
         name="attention_backward",
-    )(ranges, qseg, kseg, q, kv, kv, d_att, mixed, lse)
-    return dq, jnp.concatenate([dk_far, dv_far], axis=1), jnp.concatenate([dk_own, dv_own], axis=1)
+    )(ranges, qseg, kseg, q, *pieces, d_att, mixed, lse)
 
 
 def exchange(part):
@@ -498,6 +532,22 @@
     count = lax.axis_size("seq")
     route = [(i - distance, i) for i in range(count) if 0 <= i - distance < count]
     return lax.ppermute(block, "seq", route)
+
+
+def across_cores(block):
+    return lax.ppermute(block, "seq", [(i, i ^ 1) for i in range(lax.axis_size("seq"))])
+
+
+def across_chips(block):
+    count = lax.axis_size("seq")
+    route = [(i, i + 1 if i % 2 else i - 1) for i in range(count)]
+    return lax.ppermute(block, "seq", [(i, j) for i, j in route if 0 <= j < count])
+
+
+def chip_along(block, step):
+    count = lax.axis_size("seq")
+    route = [(i, i - 2 * step if i % 2 else i + 2 * step) for i in range(count)]
+    return lax.ppermute(block, "seq", [(i, j) for i, j in route if 0 <= j < count])
 
 
 def layer_norm(values, gain, shift):
@@ -566,6 +616,7 @@
     total = devices * rows
     first = lax.axis_index("seq") * rows
     index = lax.axis_index("heads")
+    odd = lax.axis_index("seq") % 2
     local = project.shape[0]
     hidden_units = expand.shape[1]
 
@@ -576,10 +627,15 @@
     w_small = gathered(small[None])
     w_first = gathered(
         jnp.concatenate(
-            [project[:, 0], project[:, 1], project[:, 2], combine.T], axis=1
+            [project[:, 0]]
+            + [project[:, c, 128 * h : 128 * h + 128] for h in range(PAIRS) for c in (1, 2)]
+            + [combine.T],
+            axis=1,
         ).astype(bf16)
     )
     w_second = gathered(jnp.concatenate([expand, shrink.T], axis=1).astype(bf16))
+    w_combine = w_first[:, 3 * HALF :]
+    w_combine_far = exchange(w_combine)
     cuts = [unitbias.size, chanbias.size, outbias.size, normparams.size]
     parts, at = [], 0
     for size in cuts:
@@ -595,7 +651,7 @@
     ends = jnp.sum(jnp.where(order[None, :] <= order[:, None], lengths[None, :], 0), axis=1).astype(i32)
     starts = ends - lengths
     plan = block_plan(starts, ends, first)
-    reach = attention_plan(starts, ends, first)
+    reach = attention_plan(starts, ends, first, odd)
 
     x_half = lax.dynamic_slice_in_dim(frames, index * HALF, HALF, 1).astype(bf16)
     window = jnp.concatenate(
@@ -609,24 +665,33 @@
     proj = dot(h1_half, w_first[:, : 3 * HALF], 1, 0)
     scale = HEAD ** (-0.5)
     queries = ((proj[:, :HALF] + b_chan[1]) * scale).astype(bf16)
-    keys = proj[:, HALF : 2 * HALF].astype(bf16)
-    values = (proj[:, 2 * HALF :] + b_chan[2]).astype(bf16)
-    both = jnp.concatenate([keys, values], axis=1)
-    near = REACH - rows
-    span = jnp.concatenate(
-        [
-            passed(both[rows - near :], 2),
-            passed(both, 1),
-            both,
-            passed(both, -1),
-            passed(both[:near], -2),
-        ],
-        axis=0,
-    )
-    mixed, lse = attend(reach, queries, span)
-    attended = mixed.astype(bf16)
-    w_combine = w_first[:, 3 * HALF :]
-    branch = pair_sum(dot(attended, w_combine, 1, 1))
+    kv_bias = b_chan[2].reshape(PAIRS, 1, 128)
+    kv_bias = jnp.concatenate([jnp.zeros_like(kv_bias), kv_bias], axis=1).reshape(-1)
+    both = (proj[:, HALF:] + kv_bias).astype(bf16)
+    near = NEAR
+    beside = across_chips(both)
+    further = chip_along(jnp.where(odd == 1, both[:near], both[rows - near :]), 1)
+    pieces = (
+        both,
+        across_cores(both),
+        beside,
+        further,
+        across_cores(jnp.where(odd == 1, beside[:near], beside[rows - near :])),
+    )
+    mixed, attended, attended_far, lse = [], [], [], []
+    for h in range(PAIRS):
+        if h == 0:
+            q_part, w_combine_far = lax.optimization_barrier((queries, w_combine_far))
+        if h >= 2:
+            q_part, attended_far[h - 2] = lax.optimization_barrier((queries, attended_far[h - 2]))
+        mixed_part, half, lse_part = attend(reach, h, q_part, pieces)
+        mixed.append(mixed_part)
+        lse.append(lse_part)
+        attended.append(half)
+        attended_far.append(exchange(half))
+    attended = jnp.concatenate(attended, axis=1)
+    attended_all = side_by_side(attended, jnp.concatenate(attended_far, axis=1), index)
+    branch = dot(attended_all, side_by_side(w_combine, w_combine_far, index), 1, 1)
     h2, norm1_back = jax.vjp(layer_norm, h1 + branch + b_out[0], norms[1, 0], norms[1, 1])
     h2_half = h2.astype(bf16)
     w_expand = w_second[:, :hidden_units]
@@ -644,55 +709,68 @@
     unit_grad = jnp.sum(d_inner, axis=0)
     d_inner_half = d_inner.astype(bf16)
     dh2 = dx3 + pair_sum(dot(d_inner_half, w_expand, 1, 1))
-    second_sum = scattered(
-        jnp.concatenate(
-            [dot(h2_half, d_inner_half, 0, 0).astype(bf16), dot(d_out, hidden_half, 0, 0).astype(bf16)],
-            axis=1,
-        )
-    ).astype(f32)
+    second_part = jnp.concatenate(
+        [dot(h2_half, d_inner_half, 0, 0).astype(bf16), dot(d_out, hidden_half, 0, 0).astype(bf16)],
+        axis=1,
+    )
     dx2, gain1_grad, shift1_grad = norm1_back(dh2)
     branch_bias_grad = jnp.sum(dx2, axis=0)
     d_branch = dx2.astype(bf16)
     d_att = dot(d_branch, w_combine, 1, 0).astype(bf16)
-    dq_half, far, own = attend_back(reach, queries, span, d_att, mixed, lse)
-    d_both = own
-    for distance, lo, hi, to in (
-        (2, 0, near, rows - near),
-        (1, near, REACH, 0),
-        (-1, REACH, REACH + rows, 0),
-        (-2, REACH + rows, 2 * REACH, 0),
-    ):
-        back = passed(far[lo:hi], -distance).astype(f32)
-        pad = (to, rows - to - back.shape[0])
-        d_both = d_both + jnp.pad(back, (pad, (0, 0)))
-    d_both_half = d_both.astype(bf16)
+    d_att, second_part = lax.optimization_barrier((d_att, second_part))
+    second_sum = scattered(second_part).astype(f32)
+    dq_parts, kv_parts = [], []
+    arrived = {}
+    for h in range(PAIRS):
+        d_part = d_att
+        if h >= 1:
+            d_part, passed_on = lax.optimization_barrier((d_part, passed_on))
+            chip = (chip.astype(f32) + passed_on).astype(bf16)
+            arrived[h - 1] = (across_cores(core), across_chips(chip), chip_along(far, -1), own)
+        if h >= 2:
+            d_part, arrived[h - 2] = lax.optimization_barrier((d_part, arrived[h - 2]))
+        dq_part, own, core, chip, far, near_far = attend_back(
+            reach, h, queries, pieces, d_part, mixed[h], lse[h]
+        )
+        passed_on = across_cores(near_far).astype(f32)
+        none = jnp.zeros_like(passed_on)
+        passed_on = jnp.concatenate(
+            [jnp.where(odd == 1, passed_on, none), jnp.where(odd == 1, none, passed_on)], axis=0
+        )
+        dq_parts.append(dq_part)
+    chip = (chip.astype(f32) + passed_on).astype(bf16)
+    arrived[PAIRS - 1] = (across_cores(core), across_chips(chip), chip_along(far, -1), own)
+    for h in range(PAIRS):
+        core, chip, far, own = arrived[h]
+        far = far.astype(f32)
+        none = jnp.zeros_like(far)
+        far = jnp.concatenate([jnp.where(odd == 1, far, none), jnp.where(odd == 1, none, far)], axis=0)
+        kv_parts.append((own + core.astype(f32) + chip.astype(f32) + far).astype(bf16))
+    dq_half = jnp.concatenate(dq_parts, axis=1)
+    d_both_half = jnp.concatenate(kv_parts, axis=1)
     stacked = jnp.concatenate([dq_half, d_both_half], axis=1)
     query_bias_grad = jnp.sum(dq_half.astype(f32), axis=0)
-    value_bias_grad = jnp.sum(d_both_half[:, HALF:].astype(f32), axis=0)
+    value_bias_grad = jnp.sum(
+        d_both_half.astype(f32), axis=0
+    ).reshape(PAIRS, 2, 128)[:, 1].reshape(-1)
     dh1 = dx2 + pair_sum(dot(stacked, w_first[:, : 3 * HALF], 1, 1))
-    first_sum = scattered(
+    first_part = (
         jnp.concatenate(
             [dot(h1_half, stacked, 0, 0).astype(bf16), dot(d_branch, attended, 0, 0).astype(bf16)],
             axis=1,
         )
-    ).astype(f32)
+    )
+    first_part, second_sum = lax.optimization_barrier((first_part, second_sum))
+    first_sum = scattered(first_part).astype(f32)
     dx1, gain0_grad, shift0_grad = norm0_back(dh1)
     d_spread = lax.dynamic_slice_in_dim(dx1, index * HALF, HALF, 1)
     d_conv = jax.vjp(gelu_exact, pre)[1](d_spread)[0]
     conv_bias_grad = jnp.sum(d_conv, axis=0)
     d_conv_half = d_conv.astype(bf16)
-    kernel_sum = scattered(tap_grad(plan, window, d_conv_half)).astype(f32)
-    d_window = jnp.concatenate(
-        [passed(d_conv_half[rows - HALO :], 1), d_conv_half, passed(d_conv_half[:HALO], -1)], axis=0
-    )
-    d_input = conv(plan, d_window, w_kernel, True).astype(bf16)
-    frames_grad = dx1 + side_by_side(d_input, exchange(d_input), index).astype(f32)
-
     spread_out = lambda grad, lead: jnp.transpose(
         grad.reshape(lead, devices, -1), (1, 0, 2)
     ).reshape(devices, -1)
-    small_sum = scattered(
-        jnp.concatenate(
+    small_part = jnp.concatenate(
             [
                 unit_grad.reshape(devices, -1),
                 spread_out(jnp.stack([conv_bias_grad, query_bias_grad, value_bias_grad]), 3),
@@ -706,7 +784,19 @@
             ],
             axis=1,
         )
-    )[0]
+    small_part = jnp.pad(small_part, ((0, 0), (0, EXTRA * HALF - small_part.shape[1])))
+    small_part = small_part.astype(bf16).reshape(devices, EXTRA, HALF)
+    tap_part = tap_grad(plan, window, d_conv_half, small_part)
+    tap_part, first_sum = lax.optimization_barrier((tap_part, first_sum))
+    tap_sum = scattered(tap_part)[0].astype(f32)
+    kernel_sum = tap_sum[:-EXTRA].reshape(TAPS // devices, CG, HALF)
+    small_sum = tap_sum[-EXTRA:].reshape(-1)
+    d_window = jnp.concatenate(
+        [passed(d_conv_half[rows - HALO :], 1), d_conv_half, passed(d_conv_half[:HALO], -1)], axis=0
+    )
+    d_input = conv(plan, d_window, w_kernel, True).astype(bf16)
+    frames_grad = dx1 + side_by_side(d_input, exchange(d_input), index).astype(f32)
+
     pieces, at = [], 0
     for size in cuts:
         pieces.append(small_sum[at : at + size])
@@ -715,7 +805,10 @@
     chan_sum = pieces[1].reshape(chanbias.shape)
     out_sum = pieces[2].reshape(outbias.shape)
     norm_sum = pieces[3].reshape(normparams.shape)
-    project_sum = jnp.stack([first_sum[:, HALF * i : HALF * (i + 1)] for i in range(3)], axis=1)
+    kv_sum = first_sum[:, HALF : 3 * HALF].reshape(local, PAIRS, 2, 128)
+    project_sum = jnp.stack(
+        [first_sum[:, :HALF]] + [kv_sum[:, :, c].reshape(local, HALF) for c in range(2)], axis=1
+    )
 
     root = total**0.5
     small_rate = 0.1 / root

time: 851 us -> 787 us (0.925)
  blocking collectives: 165 us -> 25.2 us
  Pallas kernels: 197 us -> 229 us
  waiting for transfers between devices: 170 us -> 191 us
  other arithmetic: 69.5 us -> 81.8 us
    unnamed x1 -> x0, blocking collectives: 140 us -> none
    ppermute x12 -> x4, starting transfers between devices: 111 us -> 16.2 us  [passed(): return lax.ppermute(block, 'seq', route)]
    ppermute x0 -> x16, starting transfers between devices: none -> 91.1 us  [the longest x8 76.9 us: across_cores(): lax.ppermute(block, 'seq', [(i, i ^ 1) for i in range(lax.axis_size('seq'...]
    ppermute x12 -> x4, waiting for transfers between devices: 58.1 us -> 0.01 us  [passed(): return lax.ppermute(block, 'seq', route)]
    reduce_scatter x3, waiting for transfers between devices: 0.02 us -> 34.5 us  [scattered(): return lax.psum_scatter(whole_sum, 'seq', scatter_dimension=0, tiled=True)]
    pallas_call x2 -> x6, Pallas kernels: 69.6 us -> 103 us  [the longest x3 55.7 us: attend_back(): pl.pallas_call(backward_kernel, grid=(ROWS // QT,), out_shape=(jax.ShapeD...]
    ppermute x6 -> x9, waiting for transfers between devices: 91.8 us -> 123 us  [exchange(): return lax.ppermute(part, 'heads', [(0, 1), (1, 0)])]
    ppermute x0 -> x16, waiting for transfers between devices: none -> 12.9 us  [the longest x4 12.9 us: chip_along(): lax.ppermute(block, 'seq', [(i, j) for i, j in route if 0 <= j < count])]
  transfers between devices with their start and end apart: 24 -> 35, of which waited for: 10 -> 11; matrix products, arithmetic and copies ran while one was open for 11% -> 14% of each run, Pallas kernels for 19% -> 27%
where the time goes in v2:
time: 787 us; the launch traced here: 774 us
  Pallas kernels  229 us (29%)
  waiting for transfers between devices  191 us (24%)
  starting transfers between devices  122 us (16%)
  other arithmetic  81.8 us (10%)
  matrix products  63.6 us (8%)
  local copies, waits for them, and re-layouts  42.5 us (5%)
  blocking collectives  25.2 us (3%)
  between operations  18.5 us (2%)
    ppermute x9, waiting for transfers between devices, exchange(): return lax.ppermute(part, 'heads', [(0, 1), (1, 0)])  123 us
    pallas_call x2, Pallas kernels, conv(): pl.pallas_call(functools.partial(conv_kernel, back), grid=(4,), out_shape...  86.2 us
    ppermute x8, starting transfers between devices, across_cores(): lax.ppermute(block, 'seq', [(i, i ^ 1) for i in range(lax.axis_size('seq'...  76.9 us
    dot_general x12, matrix products, dot(): lax.dot_general(a, b, (((ca,), (cb,)), ((), ())), preferred_element_type=...  63.6 us
    pallas_call x3, Pallas kernels, attend_back(): pl.pallas_call(backward_kernel, grid=(ROWS // QT,), out_shape=(jax.ShapeD...  55.7 us
    pallas_call x3, Pallas kernels, attend(): pl.pallas_call(forward_kernel, grid=(ROWS // QT,), out_shape=(jax.ShapeDt...  47 us
    pallas_call x1, Pallas kernels, tap_grad(): pl.pallas_call(tap_grad_kernel, grid=(4,), out_shape=jax.ShapeDtypeStruct...  40.7 us
    reduce_scatter x3, waiting for transfers between devices, scattered(): return lax.psum_scatter(whole_sum, 'seq', scatter_dimension=0, tiled=True)  34.5 us
  transfers between devices with their start and end apart: 35, of which 11 were waited for; matrix products, arithmetic and copies ran while one was open for 14% of the time, Pallas kernels for 27%

profile of v2, /device:TPU:0, one launch (start us, length us, event | category | flops | bytes accessed | tf_op | source)
XLA Modules:
  0.0 773.9 jit_solution(8103796826961818125)
XLA Ops:
  17.3 25.2 %all-gather = bf16[16,1,552]{2,1,0:T(2,128)(2,1)S(1)} all-gather(bf16[1,1,552]{2,1,0:T(2,128)(2,1)S(1)} %maximum_bitcast_fusion.2), channel_id=1, replica_groups=mesh['seq'=16,'heads'=2] {'seq'}, dimensions={0}, use_global_device_ids=true | all-gather | bytes 18768 | tf_op jit(solution)/shard_map/all_gather | solution.py:575
  47.1 20.0 %all-gather.5.cloned.1.call-done.k_ref = bf16[128,48,384]{2,1,0:T(8,128)(2,1)} async-done(((bf16[8,48,384]{2,1,0:T(8,128)(2,1)}), bf16[128,48,384]{2,1,0:T(8,128)(2,1)}) %all-gather.5.cloned.1.call-update) | async-done | bytes 4718608 | tf_op jit(solution)/shard_map/all_gather | solution.py:575
  69.9 42.7 %conv_forward.1 = f32[1024,384]{1,0:T(8,128)} custom-call(s32[1]{0:T(128)} %bitcast.1.chunks_ref, s32[8,1152]{1,0:T(8,128)} %broadcast_in_dim.84.prow_ref, s32[1152,128]{1,0:T(8,128)} %broadcast_in_dim.142.pcol_ref, s32[1408,128]{1,0:T(8,128)} %broadcast_in_dim.145.bseg_ref, bf16[1152,384]{1,0:T(8,128)(2,1)} %pad_maximum_fusion.4.x_ref, ...), custom_call_target="tpu_custom_call" | custom-call | flops 30000001024 | bytes 9000000 | tf_op jit(solution)/shard_map/conv_forward/pallas_call | solution.py:173
  112.7 5.5 multiply_convert_fusion.1
  121.5 16.5 %collective-permute-done.2 = bf16[1024,384]{1,0:T(8,128)(2,1)} collective-permute-done((bf16[1024,384]{1,0:T(8,128)(2,1)S(1)}, bf16[1024,384]{1,0:T(8,128)(2,1)}, u32[]{:S(2)}, u32[]{:S(2)}) %collective-permute-start.2) | collective-permute-done | bytes 786464 | tf_op jit(solution)/shard_map/ppermute | solution.py:515
  138.0 3.4 fusion.95
  141.9 3.9 fusion.38
  154.9 5.2 collective-permute-start.6
  162.4 48.7 %collective-permute-start.7 = (bf16[512,768]{1,0:T(8,128)(2,1)}, bf16[512,768]{1,0:T(8,128)(2,1)}, u32[]{:S(2)}, u32[]{:S(2)}) collective-permute-start(bf16[512,768]{1,0:T(8,128)(2,1)} %slice_select_fusion), channel_id=1, source_target_pairs={{0,2},{2,0},{4,6},{6,4},{8,10},{10,8},{12,14},{14,12},{16,18},{18,... | collective-permute-start | bytes 2359304 | tf_op jit(solution)/shard_map/ppermute | solution.py:538
  218.4 10.5 %collective-permute-done.3 = bf16[768,384]{1,0:T(8,128)(2,1)} collective-permute-done((bf16[768,384]{1,0:T(8,128)(2,1)}, bf16[768,384]{1,0:T(8,128)(2,1)}, u32[]{:S(2)}, u32[]{:S(2)}) %collective-permute-start.3) | collective-permute-done | bytes 589856 | tf_op jit(solution)/shard_map/ppermute | solution.py:515
  228.9 3.0 broadcast_in_dim.152.kseg_ref
  232.5 15.6 %attention_forward.3 = (f32[1024,128]{1,0:T(8,128)}, bf16[1024,128]{1,0:T(8,128)(2,1)}, f32[8,1024]{1,0:T(8,128)}) custom-call(s32[3,8]{1,0:T(4,128)} %add_add_fusion.7.range_ref, s32[8,1024]{1,0:T(8,128)} %broadcast_in_dim.151.qseg_ref, s32[4096,128]{1,0:T(8,128)} %broadcast_in_dim.152.kseg_ref, bf16[1024,384]{1,0:T(8,128)(2,1)} %fusion.27.q_ref, ...), custom_call_target="tpu_custom_call" | custom-call | flops 8000000000 | bytes 8000000 | tf_op jit(solution)/shard_map/attention_forward/pallas_call | solution.py:399
  249.9 15.6 %attention_forward.4 = (f32[1024,128]{1,0:T(8,128)}, bf16[1024,128]{1,0:T(8,128)(2,1)}, f32[8,1024]{1,0:T(8,128)}) custom-call(s32[3,8]{1,0:T(4,128)} %add_add_fusion.7.range_ref, s32[8,1024]{1,0:T(8,128)} %broadcast_in_dim.151.qseg_ref, s32[4096,128]{1,0:T(8,128)} %broadcast_in_dim.152.kseg_ref, bf16[1024,384]{1,0:T(8,128)(2,1)} %fusion.27.q_ref, ...), custom_call_target="tpu_custom_call" | custom-call | flops 8000000000 | bytes 8000000 | tf_op jit(solution)/shard_map/attention_forward/pallas_call | solution.py:399
  265.9 15.7 %attention_forward.5 = (f32[1024,128]{1,0:T(8,128)}, bf16[1024,128]{1,0:T(8,128)(2,1)}, f32[8,1024]{1,0:T(8,128)}) custom-call(s32[3,8]{1,0:T(4,128)} %add_add_fusion.7.range_ref, s32[8,1024]{1,0:T(8,128)} %broadcast_in_dim.151.qseg_ref, s32[4096,128]{1,0:T(8,128)} %broadcast_in_dim.152.kseg_ref, bf16[1024,384]{1,0:T(8,128)(2,1)} %fusion.27.q_ref, ...), custom_call_target="tpu_custom_call" | custom-call | flops 8000000000 | bytes 8000000 | tf_op jit(solution)/shard_map/attention_forward/pallas_call | solution.py:399
  284.7 4.6 collective-permute-done.10
  294.7 3.5 fusion.100
  300.4 20.3 %multiply_convert_fusion = (bf16[1024,1536]{1,0:T(8,128)(2,1)S(1)}, f32[1024,1536]{1,0:T(8,128)}, f32[1024,1536]{1,0:T(8,128)}) fusion(f32[1536]{0:T(1024)S(1)} %reshape.603, bf16[768,3072]{1,0:T(8,128)(2,1)} %all-gather.9.cloned.1.call-done, f32[1024,768]{1,0:T(8,128)} %copy-done, f32[768]{0:T(1024)S(1)} %get-tuple-element.155, ...), kind=kOutput, calls=%fused_computation.3 | convolution fusion | flops 2523660288 | bytes 21254144 | tf_op jit(solution)/shard_map/dot_general | solution.py:571
  320.7 3.7 fusion.22
  326.3 35.1 %collective-permute-done.11 = bf16[1024,768]{1,0:T(8,128)(2,1)} collective-permute-done((bf16[1024,768]{1,0:T(8,128)(2,1)}, bf16[1024,768]{1,0:T(8,128)(2,1)}, u32[]{:S(2)}, u32[]{:S(2)}) %collective-permute-start.11) | collective-permute-done | bytes 1572896 | tf_op jit(solution)/shard_map/ppermute | solution.py:515
  361.4 4.2 fusion.93
  369.1 2.7 fusion.92
  373.0 7.1 fusion.101
  380.1 4.1 fusion.19
  386.0 3.0 convolution_convert_fusion
  389.0 3.2 convolution_convert_fusion.1
  392.3 2.7 pad_maximum_fusion
  395.0 26.4 %collective-permute-done.12 = bf16[1024,768]{1,0:T(8,128)(2,1)} collective-permute-done((bf16[1024,768]{1,0:T(8,128)(2,1)}, bf16[1024,768]{1,0:T(8,128)(2,1)}, u32[]{:S(2)}, u32[]{:S(2)}) %collective-permute-start.12) | collective-permute-done | bytes 1572896 | tf_op jit(solution)/shard_map/ppermute | solution.py:515
  421.3 4.8 multiply_reduce_fusion.1
  429.3 3.0 convolution_convert_fusion.4.do_ref
  432.3 18.5 %attention_backward.3 = (bf16[1024,128]{1,0:T(8,128)(2,1)}, f32[1024,256]{1,0:T(8,128)}, bf16[1024,256]{1,0:T(8,128)(2,1)}, bf16[1024,256]{1,0:T(8,128)(2,1)}, b...) custom-call(s32[3,8]{1,0:T(4,128)} %add_add_fusion.7.range_ref, s32[8,1024]{1,0:T(8,128)} %broadcast_in_dim.151.qseg_ref, ...), custom_call_target="tpu_custom_call" | custom-call | flops 8000000000 | bytes 12000000 | tf_op jit(solution)/shard_map/attention_backward/pallas_call | solution.py:482
  455.3 18.6 %attention_backward.4 = (bf16[1024,128]{1,0:T(8,128)(2,1)}, f32[1024,256]{1,0:T(8,128)}, bf16[1024,256]{1,0:T(8,128)(2,1)}, bf16[1024,256]{1,0:T(8,128)(2,1)}, b...) custom-call(s32[3,8]{1,0:T(4,128)} %add_add_fusion.7.range_ref, s32[8,1024]{1,0:T(8,128)} %broadcast_in_dim.151.qseg_ref, ...), custom_call_target="tpu_custom_call" | custom-call | flops 8000000000 | bytes 12000000 | tf_op jit(solution)/shard_map/attention_backward/pallas_call | solution.py:482
  480.4 6.6 collective-permute-start.18
  487.3 12.9 %collective-permute-done.20 = bf16[512,256]{1,0:T(8,128)(2,1)S(1)} collective-permute-done((bf16[512,256]{1,0:T(8,128)(2,1)}, bf16[512,256]{1,0:T(8,128)(2,1)S(1)}, u32[]{:S(2)}, u32[]{:S(2)}) %collective-permute-start.20) | collective-permute-done | bytes 262176 | tf_op jit(solution)/shard_map/ppermute | solution.py:550
  501.8 18.7 %attention_backward.5 = (bf16[1024,128]{1,0:T(8,128)(2,1)}, f32[1024,256]{1,0:T(8,128)}, bf16[1024,256]{1,0:T(8,128)(2,1)}, bf16[1024,256]{1,0:T(8,128)(2,1)}, b...) custom-call(s32[3,8]{1,0:T(4,128)} %add_add_fusion.7.range_ref, s32[8,1024]{1,0:T(8,128)} %broadcast_in_dim.151.qseg_ref, ...), custom_call_target="tpu_custom_call" | custom-call | flops 8000000000 | bytes 12000000 | tf_op jit(solution)/shard_map/attention_backward/pallas_call | solution.py:482
  520.5 13.7 %collective-permute-start.22 = (bf16[512,256]{1,0:T(8,128)(2,1)}, bf16[512,256]{1,0:T(8,128)(2,1)S(1)}, u32[]{:S(2)}, u32[]{:S(2)}) collective-permute-start(bf16[512,256]{1,0:T(8,128)(2,1)} %get-tuple-element.132), channel_id=1, source_target_pairs={{0,2},{2,0},{4,6},{6,4},{8,10},{10,8},{12,14},{14,12},{16,18},{18,... | collective-permute-start | bytes 786440 | tf_op jit(solution)/shard_map/ppermute | solution.py:538
  536.6 3.2 collective-permute-start.21
  541.5 2.8 constant_dynamic-update-slice_fusion.22
  550.5 3.5 convolution_convert_fusion.3
  555.9 4.0 convolution_convert_fusion.5
  562.1 4.3 convolution_convert_fusion.2
  568.0 14.0 %collective-permute-done.25 = bf16[1024,768]{1,0:T(8,128)(2,1)} collective-permute-done((bf16[1024,768]{1,0:T(8,128)(2,1)}, bf16[1024,768]{1,0:T(8,128)(2,1)}, u32[]{:S(2)}, u32[]{:S(2)}) %collective-permute-start.25) | collective-permute-done | bytes 1572896 | tf_op jit(solution)/shard_map/ppermute | solution.py:515
  582.0 4.0 multiply_reduce_fusion.2
  592.9 11.2 %collective-permute-start.26 = (bf16[64,384]{1,0:T(8,128)(2,1)S(1)}, bf16[64,384]{1,0:T(8,128)(2,1)S(1)}, u32[]{:S(2)}, u32[]{:S(2)}) collective-permute-start(bf16[64,384]{1,0:T(8,128)(2,1)S(1)} %get-tuple-element.230), channel_id=1, source_target_pairs={{0,2},{2,4},{4,6},{6,8},{8,10},{10,12},{12,14},{14,16},{16,18},{18... | collective-permute-start | bytes 147464 | tf_op jit(solution)/shard_map/ppermute | solution.py:534
  606.8 40.7 %tap_gradient.1 = bf16[16,400,384]{2,1,0:T(8,128)(2,1)} custom-call(s32[1]{0:T(128)} %bitcast.1.chunks_ref, s32[8,1152]{1,0:T(8,128)} %broadcast_in_dim.84.prow_ref, s32[1408,128]{1,0:T(8,128)} %broadcast_in_dim.145.bseg_ref, bf16[1152,384]{1,0:T(8,128)(2,1)} %pad_maximum_fusion.4.x_ref, bf16[1024,384]{1,0:T(8,128)(2,1)} %copy-done.11, ...), custom_call_target="tpu_custom_call" | custom-call | flops 40000000000 | bytes 9000000 | tf_op jit(solution)/shard_map/tap_gradient/pallas_call | solution.py:266
  647.4 30.0 %reduce-scatter.6.cloned.1.call-done = bf16[48,1536]{1,0:T(8,128)(2,1)} async-done(((bf16[768,1536]{1,0:T(8,128)(2,1)}), bf16[48,1536]{1,0:T(8,128)(2,1)}) %reduce-scatter.6.cloned.1.call-update) | async-done | bytes 147472 | tf_op jit(solution)/shard_map/reduce_scatter | solution.py:579
  679.4 43.4 %conv_back.1 = f32[1024,384]{1,0:T(8,128)} custom-call(s32[1]{0:T(128)} %bitcast.1.chunks_ref, s32[8,1152]{1,0:T(8,128)} %broadcast_in_dim.84.prow_ref, s32[1152,128]{1,0:T(8,128)} %broadcast_in_dim.142.pcol_ref, s32[1408,128]{1,0:T(8,128)} %broadcast_in_dim.145.bseg_ref, bf16[1152,384]{1,0:T(8,128)(2,1)} %pad_maximum_fusion.5.x_ref, ...), custom_call_target="tpu_custom_call" | custom-call | flops 30000001024 | bytes 9000000 | tf_op jit(solution)/shard_map/conv_back/pallas_call | solution.py:173
  725.9 16.3 %collective-permute-done.28 = bf16[1024,384]{1,0:T(8,128)(2,1)S(1)} collective-permute-done((bf16[1024,384]{1,0:T(8,128)(2,1)S(1)}, bf16[1024,384]{1,0:T(8,128)(2,1)S(1)}, u32[]{:S(2)}, u32[]{:S(2)}) %collective-permute-start.28) | collective-permute-done | bytes 786464 | tf_op jit(solution)/shard_map/ppermute | solution.py:515
  753.1 4.5 reduce-scatter.8.cloned.1.call-done
  (417 shorter events, 124.6 us)
Async XLA Ops:
  7.3 59.9 %all-gather.5.cloned.1.call-start = ((), (), s32[]{:S(2)}) async-start(), calls=%async_computation.3 | async-start | bytes 5013504 | tf_op jit(solution)/shard_map/all_gather | solution.py:575
  9.2 132.6 %all-gather.7.cloned.1.call-start = ((), (), s32[]{:S(2)}) async-start(), calls=%async_computation.4 | async-start | bytes 2506752 | tf_op jit(solution)/shard_map/all_gather | solution.py:575
  10.8 35.3 %collective-permute-start = (bf16[64,384]{1,0:T(8,128)(2,1)S(1)}, bf16[64,384]{1,0:T(8,128)(2,1)S(1)}, u32[]{:S(2)}, u32[]{:S(2)}) collective-permute-start(bf16[64,384]{1,0:T(8,128)(2,1)S(1)} %get-tuple-element.232), channel_id=1, source_target_pairs={{0,2},{2,4},{4,6},{6,8},{8,10},{10,12},{12,14},{14,16},{16,18},{18... | collective-permute-start | bytes 147464 | tf_op jit(solution)/shard_map/ppermute | solution.py:534
  13.2 32.9 %collective-permute-start.1 = (bf16[64,384]{1,0:T(8,128)(2,1)S(1)}, bf16[64,384]{1,0:T(8,128)(2,1)S(1)}, u32[]{:S(2)}, u32[]{:S(2)}) collective-permute-start(bf16[64,384]{1,0:T(8,128)(2,1)S(1)} %get-tuple-element.233), channel_id=1, source_target_pairs={{2,0},{4,2},{6,4},{8,6},{10,8},{12,10},{14,12},{16,14},{18,16},{20... | collective-permute-start | bytes 147464 | tf_op jit(solution)/shard_map/ppermute | solution.py:534
  16.3 284.1 %all-gather.9.cloned.1.call-start = ((), (), s32[]{:S(2)}) async-start(), calls=%async_computation.5 | async-start | bytes 5013504 | tf_op jit(solution)/shard_map/all_gather | solution.py:575
  46.1 66.6 %copy-start.52 = (f32[384]{0:T(512)}, f32[384]{0:T(512)S(1)}, u32[]{:S(2)}) copy-start(f32[384]{0:T(512)S(1)} %add.467) | copy-start | bytes 4612
  118.2 19.8 %collective-permute-start.2 = (bf16[1024,384]{1,0:T(8,128)(2,1)S(1)}, bf16[1024,384]{1,0:T(8,128)(2,1)}, u32[]{:S(2)}, u32[]{:S(2)}) collective-permute-start(bf16[1024,384]{1,0:T(8,128)(2,1)S(1)} %get-tuple-element.219), channel_id=1, source_target_pairs={{0,1},{1,0},{2,3},{3,2},{4,5},{5,4},{6,7},{7,6},{8,9},{9,8},{10,11... | collective-permute-start | bytes 2359304 | tf_op jit(solution)/shard_map/ppermute | solution.py:515
  120.5 485.0 %reduce-scatter.4.cloned.1.call-start = ((), (), s32[]{:S(2)}) async-start(), calls=%async_computation.6 | async-start | bytes 5013504 | tf_op jit(solution)/shard_map/reduce_scatter | solution.py:579
  149.4 10.7 %collective-permute-start.5 = (bf16[1024,768]{1,0:T(8,128)(2,1)}, bf16[1024,768]{1,0:T(8,128)(2,1)}, u32[]{:S(2)}, u32[]{:S(2)}) collective-permute-start(bf16[1024,768]{1,0:T(8,128)(2,1)} %fusion.6.k0), channel_id=1, source_target_pairs={{2,4},{4,2},{6,8},{8,6},{10,12},{12,10},{14,16},{16,14},{18,20},{2... | collective-permute-start | bytes 4718600 | tf_op jit(solution)/shard_map/ppermute | solution.py:544
  151.6 77.3 %collective-permute-start.4 = (bf16[1024,768]{1,0:T(8,128)(2,1)}, bf16[1024,768]{1,0:T(8,128)(2,1)}, u32[]{:S(2)}, u32[]{:S(2)}) collective-permute-start(bf16[1024,768]{1,0:T(8,128)(2,1)} %fusion.6.k0), channel_id=1, source_target_pairs={{0,2},{2,0},{4,6},{6,4},{8,10},{10,8},{12,14},{14,12},{16,18},{18,... | collective-permute-start | bytes 4718600 | tf_op jit(solution)/shard_map/ppermute | solution.py:538
  154.9 74.0 %collective-permute-start.6 = (bf16[512,768]{1,0:T(8,128)(2,1)}, bf16[512,768]{1,0:T(8,128)(2,1)}, u32[]{:S(2)}, u32[]{:S(2)}) collective-permute-start(bf16[512,768]{1,0:T(8,128)(2,1)} %slice_select_fusion.1), channel_id=1, source_target_pairs={{0,4},{4,8},{6,2},{8,12},{10,6},{12,16},{14,10},{16,20},{18,14},{2... | collective-permute-start | bytes 2359304 | tf_op jit(solution)/shard_map/ppermute | solution.py:550
  162.4 66.4 %collective-permute-start.7 = (bf16[512,768]{1,0:T(8,128)(2,1)}, bf16[512,768]{1,0:T(8,128)(2,1)}, u32[]{:S(2)}, u32[]{:S(2)}) collective-permute-start(bf16[512,768]{1,0:T(8,128)(2,1)} %slice_select_fusion), channel_id=1, source_target_pairs={{0,2},{2,0},{4,6},{6,4},{8,10},{10,8},{12,14},{14,12},{16,18},{18,... | collective-permute-start | bytes 2359304 | tf_op jit(solution)/shard_map/ppermute | solution.py:538
  213.3 15.6 %collective-permute-start.3 = (bf16[768,384]{1,0:T(8,128)(2,1)}, bf16[768,384]{1,0:T(8,128)(2,1)}, u32[]{:S(2)}, u32[]{:S(2)}) collective-permute-start(bf16[768,384]{1,0:T(8,128)(2,1)} %slice.260), channel_id=1, source_target_pairs={{0,1},{1,0},{2,3},{3,2},{4,5},{5,4},{6,7},{7,6},{8,9},{9,8},{10,11... | collective-permute-start | bytes 1769480 | tf_op jit(solution)/shard_map/ppermute | solution.py:515
  248.1 17.8 %collective-permute-start.8 = (bf16[1024,128]{1,0:T(8,128)(2,1)}, bf16[1024,128]{1,0:T(8,128)(2,1)S(1)}, u32[]{:S(2)}, u32[]{:S(2)}) collective-permute-start(bf16[1024,128]{1,0:T(8,128)(2,1)} %get-tuple-element.94), channel_id=1, source_target_pairs={{0,1},{1,0},{2,3},{3,2},{4,5},{5,4},{6,7},{7,6},{8,9},{9,8},{10,11... | collective-permute-start | bytes 786440 | tf_op jit(solution)/shard_map/ppermute | solution.py:515
  265.5 18.1 %collective-permute-start.9 = (bf16[1024,128]{1,0:T(8,128)(2,1)}, bf16[1024,128]{1,0:T(8,128)(2,1)}, u32[]{:S(2)}, u32[]{:S(2)}) collective-permute-start(bf16[1024,128]{1,0:T(8,128)(2,1)} %get-tuple-element.95), channel_id=1, source_target_pairs={{0,1},{1,0},{2,3},{3,2},{4,5},{5,4},{6,7},{7,6},{8,9},{9,8},{10,11... | collective-permute-start | bytes 786440 | tf_op jit(solution)/shard_map/ppermute | solution.py:515
  281.6 7.7 collective-permute-start.10
  300.4 20.3 %copy-start.76 = (bf16[768,3072]{1,0:T(8,128)(2,1)S(1)}, bf16[768,3072]{1,0:T(8,128)(2,1)}, u32[]{:S(2)}) copy-start(bf16[768,3072]{1,0:T(8,128)(2,1)} %all-gather.9.cloned.1.call-done) | copy-start | bytes 14155780
  324.5 36.9 %collective-permute-start.11 = (bf16[1024,768]{1,0:T(8,128)(2,1)}, bf16[1024,768]{1,0:T(8,128)(2,1)}, u32[]{:S(2)}, u32[]{:S(2)}) collective-permute-start(bf16[1024,768]{1,0:T(8,128)(2,1)} %fusion.22), channel_id=1, source_target_pairs={{0,1},{1,0},{2,3},{3,2},{4,5},{5,4},{6,7},{7,6},{8,9},{9,8},{10,11... | collective-permute-start | bytes 4718600 | tf_op jit(solution)/shard_map/ppermute | solution.py:515
  384.2 37.1 %collective-permute-start.12 = (bf16[1024,768]{1,0:T(8,128)(2,1)}, bf16[1024,768]{1,0:T(8,128)(2,1)}, u32[]{:S(2)}, u32[]{:S(2)}) collective-permute-start(bf16[1024,768]{1,0:T(8,128)(2,1)} %fusion.19), channel_id=1, source_target_pairs={{0,1},{1,0},{2,3},{3,2},{4,5},{5,4},{6,7},{7,6},{8,9},{9,8},{10,11... | collective-permute-start | bytes 4718600 | tf_op jit(solution)/shard_map/ppermute | solution.py:515
  395.0 31.2 %copy-start.2 = (f32[1024,768]{1,0:T(8,128)S(1)}, f32[1024,768]{1,0:T(8,128)}, u32[]{:S(2)}) copy-start(f32[1024,768]{1,0:T(8,128)} %copy-done) | copy-start | bytes 9437188
  450.8 3.4 collective-permute-start.13
  451.9 49.8 %collective-permute-start.15 = (bf16[1024,256]{1,0:T(8,128)(2,1)}, bf16[1024,256]{1,0:T(8,128)(2,1)}, u32[]{:S(2)}, u32[]{:S(2)}) collective-permute-start(bf16[1024,256]{1,0:T(8,128)(2,1)} %get-tuple-element.111), channel_id=1, source_target_pairs={{0,2},{2,0},{4,6},{6,4},{8,10},{10,8},{12,14},{14,12},{16,18},{18,... | collective-permute-start | bytes 1572872 | tf_op jit(solution)/shard_map/ppermute | solution.py:538
  452.0 49.7 %collective-permute-start.17 = (bf16[512,256]{1,0:T(8,128)(2,1)}, bf16[512,256]{1,0:T(8,128)(2,1)}, u32[]{:S(2)}, u32[]{:S(2)}) collective-permute-start(bf16[512,256]{1,0:T(8,128)(2,1)} %get-tuple-element.114), channel_id=1, source_target_pairs={{2,6},{4,0},{6,10},{8,4},{10,14},{12,8},{14,18},{16,12},{18,22},{2... | collective-permute-start | bytes 786440 | tf_op jit(solution)/shard_map/ppermute | solution.py:550
  453.3 224.1 %reduce-scatter.6.cloned.1.call-start = ((), (), s32[]{:S(2)}) async-start(), calls=%async_computation.7 | async-start | bytes 2506752 | tf_op jit(solution)/shard_map/reduce_scatter | solution.py:579
  455.3 21.2 %copy-start.32 = (bf16[1024,256]{1,0:T(8,128)(2,1)S(1)}, bf16[1024,256]{1,0:T(8,128)(2,1)}, u32[]{:S(2)}) copy-start(bf16[1024,256]{1,0:T(8,128)(2,1)} %get-tuple-element.112) | copy-start | bytes 1572868
  473.9 6.6 collective-permute-start.14
  476.6 25.2 %collective-permute-start.16 = (bf16[1024,256]{1,0:T(8,128)(2,1)S(1)}, bf16[1024,256]{1,0:T(8,128)(2,1)S(1)}, u32[]{:S(2)}, u32[]{:S(2)}) collective-permute-start(bf16[1024,256]{1,0:T(8,128)(2,1)S(1)} %add_convert_fusion.3), channel_id=1, source_target_pairs={{2,4},{4,2},{6,8},{8,6},{10,12},{12,10},{14,16},{16,14},{18,20},{2... | collective-permute-start | bytes 1572872 | tf_op jit(solution)/shard_map/ppermute | solution.py:544
  477.3 22.9 %collective-permute-start.20 = (bf16[512,256]{1,0:T(8,128)(2,1)}, bf16[512,256]{1,0:T(8,128)(2,1)S(1)}, u32[]{:S(2)}, u32[]{:S(2)}) collective-permute-start(bf16[512,256]{1,0:T(8,128)(2,1)} %get-tuple-element.128), channel_id=1, source_target_pairs={{2,6},{4,0},{6,10},{8,4},{10,14},{12,8},{14,18},{16,12},{18,22},{2... | collective-permute-start | bytes 786440 | tf_op jit(solution)/shard_map/ppermute | solution.py:550
  480.4 65.1 %collective-permute-start.18 = (bf16[1024,256]{1,0:T(8,128)(2,1)}, bf16[1024,256]{1,0:T(8,128)(2,1)}, u32[]{:S(2)}, u32[]{:S(2)}) collective-permute-start(bf16[1024,256]{1,0:T(8,128)(2,1)} %get-tuple-element.125), channel_id=1, source_target_pairs={{0,2},{2,0},{4,6},{6,4},{8,10},{10,8},{12,14},{14,12},{16,18},{18,... | collective-permute-start | bytes 1572872 | tf_op jit(solution)/shard_map/ppermute | solution.py:538
  500.2 45.3 %collective-permute-start.19 = (bf16[1024,256]{1,0:T(8,128)(2,1)S(1)}, bf16[1024,256]{1,0:T(8,128)(2,1)}, u32[]{:S(2)}, u32[]{:S(2)}) collective-permute-start(bf16[1024,256]{1,0:T(8,128)(2,1)S(1)} %add_convert_fusion.2), channel_id=1, source_target_pairs={{2,4},{4,2},{6,8},{8,6},{10,12},{12,10},{14,16},{16,14},{18,20},{2... | collective-permute-start | bytes 1572872 | tf_op jit(solution)/shard_map/ppermute | solution.py:544
  501.8 18.7 %copy-start.35 = (bf16[1024,256]{1,0:T(8,128)(2,1)}, bf16[1024,256]{1,0:T(8,128)(2,1)S(1)}, u32[]{:S(2)}) copy-start(bf16[1024,256]{1,0:T(8,128)(2,1)S(1)} %collective-permute-done.16) | copy-start | bytes 1572868
  520.5 23.8 %collective-permute-start.22 = (bf16[512,256]{1,0:T(8,128)(2,1)}, bf16[512,256]{1,0:T(8,128)(2,1)S(1)}, u32[]{:S(2)}, u32[]{:S(2)}) collective-permute-start(bf16[512,256]{1,0:T(8,128)(2,1)} %get-tuple-element.132), channel_id=1, source_target_pairs={{0,2},{2,0},{4,6},{6,4},{8,10},{10,8},{12,14},{14,12},{16,18},{18,... | collective-permute-start | bytes 786440 | tf_op jit(solution)/shard_map/ppermute | solution.py:538
  535.2 10.2 %collective-permute-start.24 = (bf16[512,256]{1,0:T(8,128)(2,1)}, bf16[512,256]{1,0:T(8,128)(2,1)S(1)}, u32[]{:S(2)}, u32[]{:S(2)}) collective-permute-start(bf16[512,256]{1,0:T(8,128)(2,1)} %get-tuple-element.133), channel_id=1, source_target_pairs={{2,6},{4,0},{6,10},{8,4},{10,14},{12,8},{14,18},{16,12},{18,22},{2... | collective-permute-start | bytes 786440 | tf_op jit(solution)/shard_map/ppermute | solution.py:550
  536.6 12.0 %collective-permute-start.21 = (bf16[1024,256]{1,0:T(8,128)(2,1)}, bf16[1024,256]{1,0:T(8,128)(2,1)S(1)}, u32[]{:S(2)}, u32[]{:S(2)}) collective-permute-start(bf16[1024,256]{1,0:T(8,128)(2,1)} %get-tuple-element.130), channel_id=1, source_target_pairs={{0,2},{2,0},{4,6},{6,4},{8,10},{10,8},{12,14},{14,12},{16,18},{18,... | collective-permute-start | bytes 1572872 | tf_op jit(solution)/shard_map/ppermute | solution.py:538
  544.6 4.0 collective-permute-start.23
  553.9 28.1 %collective-permute-start.25 = (bf16[1024,768]{1,0:T(8,128)(2,1)}, bf16[1024,768]{1,0:T(8,128)(2,1)}, u32[]{:S(2)}, u32[]{:S(2)}) collective-permute-start(bf16[1024,768]{1,0:T(8,128)(2,1)} %convolution_convert_fusion.3), channel_id=1, source_target_pairs={{0,1},{1,0},{2,3},{3,2},{4,5},{5,4},{6,7},{7,6},{8,9},{9,8},{10,11... | collective-permute-start | bytes 4718600 | tf_op jit(solution)/shard_map/ppermute | solution.py:515
  568.0 18.0 %copy-start.49 = (f32[1024]{0:T(1024)S(1)}, f32[1024]{0:T(1024)}, u32[]{:S(2)}) copy-start(f32[1024]{0:T(1024)} %copy-done.48) | copy-start | bytes 12292
  592.9 85.5 %collective-permute-start.26 = (bf16[64,384]{1,0:T(8,128)(2,1)S(1)}, bf16[64,384]{1,0:T(8,128)(2,1)S(1)}, u32[]{:S(2)}, u32[]{:S(2)}) collective-permute-start(bf16[64,384]{1,0:T(8,128)(2,1)S(1)} %get-tuple-element.230), channel_id=1, source_target_pairs={{0,2},{2,4},{4,6},{6,8},{8,10},{10,12},{12,14},{14,16},{16,18},{18... | collective-permute-start | bytes 147464 | tf_op jit(solution)/shard_map/ppermute | solution.py:534
  604.1 74.2 %collective-permute-start.27 = (bf16[64,384]{1,0:T(8,128)(2,1)S(1)}, bf16[64,384]{1,0:T(8,128)(2,1)S(1)}, u32[]{:S(2)}, u32[]{:S(2)}) collective-permute-start(bf16[64,384]{1,0:T(8,128)(2,1)S(1)} %get-tuple-element.231), channel_id=1, source_target_pairs={{2,0},{4,2},{6,4},{8,6},{10,8},{12,10},{14,12},{16,14},{18,16},{20... | collective-permute-start | bytes 147464 | tf_op jit(solution)/shard_map/ppermute | solution.py:534
  606.5 151.2 %reduce-scatter.8.cloned.1.call-start = ((), (), s32[]{:S(2)}) async-start(), calls=%async_computation.8 | async-start | bytes 5222400 | tf_op jit(solution)/shard_map/reduce_scatter | solution.py:579
  647.4 31.0 %copy-start.12 = (bf16[1024,384]{1,0:T(8,128)(2,1)S(1)}, bf16[1024,384]{1,0:T(8,128)(2,1)}, u32[]{:S(2)}) copy-start(bf16[1024,384]{1,0:T(8,128)(2,1)} %copy-done.11) | copy-start | bytes 2359300
  679.4 62.8 %copy-start.4 = (f32[1024,768]{1,0:T(8,128)S(1)}, f32[1024,768]{1,0:T(8,128)}, u32[]{:S(2)}) copy-start(f32[1024,768]{1,0:T(8,128)} %copy-done.3) | copy-start | bytes 9437188
  724.3 20.0 %copy-start.19 = (f32[1536,48]{0,1:T(8,128)S(1)}, f32[1536,48]{0,1:T(8,128)}, u32[]{:S(2)}) copy-start(f32[1536,48]{0,1:T(8,128)} %param.45) | copy-start | bytes 884740
  724.3 20.0 %copy-start.41 = (f32[1536,48]{0,1:T(8,128)S(1)}, f32[1536,48]{0,1:T(8,128)}, u32[]{:S(2)}) copy-start(f32[1536,48]{0,1:T(8,128)} %param.46) | copy-start | bytes 884740
  724.4 20.9 %copy-start.36 = (f32[1536,48]{0,1:T(8,128)S(1)}, f32[1536,48]{0,1:T(8,128)}, u32[]{:S(2)}) copy-start(f32[1536,48]{0,1:T(8,128)} %param.47) | copy-start | bytes 884740
  724.4 21.7 %copy-start.21 = (f32[48,1536]{1,0:T(8,128)S(1)}, f32[48,1536]{1,0:T(8,128)}, u32[]{:S(2)}) copy-start(f32[48,1536]{1,0:T(8,128)} %param.42) | copy-start | bytes 884740
  724.4 21.7 %copy-start.42 = (f32[48,1536]{1,0:T(8,128)S(1)}, f32[48,1536]{1,0:T(8,128)}, u32[]{:S(2)}) copy-start(f32[48,1536]{1,0:T(8,128)} %param.43) | copy-start | bytes 884740
  724.4 17.8 %collective-permute-start.28 = (bf16[1024,384]{1,0:T(8,128)(2,1)S(1)}, bf16[1024,384]{1,0:T(8,128)(2,1)S(1)}, u32[]{:S(2)}, u32[]{:S(2)}) collective-permute-start(bf16[1024,384]{1,0:T(8,128)(2,1)S(1)} %convert_element_type.264), channel_id=1, source_target_pairs={{0,1},{1,0},{2,3},{3,2},{4,5},{5,4},{6,7},{7,6},{8,9},{9,8},{10,11... | collective-permute-start | bytes 2359304 | tf_op jit(solution)/shard_map/ppermute | solution.py:515
  (71 other events, 422.8 us)
Sparse Core Ops, SparseCore 0:
  11.0 56.1 all-gather.4
  70.0 40.8 all-gather.6
  120.6 80.2 all-gather.8
  453.4 93.6 reduce-scatter.3
  606.6 70.7 reduce-scatter.5
  681.2 76.3 reduce-scatter.7

commit v3 on v2

--- a/solution.py
+++ b/solution.py
@@ -9,6 +9,7 @@
 
 HEAD = 64
 PAIRS = 3
+CHUNKS = 2
 EPSILON = 1e-05
 
 bf16, f32, i32 = jnp.bfloat16, jnp.float32, jnp.int32
@@ -285,7 +286,7 @@
             pltpu.VMEM((2, PJ, 64, 128), f32),
         ],
         compiler_params=pltpu.CompilerParams(vmem_limit_bytes=VLIM),
-        cost_estimate=pl.CostEstimate(flops=40_000_000_000, bytes_accessed=9_000_000, transcendentals=0),
+        cost_estimate=pl.CostEstimate(flops=8_000_000_000, bytes_accessed=9_000_000, transcendentals=0),
         name="tap_gradient",
     )(chunks, prow, bseg, window, d_conv, small)
 REACH = 1536
@@ -390,8 +391,9 @@
         lse_ref[e : e + 1, :] = ends[e][0] + jnp.log(ends[e][1])
 
 
-def piece_specs(h):
-    return [pl.BlockSpec((n, 256), lambda i: (0, h)) for n in (ROWS, ROWS, ROWS, NEAR, NEAR)]
+def piece_specs(h, pieces):
+    at = [h - (PAIRS - p.shape[1] // 256) if p.shape[1] > 256 else 0 for p in pieces]
+    return [pl.BlockSpec((p.shape[0], 256), lambda i, c=c: (0, c)) for p, c in zip(pieces, at)]
 
 
 def attend(plan, h, q, pieces):
@@ -410,7 +412,7 @@
             pl.BlockSpec((SPAN, 128), lambda i: (0, 0)),
             pl.BlockSpec((QT, 128), lambda i: (i, h)),
         ]
-        + piece_specs(h),
+        + piece_specs(h, pieces),
         out_specs=(
             pl.BlockSpec((QT, 128), lambda i: (i, 0)),
             pl.BlockSpec((QT, 128), lambda i: (i, 0)),
@@ -493,7 +495,7 @@
             pl.BlockSpec((SPAN, 128), lambda i: (0, 0)),
             colspec,
         ]
-        + piece_specs(h)
+        + piece_specs(h, pieces)
         + [colspec, rowspec, pl.BlockSpec((8, QT), lambda i: (0, i))],
         out_specs=(
             rowspec,
@@ -669,51 +671,81 @@
     kv_bias = jnp.concatenate([jnp.zeros_like(kv_bias), kv_bias], axis=1).reshape(-1)
     both = (proj[:, HALF:] + kv_bias).astype(bf16)
     near = NEAR
-    beside = across_chips(both)
-    further = chip_along(jnp.where(odd == 1, both[:near], both[rows - near :]), 1)
-    pieces = (
-        both,
-        across_cores(both),
-        beside,
-        further,
-        across_cores(jnp.where(odd == 1, beside[:near], beside[rows - near :])),
-    )
+
+    def fetched(lo, hi):
+        block = both[:, lo:hi]
+        head, tail = block[:near], block[rows - near :]
+        return (
+            across_cores(block),
+            across_chips(block),
+            chip_along(jnp.where(odd == 1, head, tail), 1),
+            chip_along(jnp.where(odd == 1, tail, head), -1),
+        )
+
+    early = fetched(0, 256)
+    both, early = lax.optimization_barrier((both, early))
+    late = fetched(256, 256 * PAIRS)
+    pieces = [(both,) + (early if h == 0 else late) for h in range(PAIRS)]
     mixed, attended, attended_far, lse = [], [], [], []
     for h in range(PAIRS):
         if h == 0:
             q_part, w_combine_far = lax.optimization_barrier((queries, w_combine_far))
         if h >= 2:
             q_part, attended_far[h - 2] = lax.optimization_barrier((queries, attended_far[h - 2]))
-        mixed_part, half, lse_part = attend(reach, h, q_part, pieces)
+        mixed_part, half, lse_part = attend(reach, h, q_part, pieces[h])
         mixed.append(mixed_part)
         lse.append(lse_part)
         attended.append(half)
         attended_far.append(exchange(half))
     attended = jnp.concatenate(attended, axis=1)
     attended_all = side_by_side(attended, jnp.concatenate(attended_far, axis=1), index)
-    branch = dot(attended_all, side_by_side(w_combine, w_combine_far, index), 1, 1)
-    h2, norm1_back = jax.vjp(layer_norm, h1 + branch + b_out[0], norms[1, 0], norms[1, 1])
-    h2_half = h2.astype(bf16)
+    w_combine_all = side_by_side(w_combine, w_combine_far, index)
     w_expand = w_second[:, :hidden_units]
     w_shrink = w_second[:, hidden_units:]
-    inner = dot(h2_half, w_expand, 1, 0) + b_unit
-    hidden, gelu_inner_back = jax.vjp(gelu_exact, inner)
-    hidden_half = hidden.astype(bf16)
-    outer = pair_sum(dot(hidden_half, w_shrink, 1, 1))
-    layer_out, norm2_back = jax.vjp(layer_norm, h2 + outer + b_out[1], norms[2, 0], norms[2, 1])
-    dx3, gain2_grad, shift2_grad = norm2_back(cotangent)
-    outer_bias_grad = jnp.sum(dx3, axis=0)
-    d_out = dx3.astype(bf16)
-    d_hidden = dot(d_out, w_shrink, 1, 0)
-    d_inner = gelu_inner_back(d_hidden)[0]
-    unit_grad = jnp.sum(d_inner, axis=0)
-    d_inner_half = d_inner.astype(bf16)
-    dh2 = dx3 + pair_sum(dot(d_inner_half, w_expand, 1, 1))
+    step = rows // CHUNKS
+    cuts_of = [slice(c * step, (c + 1) * step) for c in range(CHUNKS)]
+    first_half, second_half = [], []
+    for cut in cuts_of:
+        branch = dot(attended_all[cut], w_combine_all, 1, 1)
+        h2, norm1_back = jax.vjp(layer_norm, h1[cut] + branch + b_out[0], norms[1, 0], norms[1, 1])
+        h2_half = h2.astype(bf16)
+        inner = dot(h2_half, w_expand, 1, 0) + b_unit
+        hidden, gelu_inner_back = jax.vjp(gelu_exact, inner)
+        hidden_half = hidden.astype(bf16)
+        sent = dot(hidden_half, w_shrink, 1, 1).astype(bf16)
+        first_half.append((h2, norm1_back, h2_half, gelu_inner_back, hidden_half, sent, exchange(sent)))
+    sent_back = None
+    for cut, (h2, norm1_back, h2_half, gelu_inner_back, hidden_half, sent, came) in zip(
+        cuts_of, first_half
+    ):
+        if sent_back is not None:
+            came, _ = lax.optimization_barrier((came, sent_back))
+        outer = sent.astype(f32) + came.astype(f32)
+        out_part, norm2_back = jax.vjp(layer_norm, h2 + outer + b_out[1], norms[2, 0], norms[2, 1])
+        dx3, gain2_grad, shift2_grad = norm2_back(cotangent[cut])
+        d_out = dx3.astype(bf16)
+        d_hidden = dot(d_out, w_shrink, 1, 0)
+        d_inner = gelu_inner_back(d_hidden)[0]
+        d_inner_half = d_inner.astype(bf16)
+        sent_back = dot(d_inner_half, w_expand, 1, 1).astype(bf16)
+        sums = [gain2_grad, shift2_grad, jnp.sum(dx3, axis=0), jnp.sum(d_inner, axis=0)]
+        second_half.append(
+            [out_part, (sent_back, exchange(sent_back)), norm1_back, h2_half, d_inner_half, d_out, hidden_half, dx3, sums]
+        )
+    layer_out = jnp.concatenate([part[0] for part in second_half], axis=0)
+    gain2_grad, shift2_grad, outer_bias_grad, unit_grad = map(sum, zip(*[p[-1] for p in second_half]))
     second_part = jnp.concatenate(
-        [dot(h2_half, d_inner_half, 0, 0).astype(bf16), dot(d_out, hidden_half, 0, 0).astype(bf16)],
+        [
+            sum(dot(p[a], p[b], 0, 0) for p in second_half).astype(bf16)
+            for a, b in ((3, 4), (5, 6))
+        ],
         axis=1,
     )
-    dx2, gain1_grad, shift1_grad = norm1_back(dh2)
+    dx2_parts, gain1_parts, shift1_parts = zip(
+        *[p[2](p[7] + (p[1][0].astype(f32) + p[1][1].astype(f32))) for p in second_half]
+    )
+    gain1_grad, shift1_grad = sum(gain1_parts), sum(shift1_parts)
+    dx2 = jnp.concatenate(dx2_parts, axis=0)
     branch_bias_grad = jnp.sum(dx2, axis=0)
     d_branch = dx2.astype(bf16)
     d_att = dot(d_branch, w_combine, 1, 0).astype(bf16)
@@ -723,29 +755,25 @@
     arrived = {}
     for h in range(PAIRS):
         d_part = d_att
-        if h >= 1:
-            d_part, passed_on = lax.optimization_barrier((d_part, passed_on))
-            chip = (chip.astype(f32) + passed_on).astype(bf16)
-            arrived[h - 1] = (across_cores(core), across_chips(chip), chip_along(far, -1), own)
         if h >= 2:
-            d_part, arrived[h - 2] = lax.optimization_barrier((d_part, arrived[h - 2]))
-        dq_part, own, core, chip, far, near_far = attend_back(
-            reach, h, queries, pieces, d_part, mixed[h], lse[h]
-        )
-        passed_on = across_cores(near_far).astype(f32)
-        none = jnp.zeros_like(passed_on)
-        passed_on = jnp.concatenate(
-            [jnp.where(odd == 1, passed_on, none), jnp.where(odd == 1, none, passed_on)], axis=0
+            d_part, arrived[h - 2] = lax.optimization_barrier((d_att, arrived[h - 2]))
+        dq_part, own, core, chip, far, beyond = attend_back(
+            reach, h, queries, pieces[h], d_part, mixed[h], lse[h]
+        )
+        arrived[h] = (
+            across_cores(core),
+            across_chips(chip),
+            chip_along(far, -1),
+            chip_along(beyond, 1),
+            own,
         )
         dq_parts.append(dq_part)
-    chip = (chip.astype(f32) + passed_on).astype(bf16)
-    arrived[PAIRS - 1] = (across_cores(core), across_chips(chip), chip_along(far, -1), own)
     for h in range(PAIRS):
-        core, chip, far, own = arrived[h]
-        far = far.astype(f32)
-        none = jnp.zeros_like(far)
-        far = jnp.concatenate([jnp.where(odd == 1, far, none), jnp.where(odd == 1, none, far)], axis=0)
-        kv_parts.append((own + core.astype(f32) + chip.astype(f32) + far).astype(bf16))
+        core, chip, far, beyond, own = [a.astype(f32) for a in arrived[h]]
+        ends_of = jnp.concatenate(
+            [jnp.where(odd == 1, far, beyond), jnp.where(odd == 1, beyond, far)], axis=0
+        )
+        kv_parts.append((own + core + chip + ends_of).astype(bf16))
     dq_half = jnp.concatenate(dq_parts, axis=1)
     d_both_half = jnp.concatenate(kv_parts, axis=1)
     stacked = jnp.concatenate([dq_half, d_both_half], axis=1)

time: 787 us -> 705 us (0.90); the launches traced: 774 us -> 700 us
  waiting for transfers between devices: 191 us -> 143 us
  starting transfers between devices: 122 us -> 108 us
    ppermute x8 -> x5, starting transfers between devices: 76.9 us -> 20.3 us  [across_cores(): lax.ppermute(block, 'seq', [(i, i ^ 1) for i in range(lax.axis_size('seq'...]
    ppermute x9 -> x11, waiting for transfers between devices: 123 us -> 67.7 us  [exchange(): return lax.ppermute(part, 'heads', [(0, 1), (1, 0)])]
    ppermute x4 -> x10, starting transfers between devices: 9.36 us -> 42.6 us  [chip_along(): lax.ppermute(block, 'seq', [(i, j) for i, j in route if 0 <= j < count])]
    ppermute x4 -> x10, waiting for transfers between devices: 12.9 us -> 23.7 us  [chip_along(): lax.ppermute(block, 'seq', [(i, j) for i, j in route if 0 <= j < count])]
    ppermute x4, starting transfers between devices: 16.2 us -> 26.1 us  [passed(): return lax.ppermute(block, 'seq', route)]
    unnamed x193 -> x231, local copies, waits for them, and re-layouts: 25.4 us -> 19.9 us
    dot_general x12 -> x19, matrix products: 63.6 us -> 59.8 us  [dot(): lax.dot_general(a, b, (((ca,), (cb,)), ((), ())), preferred_element_type=...]
  transfers between devices with their start and end apart: 35 -> 41, of which waited for: 11 -> 16; matrix products, arithmetic and copies ran while one was open for 14% -> 19% of each run, Pallas kernels for 27% -> 33%
where the time goes in v3:
time: 705 us; the launch traced here: 700 us
  Pallas kernels  230 us (33%)
  waiting for transfers between devices  143 us (20%)
  starting transfers between devices  108 us (15%)
  other arithmetic  79.9 us (11%)
  matrix products  59.8 us (8%)
  local copies, waits for them, and re-layouts  35.4 us (5%)
  blocking collectives  25.1 us (4%)
  between operations  19 us (3%)
    pallas_call x2, Pallas kernels, conv(): pl.pallas_call(functools.partial(conv_kernel, back), grid=(4,), out_shape...  86.2 us
    ppermute x11, waiting for transfers between devices, exchange(): return lax.ppermute(part, 'heads', [(0, 1), (1, 0)])  67.7 us
    dot_general x19, matrix products, dot(): lax.dot_general(a, b, (((ca,), (cb,)), ((), ())), preferred_element_type=...  59.8 us
    pallas_call x3, Pallas kernels, attend_back(): pl.pallas_call(backward_kernel, grid=(ROWS // QT,), out_shape=(jax.ShapeD...  56.3 us
    pallas_call x3, Pallas kernels, attend(): pl.pallas_call(forward_kernel, grid=(ROWS // QT,), out_shape=(jax.ShapeDt...  47 us
    ppermute x10, starting transfers between devices, chip_along(): lax.ppermute(block, 'seq', [(i, j) for i, j in route if 0 <= j < count])  42.6 us
    pallas_call x1, Pallas kernels, tap_grad(): pl.pallas_call(tap_grad_kernel, grid=(4,), out_shape=jax.ShapeDtypeStruct...  40.6 us
    reduce_scatter x3, waiting for transfers between devices, scattered(): return lax.psum_scatter(whole_sum, 'seq', scatter_dimension=0, tiled=True)  33.6 us
  transfers between devices with their start and end apart: 41, of which 16 were waited for; matrix products, arithmetic and copies ran while one was open for 19% of the time, Pallas kernels for 33%

profile of v3, /device:TPU:0, one launch (start us, length us, event | category | flops | bytes accessed | tf_op | source)
XLA Modules:
  0.0 700.1 jit_solution(11282915203441738819)
XLA Ops:
  17.7 25.1 %all-gather = bf16[16,1,552]{2,1,0:T(2,128)(2,1)S(1)} all-gather(bf16[1,1,552]{2,1,0:T(2,128)(2,1)S(1)} %maximum_bitcast_fusion.2), channel_id=1, replica_groups=mesh['seq'=16,'heads'=2] {'seq'}, dimensions={0}, use_global_device_ids=true | all-gather | bytes 18768 | tf_op jit(solution)/shard_map/all_gather | solution.py:577
  49.1 18.0 %all-gather.5.cloned.1.call-done.k_ref = bf16[128,48,384]{2,1,0:T(8,128)(2,1)} async-done(((bf16[8,48,384]{2,1,0:T(8,128)(2,1)}), bf16[128,48,384]{2,1,0:T(8,128)(2,1)}) %all-gather.5.cloned.1.call-update) | async-done | bytes 4718608 | tf_op jit(solution)/shard_map/all_gather | solution.py:577
  69.9 43.0 %conv_forward.1 = f32[1024,384]{1,0:T(8,128)} custom-call(s32[1]{0:T(128)} %bitcast.1.chunks_ref, s32[8,1152]{1,0:T(8,128)} %broadcast_in_dim.92.prow_ref, s32[1152,128]{1,0:T(8,128)} %broadcast_in_dim.158.pcol_ref, s32[1408,128]{1,0:T(8,128)} %broadcast_in_dim.161.bseg_ref, bf16[1152,384]{1,0:T(8,128)(2,1)} %pad_maximum_fusion.4.x_ref, ...), custom_call_target="tpu_custom_call" | custom-call | flops 30000001024 | bytes 9000000 | tf_op jit(solution)/shard_map/conv_forward/pallas_call | solution.py:174
  112.9 6.2 multiply_convert_fusion.2
  123.5 16.4 %collective-permute-done.2 = bf16[1024,384]{1,0:T(8,128)(2,1)} collective-permute-done((bf16[1024,384]{1,0:T(8,128)(2,1)}, bf16[1024,384]{1,0:T(8,128)(2,1)}, u32[]{:S(2)}, u32[]{:S(2)}) %collective-permute-start.2) | collective-permute-done | bytes 786464 | tf_op jit(solution)/shard_map/ppermute | solution.py:517
  149.1 5.2 collective-permute-start.6
  156.7 8.4 %collective-permute-done.6.k3 = bf16[512,256]{1,0:T(8,128)(2,1)S(1)} collective-permute-done((bf16[512,256]{1,0:T(8,128)(2,1)S(1)}, bf16[512,256]{1,0:T(8,128)(2,1)S(1)}, u32[]{:S(2)}, u32[]{:S(2)}) %collective-permute-start.6) | collective-permute-done | bytes 262176 | tf_op jit(solution)/shard_map/ppermute | solution.py:552
  165.9 9.3 %collective-permute-start.8 = (bf16[1024,512]{1,0:T(8,128)(2,1)S(1)}, bf16[1024,512]{1,0:T(8,128)(2,1)}, u32[]{:S(2)}, u32[]{:S(2)}) collective-permute-start(bf16[1024,512]{1,0:T(8,128)(2,1)S(1)} %slice.246), channel_id=1, source_target_pairs={{0,2},{2,0},{4,6},{6,4},{8,10},{10,8},{12,14},{14,12},{16,18},{18,... | collective-permute-start | bytes 3145736 | tf_op jit(solution)/shard_map/ppermute | solution.py:540
  176.9 4.4 collective-permute-start.10
  182.6 3.0 broadcast_in_dim.168.kseg_ref
  186.2 15.6 %attention_forward.3 = (f32[1024,128]{1,0:T(8,128)}, bf16[1024,128]{1,0:T(8,128)(2,1)}, f32[8,1024]{1,0:T(8,128)}) custom-call(s32[3,8]{1,0:T(4,128)} %add_add_fusion.10.range_ref, s32[8,1024]{1,0:T(8,128)} %broadcast_in_dim.167.qseg_ref, s32[4096,128]{1,0:T(8,128)} %broadcast_in_dim.168.kseg_ref, bf16[1024,384]{1,0:T(8,128)(2,1)} %fusion.17.q_ref, ...), custom_call_target="tpu_custom_call" | custom-call | flops 8000000000 | bytes 8000000 | tf_op jit(solution)/shard_map/attention_forward/pallas_call | solution.py:401
  203.7 4.7 collective-permute-done.12
  208.4 6.5 collective-permute-done.10.k3
  215.8 15.6 %attention_forward.4 = (f32[1024,128]{1,0:T(8,128)}, bf16[1024,128]{1,0:T(8,128)(2,1)}, f32[8,1024]{1,0:T(8,128)}) custom-call(s32[3,8]{1,0:T(4,128)} %add_add_fusion.10.range_ref, s32[8,1024]{1,0:T(8,128)} %broadcast_in_dim.167.qseg_ref, s32[4096,128]{1,0:T(8,128)} %broadcast_in_dim.168.kseg_ref, bf16[1024,384]{1,0:T(8,128)(2,1)} %fusion.17.q_ref, ...), custom_call_target="tpu_custom_call" | custom-call | flops 8000000000 | bytes 8000000 | tf_op jit(solution)/shard_map/attention_forward/pallas_call | solution.py:401
  232.9 15.8 %attention_forward.5 = (f32[1024,128]{1,0:T(8,128)}, bf16[1024,128]{1,0:T(8,128)(2,1)}, f32[8,1024]{1,0:T(8,128)}) custom-call(s32[3,8]{1,0:T(4,128)} %add_add_fusion.10.range_ref, s32[8,1024]{1,0:T(8,128)} %broadcast_in_dim.167.qseg_ref, s32[4096,128]{1,0:T(8,128)} %broadcast_in_dim.168.kseg_ref, bf16[1024,384]{1,0:T(8,128)(2,1)} %fusion.17.q_ref, ...), custom_call_target="tpu_custom_call" | custom-call | flops 8000000000 | bytes 8000000 | tf_op jit(solution)/shard_map/attention_forward/pallas_call | solution.py:401
  249.8 5.6 collective-permute-done.14
  260.5 9.7 %multiply_convert_fusion.1 = (bf16[512,1536]{1,0:T(8,128)(2,1)S(1)}, f32[512,1536]{1,0:T(8,128)S(1)}, f32[512,1536]{1,0:T(8,128)S(1)}) fusion(f32[1536]{0:T(1024)S(1)} %reshape.761, bf16[768,3072]{1,0:T(8,128)(2,1)} %all-gather.9.cloned.1.call-done, f32[512,768]{1,0:T(8,128)S(1)} %get-tuple-element.287, f32[768]{0:T(1024)S(1)} %get-tuple-element.167, ...), kind=kOutput, calls=%fused_computation.34 | convolution fusion | flops 1261830144 | bytes 11812864 | tf_op jit(solution)/shard_map/dot_general | solution.py:573
  272.7 8.0 %multiply_convert_fusion = (bf16[512,1536]{1,0:T(8,128)(2,1)S(1)}, f32[512,1536]{1,0:T(8,128)S(1)}, f32[512,1536]{1,0:T(8,128)S(1)}) fusion(f32[1536]{0:T(1024)S(1)} %reshape.761, bf16[768,3072]{1,0:T(8,128)(2,1)S(1)} %copy-done.93, f32[512,768]{1,0:T(8,128)S(1)} %get-tuple-element.284, f32[512]{0:T(512)S(1)} %fusion.91, ...), kind=kOutput, calls=%fused_computation.21 | convolution fusion | flops 1261830144 | bytes 11816960 | tf_op jit(solution)/shard_map/dot_general | solution.py:573
  289.6 2.9 fusion.137
  298.8 3.9 collective-permute-done.16
  312.7 3.1 add_convert_fusion.1
  315.9 3.0 add_convert_fusion
  318.9 5.0 pad_maximum_fusion
  324.1 12.4 %collective-permute-done.18 = bf16[512,768]{1,0:T(8,128)(2,1)} collective-permute-done((bf16[512,768]{1,0:T(8,128)(2,1)}, bf16[512,768]{1,0:T(8,128)(2,1)}, u32[]{:S(2)}, u32[]{:S(2)}) %collective-permute-start.18) | collective-permute-done | bytes 786464 | tf_op jit(solution)/shard_map/ppermute | solution.py:517
  336.5 2.9 multiply_reduce_fusion.5
  339.4 2.8 multiply_reduce_fusion.6
  343.3 3.4 convolution_convert_fusion.2.do_ref
  346.8 18.5 %attention_backward.3 = (bf16[1024,128]{1,0:T(8,128)(2,1)}, f32[1024,256]{1,0:T(8,128)}, bf16[1024,256]{1,0:T(8,128)(2,1)}, bf16[1024,256]{1,0:T(8,128)(2,1)}, b...) custom-call(s32[3,8]{1,0:T(4,128)} %add_add_fusion.10.range_ref, s32[8,1024]{1,0:T(8,128)} %broadcast_in_dim.167.qseg_ref, ...), custom_call_target="tpu_custom_call" | custom-call | flops 8000000000 | bytes 12000000 | tf_op jit(solution)/shard_map/attention_backward/pallas_call | solution.py:484
  365.3 6.1 collective-permute-start.19
  374.1 19.2 %attention_backward.4 = (bf16[1024,128]{1,0:T(8,128)(2,1)}, f32[1024,256]{1,0:T(8,128)}, bf16[1024,256]{1,0:T(8,128)(2,1)}, bf16[1024,256]{1,0:T(8,128)(2,1)}, b...) custom-call(s32[3,8]{1,0:T(4,128)} %add_add_fusion.10.range_ref, s32[8,1024]{1,0:T(8,128)} %broadcast_in_dim.167.qseg_ref, ...), custom_call_target="tpu_custom_call" | custom-call | flops 8000000000 | bytes 12000000 | tf_op jit(solution)/shard_map/attention_backward/pallas_call | solution.py:484
  394.6 11.8 %collective-permute-start.26 = (bf16[512,256]{1,0:T(8,128)(2,1)}, bf16[512,256]{1,0:T(8,128)(2,1)}, u32[]{:S(2)}, u32[]{:S(2)}) collective-permute-start(bf16[512,256]{1,0:T(8,128)(2,1)} %get-tuple-element.134), channel_id=1, source_target_pairs={{0,4},{4,8},{6,2},{8,12},{10,6},{12,16},{14,10},{16,20},{18,14},{2... | collective-permute-start | bytes 786440 | tf_op jit(solution)/shard_map/ppermute | solution.py:552
  410.2 3.9 collective-permute-start.22
  414.1 7.0 %collective-permute-done.26 = bf16[512,256]{1,0:T(8,128)(2,1)} collective-permute-done((bf16[512,256]{1,0:T(8,128)(2,1)}, bf16[512,256]{1,0:T(8,128)(2,1)}, u32[]{:S(2)}, u32[]{:S(2)}) %collective-permute-start.26) | collective-permute-done | bytes 262176 | tf_op jit(solution)/shard_map/ppermute | solution.py:552
  421.1 3.8 collective-permute-start.23
  427.5 18.6 %attention_backward.5 = (bf16[1024,128]{1,0:T(8,128)(2,1)}, f32[1024,256]{1,0:T(8,128)}, bf16[1024,256]{1,0:T(8,128)(2,1)}, bf16[1024,256]{1,0:T(8,128)(2,1)}, b...) custom-call(s32[3,8]{1,0:T(4,128)} %add_add_fusion.10.range_ref, s32[8,1024]{1,0:T(8,128)} %broadcast_in_dim.167.qseg_ref, ...), custom_call_target="tpu_custom_call" | custom-call | flops 8000000000 | bytes 12000000 | tf_op jit(solution)/shard_map/attention_backward/pallas_call | solution.py:484
  447.6 10.7 %collective-permute-start.30 = (bf16[512,256]{1,0:T(8,128)(2,1)}, bf16[512,256]{1,0:T(8,128)(2,1)S(1)}, u32[]{:S(2)}, u32[]{:S(2)}) collective-permute-start(bf16[512,256]{1,0:T(8,128)(2,1)} %get-tuple-element.139), channel_id=1, source_target_pairs={{0,4},{4,8},{6,2},{8,12},{10,6},{12,16},{14,10},{16,20},{18,14},{2... | collective-permute-start | bytes 786440 | tf_op jit(solution)/shard_map/ppermute | solution.py:552
  471.2 5.0 convolution_convert_fusion.1
  477.0 3.0 convolution_convert_fusion.3
  482.2 4.2 convolution_convert_fusion
  488.2 8.8 %collective-permute-done.31 = bf16[1024,768]{1,0:T(8,128)(2,1)} collective-permute-done((bf16[1024,768]{1,0:T(8,128)(2,1)}, bf16[1024,768]{1,0:T(8,128)(2,1)}, u32[]{:S(2)}, u32[]{:S(2)}) %collective-permute-start.31) | collective-permute-done | bytes 1572896 | tf_op jit(solution)/shard_map/ppermute | solution.py:517
  497.0 5.3 multiply_reduce_fusion
  504.2 2.8 fusion.118
  512.2 21.2 %collective-permute-start.32 = (bf16[64,384]{1,0:T(8,128)(2,1)S(1)}, bf16[64,384]{1,0:T(8,128)(2,1)S(1)}, u32[]{:S(2)}, u32[]{:S(2)}) collective-permute-start(bf16[64,384]{1,0:T(8,128)(2,1)S(1)} %get-tuple-element.260), channel_id=1, source_target_pairs={{0,2},{2,4},{4,6},{6,8},{8,10},{10,12},{12,14},{14,16},{16,18},{18... | collective-permute-start | bytes 147464 | tf_op jit(solution)/shard_map/ppermute | solution.py:536
  534.7 40.6 %tap_gradient.1 = bf16[16,400,384]{2,1,0:T(8,128)(2,1)} custom-call(s32[1]{0:T(128)} %bitcast.1.chunks_ref, s32[8,1152]{1,0:T(8,128)} %broadcast_in_dim.92.prow_ref, s32[1408,128]{1,0:T(8,128)} %broadcast_in_dim.161.bseg_ref, bf16[1152,384]{1,0:T(8,128)(2,1)} %pad_maximum_fusion.4.x_ref, bf16[1024,384]{1,0:T(8,128)(2,1)} %copy-done.16, ...), custom_call_target="tpu_custom_call" | custom-call | flops 8000000000 | bytes 9000000 | tf_op jit(solution)/shard_map/tap_gradient/pallas_call | solution.py:267
  575.4 28.2 %reduce-scatter.6.cloned.1.call-done = bf16[48,1536]{1,0:T(8,128)(2,1)} async-done(((bf16[768,1536]{1,0:T(8,128)(2,1)}), bf16[48,1536]{1,0:T(8,128)(2,1)}) %reduce-scatter.6.cloned.1.call-update) | async-done | bytes 147472 | tf_op jit(solution)/shard_map/reduce_scatter | solution.py:581
  606.7 43.2 %conv_back.1 = f32[1024,384]{1,0:T(8,128)} custom-call(s32[1]{0:T(128)} %bitcast.1.chunks_ref, s32[8,1152]{1,0:T(8,128)} %broadcast_in_dim.92.prow_ref, s32[1152,128]{1,0:T(8,128)} %broadcast_in_dim.158.pcol_ref, s32[1408,128]{1,0:T(8,128)} %broadcast_in_dim.161.bseg_ref, bf16[1152,384]{1,0:T(8,128)(2,1)} %pad_maximum_fusion.5.x_ref, ...), custom_call_target="tpu_custom_call" | custom-call | flops 30000001024 | bytes 9000000 | tf_op jit(solution)/shard_map/conv_back/pallas_call | solution.py:174
  654.9 14.4 %collective-permute-done.34 = bf16[1024,384]{1,0:T(8,128)(2,1)S(1)} collective-permute-done((bf16[1024,384]{1,0:T(8,128)(2,1)S(1)}, bf16[1024,384]{1,0:T(8,128)(2,1)S(1)}, u32[]{:S(2)}, u32[]{:S(2)}) %collective-permute-start.34) | collective-permute-done | bytes 786464 | tf_op jit(solution)/shard_map/ppermute | solution.py:517
  678.6 5.3 reduce-scatter.8.cloned.1.call-done
  (491 shorter events, 139.5 us)
Async XLA Ops:
  7.2 59.9 %all-gather.5.cloned.1.call-start = ((), (), s32[]{:S(2)}) async-start(), calls=%async_computation.3 | async-start | bytes 5013504 | tf_op jit(solution)/shard_map/all_gather | solution.py:577
  9.2 112.5 %all-gather.7.cloned.1.call-start = ((), (), s32[]{:S(2)}) async-start(), calls=%async_computation.4 | async-start | bytes 2506752 | tf_op jit(solution)/shard_map/all_gather | solution.py:577
  11.1 249.4 %all-gather.9.cloned.1.call-start = ((), (), s32[]{:S(2)}) async-start(), calls=%async_computation.5 | async-start | bytes 5013504 | tf_op jit(solution)/shard_map/all_gather | solution.py:577
  11.2 31.7 %copy-start.88 = (s32[64]{0:T(128)S(1)}, s32[64]{0:T(128)}, u32[]{:S(2)}) copy-start(s32[64]{0:T(128)} %param.32) | copy-start | bytes 772
  12.7 35.3 %collective-permute-start = (bf16[64,384]{1,0:T(8,128)(2,1)S(1)}, bf16[64,384]{1,0:T(8,128)(2,1)S(1)}, u32[]{:S(2)}, u32[]{:S(2)}) collective-permute-start(bf16[64,384]{1,0:T(8,128)(2,1)S(1)} %get-tuple-element.262), channel_id=1, source_target_pairs={{0,2},{2,4},{4,6},{6,8},{8,10},{10,12},{12,14},{14,16},{16,18},{18... | collective-permute-start | bytes 147464 | tf_op jit(solution)/shard_map/ppermute | solution.py:536
  15.1 32.9 %collective-permute-start.1 = (bf16[64,384]{1,0:T(8,128)(2,1)S(1)}, bf16[64,384]{1,0:T(8,128)(2,1)S(1)}, u32[]{:S(2)}, u32[]{:S(2)}) collective-permute-start(bf16[64,384]{1,0:T(8,128)(2,1)S(1)} %get-tuple-element.263), channel_id=1, source_target_pairs={{2,0},{4,2},{6,4},{8,6},{10,8},{12,10},{14,12},{16,14},{18,16},{20... | collective-permute-start | bytes 147464 | tf_op jit(solution)/shard_map/ppermute | solution.py:536
  17.2 485.1 %reduce-scatter.4.cloned.1.call-start = ((), (), s32[]{:S(2)}) async-start(), calls=%async_computation.6 | async-start | bytes 5013504 | tf_op jit(solution)/shard_map/reduce_scatter | solution.py:581
  47.8 65.1 %copy-start.69 = (f32[384]{0:T(512)}, f32[384]{0:T(512)S(1)}, u32[]{:S(2)}) copy-start(f32[384]{0:T(512)S(1)} %add.609) | copy-start | bytes 4612
  119.1 20.7 %collective-permute-start.2 = (bf16[1024,384]{1,0:T(8,128)(2,1)}, bf16[1024,384]{1,0:T(8,128)(2,1)}, u32[]{:S(2)}, u32[]{:S(2)}) collective-permute-start(bf16[1024,384]{1,0:T(8,128)(2,1)} %get-tuple-element.244), channel_id=1, source_target_pairs={{0,1},{1,0},{2,3},{3,2},{4,5},{5,4},{6,7},{7,6},{8,9},{9,8},{10,11... | collective-permute-start | bytes 2359304 | tf_op jit(solution)/shard_map/ppermute | solution.py:517
  122.9 33.9 %collective-permute-start.3 = (bf16[768,384]{1,0:T(8,128)(2,1)S(1)}, bf16[768,384]{1,0:T(8,128)(2,1)S(1)}, u32[]{:S(2)}, u32[]{:S(2)}) collective-permute-start(bf16[768,384]{1,0:T(8,128)(2,1)S(1)} %slice.303), channel_id=1, source_target_pairs={{0,1},{1,0},{2,3},{3,2},{4,5},{5,4},{6,7},{7,6},{8,9},{9,8},{10,11... | collective-permute-start | bytes 1769480 | tf_op jit(solution)/shard_map/ppermute | solution.py:517
  148.2 28.6 %copy-start.5 = (bf16[1024,768]{1,0:T(8,128)(2,1)}, bf16[1024,768]{1,0:T(8,128)(2,1)S(1)}, u32[]{:S(2)}) copy-start(bf16[1024,768]{1,0:T(8,128)(2,1)S(1)} %fusion.2.k0) | copy-start | bytes 4718596
  148.2 17.5 %collective-permute-start.4 = (bf16[1024,256]{1,0:T(8,128)(2,1)S(1)}, bf16[1024,256]{1,0:T(8,128)(2,1)S(1)}, u32[]{:S(2)}, u32[]{:S(2)}) collective-permute-start(bf16[1024,256]{1,0:T(8,128)(2,1)S(1)} %slice.306), channel_id=1, source_target_pairs={{0,2},{2,0},{4,6},{6,4},{8,10},{10,8},{12,14},{14,12},{16,18},{18,... | collective-permute-start | bytes 1572872 | tf_op jit(solution)/shard_map/ppermute | solution.py:540
  148.3 17.4 %collective-permute-start.5 = (bf16[1024,256]{1,0:T(8,128)(2,1)S(1)}, bf16[1024,256]{1,0:T(8,128)(2,1)S(1)}, u32[]{:S(2)}, u32[]{:S(2)}) collective-permute-start(bf16[1024,256]{1,0:T(8,128)(2,1)S(1)} %slice.306), channel_id=1, source_target_pairs={{2,4},{4,2},{6,8},{8,6},{10,12},{12,10},{14,16},{16,14},{18,20},{2... | collective-permute-start | bytes 1572872 | tf_op jit(solution)/shard_map/ppermute | solution.py:546
  149.1 16.1 %collective-permute-start.6 = (bf16[512,256]{1,0:T(8,128)(2,1)S(1)}, bf16[512,256]{1,0:T(8,128)(2,1)S(1)}, u32[]{:S(2)}, u32[]{:S(2)}) collective-permute-start(bf16[512,256]{1,0:T(8,128)(2,1)S(1)} %get-tuple-element.259), channel_id=1, source_target_pairs={{0,4},{4,8},{6,2},{8,12},{10,6},{12,16},{14,10},{16,20},{18,14},{2... | collective-permute-start | bytes 786440 | tf_op jit(solution)/shard_map/ppermute | solution.py:552
  154.3 11.4 %collective-permute-start.7 = (bf16[512,256]{1,0:T(8,128)(2,1)S(1)}, bf16[512,256]{1,0:T(8,128)(2,1)S(1)}, u32[]{:S(2)}, u32[]{:S(2)}) collective-permute-start(bf16[512,256]{1,0:T(8,128)(2,1)S(1)} %get-tuple-element.258), channel_id=1, source_target_pairs={{2,6},{4,0},{6,10},{8,4},{10,14},{12,8},{14,18},{16,12},{18,22},{2... | collective-permute-start | bytes 786440 | tf_op jit(solution)/shard_map/ppermute | solution.py:552
  165.9 49.1 %collective-permute-start.8 = (bf16[1024,512]{1,0:T(8,128)(2,1)S(1)}, bf16[1024,512]{1,0:T(8,128)(2,1)}, u32[]{:S(2)}, u32[]{:S(2)}) collective-permute-start(bf16[1024,512]{1,0:T(8,128)(2,1)S(1)} %slice.246), channel_id=1, source_target_pairs={{0,2},{2,0},{4,6},{6,4},{8,10},{10,8},{12,14},{14,12},{16,18},{18,... | collective-permute-start | bytes 3145736 | tf_op jit(solution)/shard_map/ppermute | solution.py:540
  175.1 39.9 %collective-permute-start.9 = (bf16[1024,512]{1,0:T(8,128)(2,1)S(1)}, bf16[1024,512]{1,0:T(8,128)(2,1)}, u32[]{:S(2)}, u32[]{:S(2)}) collective-permute-start(bf16[1024,512]{1,0:T(8,128)(2,1)S(1)} %slice.246), channel_id=1, source_target_pairs={{2,4},{4,2},{6,8},{8,6},{10,12},{12,10},{14,16},{16,14},{18,20},{2... | collective-permute-start | bytes 3145736 | tf_op jit(solution)/shard_map/ppermute | solution.py:546
  176.9 38.0 %collective-permute-start.10 = (bf16[512,512]{1,0:T(8,128)(2,1)S(1)}, bf16[512,512]{1,0:T(8,128)(2,1)S(1)}, u32[]{:S(2)}, u32[]{:S(2)}) collective-permute-start(bf16[512,512]{1,0:T(8,128)(2,1)S(1)} %get-tuple-element.257), channel_id=1, source_target_pairs={{0,4},{4,8},{6,2},{8,12},{10,6},{12,16},{14,10},{16,20},{18,14},{2... | collective-permute-start | bytes 1572872 | tf_op jit(solution)/shard_map/ppermute | solution.py:552
  181.3 33.7 %collective-permute-start.11 = (bf16[512,512]{1,0:T(8,128)(2,1)S(1)}, bf16[512,512]{1,0:T(8,128)(2,1)}, u32[]{:S(2)}, u32[]{:S(2)}) collective-permute-start(bf16[512,512]{1,0:T(8,128)(2,1)S(1)} %get-tuple-element.256), channel_id=1, source_target_pairs={{2,6},{4,0},{6,10},{8,4},{10,14},{12,8},{14,18},{16,12},{18,22},{2... | collective-permute-start | bytes 1572872 | tf_op jit(solution)/shard_map/ppermute | solution.py:552
  201.8 6.6 collective-permute-start.12
  231.4 18.3 %collective-permute-start.13 = (bf16[1024,128]{1,0:T(8,128)(2,1)}, bf16[1024,128]{1,0:T(8,128)(2,1)S(1)}, u32[]{:S(2)}, u32[]{:S(2)}) collective-permute-start(bf16[1024,128]{1,0:T(8,128)(2,1)} %get-tuple-element.103), channel_id=1, source_target_pairs={{0,1},{1,0},{2,3},{3,2},{4,5},{5,4},{6,7},{7,6},{8,9},{9,8},{10,11... | collective-permute-start | bytes 786440 | tf_op jit(solution)/shard_map/ppermute | solution.py:517
  248.7 6.6 collective-permute-start.14
  271.6 13.6 %collective-permute-start.15 = (bf16[512,768]{1,0:T(8,128)(2,1)S(1)}, bf16[512,768]{1,0:T(8,128)(2,1)S(1)}, u32[]{:S(2)}, u32[]{:S(2)}) collective-permute-start(bf16[512,768]{1,0:T(8,128)(2,1)S(1)} %fusion.51), channel_id=1, source_target_pairs={{0,1},{1,0},{2,3},{3,2},{4,5},{5,4},{6,7},{7,6},{8,9},{9,8},{10,11... | collective-permute-start | bytes 2359304 | tf_op jit(solution)/shard_map/ppermute | solution.py:517
  282.2 20.5 %collective-permute-start.16 = (bf16[512,768]{1,0:T(8,128)(2,1)S(1)}, bf16[512,768]{1,0:T(8,128)(2,1)S(1)}, u32[]{:S(2)}, u32[]{:S(2)}) collective-permute-start(bf16[512,768]{1,0:T(8,128)(2,1)S(1)} %fusion.54), channel_id=1, source_target_pairs={{0,1},{1,0},{2,3},{3,2},{4,5},{5,4},{6,7},{7,6},{8,9},{9,8},{10,11... | collective-permute-start | bytes 2359304 | tf_op jit(solution)/shard_map/ppermute | solution.py:517
  294.9 44.6 %collective-permute-start.17 = (bf16[512,768]{1,0:T(8,128)(2,1)}, bf16[512,768]{1,0:T(8,128)(2,1)}, u32[]{:S(2)}, u32[]{:S(2)}) collective-permute-start(bf16[512,768]{1,0:T(8,128)(2,1)} %fusion.45), channel_id=1, source_target_pairs={{0,1},{1,0},{2,3},{3,2},{4,5},{5,4},{6,7},{7,6},{8,9},{9,8},{10,11... | collective-permute-start | bytes 2359304 | tf_op jit(solution)/shard_map/ppermute | solution.py:517
  311.3 25.3 %collective-permute-start.18 = (bf16[512,768]{1,0:T(8,128)(2,1)}, bf16[512,768]{1,0:T(8,128)(2,1)}, u32[]{:S(2)}, u32[]{:S(2)}) collective-permute-start(bf16[512,768]{1,0:T(8,128)(2,1)} %fusion.48), channel_id=1, source_target_pairs={{0,1},{1,0},{2,3},{3,2},{4,5},{5,4},{6,7},{7,6},{8,9},{9,8},{10,11... | collective-permute-start | bytes 2359304 | tf_op jit(solution)/shard_map/ppermute | solution.py:517
  343.2 133.7 %copy-start.13 = (f32[512,768]{1,0:T(8,128)}, f32[512,768]{1,0:T(8,128)S(1)}, u32[]{:S(2)}) copy-start(f32[512,768]{1,0:T(8,128)S(1)} %get-tuple-element.212) | copy-start | bytes 4718596
  343.2 133.7 %copy-start.14 = (f32[512,768]{1,0:T(8,128)}, f32[512,768]{1,0:T(8,128)S(1)}, u32[]{:S(2)}) copy-start(f32[512,768]{1,0:T(8,128)S(1)} %get-tuple-element.294) | copy-start | bytes 4718596
  346.7 256.9 %reduce-scatter.6.cloned.1.call-start = ((), (), s32[]{:S(2)}) async-start(), calls=%async_computation.7 | async-start | bytes 2506752 | tf_op jit(solution)/shard_map/reduce_scatter | solution.py:581
  365.3 62.2 %collective-permute-start.19 = (bf16[1024,256]{1,0:T(8,128)(2,1)}, bf16[1024,256]{1,0:T(8,128)(2,1)}, u32[]{:S(2)}, u32[]{:S(2)}) collective-permute-start(bf16[1024,256]{1,0:T(8,128)(2,1)} %get-tuple-element.116), channel_id=1, source_target_pairs={{0,2},{2,0},{4,6},{6,4},{8,10},{10,8},{12,14},{14,12},{16,18},{18,... | collective-permute-start | bytes 1572872 | tf_op jit(solution)/shard_map/ppermute | solution.py:540
  371.4 56.2 %collective-permute-start.20 = (bf16[1024,256]{1,0:T(8,128)(2,1)}, bf16[1024,256]{1,0:T(8,128)(2,1)}, u32[]{:S(2)}, u32[]{:S(2)}) collective-permute-start(bf16[1024,256]{1,0:T(8,128)(2,1)} %get-tuple-element.117), channel_id=1, source_target_pairs={{2,4},{4,2},{6,8},{8,6},{10,12},{12,10},{14,16},{16,14},{18,20},{2... | collective-permute-start | bytes 1572872 | tf_op jit(solution)/shard_map/ppermute | solution.py:546
  372.8 53.2 %collective-permute-start.21 = (bf16[512,256]{1,0:T(8,128)(2,1)}, bf16[512,256]{1,0:T(8,128)(2,1)}, u32[]{:S(2)}, u32[]{:S(2)}) collective-permute-start(bf16[512,256]{1,0:T(8,128)(2,1)} %get-tuple-element.118), channel_id=1, source_target_pairs={{2,6},{4,0},{6,10},{8,4},{10,14},{12,8},{14,18},{16,12},{18,22},{2... | collective-permute-start | bytes 786440 | tf_op jit(solution)/shard_map/ppermute | solution.py:552
  374.1 32.5 %copy-start.29 = (bf16[1024,128]{1,0:T(8,128)(2,1)S(1)}, bf16[1024,128]{1,0:T(8,128)(2,1)}, u32[]{:S(2)}) copy-start(bf16[1024,128]{1,0:T(8,128)(2,1)} %get-tuple-element.112) | copy-start | bytes 786436
  393.3 16.9 %collective-permute-start.25 = (bf16[512,256]{1,0:T(8,128)(2,1)}, bf16[512,256]{1,0:T(8,128)(2,1)}, u32[]{:S(2)}, u32[]{:S(2)}) collective-permute-start(bf16[512,256]{1,0:T(8,128)(2,1)} %get-tuple-element.133), channel_id=1, source_target_pairs={{2,6},{4,0},{6,10},{8,4},{10,14},{12,8},{14,18},{16,12},{18,22},{2... | collective-permute-start | bytes 786440 | tf_op jit(solution)/shard_map/ppermute | solution.py:552
  394.6 26.6 %collective-permute-start.26 = (bf16[512,256]{1,0:T(8,128)(2,1)}, bf16[512,256]{1,0:T(8,128)(2,1)}, u32[]{:S(2)}, u32[]{:S(2)}) collective-permute-start(bf16[512,256]{1,0:T(8,128)(2,1)} %get-tuple-element.134), channel_id=1, source_target_pairs={{0,4},{4,8},{6,2},{8,12},{10,6},{12,16},{14,10},{16,20},{18,14},{2... | collective-permute-start | bytes 786440 | tf_op jit(solution)/shard_map/ppermute | solution.py:552
  410.2 17.3 %collective-permute-start.22 = (bf16[512,256]{1,0:T(8,128)(2,1)}, bf16[512,256]{1,0:T(8,128)(2,1)S(1)}, u32[]{:S(2)}, u32[]{:S(2)}) collective-permute-start(bf16[512,256]{1,0:T(8,128)(2,1)} %get-tuple-element.119), channel_id=1, source_target_pairs={{0,4},{4,8},{6,2},{8,12},{10,6},{12,16},{14,10},{16,20},{18,14},{2... | collective-permute-start | bytes 786440 | tf_op jit(solution)/shard_map/ppermute | solution.py:552
  421.1 43.7 %collective-permute-start.23 = (bf16[1024,256]{1,0:T(8,128)(2,1)}, bf16[1024,256]{1,0:T(8,128)(2,1)S(1)}, u32[]{:S(2)}, u32[]{:S(2)}) collective-permute-start(bf16[1024,256]{1,0:T(8,128)(2,1)} %get-tuple-element.131), channel_id=1, source_target_pairs={{0,2},{2,0},{4,6},{6,4},{8,10},{10,8},{12,14},{14,12},{16,18},{18,... | collective-permute-start | bytes 1572872 | tf_op jit(solution)/shard_map/ppermute | solution.py:540
  426.0 39.5 %collective-permute-start.24 = (bf16[1024,256]{1,0:T(8,128)(2,1)}, bf16[1024,256]{1,0:T(8,128)(2,1)}, u32[]{:S(2)}, u32[]{:S(2)}) collective-permute-start(bf16[1024,256]{1,0:T(8,128)(2,1)} %get-tuple-element.132), channel_id=1, source_target_pairs={{2,4},{4,2},{6,8},{8,6},{10,12},{12,10},{14,16},{16,14},{18,20},{2... | collective-permute-start | bytes 1572872 | tf_op jit(solution)/shard_map/ppermute | solution.py:546
  446.1 21.8 %collective-permute-start.29 = (bf16[512,256]{1,0:T(8,128)(2,1)}, bf16[512,256]{1,0:T(8,128)(2,1)S(1)}, u32[]{:S(2)}, u32[]{:S(2)}) collective-permute-start(bf16[512,256]{1,0:T(8,128)(2,1)} %get-tuple-element.138), channel_id=1, source_target_pairs={{2,6},{4,0},{6,10},{8,4},{10,14},{12,8},{14,18},{16,12},{18,22},{2... | collective-permute-start | bytes 786440 | tf_op jit(solution)/shard_map/ppermute | solution.py:552
  447.6 20.3 %collective-permute-start.30 = (bf16[512,256]{1,0:T(8,128)(2,1)}, bf16[512,256]{1,0:T(8,128)(2,1)S(1)}, u32[]{:S(2)}, u32[]{:S(2)}) collective-permute-start(bf16[512,256]{1,0:T(8,128)(2,1)} %get-tuple-element.139), channel_id=1, source_target_pairs={{0,4},{4,8},{6,2},{8,12},{10,6},{12,16},{14,10},{16,20},{18,14},{2... | collective-permute-start | bytes 786440 | tf_op jit(solution)/shard_map/ppermute | solution.py:552
  458.3 9.7 %collective-permute-start.27 = (bf16[1024,256]{1,0:T(8,128)(2,1)}, bf16[1024,256]{1,0:T(8,128)(2,1)S(1)}, u32[]{:S(2)}, u32[]{:S(2)}) collective-permute-start(bf16[1024,256]{1,0:T(8,128)(2,1)} %get-tuple-element.136), channel_id=1, source_target_pairs={{0,2},{2,0},{4,6},{6,4},{8,10},{10,8},{12,14},{14,12},{16,18},{18,... | collective-permute-start | bytes 1572872 | tf_op jit(solution)/shard_map/ppermute | solution.py:540
  464.8 3.2 collective-permute-start.28
  476.2 20.7 %collective-permute-start.31 = (bf16[1024,768]{1,0:T(8,128)(2,1)}, bf16[1024,768]{1,0:T(8,128)(2,1)}, u32[]{:S(2)}, u32[]{:S(2)}) collective-permute-start(bf16[1024,768]{1,0:T(8,128)(2,1)} %convolution_convert_fusion.1), channel_id=1, source_target_pairs={{0,1},{1,0},{2,3},{3,2},{4,5},{5,4},{6,7},{7,6},{8,9},{9,8},{10,11... | collective-permute-start | bytes 4718600 | tf_op jit(solution)/shard_map/ppermute | solution.py:517
  504.2 179.7 %reduce-scatter.8.cloned.1.call-start = ((), (), s32[]{:S(2)}) async-start(), calls=%async_computation.8 | async-start | bytes 5222400 | tf_op jit(solution)/shard_map/reduce_scatter | solution.py:581
  512.2 92.3 %collective-permute-start.32 = (bf16[64,384]{1,0:T(8,128)(2,1)S(1)}, bf16[64,384]{1,0:T(8,128)(2,1)S(1)}, u32[]{:S(2)}, u32[]{:S(2)}) collective-permute-start(bf16[64,384]{1,0:T(8,128)(2,1)S(1)} %get-tuple-element.260), channel_id=1, source_target_pairs={{0,2},{2,4},{4,6},{6,8},{8,10},{10,12},{12,14},{14,16},{16,18},{18... | collective-permute-start | bytes 147464 | tf_op jit(solution)/shard_map/ppermute | solution.py:536
  533.4 71.2 %collective-permute-start.33 = (bf16[64,384]{1,0:T(8,128)(2,1)S(1)}, bf16[64,384]{1,0:T(8,128)(2,1)S(1)}, u32[]{:S(2)}, u32[]{:S(2)}) collective-permute-start(bf16[64,384]{1,0:T(8,128)(2,1)S(1)} %get-tuple-element.261), channel_id=1, source_target_pairs={{2,0},{4,2},{6,4},{8,6},{10,8},{12,10},{14,12},{16,14},{18,16},{20... | collective-permute-start | bytes 147464 | tf_op jit(solution)/shard_map/ppermute | solution.py:536
  606.7 46.4 %copy-start.12 = (f32[512,768]{1,0:T(8,128)S(1)}, f32[512,768]{1,0:T(8,128)}, u32[]{:S(2)}) copy-start(f32[512,768]{1,0:T(8,128)} %get-tuple-element.252) | copy-start | bytes 4718596
  651.5 17.8 %collective-permute-start.34 = (bf16[1024,384]{1,0:T(8,128)(2,1)S(1)}, bf16[1024,384]{1,0:T(8,128)(2,1)S(1)}, u32[]{:S(2)}, u32[]{:S(2)}) collective-permute-start(bf16[1024,384]{1,0:T(8,128)(2,1)S(1)} %convert_element_type.280), channel_id=1, source_target_pairs={{0,1},{1,0},{2,3},{3,2},{4,5},{5,4},{6,7},{7,6},{8,9},{9,8},{10,11... | collective-permute-start | bytes 2359304 | tf_op jit(solution)/shard_map/ppermute | solution.py:517
  (96 other events, 614.8 us)
Sparse Core Ops, SparseCore 0:
  10.9 56.1 all-gather.4
  70.0 40.8 all-gather.6
  113.7 56.7 all-gather.8
  346.8 112.9 reduce-scatter.3
  504.3 99.2 reduce-scatter.5
  607.4 76.3 reduce-scatter.7

commit v4 on v3

--- a/solution.py
+++ b/solution.py
@@ -17,7 +17,6 @@
 ROWS, WIN, HALF = 1024, 1152, 384
 CM, XM = 272, 304
 NQ = 33
-LCAP = 1408
 PJ = 134
 EXTRA = 16
 VLIM = 58 << 20
@@ -39,7 +38,10 @@
     w = jnp.arange(WIN, dtype=i32)
     inside = (b[None, :] <= w[:, None]) & (w[:, None] < e[None, :])
     p = jnp.sum(jnp.where(inside, 4 * bs - b + w[:, None] + 1, 0), axis=1).astype(i32) - 1
-    m = jnp.arange(LCAP, dtype=i32)
+    most = min(WIN, WIN // 4 + n)
+    maxc = -((16 - most) // CM)
+    lcap = CM * (maxc - 1) + XM
+    m = jnp.arange(lcap, dtype=i32)
     hit = (bs[None, :] <= m[:, None]) & (m[:, None] < (bs + nblk)[None, :])
     bseg = jnp.sum(jnp.where(hit, jnp.arange(1, n + 1, dtype=i32)[None, :], 0), axis=1).astype(i32) - 1
     chunks = jnp.maximum((p[HALO + ROWS - 1] // 4 - 16) // CM + 1, 1)
@@ -47,7 +49,7 @@
         jnp.reshape(chunks, (1,)).astype(i32),
         jnp.broadcast_to(p[None, :], (8, WIN)),
         jnp.broadcast_to(p[:, None], (WIN, 128)),
-        jnp.broadcast_to(bseg[:, None], (LCAP, 128)),
+        jnp.broadcast_to(bseg[:, None], (lcap, 128)),
     )
 
 
@@ -58,17 +60,9 @@
     return jnp.where(ok, 1.0, 0.0).astype(bf16)
 
 
-def build_selector(s_ref, prow, c, first, rows):
-    for t in range(4):
-        pos = 4 * (iota((rows, prow.shape[1]), 0) + (CM * c + first)) + t
-        s_ref[t] = jnp.where(pos == prow, 1.0, 0.0).astype(bf16)
-
-
-def build_blocks(s_ref, dup, rows):
-    y = [
-        jnp.dot(s_ref[t], dup, preferred_element_type=f32).astype(bf16) for t in range(4)
-    ]
-    low = iota((rows, 128), 1) < 64
+def build_blocks(s_ref, dup):
+    y = [jnp.dot(s_ref[0, t], dup, preferred_element_type=f32).astype(bf16) for t in range(4)]
+    low = iota((XM, 128), 1) < 64
     out = []
     for g in range(2):
         tiles = [v[:, 128 * g : 128 * g + 128] for v in y]
@@ -92,203 +86,297 @@
             p_ref[g, pl.ds(j0 + 3, step), 0:CG, 64:128] = d[:, :, 128 * g + 64 : 128 * g + 128]
 
 
-def conv_kernel(
-    back, chunks_ref, prow_ref, pcol_ref, bseg_ref, x_ref, k_ref, out_ref, s_ref, mask_ref, p_ref, xb_ref
-):
-    h = pl.program_id(0)
-    base_tile = h // 2
-    chunks = chunks_ref[0]
+def pair_lanes(h):
+    base_tile = h >> 1
+    return base_tile, pl.ds(pl.multiple_of(base_tile * 128, 128), 256)
+
+
+def prepare_kernel(n_ref, *refs):
+    @pl.when(pl.program_id(0) < n_ref[0])
+    def _():
+        prepare_chunk(pl.program_id(0), *refs)
+
+
+def prepare_chunk(c, prow_ref, pcol_ref, bseg_ref, x_ref, s_ref, r_ref, mask_ref, tmask_ref, xb_ref, xt_ref):
+    prow = prow_ref[0:1, :]
+    for t in range(4):
+        pos = 4 * (iota((XM, WIN), 0) + CM * c) + t
+        s_ref[0, t] = jnp.where(pos == prow, 1.0, 0.0).astype(bf16)
+    pcol = pcol_ref[HALO : HALO + ROWS, :]
+    lane = iota((ROWS, 4 * CM), 1)
+    phase = sum([(lane >= CM * t).astype(i32) for t in range(1, 4)])
+    spot = 4 * (16 + CM * c) + 4 * lane - (4 * CM - 1) * phase
+    wide = jnp.concatenate([pcol] * 9, axis=1)[:, : 4 * CM]
+    r_ref[0] = jnp.where(wide == spot, 1.0, 0.0).astype(bf16)
+    seg = bseg_ref[pl.ds(pl.multiple_of(CM * c, 16), XM), :]
+    none = jnp.full((32, 128), -7, i32)
+    own = jnp.concatenate([none, seg[16 : 16 + CM], none], axis=0)
+    for q in range(NQ):
+        same = seg[q : q + CM] == seg[16 : 16 + CM]
+        mask_ref[0, q] = jnp.where(same, 1.0, 0.0).astype(bf16)
+        same = seg == own[32 - q : 32 - q + XM]
+        tmask_ref[0, q] = jnp.where(same, 1.0, 0.0).astype(bf16)
+    for h in range(4):
+        base = 128 * (h // 2)
+        sel = select_pair(h, 256, base)
+        dup = jnp.dot(x_ref[:, base : base + 256], sel, preferred_element_type=f32).astype(bf16)
+        for g, block in enumerate(build_blocks(s_ref, dup)):
+            xb_ref[0, 2 * h + g] = block
+            xt_ref[0, 2 * h + g] = block.T
+
+
+def fixed(shape):
+    return pl.BlockSpec(shape, lambda *_: (0,) * len(shape))
+
+
+def chunk_count(plan):
+    return (plan[3].shape[0] - XM) // CM + 1
+
+
+def call(kernel, name, grid, plan, in_specs, out_specs, out_shape, scratch, flops, args):
+    return pl.pallas_call(
+        kernel,
+        grid_spec=pltpu.PrefetchScalarGridSpec(
+            num_scalar_prefetch=1,
+            grid=grid,
+            in_specs=in_specs,
+            out_specs=out_specs,
+            scratch_shapes=scratch,
+        ),
+        out_shape=out_shape,
+        compiler_params=pltpu.CompilerParams(vmem_limit_bytes=VLIM),
+        cost_estimate=pl.CostEstimate(flops=flops, bytes_accessed=15_000_000, transcendentals=0),
+        name=name,
+    )(plan[0], *args)
+
+
+def prepare(plan, window):
+    chunks, prow, pcol, bseg = plan
+    shapes = ((4, XM, WIN), (ROWS, 4 * CM), (NQ, CM, 128), (NQ, XM, 128), (8, XM, 256), (8, 256, XM))
+    maxc = chunk_count(plan)
+    return call(
+        prepare_kernel,
+        "conv_prepare",
+        (maxc,),
+        plan,
+        [fixed(a.shape) for a in (prow, pcol, bseg, window)],
+        tuple(
+            pl.BlockSpec((1,) + s, lambda c, n, k=len(s): (jnp.minimum(c, n[0] - 1),) + (0,) * k)
+            for s in shapes
+        ),
+        tuple(jax.ShapeDtypeStruct((maxc,) + s, bf16) for s in shapes),
+        [],
+        10_000_000_000,
+        (prow, pcol, bseg, window),
+    )
+
+
+def conv_forward_kernel(n_ref, *refs):
+    c, h = pl.program_id(0), pl.program_id(1)
+
+    @pl.when(c < n_ref[0])
+    def _():
+        conv_chunk(False, c, h, *refs)
+
+
+def conv_back_kernel(n_ref, d_ref, s_ref, *refs):
+    c, h = pl.program_id(0), pl.program_id(1)
+
+    @pl.when(c < n_ref[0])
+    def _():
+        conv_chunk(True, c, h, (d_ref, s_ref), *refs)
+
+
+def conv_chunk(back, c, h, x_ref, mask_ref, r_ref, k_ref, out_ref, *rest):
+    base_tile, lanes = pair_lanes(h)
+    if back:
+        s_ref, (xb_ref, o_ref) = x_ref[1], rest
+        p_ref = k_ref
+        sel = select_pair(h, 256, 128 * base_tile)
+        dup = jnp.dot(x_ref[0][:, lanes], sel, preferred_element_type=f32).astype(bf16)
+        for g, block in enumerate(build_blocks(s_ref, dup)):
+            xb_ref[0, g] = block
+    else:
+        xb_ref = x_ref
+        p_ref, o_ref = rest
+        build_taps(k_ref, select_pair(h, 256, 128 * base_tile), p_ref, base_tile)
 
     @pl.when(h == 0)
     def _():
-        out_ref[...] = jnp.zeros_like(out_ref)
-
-    sel = select_pair(h, 256, 128 * base_tile)
-    build_taps(k_ref, sel, p_ref, base_tile)
-    lanes = pl.ds(pl.multiple_of(base_tile * 128, 128), 256)
-    dup = jnp.dot(x_ref[:, lanes], sel, preferred_element_type=f32).astype(bf16)
-
-    def chunk(c, carry):
-        @pl.when((h == 0) | (chunks > 1))
+        o_ref[...] = jnp.zeros_like(o_ref)
+
+    total = [jnp.zeros((CM, 256), f32) for _ in range(4)]
+    for g in range(2):
+        acc = jnp.zeros((CM, 256), f32)
+        for q in range(NQ):
+            m = mask_ref[0, q]
+            xs = xb_ref[0, g, q : q + CM, :] * jnp.concatenate([m, m], axis=1)
+            if back:
+                a, b = 130 - 4 * q, 128 - 4 * q
+            else:
+                a, b = 4 * q + 2, 4 * q
+            w = jnp.concatenate(
+                [p_ref[g, a : a + 4].reshape(256, 128), p_ref[g, b : b + 4].reshape(256, 128)],
+                axis=1,
+            )
+            dims = (((1,), (1 if back else 0,)), ((), ()))
+            acc = acc + lax.dot_general(xs, w, dims, preferred_element_type=f32)
+        acc = acc.astype(bf16)
+        row = iota((256, 256), 0)
+        target = CG * (2 * h + g) - 128 * base_tile + (row & 63)
+        hit = ((row & 63) < CG) & (iota((256, 256), 1) == target)
+        for t in range(4):
+            fold = jnp.where(hit & ((row >> 6) == t), 1.0, 0.0).astype(bf16)
+            total[t] = total[t] + jnp.dot(acc, fold, preferred_element_type=f32)
+    for t in range(4):
+        o_ref[CM * t : CM * t + CM, lanes] += total[t].astype(bf16)
+
+    @pl.when(h == 3)
+    def _():
+        y = jnp.dot(r_ref[0], o_ref[...], preferred_element_type=f32)
+
+        @pl.when(c == 0)
         def _():
-            build_selector(s_ref, prow_ref[0:1, :], c, 0, XM)
-            seg = bseg_ref[pl.ds(pl.multiple_of(CM * c, 16), XM), :]
-            for q in range(NQ):
-                same = seg[q : q + CM] == seg[16 : 16 + CM]
-                mask_ref[q] = jnp.where(same, 1.0, 0.0).astype(bf16)
-
-        xb = build_blocks(s_ref, dup, XM)
-        for g in range(2):
-            xb_ref[g] = xb[g]
-        pcol = pcol_ref[pl.ds(HALO, ROWS), :]
-        local = (pcol >> 2) - (16 + CM * c)
-        place = jnp.where(
-            jnp.concatenate([local] * 3, axis=1)[:, :CM] == iota((ROWS, CM), 1), 1.0, 0.0
-        ).astype(bf16)
-        phase = pcol & 3
-        hi = iota((ROWS, 128), 1) >> 6
-        pick = jnp.concatenate([phase == hi, phase == hi + 2], axis=1)
-        total = jnp.zeros((ROWS, 256), f32)
-        for g in range(2):
-            acc = jnp.zeros((CM, 256), f32)
-            for q in range(NQ):
-                m = mask_ref[q]
-                xs = xb_ref[g, q : q + CM, :] * jnp.concatenate([m, m], axis=1)
-                if back:
-                    a, b = 130 - 4 * q, 128 - 4 * q
-                else:
-                    a, b = 4 * q + 2, 4 * q
-                w = jnp.concatenate(
-                    [
-                        p_ref[g, a : a + 4].reshape(256, 128),
-                        p_ref[g, b : b + 4].reshape(256, 128),
-                    ],
-                    axis=1,
-                )
-                dims = (((1,), (1 if back else 0,)), ((), ()))
-                acc = acc + lax.dot_general(xs, w, dims, preferred_element_type=f32)
-            y = jnp.dot(place, acc.astype(bf16), preferred_element_type=f32)
-            y = jnp.where(pick, y, 0.0).astype(bf16)
-            lane = iota((256, 256), 1)
-            row = iota((256, 256), 0) & 63
-            fold = (row < CG) & (lane == CG * (2 * h + g) - 128 * base_tile + row)
-            total = total + jnp.dot(
-                y, jnp.where(fold, 1.0, 0.0).astype(bf16), preferred_element_type=f32
-            )
-        out_ref[:, lanes] += total
-        return carry
-
-    lax.fori_loop(0, chunks, chunk, 0)
-
-
-def smem():
-    return pl.BlockSpec(memory_space=pltpu.SMEM)
-
-
-def whole(shape):
-    return pl.BlockSpec(shape, lambda h: (0,) * len(shape))
-
-
-def conv(plan, window, taps, back):
-    chunks, prow, pcol, bseg = plan
-    return pl.pallas_call(
-        functools.partial(conv_kernel, back),
-        grid=(4,),
-        out_shape=jax.ShapeDtypeStruct((ROWS, HALF), f32),
-        in_specs=[
-            smem(),
-            whole((8, WIN)),
-            whole((WIN, 128)),
-            whole((LCAP, 128)),
-            whole((WIN, HALF)),
-            whole((TAPS, CG, HALF)),
+            out_ref[...] = y
+
+        @pl.when(c > 0)
+        def _():
+            out_ref[...] += y
+
+
+def by_chunk(shape):
+    return pl.BlockSpec(
+        (1,) + shape, lambda c, h, n: (jnp.minimum(c, n[0] - 1),) + (0,) * len(shape)
+    )
+
+
+def by_pair(shape):
+    return pl.BlockSpec(
+        (2,) + shape, lambda c, h, n: (jnp.where(c < n[0], h, 3),) + (0,) * len(shape)
+    )
+
+
+def conv(plan, ready, taps):
+    _, r, mask, _, xb, _ = ready
+    x_spec = pl.BlockSpec(
+        (1, 2, XM, 256),
+        lambda c, h, n: (jnp.minimum(c, n[0] - 1), jnp.where(c < n[0], h, 3), 0, 0),
+    )
+    return call(
+        conv_forward_kernel,
+        "conv_forward",
+        (chunk_count(plan), 4),
+        plan,
+        [x_spec, by_chunk((NQ, CM, 128)), by_chunk((ROWS, 4 * CM)), fixed((TAPS, CG, HALF))],
+        (fixed((ROWS, HALF)), by_pair((PJ, 64, 128))),
+        (
+            jax.ShapeDtypeStruct((ROWS, HALF), f32),
+            jax.ShapeDtypeStruct((8, PJ, 64, 128), bf16),
+        ),
+        [pltpu.VMEM((4 * CM, HALF), bf16)],
+        25_000_000_000,
+        (xb, mask, r, taps),
+    )
+
+
+def conv_back(plan, ready, window, spread_taps):
+    s, r, mask, _, _, _ = ready
+    return call(
+        conv_back_kernel,
+        "conv_back",
+        (chunk_count(plan), 4),
+        plan,
+        [
+            fixed((WIN, HALF)),
+            by_chunk((4, XM, WIN)),
+            by_chunk((NQ, CM, 128)),
+            by_chunk((ROWS, 4 * CM)),
+            by_pair((PJ, 64, 128)),
         ],
-        out_specs=whole((ROWS, HALF)),
-        scratch_shapes=[
-            pltpu.VMEM((4, XM, WIN), bf16),
-            pltpu.VMEM((NQ, CM, 128), bf16),
-            pltpu.VMEM((2, PJ, 64, 128), bf16),
-            pltpu.VMEM((2, XM, 256), bf16),
-        ],
-        compiler_params=pltpu.CompilerParams(vmem_limit_bytes=VLIM),
-        cost_estimate=pl.CostEstimate(flops=30_000_000_000, bytes_accessed=9_000_000, transcendentals=0),
-        name="conv_back" if back else "conv_forward",
-    )(chunks, prow, pcol, bseg, window, taps)
-
-
-def tap_grad_kernel(
-    chunks_ref, prow_ref, bseg_ref, x_ref, d_ref, small_ref, out_ref, s_ref, sd_ref, mask_ref, xt_ref, dp_ref, acc_ref
-):
-    h = pl.program_id(0)
-    base_tile = h // 2
-    chunks = chunks_ref[0]
-
-    @pl.when(h == 0)
+        fixed((ROWS, HALF)),
+        jax.ShapeDtypeStruct((ROWS, HALF), f32),
+        [pltpu.VMEM((1, 2, XM, 256), bf16), pltpu.VMEM((4 * CM, HALF), bf16)],
+        25_000_000_000,
+        (window, s, mask, r, spread_taps),
+    )
+
+
+def tap_grad_kernel(n_ref, xt_ref, s_ref, mask_ref, d_ref, small_ref, out_ref, dp_ref, acc_ref):
+    h, c = pl.program_id(0), pl.program_id(1)
+    base_tile, lanes = pair_lanes(h)
+
+    @pl.when((h == 0) & (c == 0))
     def _():
         out_ref[...] = jnp.zeros_like(out_ref)
         out_ref[:, out_ref.shape[1] - EXTRA :, :] = small_ref[...]
         dp_ref[...] = jnp.zeros_like(dp_ref)
 
-    acc_ref[...] = jnp.zeros_like(acc_ref)
-    sel = select_pair(h, 256, 128 * base_tile)
-    lanes = pl.ds(pl.multiple_of(base_tile * 128, 128), 256)
-    xdup = jnp.dot(x_ref[:, lanes], sel, preferred_element_type=f32).astype(bf16)
-    ddup = jnp.dot(d_ref[:, lanes], sel, preferred_element_type=f32).astype(bf16)
-
-    def chunk(c, carry):
-        @pl.when((h == 0) | (chunks > 1))
-        def _():
-            build_selector(s_ref, prow_ref[0:1, :], c, 0, XM)
-            build_selector(sd_ref, prow_ref[0:1, HALO : HALO + ROWS], c, 16, CM)
-            seg = bseg_ref[pl.ds(pl.multiple_of(CM * c, 16), XM), :]
-            none = jnp.full((32, 128), -7, i32)
-            own = jnp.concatenate([none, seg[16 : 16 + CM], none], axis=0)
-            for q in range(NQ):
-                same = seg == own[32 - q : 32 - q + XM]
-                mask_ref[q] = jnp.where(same, 1.0, 0.0).astype(bf16)
-
-        xb = build_blocks(s_ref, xdup, XM)
-        db = build_blocks(sd_ref, ddup, CM)
-        for g in range(2):
-            xt_ref[g] = xb[g].T
-            dp_ref[g, 32 : 32 + CM, :] = db[g]
+    @pl.when(c == 0)
+    def _():
+        acc_ref[...] = jnp.zeros_like(acc_ref)
+
+    @pl.when(c < n_ref[0])
+    def _():
+        sel = select_pair(h, 256, 128 * base_tile)
+        ddup = jnp.dot(d_ref[:, lanes], sel, preferred_element_type=f32).astype(bf16)
+        for g, block in enumerate(build_blocks(s_ref, ddup)):
+            dp_ref[g, 32 : 32 + CM, :] = block[16 : 16 + CM]
         for g in range(2):
             for q in range(NQ):
-                m = mask_ref[q]
+                m = mask_ref[0, q]
                 ds = dp_ref[g, 32 - q : 32 - q + XM, :] * jnp.concatenate([m, m], axis=1)
-                part = jnp.dot(xt_ref[g], ds, preferred_element_type=f32)
+                part = jnp.dot(xt_ref[0, g], ds, preferred_element_type=f32)
                 acc_ref[g, 4 * q + 2 : 4 * q + 6] += part[:, 0:128].reshape(4, 64, 128)
                 acc_ref[g, 4 * q : 4 * q + 4] += part[:, 128:256].reshape(4, 64, 128)
-        return carry
-
-    lax.fori_loop(0, chunks, chunk, 0)
-    per = TAPS // out_ref.shape[0]
-    low = iota((1, 1, 128), 2) < 64
-    row = iota((128, 256), 0)
-    lane = iota((128, 256), 1)
-    src = CG * (2 * h + (row >> 6)) + (row & 63) - 128 * base_tile
-    back = jnp.where(((row & 63) < CG) & (lane == src), 1.0, 0.0).astype(bf16)
-    step = 16
-    for j0 in range(0, TAPS, step):
-        now = [acc_ref[g, j0 + 2 : j0 + 2 + step, 0:CG, :] for g in range(2)]
-        nxt = [acc_ref[g, j0 + 3 : j0 + 3 + step, 0:CG, :] for g in range(2)]
-        here = jnp.where(low, now[0], nxt[1]).reshape(step * CG, 128)
-        far = jnp.where(low, now[1], nxt[0]).reshape(step * CG, 128)
-        both = (here + pltpu.roll(far, 64, 1)).astype(bf16)
-        o = jnp.dot(both, back, preferred_element_type=f32).astype(bf16)
-        o = o.reshape(step // per, per * CG, 256)
-        out_ref[j0 // per : (j0 + step) // per, 0 : per * CG, lanes] += o
-
-
-def tap_grad(plan, window, d_conv, small):
-    chunks, prow, pcol, bseg = plan
+
+    @pl.when(c == pl.num_programs(1) - 1)
+    def _():
+        per = TAPS // out_ref.shape[0]
+        low = iota((1, 1, 128), 2) < 64
+        row = iota((128, 256), 0)
+        src = CG * (2 * h + (row >> 6)) + (row & 63) - 128 * base_tile
+        back = jnp.where(((row & 63) < CG) & (iota((128, 256), 1) == src), 1.0, 0.0).astype(bf16)
+        step = 16
+        for j0 in range(0, TAPS, step):
+            now = [acc_ref[g, j0 + 2 : j0 + 2 + step, 0:CG, :] for g in range(2)]
+            nxt = [acc_ref[g, j0 + 3 : j0 + 3 + step, 0:CG, :] for g in range(2)]
+            here = jnp.where(low, now[0], nxt[1]).reshape(step * CG, 128)
+            far = jnp.where(low, now[1], nxt[0]).reshape(step * CG, 128)
+            both = (here + pltpu.roll(far, 64, 1)).astype(bf16)
+            o = jnp.dot(both, back, preferred_element_type=f32).astype(bf16)
+            o = o.reshape(step // per, per * CG, 256)
+            out_ref[j0 // per : (j0 + step) // per, 0 : per * CG, lanes] += o
+
+
+def tap_grad(plan, ready, d_own, small):
+    s, _, _, tmask, _, xt = ready
     devices = small.shape[0]
     shape = (devices, TAPS // devices * CG + EXTRA, HALF)
-    return pl.pallas_call(
+    chunked = lambda sh: pl.BlockSpec(
+        (1,) + sh, lambda h, c, n: (jnp.minimum(c, n[0] - 1),) + (0,) * len(sh)
+    )
+    x_spec = pl.BlockSpec((1, 2, 256, XM), lambda h, c, n: (jnp.minimum(c, n[0] - 1), h, 0, 0))
+    return call(
         tap_grad_kernel,
-        grid=(4,),
-        out_shape=jax.ShapeDtypeStruct(shape, bf16),
-        in_specs=[
-            smem(),
-            whole((8, WIN)),
-            whole((LCAP, 128)),
-            whole((WIN, HALF)),
-            whole((ROWS, HALF)),
-            whole(small.shape),
+        "tap_gradient",
+        (4, chunk_count(plan)),
+        plan,
+        [
+            x_spec,
+            chunked((4, XM, WIN)),
+            chunked((NQ, XM, 128)),
+            fixed((WIN, HALF)),
+            fixed(small.shape),
         ],
-        out_specs=whole(shape),
-        scratch_shapes=[
-            pltpu.VMEM((4, XM, WIN), bf16),
-            pltpu.VMEM((4, CM, ROWS), bf16),
-            pltpu.VMEM((NQ, XM, 128), bf16),
-            pltpu.VMEM((2, 256, XM), bf16),
+        fixed(shape),
+        jax.ShapeDtypeStruct(shape, bf16),
+        [
             pltpu.VMEM((2, 32 + CM + 32, 256), bf16),
             pltpu.VMEM((2, PJ, 64, 128), f32),
         ],
-        compiler_params=pltpu.CompilerParams(vmem_limit_bytes=VLIM),
-        cost_estimate=pl.CostEstimate(flops=8_000_000_000, bytes_accessed=9_000_000, transcendentals=0),
-        name="tap_gradient",
-    )(chunks, prow, bseg, window, d_conv, small)
+        1_000_000_000,
+        (xt, s, tmask, d_own, small),
+    )
 REACH = 1536
 SPAN = ROWS + 2 * REACH
 QT, KT = 128, 1664
@@ -659,7 +747,9 @@
     window = jnp.concatenate(
         [passed(x_half[rows - HALO :], 1), x_half, passed(x_half[:HALO], -1)], axis=0
     )
-    pre = conv(plan, window, w_kernel, False) + b_chan[0]
+    ready = prepare(plan, window)
+    conv_out, spread_taps = conv(plan, ready, w_kernel)
+    pre = conv_out + b_chan[0]
     spread_part = gelu_exact(pre).astype(bf16)
     spread = side_by_side(spread_part, exchange(spread_part), index)
     h1, norm0_back = jax.vjp(layer_norm, frames + spread.astype(f32), norms[0, 0], norms[0, 1])
@@ -756,7 +846,9 @@
     for h in range(PAIRS):
         d_part = d_att
         if h >= 2:
-            d_part, arrived[h - 2] = lax.optimization_barrier((d_att, arrived[h - 2]))
+            two = arrived[h - 2][:2]
+            d_part, two = lax.optimization_barrier((d_att, two))
+            arrived[h - 2] = two + arrived[h - 2][2:]
         dq_part, own, core, chip, far, beyond = attend_back(
             reach, h, queries, pieces[h], d_part, mixed[h], lse[h]
         )
@@ -781,7 +873,9 @@
     value_bias_grad = jnp.sum(
         d_both_half.astype(f32), axis=0
     ).reshape(PAIRS, 2, 128)[:, 1].reshape(-1)
-    dh1 = dx2 + pair_sum(dot(stacked, w_first[:, : 3 * HALF], 1, 1))
+    dh1_half = dot(stacked, w_first[:, : 3 * HALF], 1, 1).astype(bf16)
+    dh1_half, second_sum = lax.optimization_barrier((dh1_half, second_sum))
+    dh1 = dx2 + (dh1_half.astype(f32) + exchange(dh1_half).astype(f32))
     first_part = (
         jnp.concatenate(
             [dot(h1_half, stacked, 0, 0).astype(bf16), dot(d_branch, attended, 0, 0).astype(bf16)],
@@ -814,7 +908,8 @@
         )
     small_part = jnp.pad(small_part, ((0, 0), (0, EXTRA * HALF - small_part.shape[1])))
     small_part = small_part.astype(bf16).reshape(devices, EXTRA, HALF)
-    tap_part = tap_grad(plan, window, d_conv_half, small_part)
+    d_own = jnp.pad(d_conv_half, ((HALO, HALO), (0, 0)))
+    tap_part = tap_grad(plan, ready, d_own, small_part)
     tap_part, first_sum = lax.optimization_barrier((tap_part, first_sum))
     tap_sum = scattered(tap_part)[0].astype(f32)
     kernel_sum = tap_sum[:-EXTRA].reshape(TAPS // devices, CG, HALF)
@@ -822,7 +917,7 @@
     d_window = jnp.concatenate(
         [passed(d_conv_half[rows - HALO :], 1), d_conv_half, passed(d_conv_half[:HALO], -1)], axis=0
     )
-    d_input = conv(plan, d_window, w_kernel, True).astype(bf16)
+    d_input = conv_back(plan, ready, d_window, spread_taps).astype(bf16)
     frames_grad = dx1 + side_by_side(d_input, exchange(d_input), index).astype(f32)
 
     pieces, at = [], 0

time: 705 us -> 680 us (0.965)
  Pallas kernels: 230 us -> 210 us
  waiting for transfers between devices: 143 us -> 155 us
  starting transfers between devices: 108 us -> 99 us
    pallas_call x3 -> x4, Pallas kernels: 127 us -> 107 us  [call(): pl.pallas_call(kernel, grid_spec=pltpu.PrefetchScalarGridSpec(num_scalar_...]
    ppermute x10, waiting for transfers between devices: 23.7 us -> 36.9 us  [chip_along(): lax.ppermute(block, 'seq', [(i, j) for i, j in route if 0 <= j < count])]
    ppermute x4, starting transfers between devices: 26.1 us -> 14.4 us  [passed(): return lax.ppermute(block, 'seq', route)]
    ppermute x11, waiting for transfers between devices: 67.7 us -> 77.4 us  [exchange(): return lax.ppermute(part, 'heads', [(0, 1), (1, 0)])]
    ppermute x10, starting transfers between devices: 42.6 us -> 51.4 us  [chip_along(): lax.ppermute(block, 'seq', [(i, j) for i, j in route if 0 <= j < count])]
    unnamed x231 -> x223, local copies, waits for them, and re-layouts: 19.9 us -> 20 us
  transfers between devices with their start and end apart: 41 -> 41, of which waited for: 16 -> 15; matrix products, arithmetic and copies ran while one was open for 19% -> 18% of each run, Pallas kernels for 33% -> 31%
where the time goes in v4:
time: 680 us; the launch traced here: 673 us
  Pallas kernels  210 us (31%)
  waiting for transfers between devices  155 us (23%)
  starting transfers between devices  99 us (15%)
  other arithmetic  75.1 us (11%)
  matrix products  57 us (8%)
  local copies, waits for them, and re-layouts  35.2 us (5%)
  blocking collectives  23.2 us (3%)
  between operations  18.8 us (3%)
    pallas_call x4, Pallas kernels, call(): pl.pallas_call(kernel, grid_spec=pltpu.PrefetchScalarGridSpec(num_scalar_...  107 us
    ppermute x11, waiting for transfers between devices, exchange(): return lax.ppermute(part, 'heads', [(0, 1), (1, 0)])  77.4 us
    dot_general x19, matrix products, dot(): lax.dot_general(a, b, (((ca,), (cb,)), ((), ())), preferred_element_type=...  57 us
    pallas_call x3, Pallas kernels, attend_back(): pl.pallas_call(backward_kernel, grid=(ROWS // QT,), out_shape=(jax.ShapeD...  55.9 us
    ppermute x10, starting transfers between devices, chip_along(): lax.ppermute(block, 'seq', [(i, j) for i, j in route if 0 <= j < count])  51.4 us
    pallas_call x3, Pallas kernels, attend(): pl.pallas_call(forward_kernel, grid=(ROWS // QT,), out_shape=(jax.ShapeDt...  46.9 us
    ppermute x10, waiting for transfers between devices, chip_along(): lax.ppermute(block, 'seq', [(i, j) for i, j in route if 0 <= j < count])  36.9 us
    reduce_scatter x3, waiting for transfers between devices, scattered(): return lax.psum_scatter(whole_sum, 'seq', scatter_dimension=0, tiled=True)  29.5 us
  transfers between devices with their start and end apart: 41, of which 15 were waited for; matrix products, arithmetic and copies ran while one was open for 18% of the time, Pallas kernels for 31%

profile of v4, /device:TPU:0, one launch (start us, length us, event | category | flops | bytes accessed | tf_op | source)
XLA Modules:
  0.0 673.0 jit_solution(8764345756012925784)
XLA Ops:
  14.0 3.0 collective-permute-start
  18.4 23.2 %all-gather = bf16[16,1,552]{2,1,0:T(2,128)(2,1)S(1)} all-gather(bf16[1,1,552]{2,1,0:T(2,128)(2,1)S(1)} %maximum_bitcast_fusion.2), channel_id=1, replica_groups=mesh['seq'=16,'heads'=2] {'seq'}, dimensions={0}, use_global_device_ids=true | all-gather | bytes 18768 | tf_op jit(solution)/shard_map/all_gather | solution.py:665
  50.2 13.2 %conv_prepare.1 = (bf16[2,4,304,1152]{3,2,1,0:T(8,128)(2,1)}, bf16[2,1024,1088]{2,1,0:T(8,128)(2,1)}, bf16[2,33,272,128]{3,2,1,0:T(8,128)(2,1)}, bf16[2,33,304,1...) custom-call(s32[1]{0:T(128)} %bitcast.1.n_ref, ...), custom_call_target="tpu_custom_call" | custom-call | flops 10000000000 | bytes 15000000 | tf_op jit(solution)/shard_map/conv_prepare/pallas_call | solution.py:137
  63.4 3.8 all-gather.5.cloned.1.call-done.refs_3_
  67.1 28.2 %conv_forward.1 = (f32[1024,384]{1,0:T(8,128)}, bf16[8,134,64,128]{3,2,1,0:T(8,128)(2,1)}) custom-call(s32[1]{0:T(128)} %bitcast.1.n_ref, bf16[2,8,304,256]{3,2,1,0:T(8,128)(2,1)} %get-tuple-element.103.refs_0_, bf16[2,33,272,128]{3,2,1,0:T(8,128)(2,1)} %get-tuple-element.104.refs_1_.refs_0_, bf16[2,1024,1088]{2,1,0:T(8,128)(2,1)} %get-tuple-element.105.refs_2_.refs_1_, ...), custom_call_target="tpu_custom_call" | custom-call | flops 24999999488 | bytes 15000000 | tf_op jit(solution)/shard_map/conv_forward/pallas_call | solution.py:137
  95.3 5.7 multiply_convert_fusion.2
  103.7 7.2 %all-gather.7.cloned.1.call-done = bf16[768,1536]{1,0:T(8,128)(2,1)} async-done(((bf16[48,1536]{1,0:T(8,128)(2,1)}), bf16[768,1536]{1,0:T(8,128)(2,1)}) %all-gather.7.cloned.1.call-update) | async-done | bytes 2359312 | tf_op jit(solution)/shard_map/all_gather | solution.py:665
  113.6 8.2 %collective-permute-done.2 = bf16[1024,384]{1,0:T(8,128)(2,1)} collective-permute-done((bf16[1024,384]{1,0:T(8,128)(2,1)}, bf16[1024,384]{1,0:T(8,128)(2,1)}, u32[]{:S(2)}, u32[]{:S(2)}) %collective-permute-start.2) | collective-permute-done | bytes 786464 | tf_op jit(solution)/shard_map/ppermute | solution.py:605
  131.1 18.3 %collective-permute-start.6 = (bf16[512,256]{1,0:T(8,128)(2,1)S(1)}, bf16[512,256]{1,0:T(8,128)(2,1)S(1)}, u32[]{:S(2)}, u32[]{:S(2)}) collective-permute-start(bf16[512,256]{1,0:T(8,128)(2,1)S(1)} %get-tuple-element.273), channel_id=1, source_target_pairs={{0,4},{4,8},{6,2},{8,12},{10,6},{12,16},{14,10},{16,20},{18,14},{2... | collective-permute-start | bytes 786440 | tf_op jit(solution)/shard_map/ppermute | solution.py:640
  151.8 15.5 %collective-permute-done.6.k3 = bf16[512,256]{1,0:T(8,128)(2,1)S(1)} collective-permute-done((bf16[512,256]{1,0:T(8,128)(2,1)S(1)}, bf16[512,256]{1,0:T(8,128)(2,1)S(1)}, u32[]{:S(2)}, u32[]{:S(2)}) %collective-permute-start.6) | collective-permute-done | bytes 262176 | tf_op jit(solution)/shard_map/ppermute | solution.py:640
  170.5 4.5 collective-permute-start.10
  176.9 2.9 broadcast_in_dim.168.kseg_ref
  179.8 15.7 %attention_forward.3 = (f32[1024,128]{1,0:T(8,128)}, bf16[1024,128]{1,0:T(8,128)(2,1)}, f32[8,1024]{1,0:T(8,128)}) custom-call(s32[3,8]{1,0:T(4,128)} %add_add_fusion.10.range_ref, s32[8,1024]{1,0:T(8,128)} %broadcast_in_dim.167.qseg_ref, s32[4096,128]{1,0:T(8,128)} %broadcast_in_dim.168.kseg_ref, bf16[1024,384]{1,0:T(8,128)(2,1)} %fusion.17.q_ref, ...), custom_call_target="tpu_custom_call" | custom-call | flops 8000000000 | bytes 8000000 | tf_op jit(solution)/shard_map/attention_forward/pallas_call | solution.py:489
  197.2 4.9 collective-permute-done.12
  202.1 7.5 %collective-permute-done.10.k3 = bf16[512,512]{1,0:T(8,128)(2,1)S(1)} collective-permute-done((bf16[512,512]{1,0:T(8,128)(2,1)S(1)}, bf16[512,512]{1,0:T(8,128)(2,1)S(1)}, u32[]{:S(2)}, u32[]{:S(2)}) %collective-permute-start.10) | collective-permute-done | bytes 524320 | tf_op jit(solution)/shard_map/ppermute | solution.py:640
  210.4 15.6 %attention_forward.4 = (f32[1024,128]{1,0:T(8,128)}, bf16[1024,128]{1,0:T(8,128)(2,1)}, f32[8,1024]{1,0:T(8,128)}) custom-call(s32[3,8]{1,0:T(4,128)} %add_add_fusion.10.range_ref, s32[8,1024]{1,0:T(8,128)} %broadcast_in_dim.167.qseg_ref, s32[4096,128]{1,0:T(8,128)} %broadcast_in_dim.168.kseg_ref, bf16[1024,384]{1,0:T(8,128)(2,1)} %fusion.17.q_ref, ...), custom_call_target="tpu_custom_call" | custom-call | flops 8000000000 | bytes 8000000 | tf_op jit(solution)/shard_map/attention_forward/pallas_call | solution.py:489
  227.6 15.6 %attention_forward.5 = (f32[1024,128]{1,0:T(8,128)}, bf16[1024,128]{1,0:T(8,128)(2,1)}, f32[8,1024]{1,0:T(8,128)}) custom-call(s32[3,8]{1,0:T(4,128)} %add_add_fusion.10.range_ref, s32[8,1024]{1,0:T(8,128)} %broadcast_in_dim.167.qseg_ref, s32[4096,128]{1,0:T(8,128)} %broadcast_in_dim.168.kseg_ref, bf16[1024,384]{1,0:T(8,128)(2,1)} %fusion.17.q_ref, ...), custom_call_target="tpu_custom_call" | custom-call | flops 8000000000 | bytes 8000000 | tf_op jit(solution)/shard_map/attention_forward/pallas_call | solution.py:489
  244.2 5.6 collective-permute-done.14
  255.3 9.7 %multiply_convert_fusion.1 = (bf16[512,1536]{1,0:T(8,128)(2,1)S(1)}, f32[512,1536]{1,0:T(8,128)S(1)}, f32[512,1536]{1,0:T(8,128)S(1)}) fusion(f32[1536]{0:T(1024)S(1)} %reshape.761, bf16[768,3072]{1,0:T(8,128)(2,1)} %all-gather.9.cloned.1.call-done, f32[512,768]{1,0:T(8,128)S(1)} %get-tuple-element.303, f32[768]{0:T(1024)S(1)} %get-tuple-element.181, ...), kind=kOutput, calls=%fused_computation.34 | convolution fusion | flops 1261830144 | bytes 11812864 | tf_op jit(solution)/shard_map/dot_general | solution.py:661
  267.4 8.0 %multiply_convert_fusion = (bf16[512,1536]{1,0:T(8,128)(2,1)S(1)}, f32[512,1536]{1,0:T(8,128)S(1)}, f32[512,1536]{1,0:T(8,128)S(1)}) fusion(f32[1536]{0:T(1024)S(1)} %reshape.761, bf16[768,3072]{1,0:T(8,128)(2,1)S(1)} %copy-done.89, f32[512,768]{1,0:T(8,128)S(1)} %get-tuple-element.300, f32[512]{0:T(512)S(1)} %fusion.91, ...), kind=kOutput, calls=%fused_computation.21 | convolution fusion | flops 1261830144 | bytes 11816960 | tf_op jit(solution)/shard_map/dot_general | solution.py:661
  283.3 2.8 fusion.138
  292.1 5.3 collective-permute-done.16
  300.9 2.8 fusion.139
  313.5 17.7 %collective-permute-done.18 = bf16[512,768]{1,0:T(8,128)(2,1)} collective-permute-done((bf16[512,768]{1,0:T(8,128)(2,1)}, bf16[512,768]{1,0:T(8,128)(2,1)}, u32[]{:S(2)}, u32[]{:S(2)}) %collective-permute-start.18) | collective-permute-done | bytes 786464 | tf_op jit(solution)/shard_map/ppermute | solution.py:605
  331.2 2.9 multiply_reduce_fusion.5
  334.1 2.8 multiply_reduce_fusion.6
  337.9 3.4 convolution_convert_fusion.2.do_ref
  341.7 18.4 %attention_backward.3 = (bf16[1024,128]{1,0:T(8,128)(2,1)}, f32[1024,256]{1,0:T(8,128)}, bf16[1024,256]{1,0:T(8,128)(2,1)}, bf16[1024,256]{1,0:T(8,128)(2,1)}, b...) custom-call(s32[3,8]{1,0:T(4,128)} %add_add_fusion.10.range_ref, s32[8,1024]{1,0:T(8,128)} %broadcast_in_dim.167.qseg_ref, ...), custom_call_target="tpu_custom_call" | custom-call | flops 8000000000 | bytes 12000000 | tf_op jit(solution)/shard_map/attention_backward/pallas_call | solution.py:572
  360.2 8.1 %collective-permute-start.19 = (bf16[1024,256]{1,0:T(8,128)(2,1)}, bf16[1024,256]{1,0:T(8,128)(2,1)}, u32[]{:S(2)}, u32[]{:S(2)}) collective-permute-start(bf16[1024,256]{1,0:T(8,128)(2,1)} %get-tuple-element.127), channel_id=1, source_target_pairs={{0,2},{2,0},{4,6},{6,4},{8,10},{10,8},{12,14},{14,12},{16,18},{18,... | collective-permute-start | bytes 1572872 | tf_op jit(solution)/shard_map/ppermute | solution.py:628
  369.7 8.0 %collective-permute-start.22 = (bf16[512,256]{1,0:T(8,128)(2,1)}, bf16[512,256]{1,0:T(8,128)(2,1)}, u32[]{:S(2)}, u32[]{:S(2)}) collective-permute-start(bf16[512,256]{1,0:T(8,128)(2,1)} %get-tuple-element.137), channel_id=1, source_target_pairs={{0,4},{4,8},{6,2},{8,12},{10,6},{12,16},{14,10},{16,20},{18,14},{2... | collective-permute-start | bytes 786440 | tf_op jit(solution)/shard_map/ppermute | solution.py:640
  379.0 18.9 %attention_backward.4 = (bf16[1024,128]{1,0:T(8,128)(2,1)}, f32[1024,256]{1,0:T(8,128)}, bf16[1024,256]{1,0:T(8,128)(2,1)}, bf16[1024,256]{1,0:T(8,128)(2,1)}, b...) custom-call(s32[3,8]{1,0:T(4,128)} %add_add_fusion.10.range_ref, s32[8,1024]{1,0:T(8,128)} %broadcast_in_dim.167.qseg_ref, ...), custom_call_target="tpu_custom_call" | custom-call | flops 8000000000 | bytes 12000000 | tf_op jit(solution)/shard_map/attention_backward/pallas_call | solution.py:572
  398.0 5.6 collective-permute-start.26
  409.4 10.4 %collective-permute-done.26 = bf16[512,256]{1,0:T(8,128)(2,1)} collective-permute-done((bf16[512,256]{1,0:T(8,128)(2,1)}, bf16[512,256]{1,0:T(8,128)(2,1)}, u32[]{:S(2)}, u32[]{:S(2)}) %collective-permute-start.26) | collective-permute-done | bytes 262176 | tf_op jit(solution)/shard_map/ppermute | solution.py:640
  423.4 18.5 %attention_backward.5 = (bf16[1024,128]{1,0:T(8,128)(2,1)}, f32[1024,256]{1,0:T(8,128)}, bf16[1024,256]{1,0:T(8,128)(2,1)}, bf16[1024,256]{1,0:T(8,128)(2,1)}, b...) custom-call(s32[3,8]{1,0:T(4,128)} %add_add_fusion.10.range_ref, s32[8,1024]{1,0:T(8,128)} %broadcast_in_dim.167.qseg_ref, ...), custom_call_target="tpu_custom_call" | custom-call | flops 8000000000 | bytes 12000000 | tf_op jit(solution)/shard_map/attention_backward/pallas_call | solution.py:572
  441.9 8.6 %collective-permute-start.30 = (bf16[512,256]{1,0:T(8,128)(2,1)}, bf16[512,256]{1,0:T(8,128)(2,1)S(1)}, u32[]{:S(2)}, u32[]{:S(2)}) collective-permute-start(bf16[512,256]{1,0:T(8,128)(2,1)} %get-tuple-element.147), channel_id=1, source_target_pairs={{0,4},{4,8},{6,2},{8,12},{10,6},{12,16},{14,10},{16,20},{18,14},{2... | collective-permute-start | bytes 786440 | tf_op jit(solution)/shard_map/ppermute | solution.py:640
  454.2 2.9 constant_dynamic-update-slice_fusion.22
  457.0 4.0 collective-permute-start.27
  463.3 3.5 collective-permute-done.30
  469.0 5.1 convolution_convert_fusion.1
  476.2 3.0 convolution_convert_fusion.3
  481.5 4.2 convolution_convert_fusion
  487.4 19.7 %collective-permute-done.31 = bf16[1024,768]{1,0:T(8,128)(2,1)} collective-permute-done((bf16[1024,768]{1,0:T(8,128)(2,1)}, bf16[1024,768]{1,0:T(8,128)(2,1)}, u32[]{:S(2)}, u32[]{:S(2)}) %collective-permute-start.31) | collective-permute-done | bytes 1572896 | tf_op jit(solution)/shard_map/ppermute | solution.py:605
  507.1 4.4 multiply_reduce_fusion
  518.1 8.8 %collective-permute-start.32 = (bf16[64,384]{1,0:T(8,128)(2,1)S(1)}, bf16[64,384]{1,0:T(8,128)(2,1)S(1)}, u32[]{:S(2)}, u32[]{:S(2)}) collective-permute-start(bf16[64,384]{1,0:T(8,128)(2,1)S(1)} %get-tuple-element.276), channel_id=1, source_target_pairs={{0,2},{2,4},{4,6},{6,8},{8,10},{10,12},{12,14},{14,16},{16,18},{18... | collective-permute-start | bytes 147464 | tf_op jit(solution)/shard_map/ppermute | solution.py:624
  529.7 39.0 %tap_gradient.1 = bf16[16,400,384]{2,1,0:T(8,128)(2,1)} custom-call(s32[1]{0:T(128)} %bitcast.1.n_ref, bf16[2,8,256,304]{3,2,1,0:T(8,128)(2,1)} %get-tuple-element.152.xt_ref, bf16[2,4,304,1152]{3,2,1,0:T(8,128)(2,1)} %get-tuple-element.150.s_ref, bf16[2,33,304,128]{3,2,1,0:T(8,128)(2,1)} %get-tuple-element.153.mask_ref, ...), custom_call_target="tpu_custom_call" | custom-call | flops 1000000000 | bytes 15000000 | tf_op jit(solution)/shard_map/tap_gradient/pallas_call | solution.py:137
  575.7 26.7 %conv_back.1 = f32[1024,384]{1,0:T(8,128)} custom-call(s32[1]{0:T(128)} %bitcast.1.n_ref, bf16[1152,384]{1,0:T(8,128)(2,1)} %get-tuple-element.275.d_ref, bf16[2,4,304,1152]{3,2,1,0:T(8,128)(2,1)} %get-tuple-element.150.s_ref, bf16[2,33,272,128]{3,2,1,0:T(8,128)(2,1)} %get-tuple-element.104.refs_1_.refs_0_, ...), custom_call_target="tpu_custom_call" | custom-call | flops 24999999488 | bytes 15000000 | tf_op jit(solution)/shard_map/conv_back/pallas_call | solution.py:137
  606.0 15.6 %collective-permute-done.34 = bf16[1024,384]{1,0:T(8,128)(2,1)S(1)} collective-permute-done((bf16[1024,384]{1,0:T(8,128)(2,1)S(1)}, bf16[1024,384]{1,0:T(8,128)(2,1)S(1)}, u32[]{:S(2)}, u32[]{:S(2)}) %collective-permute-start.34) | collective-permute-done | bytes 786464 | tf_op jit(solution)/shard_map/ppermute | solution.py:605
  627.4 29.5 %reduce-scatter.8.cloned.1.call-done = bf16[1,400,384]{2,1,0:T(8,128)(2,1)} async-done(((bf16[16,400,384]{2,1,0:T(8,128)(2,1)}), bf16[1,400,384]{2,1,0:T(8,128)(2,1)}) %reduce-scatter.8.cloned.1.call-update) | async-done | bytes 307216 | tf_op jit(solution)/shard_map/reduce_scatter | solution.py:669
  (484 shorter events, 137.4 us)
Async XLA Ops:
  7.2 59.9 %all-gather.5.cloned.1.call-start = ((), (), s32[]{:S(2)}) async-start(), calls=%async_computation.3 | async-start | bytes 5013504 | tf_op jit(solution)/shard_map/all_gather | solution.py:665
  9.2 101.7 %all-gather.7.cloned.1.call-start = ((), (), s32[]{:S(2)}) async-start(), calls=%async_computation.4 | async-start | bytes 2506752 | tf_op jit(solution)/shard_map/all_gather | solution.py:665
  11.1 244.2 %all-gather.9.cloned.1.call-start = ((), (), s32[]{:S(2)}) async-start(), calls=%async_computation.5 | async-start | bytes 5013504 | tf_op jit(solution)/shard_map/all_gather | solution.py:665
  12.7 34.0 %collective-permute-start.1 = (bf16[64,384]{1,0:T(8,128)(2,1)S(1)}, bf16[64,384]{1,0:T(8,128)(2,1)S(1)}, u32[]{:S(2)}, u32[]{:S(2)}) collective-permute-start(bf16[64,384]{1,0:T(8,128)(2,1)S(1)} %get-tuple-element.279), channel_id=1, source_target_pairs={{2,0},{4,2},{6,4},{8,6},{10,8},{12,10},{14,12},{16,14},{18,16},{20... | collective-permute-start | bytes 147464 | tf_op jit(solution)/shard_map/ppermute | solution.py:624
  14.0 32.7 %collective-permute-start = (bf16[64,384]{1,0:T(8,128)(2,1)S(1)}, bf16[64,384]{1,0:T(8,128)(2,1)S(1)}, u32[]{:S(2)}, u32[]{:S(2)}) collective-permute-start(bf16[64,384]{1,0:T(8,128)(2,1)S(1)} %get-tuple-element.278), channel_id=1, source_target_pairs={{0,2},{2,4},{4,6},{6,8},{8,10},{10,12},{12,14},{14,16},{16,18},{18... | collective-permute-start | bytes 147464 | tf_op jit(solution)/shard_map/ppermute | solution.py:624
  17.9 456.3 %reduce-scatter.4.cloned.1.call-start = ((), (), s32[]{:S(2)}) async-start(), calls=%async_computation.6 | async-start | bytes 5013504 | tf_op jit(solution)/shard_map/reduce_scatter | solution.py:669
  46.2 49.2 %copy-start.65 = (f32[384]{0:T(512)}, f32[384]{0:T(512)S(1)}, u32[]{:S(2)}) copy-start(f32[384]{0:T(512)S(1)} %add.611) | copy-start | bytes 4612
  101.1 20.7 %collective-permute-start.2 = (bf16[1024,384]{1,0:T(8,128)(2,1)}, bf16[1024,384]{1,0:T(8,128)(2,1)}, u32[]{:S(2)}, u32[]{:S(2)}) collective-permute-start(bf16[1024,384]{1,0:T(8,128)(2,1)} %get-tuple-element.258), channel_id=1, source_target_pairs={{0,1},{1,0},{2,3},{3,2},{4,5},{5,4},{6,7},{7,6},{8,9},{9,8},{10,11... | collective-permute-start | bytes 2359304 | tf_op jit(solution)/shard_map/ppermute | solution.py:605
  112.0 39.8 %collective-permute-start.3 = (bf16[768,384]{1,0:T(8,128)(2,1)S(1)}, bf16[768,384]{1,0:T(8,128)(2,1)S(1)}, u32[]{:S(2)}, u32[]{:S(2)}) collective-permute-start(bf16[768,384]{1,0:T(8,128)(2,1)S(1)} %slice.303), channel_id=1, source_target_pairs={{0,1},{1,0},{2,3},{3,2},{4,5},{5,4},{6,7},{7,6},{8,9},{9,8},{10,11... | collective-permute-start | bytes 1769480 | tf_op jit(solution)/shard_map/ppermute | solution.py:605
  130.2 40.1 %copy-start.5 = (bf16[1024,768]{1,0:T(8,128)(2,1)}, bf16[1024,768]{1,0:T(8,128)(2,1)S(1)}, u32[]{:S(2)}) copy-start(bf16[1024,768]{1,0:T(8,128)(2,1)S(1)} %fusion.2.k0) | copy-start | bytes 4718596
  130.3 37.0 %collective-permute-start.4 = (bf16[1024,256]{1,0:T(8,128)(2,1)S(1)}, bf16[1024,256]{1,0:T(8,128)(2,1)S(1)}, u32[]{:S(2)}, u32[]{:S(2)}) collective-permute-start(bf16[1024,256]{1,0:T(8,128)(2,1)S(1)} %slice.306), channel_id=1, source_target_pairs={{0,2},{2,0},{4,6},{6,4},{8,10},{10,8},{12,14},{14,12},{16,18},{18,... | collective-permute-start | bytes 1572872 | tf_op jit(solution)/shard_map/ppermute | solution.py:628
  130.4 37.0 %collective-permute-start.5 = (bf16[1024,256]{1,0:T(8,128)(2,1)S(1)}, bf16[1024,256]{1,0:T(8,128)(2,1)S(1)}, u32[]{:S(2)}, u32[]{:S(2)}) collective-permute-start(bf16[1024,256]{1,0:T(8,128)(2,1)S(1)} %slice.306), channel_id=1, source_target_pairs={{2,4},{4,2},{6,8},{8,6},{10,12},{12,10},{14,16},{16,14},{18,20},{2... | collective-permute-start | bytes 1572872 | tf_op jit(solution)/shard_map/ppermute | solution.py:634
  131.1 36.2 %collective-permute-start.6 = (bf16[512,256]{1,0:T(8,128)(2,1)S(1)}, bf16[512,256]{1,0:T(8,128)(2,1)S(1)}, u32[]{:S(2)}, u32[]{:S(2)}) collective-permute-start(bf16[512,256]{1,0:T(8,128)(2,1)S(1)} %get-tuple-element.273), channel_id=1, source_target_pairs={{0,4},{4,8},{6,2},{8,12},{10,6},{12,16},{14,10},{16,20},{18,14},{2... | collective-permute-start | bytes 786440 | tf_op jit(solution)/shard_map/ppermute | solution.py:640
  149.5 17.9 %collective-permute-start.7 = (bf16[512,256]{1,0:T(8,128)(2,1)S(1)}, bf16[512,256]{1,0:T(8,128)(2,1)S(1)}, u32[]{:S(2)}, u32[]{:S(2)}) collective-permute-start(bf16[512,256]{1,0:T(8,128)(2,1)S(1)} %get-tuple-element.272), channel_id=1, source_target_pairs={{2,6},{4,0},{6,10},{8,4},{10,14},{12,8},{14,18},{16,12},{18,22},{2... | collective-permute-start | bytes 786440 | tf_op jit(solution)/shard_map/ppermute | solution.py:640
  167.4 42.2 %collective-permute-start.8 = (bf16[1024,512]{1,0:T(8,128)(2,1)S(1)}, bf16[1024,512]{1,0:T(8,128)(2,1)}, u32[]{:S(2)}, u32[]{:S(2)}) collective-permute-start(bf16[1024,512]{1,0:T(8,128)(2,1)S(1)} %slice.246), channel_id=1, source_target_pairs={{0,2},{2,0},{4,6},{6,4},{8,10},{10,8},{12,14},{14,12},{16,18},{18,... | collective-permute-start | bytes 3145736 | tf_op jit(solution)/shard_map/ppermute | solution.py:628
  168.7 40.9 %collective-permute-start.9 = (bf16[1024,512]{1,0:T(8,128)(2,1)S(1)}, bf16[1024,512]{1,0:T(8,128)(2,1)}, u32[]{:S(2)}, u32[]{:S(2)}) collective-permute-start(bf16[1024,512]{1,0:T(8,128)(2,1)S(1)} %slice.246), channel_id=1, source_target_pairs={{2,4},{4,2},{6,8},{8,6},{10,12},{12,10},{14,16},{16,14},{18,20},{2... | collective-permute-start | bytes 3145736 | tf_op jit(solution)/shard_map/ppermute | solution.py:634
  170.5 39.2 %collective-permute-start.10 = (bf16[512,512]{1,0:T(8,128)(2,1)S(1)}, bf16[512,512]{1,0:T(8,128)(2,1)S(1)}, u32[]{:S(2)}, u32[]{:S(2)}) collective-permute-start(bf16[512,512]{1,0:T(8,128)(2,1)S(1)} %get-tuple-element.271), channel_id=1, source_target_pairs={{0,4},{4,8},{6,2},{8,12},{10,6},{12,16},{14,10},{16,20},{18,14},{2... | collective-permute-start | bytes 1572872 | tf_op jit(solution)/shard_map/ppermute | solution.py:640
  175.0 34.6 %collective-permute-start.11 = (bf16[512,512]{1,0:T(8,128)(2,1)S(1)}, bf16[512,512]{1,0:T(8,128)(2,1)}, u32[]{:S(2)}, u32[]{:S(2)}) collective-permute-start(bf16[512,512]{1,0:T(8,128)(2,1)S(1)} %get-tuple-element.270), channel_id=1, source_target_pairs={{2,6},{4,0},{6,10},{8,4},{10,14},{12,8},{14,18},{16,12},{18,22},{2... | collective-permute-start | bytes 1572872 | tf_op jit(solution)/shard_map/ppermute | solution.py:640
  195.5 6.6 collective-permute-start.12
  226.0 18.1 %collective-permute-start.13 = (bf16[1024,128]{1,0:T(8,128)(2,1)}, bf16[1024,128]{1,0:T(8,128)(2,1)S(1)}, u32[]{:S(2)}, u32[]{:S(2)}) collective-permute-start(bf16[1024,128]{1,0:T(8,128)(2,1)} %get-tuple-element.114), channel_id=1, source_target_pairs={{0,1},{1,0},{2,3},{3,2},{4,5},{5,4},{6,7},{7,6},{8,9},{9,8},{10,11... | collective-permute-start | bytes 786440 | tf_op jit(solution)/shard_map/ppermute | solution.py:605
  243.2 6.6 collective-permute-start.14
  266.4 12.5 %collective-permute-start.15 = (bf16[512,768]{1,0:T(8,128)(2,1)S(1)}, bf16[512,768]{1,0:T(8,128)(2,1)S(1)}, u32[]{:S(2)}, u32[]{:S(2)}) collective-permute-start(bf16[512,768]{1,0:T(8,128)(2,1)S(1)} %fusion.51), channel_id=1, source_target_pairs={{0,1},{1,0},{2,3},{3,2},{4,5},{5,4},{6,7},{7,6},{8,9},{9,8},{10,11... | collective-permute-start | bytes 2359304 | tf_op jit(solution)/shard_map/ppermute | solution.py:605
  276.8 20.5 %collective-permute-start.16 = (bf16[512,768]{1,0:T(8,128)(2,1)S(1)}, bf16[512,768]{1,0:T(8,128)(2,1)S(1)}, u32[]{:S(2)}, u32[]{:S(2)}) collective-permute-start(bf16[512,768]{1,0:T(8,128)(2,1)S(1)} %fusion.54), channel_id=1, source_target_pairs={{0,1},{1,0},{2,3},{3,2},{4,5},{5,4},{6,7},{7,6},{8,9},{9,8},{10,11... | collective-permute-start | bytes 2359304 | tf_op jit(solution)/shard_map/ppermute | solution.py:605
  288.4 45.7 %collective-permute-start.17 = (bf16[512,768]{1,0:T(8,128)(2,1)}, bf16[512,768]{1,0:T(8,128)(2,1)}, u32[]{:S(2)}, u32[]{:S(2)}) collective-permute-start(bf16[512,768]{1,0:T(8,128)(2,1)} %fusion.45), channel_id=1, source_target_pairs={{0,1},{1,0},{2,3},{3,2},{4,5},{5,4},{6,7},{7,6},{8,9},{9,8},{10,11... | collective-permute-start | bytes 2359304 | tf_op jit(solution)/shard_map/ppermute | solution.py:605
  306.0 25.2 %collective-permute-start.18 = (bf16[512,768]{1,0:T(8,128)(2,1)}, bf16[512,768]{1,0:T(8,128)(2,1)}, u32[]{:S(2)}, u32[]{:S(2)}) collective-permute-start(bf16[512,768]{1,0:T(8,128)(2,1)} %fusion.48), channel_id=1, source_target_pairs={{0,1},{1,0},{2,3},{3,2},{4,5},{5,4},{6,7},{7,6},{8,9},{9,8},{10,11... | collective-permute-start | bytes 2359304 | tf_op jit(solution)/shard_map/ppermute | solution.py:605
  337.9 138.3 %copy-start.13 = (f32[512,768]{1,0:T(8,128)}, f32[512,768]{1,0:T(8,128)S(1)}, u32[]{:S(2)}) copy-start(f32[512,768]{1,0:T(8,128)S(1)} %get-tuple-element.226) | copy-start | bytes 4718596
  337.9 138.3 %copy-start.14 = (f32[512,768]{1,0:T(8,128)}, f32[512,768]{1,0:T(8,128)S(1)}, u32[]{:S(2)}) copy-start(f32[512,768]{1,0:T(8,128)S(1)} %get-tuple-element.310) | copy-start | bytes 4718596
  341.4 227.3 %reduce-scatter.6.cloned.1.call-start = ((), (), s32[]{:S(2)}) async-start(), calls=%async_computation.7 | async-start | bytes 2506752 | tf_op jit(solution)/shard_map/reduce_scatter | solution.py:669
  360.2 63.2 %collective-permute-start.19 = (bf16[1024,256]{1,0:T(8,128)(2,1)}, bf16[1024,256]{1,0:T(8,128)(2,1)}, u32[]{:S(2)}, u32[]{:S(2)}) collective-permute-start(bf16[1024,256]{1,0:T(8,128)(2,1)} %get-tuple-element.127), channel_id=1, source_target_pairs={{0,2},{2,0},{4,6},{6,4},{8,10},{10,8},{12,14},{14,12},{16,18},{18,... | collective-permute-start | bytes 1572872 | tf_op jit(solution)/shard_map/ppermute | solution.py:628
  368.3 55.1 %collective-permute-start.20 = (bf16[1024,256]{1,0:T(8,128)(2,1)}, bf16[1024,256]{1,0:T(8,128)(2,1)}, u32[]{:S(2)}, u32[]{:S(2)}) collective-permute-start(bf16[1024,256]{1,0:T(8,128)(2,1)} %get-tuple-element.128), channel_id=1, source_target_pairs={{2,4},{4,2},{6,8},{8,6},{10,12},{12,10},{14,16},{16,14},{18,20},{2... | collective-permute-start | bytes 1572872 | tf_op jit(solution)/shard_map/ppermute | solution.py:634
  369.7 36.6 %collective-permute-start.22 = (bf16[512,256]{1,0:T(8,128)(2,1)}, bf16[512,256]{1,0:T(8,128)(2,1)}, u32[]{:S(2)}, u32[]{:S(2)}) collective-permute-start(bf16[512,256]{1,0:T(8,128)(2,1)} %get-tuple-element.137), channel_id=1, source_target_pairs={{0,4},{4,8},{6,2},{8,12},{10,6},{12,16},{14,10},{16,20},{18,14},{2... | collective-permute-start | bytes 786440 | tf_op jit(solution)/shard_map/ppermute | solution.py:640
  377.7 29.9 %collective-permute-start.21 = (bf16[512,256]{1,0:T(8,128)(2,1)}, bf16[512,256]{1,0:T(8,128)(2,1)}, u32[]{:S(2)}, u32[]{:S(2)}) collective-permute-start(bf16[512,256]{1,0:T(8,128)(2,1)} %get-tuple-element.136), channel_id=1, source_target_pairs={{2,6},{4,0},{6,10},{8,4},{10,14},{12,8},{14,18},{16,12},{18,22},{2... | collective-permute-start | bytes 786440 | tf_op jit(solution)/shard_map/ppermute | solution.py:640
  398.0 21.8 %collective-permute-start.26 = (bf16[512,256]{1,0:T(8,128)(2,1)}, bf16[512,256]{1,0:T(8,128)(2,1)}, u32[]{:S(2)}, u32[]{:S(2)}) collective-permute-start(bf16[512,256]{1,0:T(8,128)(2,1)} %get-tuple-element.142), channel_id=1, source_target_pairs={{0,4},{4,8},{6,2},{8,12},{10,6},{12,16},{14,10},{16,20},{18,14},{2... | collective-permute-start | bytes 786440 | tf_op jit(solution)/shard_map/ppermute | solution.py:640
  406.3 16.0 %collective-permute-start.25 = (bf16[512,256]{1,0:T(8,128)(2,1)}, bf16[512,256]{1,0:T(8,128)(2,1)S(1)}, u32[]{:S(2)}, u32[]{:S(2)}) collective-permute-start(bf16[512,256]{1,0:T(8,128)(2,1)} %get-tuple-element.141), channel_id=1, source_target_pairs={{2,6},{4,0},{6,10},{8,4},{10,14},{12,8},{14,18},{16,12},{18,22},{2... | collective-permute-start | bytes 786440 | tf_op jit(solution)/shard_map/ppermute | solution.py:640
  407.6 49.4 %collective-permute-start.24 = (bf16[1024,256]{1,0:T(8,128)(2,1)}, bf16[1024,256]{1,0:T(8,128)(2,1)S(1)}, u32[]{:S(2)}, u32[]{:S(2)}) collective-permute-start(bf16[1024,256]{1,0:T(8,128)(2,1)} %get-tuple-element.140), channel_id=1, source_target_pairs={{2,4},{4,2},{6,8},{8,6},{10,12},{12,10},{14,16},{16,14},{18,20},{2... | collective-permute-start | bytes 1572872 | tf_op jit(solution)/shard_map/ppermute | solution.py:634
  419.8 41.2 %collective-permute-start.23 = (bf16[1024,256]{1,0:T(8,128)(2,1)}, bf16[1024,256]{1,0:T(8,128)(2,1)}, u32[]{:S(2)}, u32[]{:S(2)}) collective-permute-start(bf16[1024,256]{1,0:T(8,128)(2,1)} %get-tuple-element.139), channel_id=1, source_target_pairs={{0,2},{2,0},{4,6},{6,4},{8,10},{10,8},{12,14},{14,12},{16,18},{18,... | collective-permute-start | bytes 1572872 | tf_op jit(solution)/shard_map/ppermute | solution.py:628
  441.9 25.0 %collective-permute-start.30 = (bf16[512,256]{1,0:T(8,128)(2,1)}, bf16[512,256]{1,0:T(8,128)(2,1)S(1)}, u32[]{:S(2)}, u32[]{:S(2)}) collective-permute-start(bf16[512,256]{1,0:T(8,128)(2,1)} %get-tuple-element.147), channel_id=1, source_target_pairs={{0,4},{4,8},{6,2},{8,12},{10,6},{12,16},{14,10},{16,20},{18,14},{2... | collective-permute-start | bytes 786440 | tf_op jit(solution)/shard_map/ppermute | solution.py:640
  450.5 16.4 %collective-permute-start.29 = (bf16[512,256]{1,0:T(8,128)(2,1)}, bf16[512,256]{1,0:T(8,128)(2,1)S(1)}, u32[]{:S(2)}, u32[]{:S(2)}) collective-permute-start(bf16[512,256]{1,0:T(8,128)(2,1)} %get-tuple-element.146), channel_id=1, source_target_pairs={{2,6},{4,0},{6,10},{8,4},{10,14},{12,8},{14,18},{16,12},{18,22},{2... | collective-permute-start | bytes 786440 | tf_op jit(solution)/shard_map/ppermute | solution.py:640
  451.8 15.2 %collective-permute-start.28 = (bf16[1024,256]{1,0:T(8,128)(2,1)}, bf16[1024,256]{1,0:T(8,128)(2,1)S(1)}, u32[]{:S(2)}, u32[]{:S(2)}) collective-permute-start(bf16[1024,256]{1,0:T(8,128)(2,1)} %get-tuple-element.145), channel_id=1, source_target_pairs={{2,4},{4,2},{6,8},{8,6},{10,12},{12,10},{14,16},{16,14},{18,20},{2... | collective-permute-start | bytes 1572872 | tf_op jit(solution)/shard_map/ppermute | solution.py:634
  457.0 9.9 %collective-permute-start.27 = (bf16[1024,256]{1,0:T(8,128)(2,1)S(1)}, bf16[1024,256]{1,0:T(8,128)(2,1)S(1)}, u32[]{:S(2)}, u32[]{:S(2)}) collective-permute-start(bf16[1024,256]{1,0:T(8,128)(2,1)S(1)} %copy-done.95), channel_id=1, source_target_pairs={{0,2},{2,0},{4,6},{6,4},{8,10},{10,8},{12,14},{14,12},{16,18},{18,... | collective-permute-start | bytes 1572872 | tf_op jit(solution)/shard_map/ppermute | solution.py:628
  476.0 31.1 %collective-permute-start.31 = (bf16[1024,768]{1,0:T(8,128)(2,1)}, bf16[1024,768]{1,0:T(8,128)(2,1)}, u32[]{:S(2)}, u32[]{:S(2)}) collective-permute-start(bf16[1024,768]{1,0:T(8,128)(2,1)} %convolution_convert_fusion.1), channel_id=1, source_target_pairs={{0,1},{1,0},{2,3},{3,2},{4,5},{5,4},{6,7},{7,6},{8,9},{9,8},{10,11... | collective-permute-start | bytes 4718600 | tf_op jit(solution)/shard_map/ppermute | solution.py:605
  487.3 169.5 %reduce-scatter.8.cloned.1.call-start = ((), (), s32[]{:S(2)}) async-start(), calls=%async_computation.8 | async-start | bytes 5222400 | tf_op jit(solution)/shard_map/reduce_scatter | solution.py:669
  516.8 11.5 %collective-permute-start.33 = (bf16[64,384]{1,0:T(8,128)(2,1)S(1)}, bf16[64,384]{1,0:T(8,128)(2,1)S(1)}, u32[]{:S(2)}, u32[]{:S(2)}) collective-permute-start(bf16[64,384]{1,0:T(8,128)(2,1)S(1)} %get-tuple-element.277), channel_id=1, source_target_pairs={{2,0},{4,2},{6,4},{8,6},{10,8},{12,10},{14,12},{16,14},{18,16},{20... | collective-permute-start | bytes 147464 | tf_op jit(solution)/shard_map/ppermute | solution.py:624
  518.1 10.2 %collective-permute-start.32 = (bf16[64,384]{1,0:T(8,128)(2,1)S(1)}, bf16[64,384]{1,0:T(8,128)(2,1)S(1)}, u32[]{:S(2)}, u32[]{:S(2)}) collective-permute-start(bf16[64,384]{1,0:T(8,128)(2,1)S(1)} %get-tuple-element.276), channel_id=1, source_target_pairs={{0,2},{2,4},{4,6},{6,8},{8,10},{10,12},{12,14},{14,16},{16,18},{18... | collective-permute-start | bytes 147464 | tf_op jit(solution)/shard_map/ppermute | solution.py:624
  604.0 17.6 %collective-permute-start.34 = (bf16[1024,384]{1,0:T(8,128)(2,1)S(1)}, bf16[1024,384]{1,0:T(8,128)(2,1)S(1)}, u32[]{:S(2)}, u32[]{:S(2)}) collective-permute-start(bf16[1024,384]{1,0:T(8,128)(2,1)S(1)} %convert_element_type.283), channel_id=1, source_target_pairs={{0,1},{1,0},{2,3},{3,2},{4,5},{5,4},{6,7},{7,6},{8,9},{9,8},{10,11... | collective-permute-start | bytes 2359304 | tf_op jit(solution)/shard_map/ppermute | solution.py:605
  625.1 34.4 %copy-start.41 = (f32[384,48]{0,1:T(8,128)}, f32[384,48]{0,1:T(8,128)S(1)}, u32[]{:S(2)}) copy-start(f32[384,48]{0,1:T(8,128)S(1)} %get-tuple-element.212) | copy-start | bytes 221188
  625.8 33.7 %copy-start.38 = (f32[384,48,8]{0,2,1:T(8,128)S(1)}, f32[384,48,8]{0,2,1:T(8,128)}, u32[]{:S(2)}) copy-start(f32[384,48,8]{0,2,1:T(8,128)} %param.34) | copy-start | bytes 1769476
  626.6 34.3 %copy-start.33 = (f32[48,3,384]{2,0,1:T(8,128)}, f32[48,3,384]{2,0,1:T(8,128)S(1)}, u32[]{:S(2)}) copy-start(f32[48,3,384]{2,0,1:T(8,128)S(1)} %get-tuple-element.216) | copy-start | bytes 663556
  (92 other events, 768.3 us)
Sparse Core Ops, SparseCore 0:
  10.9 56.1 all-gather.4
  70.0 40.8 all-gather.6
  113.8 67.5 all-gather.8
  341.5 114.2 reduce-scatter.3
  487.4 77.6 reduce-scatter.5
  569.8 87.0 reduce-scatter.7

commit v5 on v4

--- a/solution.py
+++ b/solution.py
@@ -301,7 +301,7 @@
     )
 
 
-def tap_grad_kernel(n_ref, xt_ref, s_ref, mask_ref, d_ref, small_ref, out_ref, dp_ref, acc_ref):
+def tap_grad_kernel(n_ref, xt_ref, s_ref, mask_ref, d_ref, small_ref, out_ref, dp_ref, acc_ref, sum_ref):
     h, c = pl.program_id(0), pl.program_id(1)
     base_tile, lanes = pair_lanes(h)
 
@@ -310,10 +310,6 @@
         out_ref[...] = jnp.zeros_like(out_ref)
         out_ref[:, out_ref.shape[1] - EXTRA :, :] = small_ref[...]
         dp_ref[...] = jnp.zeros_like(dp_ref)
-
-    @pl.when(c == 0)
-    def _():
-        acc_ref[...] = jnp.zeros_like(acc_ref)
 
     @pl.when(c < n_ref[0])
     def _():
@@ -322,12 +318,24 @@
         for g, block in enumerate(build_blocks(s_ref, ddup)):
             dp_ref[g, 32 : 32 + CM, :] = block[16 : 16 + CM]
         for g in range(2):
+            carry = jnp.zeros((128, 128), f32)
             for q in range(NQ):
                 m = mask_ref[0, q]
                 ds = dp_ref[g, 32 - q : 32 - q + XM, :] * jnp.concatenate([m, m], axis=1)
                 part = jnp.dot(xt_ref[0, g], ds, preferred_element_type=f32)
-                acc_ref[g, 4 * q + 2 : 4 * q + 6] += part[:, 0:128].reshape(4, 64, 128)
-                acc_ref[g, 4 * q : 4 * q + 4] += part[:, 128:256].reshape(4, 64, 128)
+                left, right = part[:, 0:128], part[:, 128:256]
+                acc_ref[g, 4 * q : 4 * q + 2] = (right[0:128] + carry).reshape(2, 64, 128)
+                acc_ref[g, 4 * q + 2 : 4 * q + 4] = (left[0:128] + right[128:256]).reshape(2, 64, 128)
+                carry = left[128:256]
+            acc_ref[g, 4 * NQ : 4 * NQ + 2] = carry.reshape(2, 64, 128)
+
+        @pl.when(c > 0)
+        def _():
+            acc_ref[...] += sum_ref[...]
+
+        @pl.when(c < n_ref[0] - 1)
+        def _():
+            sum_ref[...] = acc_ref[...]
 
     @pl.when(c == pl.num_programs(1) - 1)
     def _():
@@ -373,13 +381,14 @@
         [
             pltpu.VMEM((2, 32 + CM + 32, 256), bf16),
             pltpu.VMEM((2, PJ, 64, 128), f32),
+            pltpu.VMEM((2, PJ, 64, 128), f32),
         ],
         1_000_000_000,
         (xt, s, tmask, d_own, small),
     )
 REACH = 1536
 SPAN = ROWS + 2 * REACH
-QT, KT = 128, 1664
+QT_AHEAD, QT_BACK, KT = 512, 256, 1664
 NEAR = REACH - ROWS
 NEG = -1e30
 
@@ -392,19 +401,25 @@
     kseg = segment_count(ends, w)
     kseg = jnp.where(w < 0, -1, kseg)
     qseg = kseg[REACH : REACH + ROWS]
-    edge = qseg.reshape(ROWS // QT, QT)
     n = jnp.arange(starts.shape[0], dtype=i32)
-    head = jnp.sum(jnp.where(n[None] == edge[:, :1], starts[None], 0), axis=1) - (first - REACH)
-    tail = jnp.sum(jnp.where(n[None] == edge[:, -1:], ends[None], 0), axis=1) - (first - REACH)
-    lo = jnp.clip(head // 128, 0, SPAN // 128)
-    hi = jnp.clip((tail + 127) // 128, 1, SPAN // 128)
-    tiles = jnp.maximum((hi - lo + KT // 128 - 1) // (KT // 128), 1)
-    lo = jnp.minimum(lo, SPAN // 128 - tiles * (KT // 128))
+
+    def tiles_of(rows):
+        edge = qseg.reshape(ROWS // rows, rows)
+        head = jnp.sum(jnp.where(n[None] == edge[:, :1], starts[None], 0), axis=1) - (first - REACH)
+        tail = jnp.sum(jnp.where(n[None] == edge[:, -1:], ends[None], 0), axis=1) - (first - REACH)
+        lo = jnp.clip(head // 128, 0, SPAN // 128)
+        hi = jnp.clip((tail + 127) // 128, 1, SPAN // 128)
+        tiles = jnp.maximum((hi - lo + KT // 128 - 1) // (KT // 128), 1)
+        lo = jnp.minimum(lo, SPAN // 128 - tiles * (KT // 128))
+        return jnp.stack([lo, tiles, jnp.full_like(lo, odd)]).astype(i32)
+
     return (
-        jnp.stack([lo, tiles, jnp.full_like(lo, odd)]).astype(i32),
+        tiles_of(QT_AHEAD),
+        tiles_of(QT_BACK),
         jnp.broadcast_to(qseg[None], (8, ROWS)),
         jnp.broadcast_to(kseg[:, None], (SPAN, 128)),
     )
+
 
 def split_heads(a):
     low = iota(a.shape, 1) < 64
@@ -436,7 +451,7 @@
 
 def same_segment(kseg_ref, qseg_ref, at):
     ks = kseg_ref[at, :]
-    ks = jnp.concatenate([ks] * (QT // 128), axis=1) if QT > 128 else ks
+    ks = jnp.concatenate([ks] * (qseg_ref.shape[1] // 128), axis=1)
     return ks == qseg_ref[0:1, :]
 
 
@@ -470,7 +485,7 @@
             out.append((new, l, acc))
         return tuple(out)
 
-    start = (jnp.full((1, QT), NEG, f32), jnp.zeros((1, QT), f32), jnp.zeros((64, QT), f32))
+    start = (jnp.full((1, QT_AHEAD), NEG, f32), jnp.zeros((1, QT_AHEAD), f32), jnp.zeros((64, QT_AHEAD), f32))
     ends = lax.fori_loop(0, count, tile, (start, start))
     o = jnp.concatenate([acc / l for _, l, acc in ends], axis=0).T
     o_ref[...] = o
@@ -485,10 +500,10 @@
 
 
 def attend(plan, h, q, pieces):
-    ranges, qseg, kseg = plan
+    ranges, _, qseg, kseg = plan
     return pl.pallas_call(
         forward_kernel,
-        grid=(ROWS // QT,),
+        grid=(ROWS // QT_AHEAD,),
         out_shape=(
             jax.ShapeDtypeStruct((ROWS, 128), f32),
             jax.ShapeDtypeStruct((ROWS, 128), bf16),
@@ -496,15 +511,15 @@
         ),
         in_specs=[
             pl.BlockSpec(memory_space=pltpu.SMEM),
-            pl.BlockSpec((8, QT), lambda i: (0, i)),
+            pl.BlockSpec((8, QT_AHEAD), lambda i: (0, i)),
             pl.BlockSpec((SPAN, 128), lambda i: (0, 0)),
-            pl.BlockSpec((QT, 128), lambda i: (i, h)),
+            pl.BlockSpec((QT_AHEAD, 128), lambda i: (i, h)),
         ]
         + piece_specs(h, pieces),
         out_specs=(
-            pl.BlockSpec((QT, 128), lambda i: (i, 0)),
-            pl.BlockSpec((QT, 128), lambda i: (i, 0)),
-            pl.BlockSpec((8, QT), lambda i: (0, i)),
+            pl.BlockSpec((QT_AHEAD, 128), lambda i: (i, 0)),
+            pl.BlockSpec((QT_AHEAD, 128), lambda i: (i, 0)),
+            pl.BlockSpec((8, QT_AHEAD), lambda i: (0, i)),
         ),
         scratch_shapes=[pltpu.VMEM((SPAN, 256), bf16), pltpu.VMEM((128, SPAN), bf16)],
         compiler_params=pltpu.CompilerParams(vmem_limit_bytes=VLIM),
@@ -516,7 +531,7 @@
 def backward_kernel(range_ref, qseg_ref, kseg_ref, q_ref, k0, k1, k2, k3, k4, do_ref, o_ref, lse_ref,
                     dq_ref, own_ref, f1, f2, f3, f4, span_ref, kt_ref, dkv_ref):
     qi = pl.program_id(0)
-    last = ROWS // QT - 1
+    last = ROWS // QT_BACK - 1
 
     @pl.when(qi == 0)
     def _():
@@ -553,7 +568,7 @@
         dkv_ref[at, 128:256] += jnp.dot(jnp.concatenate(ps, axis=1), docat, preferred_element_type=f32)
         return tuple(out)
 
-    zero = jnp.zeros((64, QT), f32)
+    zero = jnp.zeros((64, QT_BACK), f32)
     dqt = lax.fori_loop(0, count, tile, (zero, zero))
     dq = jnp.concatenate(dqt, axis=0).T
     dq_ref[...] = dq.astype(bf16) * jnp.asarray(0.125, bf16)
@@ -566,12 +581,12 @@
 
 
 def attend_back(plan, h, q, pieces, d_att, mixed, lse):
-    ranges, qseg, kseg = plan
-    rowspec = pl.BlockSpec((QT, 128), lambda i: (i, 0))
-    colspec = pl.BlockSpec((QT, 128), lambda i: (i, h))
+    _, ranges, qseg, kseg = plan
+    rowspec = pl.BlockSpec((QT_BACK, 128), lambda i: (i, 0))
+    colspec = pl.BlockSpec((QT_BACK, 128), lambda i: (i, h))
     return pl.pallas_call(
         backward_kernel,
-        grid=(ROWS // QT,),
+        grid=(ROWS // QT_BACK,),
         out_shape=(
             jax.ShapeDtypeStruct((ROWS, 128), bf16),
             jax.ShapeDtypeStruct((ROWS, 256), f32),
@@ -579,12 +594,12 @@
         + tuple(jax.ShapeDtypeStruct((n, 256), bf16) for n in (ROWS, ROWS, NEAR, NEAR)),
         in_specs=[
             pl.BlockSpec(memory_space=pltpu.SMEM),
-            pl.BlockSpec((8, QT), lambda i: (0, i)),
+            pl.BlockSpec((8, QT_BACK), lambda i: (0, i)),
             pl.BlockSpec((SPAN, 128), lambda i: (0, 0)),
             colspec,
         ]
         + piece_specs(h, pieces)
-        + [colspec, rowspec, pl.BlockSpec((8, QT), lambda i: (0, i))],
+        + [colspec, rowspec, pl.BlockSpec((8, QT_BACK), lambda i: (0, i))],
         out_specs=(
             rowspec,
             pl.BlockSpec((ROWS, 256), lambda i: (0, 0)),
@@ -747,6 +762,7 @@
     window = jnp.concatenate(
         [passed(x_half[rows - HALO :], 1), x_half, passed(x_half[:HALO], -1)], axis=0
     )
+    window, reach = lax.optimization_barrier((window, reach))
     ready = prepare(plan, window)
     conv_out, spread_taps = conv(plan, ready, w_kernel)
     pre = conv_out + b_chan[0]
@@ -778,7 +794,8 @@
     pieces = [(both,) + (early if h == 0 else late) for h in range(PAIRS)]
     mixed, attended, attended_far, lse = [], [], [], []
     for h in range(PAIRS):
-        if h == 0:
+        q_part = queries
+        if h == 1:
             q_part, w_combine_far = lax.optimization_barrier((queries, w_combine_far))
         if h >= 2:
             q_part, attended_far[h - 2] = lax.optimization_barrier((queries, attended_far[h - 2]))
@@ -909,13 +926,15 @@
     small_part = jnp.pad(small_part, ((0, 0), (0, EXTRA * HALF - small_part.shape[1])))
     small_part = small_part.astype(bf16).reshape(devices, EXTRA, HALF)
     d_own = jnp.pad(d_conv_half, ((HALO, HALO), (0, 0)))
-    tap_part = tap_grad(plan, ready, d_own, small_part)
-    tap_part, first_sum = lax.optimization_barrier((tap_part, first_sum))
+    tap_raw = tap_grad(plan, ready, d_own, small_part)
+    tap_part, first_sum = lax.optimization_barrier((tap_raw, first_sum))
     tap_sum = scattered(tap_part)[0].astype(f32)
     kernel_sum = tap_sum[:-EXTRA].reshape(TAPS // devices, CG, HALF)
     small_sum = tap_sum[-EXTRA:].reshape(-1)
+    d_rim = jnp.concatenate([d_conv_half[:HALO], d_conv_half[rows - HALO :]], axis=0)
+    d_rim, _ = lax.optimization_barrier((d_rim, tap_raw))
     d_window = jnp.concatenate(
-        [passed(d_conv_half[rows - HALO :], 1), d_conv_half, passed(d_conv_half[:HALO], -1)], axis=0
+        [passed(d_rim[HALO:], 1), d_conv_half, passed(d_rim[:HALO], -1)], axis=0
     )
     d_input = conv_back(plan, ready, d_window, spread_taps).astype(bf16)
     frames_grad = dx1 + side_by_side(d_input, exchange(d_input), index).astype(f32)

time: 680 us -> 660 us (0.971)
  Pallas kernels: 210 us -> 183 us
  starting transfers between devices: 99 us -> 108 us
    pallas_call x6, Pallas kernels: 103 us -> 77.8 us  [the longest x3 46.9 us: attend_back(): pl.pallas_call(backward_kernel, grid=(ROWS // QT_BACK,), out_shape=(jax.S...]
    reduce_scatter x3, waiting for transfers between devices: 29.5 us -> 10.7 us  [scattered(): return lax.psum_scatter(whole_sum, 'seq', scatter_dimension=0, tiled=True)]
    ppermute x10, waiting for transfers between devices: 36.9 us -> 49.8 us  [chip_along(): lax.ppermute(block, 'seq', [(i, j) for i, j in route if 0 <= j < count])]
  transfers between devices with their start and end apart: 41 -> 41, of which waited for: 15 -> 15; matrix products, arithmetic and copies ran while one was open for 18% -> 19% of each run, Pallas kernels for 31% -> 28%
where the time goes in v5:
time: 660 us; the launch traced here: 654 us
  Pallas kernels  183 us (28%)
  waiting for transfers between devices  150 us (23%)
  starting transfers between devices  108 us (16%)
  other arithmetic  78.4 us (12%)
  matrix products  57.1 us (9%)
  local copies, waits for them, and re-layouts  35.6 us (5%)
  blocking collectives  23.3 us (4%)
  between operations  18.9 us (3%)
    pallas_call x4, Pallas kernels, call(): pl.pallas_call(kernel, grid_spec=pltpu.PrefetchScalarGridSpec(num_scalar_...  105 us
    ppermute x11, waiting for transfers between devices, exchange(): return lax.ppermute(part, 'heads', [(0, 1), (1, 0)])  81.9 us
    ppermute x10, starting transfers between devices, chip_along(): lax.ppermute(block, 'seq', [(i, j) for i, j in route if 0 <= j < count])  57.6 us
    dot_general x19, matrix products, dot(): lax.dot_general(a, b, (((ca,), (cb,)), ((), ())), preferred_element_type=...  57.1 us
    ppermute x10, waiting for transfers between devices, chip_along(): lax.ppermute(block, 'seq', [(i, j) for i, j in route if 0 <= j < count])  49.8 us
    pallas_call x3, Pallas kernels, attend_back(): pl.pallas_call(backward_kernel, grid=(ROWS // QT_BACK,), out_shape=(jax.S...  46.9 us
    pallas_call x3, Pallas kernels, attend(): pl.pallas_call(forward_kernel, grid=(ROWS // QT_AHEAD,), out_shape=(jax.S...  30.9 us
    all_gather x1, blocking collectives, gathered(): return lax.all_gather(shard, 'seq', axis=0, tiled=True)  23.3 us
  transfers between devices with their start and end apart: 41, of which 15 were waited for; matrix products, arithmetic and copies ran while one was open for 19% of the time, Pallas kernels for 28%

profile of v5, /device:TPU:0, one launch (start us, length us, event | category | flops | bytes accessed | tf_op | source)
XLA Modules:
  0.0 654.3 jit_solution(877373220324799811)
XLA Ops:
  12.2 3.0 collective-permute-start
  16.9 23.3 %all-gather = bf16[16,1,552]{2,1,0:T(2,128)(2,1)S(1)} all-gather(bf16[1,1,552]{2,1,0:T(2,128)(2,1)S(1)} %maximum_bitcast_fusion.2), channel_id=1, replica_groups=mesh['seq'=16,'heads'=2] {'seq'}, dimensions={0}, use_global_device_ids=true | all-gather | bytes 18768 | tf_op jit(solution)/shard_map/all_gather | solution.py:680
  48.5 2.9 broadcast_in_dim.196.kseg_ref
  53.9 13.1 %conv_prepare.1 = (bf16[2,4,304,1152]{3,2,1,0:T(8,128)(2,1)}, bf16[2,1024,1088]{2,1,0:T(8,128)(2,1)}, bf16[2,33,272,128]{3,2,1,0:T(8,128)(2,1)}, bf16[2,33,304,1...) custom-call(s32[1]{0:T(128)} %bitcast.1.n_ref, ...), custom_call_target="tpu_custom_call" | custom-call | flops 10000000000 | bytes 15000000 | tf_op jit(solution)/shard_map/conv_prepare/pallas_call | solution.py:137
  67.1 28.1 %conv_forward.1 = (f32[1024,384]{1,0:T(8,128)}, bf16[8,134,64,128]{3,2,1,0:T(8,128)(2,1)}) custom-call(s32[1]{0:T(128)} %bitcast.1.n_ref, bf16[2,8,304,256]{3,2,1,0:T(8,128)(2,1)} %get-tuple-element.110.refs_0_, bf16[2,33,272,128]{3,2,1,0:T(8,128)(2,1)} %get-tuple-element.111.refs_1_.refs_0_, bf16[2,1024,1088]{2,1,0:T(8,128)(2,1)} %get-tuple-element.112.refs_2_.refs_1_, ...), custom_call_target="tpu_custom_call" | custom-call | flops 24999999488 | bytes 15000000 | tf_op jit(solution)/shard_map/conv_forward/pallas_call | solution.py:137
  95.3 5.6 multiply_convert_fusion.2
  103.9 7.0 %all-gather.7.cloned.1.call-done = bf16[768,1536]{1,0:T(8,128)(2,1)} async-done(((bf16[48,1536]{1,0:T(8,128)(2,1)}), bf16[768,1536]{1,0:T(8,128)(2,1)}) %all-gather.7.cloned.1.call-update) | async-done | bytes 2359312 | tf_op jit(solution)/shard_map/all_gather | solution.py:680
  113.6 8.0 %collective-permute-done.2 = bf16[1024,384]{1,0:T(8,128)(2,1)} collective-permute-done((bf16[1024,384]{1,0:T(8,128)(2,1)}, bf16[1024,384]{1,0:T(8,128)(2,1)}, u32[]{:S(2)}, u32[]{:S(2)}) %collective-permute-start.2) | collective-permute-done | bytes 786464 | tf_op jit(solution)/shard_map/ppermute | solution.py:620
  131.0 5.2 collective-permute-start.5
  138.6 18.8 %collective-permute-done.5.k3 = bf16[512,256]{1,0:T(8,128)(2,1)S(1)} collective-permute-done((bf16[512,256]{1,0:T(8,128)(2,1)S(1)}, bf16[512,256]{1,0:T(8,128)(2,1)S(1)}, u32[]{:S(2)}, u32[]{:S(2)}) %collective-permute-start.5) | collective-permute-done | bytes 262176 | tf_op jit(solution)/shard_map/ppermute | solution.py:655
  157.5 11.1 %collective-permute-start.8 = (bf16[1024,512]{1,0:T(8,128)(2,1)S(1)}, bf16[1024,512]{1,0:T(8,128)(2,1)}, u32[]{:S(2)}, u32[]{:S(2)}) collective-permute-start(bf16[1024,512]{1,0:T(8,128)(2,1)S(1)} %slice.263), channel_id=1, source_target_pairs={{0,2},{2,0},{4,6},{6,4},{8,10},{10,8},{12,14},{14,12},{16,18},{18,... | collective-permute-start | bytes 3145736 | tf_op jit(solution)/shard_map/ppermute | solution.py:643
  170.3 4.5 collective-permute-start.10
  176.6 10.3 %attention_forward.3 = (f32[1024,128]{1,0:T(8,128)}, bf16[1024,128]{1,0:T(8,128)(2,1)}, f32[8,1024]{1,0:T(8,128)}) custom-call(s32[3,2]{1,0:T(4,128)} %add_add_fusion.10.range_ref, s32[8,1024]{1,0:T(8,128)} %broadcast_in_dim.195.qseg_ref, s32[4096,128]{1,0:T(8,128)} %broadcast_in_dim.196.kseg_ref, bf16[1024,384]{1,0:T(8,128)(2,1)} %fusion.17.q_ref, ...), custom_call_target="tpu_custom_call" | custom-call | flops 8000000000 | bytes 8000000 | tf_op jit(solution)/shard_map/attention_forward/pallas_call | solution.py:504
  188.6 4.9 collective-permute-done.12
  193.6 16.0 %collective-permute-done.10.k3 = bf16[512,512]{1,0:T(8,128)(2,1)S(1)} collective-permute-done((bf16[512,512]{1,0:T(8,128)(2,1)S(1)}, bf16[512,512]{1,0:T(8,128)(2,1)S(1)}, u32[]{:S(2)}, u32[]{:S(2)}) %collective-permute-start.10) | collective-permute-done | bytes 524320 | tf_op jit(solution)/shard_map/ppermute | solution.py:655
  210.3 10.2 %attention_forward.4 = (f32[1024,128]{1,0:T(8,128)}, bf16[1024,128]{1,0:T(8,128)(2,1)}, f32[8,1024]{1,0:T(8,128)}) custom-call(s32[3,2]{1,0:T(4,128)} %add_add_fusion.10.range_ref, s32[8,1024]{1,0:T(8,128)} %broadcast_in_dim.195.qseg_ref, s32[4096,128]{1,0:T(8,128)} %broadcast_in_dim.196.kseg_ref, bf16[1024,384]{1,0:T(8,128)(2,1)} %fusion.17.q_ref, ...), custom_call_target="tpu_custom_call" | custom-call | flops 8000000000 | bytes 8000000 | tf_op jit(solution)/shard_map/attention_forward/pallas_call | solution.py:504
  222.1 10.4 %attention_forward.5 = (f32[1024,128]{1,0:T(8,128)}, bf16[1024,128]{1,0:T(8,128)(2,1)}, f32[8,1024]{1,0:T(8,128)}) custom-call(s32[3,2]{1,0:T(4,128)} %add_add_fusion.10.range_ref, s32[8,1024]{1,0:T(8,128)} %broadcast_in_dim.195.qseg_ref, s32[4096,128]{1,0:T(8,128)} %broadcast_in_dim.196.kseg_ref, bf16[1024,384]{1,0:T(8,128)(2,1)} %fusion.17.q_ref, ...), custom_call_target="tpu_custom_call" | custom-call | flops 8000000000 | bytes 8000000 | tf_op jit(solution)/shard_map/attention_forward/pallas_call | solution.py:504
  233.5 5.7 collective-permute-done.14
  244.6 9.7 %multiply_convert_fusion.1 = (bf16[512,1536]{1,0:T(8,128)(2,1)S(1)}, f32[512,1536]{1,0:T(8,128)S(1)}, f32[512,1536]{1,0:T(8,128)S(1)}) fusion(f32[1536]{0:T(1024)S(1)} %reshape.934, bf16[768,3072]{1,0:T(8,128)(2,1)} %all-gather.9.cloned.1.call-done, f32[512,768]{1,0:T(8,128)S(1)} %get-tuple-element.319, f32[768]{0:T(1024)S(1)} %get-tuple-element.193, ...), kind=kOutput, calls=%fused_computation.34 | convolution fusion | flops 1261830144 | bytes 11812864 | tf_op jit(solution)/shard_map/dot_general | solution.py:676
  256.5 8.0 %multiply_convert_fusion = (bf16[512,1536]{1,0:T(8,128)(2,1)S(1)}, f32[512,1536]{1,0:T(8,128)S(1)}, f32[512,1536]{1,0:T(8,128)S(1)}) fusion(f32[1536]{0:T(1024)S(1)} %reshape.934, bf16[768,3072]{1,0:T(8,128)(2,1)S(1)} %copy-done.89, f32[512,768]{1,0:T(8,128)S(1)} %get-tuple-element.316, f32[512]{0:T(512)S(1)} %fusion.93, ...), kind=kOutput, calls=%fused_computation.21 | convolution fusion | flops 1261830144 | bytes 11816960 | tf_op jit(solution)/shard_map/dot_general | solution.py:676
  267.5 3.2 collective-permute-done.15
  275.1 3.0 fusion.144
  284.1 3.4 collective-permute-done.16
  302.6 18.7 %collective-permute-done.18 = bf16[512,768]{1,0:T(8,128)(2,1)} collective-permute-done((bf16[512,768]{1,0:T(8,128)(2,1)}, bf16[512,768]{1,0:T(8,128)(2,1)}, u32[]{:S(2)}, u32[]{:S(2)}) %collective-permute-start.18) | collective-permute-done | bytes 786464 | tf_op jit(solution)/shard_map/ppermute | solution.py:620
  321.3 2.9 multiply_reduce_fusion.5
  328.1 3.4 convolution_convert_fusion.2.do_ref
  331.8 15.6 %attention_backward.3 = (bf16[1024,128]{1,0:T(8,128)(2,1)}, f32[1024,256]{1,0:T(8,128)}, bf16[1024,256]{1,0:T(8,128)(2,1)}, bf16[1024,256]{1,0:T(8,128)(2,1)}, b...) custom-call(s32[3,4]{1,0:T(4,128)} %add_add_fusion.11.range_ref, s32[8,1024]{1,0:T(8,128)} %broadcast_in_dim.195.qseg_ref, ...), custom_call_target="tpu_custom_call" | custom-call | flops 8000000000 | bytes 12000000 | tf_op jit(solution)/shard_map/attention_backward/pallas_call | solution.py:587
  347.4 5.7 collective-permute-start.19
  354.5 16.7 %collective-permute-start.22 = (bf16[512,256]{1,0:T(8,128)(2,1)}, bf16[512,256]{1,0:T(8,128)(2,1)}, u32[]{:S(2)}, u32[]{:S(2)}) collective-permute-start(bf16[512,256]{1,0:T(8,128)(2,1)} %get-tuple-element.148), channel_id=1, source_target_pairs={{0,4},{4,8},{6,2},{8,12},{10,6},{12,16},{14,10},{16,20},{18,14},{2... | collective-permute-start | bytes 786440 | tf_op jit(solution)/shard_map/ppermute | solution.py:655
  372.5 15.8 %attention_backward.4 = (bf16[1024,128]{1,0:T(8,128)(2,1)}, f32[1024,256]{1,0:T(8,128)}, bf16[1024,256]{1,0:T(8,128)(2,1)}, bf16[1024,256]{1,0:T(8,128)(2,1)}, b...) custom-call(s32[3,4]{1,0:T(4,128)} %add_add_fusion.11.range_ref, s32[8,1024]{1,0:T(8,128)} %broadcast_in_dim.195.qseg_ref, ...), custom_call_target="tpu_custom_call" | custom-call | flops 8000000000 | bytes 12000000 | tf_op jit(solution)/shard_map/attention_backward/pallas_call | solution.py:587
  388.2 10.5 %collective-permute-start.26 = (bf16[512,256]{1,0:T(8,128)(2,1)}, bf16[512,256]{1,0:T(8,128)(2,1)}, u32[]{:S(2)}, u32[]{:S(2)}) collective-permute-start(bf16[512,256]{1,0:T(8,128)(2,1)} %get-tuple-element.153), channel_id=1, source_target_pairs={{0,4},{4,8},{6,2},{8,12},{10,6},{12,16},{14,10},{16,20},{18,14},{2... | collective-permute-start | bytes 786440 | tf_op jit(solution)/shard_map/ppermute | solution.py:655
  404.6 10.2 %collective-permute-done.26 = bf16[512,256]{1,0:T(8,128)(2,1)} collective-permute-done((bf16[512,256]{1,0:T(8,128)(2,1)}, bf16[512,256]{1,0:T(8,128)(2,1)}, u32[]{:S(2)}, u32[]{:S(2)}) %collective-permute-start.26) | collective-permute-done | bytes 262176 | tf_op jit(solution)/shard_map/ppermute | solution.py:655
  415.9 15.6 %attention_backward.5 = (bf16[1024,128]{1,0:T(8,128)(2,1)}, f32[1024,256]{1,0:T(8,128)}, bf16[1024,256]{1,0:T(8,128)(2,1)}, bf16[1024,256]{1,0:T(8,128)(2,1)}, b...) custom-call(s32[3,4]{1,0:T(4,128)} %add_add_fusion.11.range_ref, s32[8,1024]{1,0:T(8,128)} %broadcast_in_dim.195.qseg_ref, ...), custom_call_target="tpu_custom_call" | custom-call | flops 8000000000 | bytes 12000000 | tf_op jit(solution)/shard_map/attention_backward/pallas_call | solution.py:587
  431.5 13.8 %collective-permute-start.30 = (bf16[512,256]{1,0:T(8,128)(2,1)}, bf16[512,256]{1,0:T(8,128)(2,1)S(1)}, u32[]{:S(2)}, u32[]{:S(2)}) collective-permute-start(bf16[512,256]{1,0:T(8,128)(2,1)} %get-tuple-element.158), channel_id=1, source_target_pairs={{0,4},{4,8},{6,2},{8,12},{10,6},{12,16},{14,10},{16,20},{18,14},{2... | collective-permute-start | bytes 786440 | tf_op jit(solution)/shard_map/ppermute | solution.py:655
  449.4 2.9 constant_dynamic-update-slice_fusion.22
  452.3 4.0 collective-permute-start.27
  458.6 4.7 collective-permute-done.30
  465.5 5.1 convolution_convert_fusion.1
  473.2 3.0 convolution_convert_fusion.3
  478.5 4.2 convolution_convert_fusion
  484.4 20.8 %collective-permute-done.31 = bf16[1024,768]{1,0:T(8,128)(2,1)} collective-permute-done((bf16[1024,768]{1,0:T(8,128)(2,1)}, bf16[1024,768]{1,0:T(8,128)(2,1)}, u32[]{:S(2)}, u32[]{:S(2)}) %collective-permute-start.31) | collective-permute-done | bytes 1572896 | tf_op jit(solution)/shard_map/ppermute | solution.py:620
  505.2 5.3 multiply_reduce_fusion
  519.4 36.6 %tap_gradient.1 = bf16[16,400,384]{2,1,0:T(8,128)(2,1)} custom-call(s32[1]{0:T(128)} %bitcast.1.n_ref, bf16[2,8,256,304]{3,2,1,0:T(8,128)(2,1)} %get-tuple-element.161.xt_ref, bf16[2,4,304,1152]{3,2,1,0:T(8,128)(2,1)} %get-tuple-element.162.s_ref, bf16[2,33,304,128]{3,2,1,0:T(8,128)(2,1)} %get-tuple-element.163.mask_ref, bf16[1152,384]{1,0:T(8,128)(2,1)} %pad.10.d_ref, ...), custom_call_target="tpu_custom_call" | custom-call | flops 1000000000 | bytes 15000000 | tf_op jit(solution)/shard_map/tap_gradient/pallas_call | solution.py:137
  558.4 3.4 pad_maximum_fusion.1
  564.0 7.2 %collective-permute-start.32 = (bf16[64,384]{1,0:T(8,128)(2,1)S(1)}, bf16[64,384]{1,0:T(8,128)(2,1)S(1)}, u32[]{:S(2)}, u32[]{:S(2)}) collective-permute-start(bf16[64,384]{1,0:T(8,128)(2,1)S(1)} %get-tuple-element.304), channel_id=1, source_target_pairs={{0,2},{2,4},{4,6},{6,8},{8,10},{10,12},{12,14},{14,16},{16,18},{18... | collective-permute-start | bytes 147464 | tf_op jit(solution)/shard_map/ppermute | solution.py:639
  573.2 27.3 %conv_back.1 = f32[1024,384]{1,0:T(8,128)} custom-call(s32[1]{0:T(128)} %bitcast.1.n_ref, bf16[1152,384]{1,0:T(8,128)(2,1)} %pad_maximum_fusion.5.d_ref, bf16[2,4,304,1152]{3,2,1,0:T(8,128)(2,1)} %get-tuple-element.162.s_ref, bf16[2,33,272,128]{3,2,1,0:T(8,128)(2,1)} %get-tuple-element.111.refs_1_.refs_0_, ...), custom_call_target="tpu_custom_call" | custom-call | flops 24999999488 | bytes 15000000 | tf_op jit(solution)/shard_map/conv_back/pallas_call | solution.py:137
  604.4 17.2 %collective-permute-done.34 = bf16[1024,384]{1,0:T(8,128)(2,1)S(1)} collective-permute-done((bf16[1024,384]{1,0:T(8,128)(2,1)S(1)}, bf16[1024,384]{1,0:T(8,128)(2,1)S(1)}, u32[]{:S(2)}, u32[]{:S(2)}) %collective-permute-start.34) | collective-permute-done | bytes 786464 | tf_op jit(solution)/shard_map/ppermute | solution.py:620
  627.4 10.7 %reduce-scatter.8.cloned.1.call-done = bf16[1,400,384]{2,1,0:T(8,128)(2,1)} async-done(((bf16[16,400,384]{2,1,0:T(8,128)(2,1)}), bf16[1,400,384]{2,1,0:T(8,128)(2,1)}) %reduce-scatter.8.cloned.1.call-update) | async-done | bytes 307216 | tf_op jit(solution)/shard_map/reduce_scatter | solution.py:684
  (495 shorter events, 138.8 us)
Async XLA Ops:
  7.3 59.9 %all-gather.5.cloned.1.call-start = ((), (), s32[]{:S(2)}) async-start(), calls=%async_computation.3 | async-start | bytes 5013504 | tf_op jit(solution)/shard_map/all_gather | solution.py:680
  9.3 101.6 %all-gather.7.cloned.1.call-start = ((), (), s32[]{:S(2)}) async-start(), calls=%async_computation.4 | async-start | bytes 2506752 | tf_op jit(solution)/shard_map/all_gather | solution.py:680
  10.9 35.9 %collective-permute-start.1 = (bf16[64,384]{1,0:T(8,128)(2,1)S(1)}, bf16[64,384]{1,0:T(8,128)(2,1)S(1)}, u32[]{:S(2)}, u32[]{:S(2)}) collective-permute-start(bf16[64,384]{1,0:T(8,128)(2,1)S(1)} %get-tuple-element.291), channel_id=1, source_target_pairs={{2,0},{4,2},{6,4},{8,6},{10,8},{12,10},{14,12},{16,14},{18,16},{20... | collective-permute-start | bytes 147464 | tf_op jit(solution)/shard_map/ppermute | solution.py:639
  12.2 34.7 %collective-permute-start = (bf16[64,384]{1,0:T(8,128)(2,1)S(1)}, bf16[64,384]{1,0:T(8,128)(2,1)S(1)}, u32[]{:S(2)}, u32[]{:S(2)}) collective-permute-start(bf16[64,384]{1,0:T(8,128)(2,1)S(1)} %get-tuple-element.290), channel_id=1, source_target_pairs={{0,2},{2,4},{4,6},{6,8},{8,10},{10,12},{12,14},{14,16},{16,18},{18... | collective-permute-start | bytes 147464 | tf_op jit(solution)/shard_map/ppermute | solution.py:639
  16.1 228.5 %all-gather.9.cloned.1.call-start = ((), (), s32[]{:S(2)}) async-start(), calls=%async_computation.5 | async-start | bytes 5013504 | tf_op jit(solution)/shard_map/all_gather | solution.py:680
  46.8 48.5 %copy-start.65 = (f32[384]{0:T(512)}, f32[384]{0:T(512)S(1)}, u32[]{:S(2)}) copy-start(f32[384]{0:T(512)S(1)} %add.698) | copy-start | bytes 4612
  100.9 20.7 %collective-permute-start.2 = (bf16[1024,384]{1,0:T(8,128)(2,1)}, bf16[1024,384]{1,0:T(8,128)(2,1)}, u32[]{:S(2)}, u32[]{:S(2)}) collective-permute-start(bf16[1024,384]{1,0:T(8,128)(2,1)} %get-tuple-element.272), channel_id=1, source_target_pairs={{0,1},{1,0},{2,3},{3,2},{4,5},{5,4},{6,7},{7,6},{8,9},{9,8},{10,11... | collective-permute-start | bytes 2359304 | tf_op jit(solution)/shard_map/ppermute | solution.py:620
  103.2 367.4 %reduce-scatter.4.cloned.1.call-start = ((), (), s32[]{:S(2)}) async-start(), calls=%async_computation.6 | async-start | bytes 5013504 | tf_op jit(solution)/shard_map/reduce_scatter | solution.py:684
  112.0 74.8 %collective-permute-start.7 = (bf16[768,384]{1,0:T(8,128)(2,1)S(1)}, bf16[768,384]{1,0:T(8,128)(2,1)S(1)}, u32[]{:S(2)}, u32[]{:S(2)}) collective-permute-start(bf16[768,384]{1,0:T(8,128)(2,1)S(1)} %slice.329), channel_id=1, source_target_pairs={{0,1},{1,0},{2,3},{3,2},{4,5},{5,4},{6,7},{7,6},{8,9},{9,8},{10,11... | collective-permute-start | bytes 1769480 | tf_op jit(solution)/shard_map/ppermute | solution.py:620
  130.1 40.1 %copy-start.5 = (bf16[1024,768]{1,0:T(8,128)(2,1)}, bf16[1024,768]{1,0:T(8,128)(2,1)S(1)}, u32[]{:S(2)}) copy-start(bf16[1024,768]{1,0:T(8,128)(2,1)S(1)} %fusion.2.k0) | copy-start | bytes 4718596
  130.2 27.2 %collective-permute-start.3 = (bf16[1024,256]{1,0:T(8,128)(2,1)S(1)}, bf16[1024,256]{1,0:T(8,128)(2,1)S(1)}, u32[]{:S(2)}, u32[]{:S(2)}) collective-permute-start(bf16[1024,256]{1,0:T(8,128)(2,1)S(1)} %slice.326), channel_id=1, source_target_pairs={{0,2},{2,0},{4,6},{6,4},{8,10},{10,8},{12,14},{14,12},{16,18},{18,... | collective-permute-start | bytes 1572872 | tf_op jit(solution)/shard_map/ppermute | solution.py:643
  130.3 27.2 %collective-permute-start.4 = (bf16[1024,256]{1,0:T(8,128)(2,1)S(1)}, bf16[1024,256]{1,0:T(8,128)(2,1)S(1)}, u32[]{:S(2)}, u32[]{:S(2)}) collective-permute-start(bf16[1024,256]{1,0:T(8,128)(2,1)S(1)} %slice.326), channel_id=1, source_target_pairs={{2,4},{4,2},{6,8},{8,6},{10,12},{12,10},{14,16},{16,14},{18,20},{2... | collective-permute-start | bytes 1572872 | tf_op jit(solution)/shard_map/ppermute | solution.py:649
  131.0 26.4 %collective-permute-start.5 = (bf16[512,256]{1,0:T(8,128)(2,1)S(1)}, bf16[512,256]{1,0:T(8,128)(2,1)S(1)}, u32[]{:S(2)}, u32[]{:S(2)}) collective-permute-start(bf16[512,256]{1,0:T(8,128)(2,1)S(1)} %get-tuple-element.287), channel_id=1, source_target_pairs={{0,4},{4,8},{6,2},{8,12},{10,6},{12,16},{14,10},{16,20},{18,14},{2... | collective-permute-start | bytes 786440 | tf_op jit(solution)/shard_map/ppermute | solution.py:655
  136.3 21.1 %collective-permute-start.6 = (bf16[512,256]{1,0:T(8,128)(2,1)S(1)}, bf16[512,256]{1,0:T(8,128)(2,1)S(1)}, u32[]{:S(2)}, u32[]{:S(2)}) collective-permute-start(bf16[512,256]{1,0:T(8,128)(2,1)S(1)} %get-tuple-element.286), channel_id=1, source_target_pairs={{2,6},{4,0},{6,10},{8,4},{10,14},{12,8},{14,18},{16,12},{18,22},{2... | collective-permute-start | bytes 786440 | tf_op jit(solution)/shard_map/ppermute | solution.py:655
  157.5 52.0 %collective-permute-start.8 = (bf16[1024,512]{1,0:T(8,128)(2,1)S(1)}, bf16[1024,512]{1,0:T(8,128)(2,1)}, u32[]{:S(2)}, u32[]{:S(2)}) collective-permute-start(bf16[1024,512]{1,0:T(8,128)(2,1)S(1)} %slice.263), channel_id=1, source_target_pairs={{0,2},{2,0},{4,6},{6,4},{8,10},{10,8},{12,14},{14,12},{16,18},{18,... | collective-permute-start | bytes 3145736 | tf_op jit(solution)/shard_map/ppermute | solution.py:643
  168.6 40.9 %collective-permute-start.9 = (bf16[1024,512]{1,0:T(8,128)(2,1)S(1)}, bf16[1024,512]{1,0:T(8,128)(2,1)}, u32[]{:S(2)}, u32[]{:S(2)}) collective-permute-start(bf16[1024,512]{1,0:T(8,128)(2,1)S(1)} %slice.263), channel_id=1, source_target_pairs={{2,4},{4,2},{6,8},{8,6},{10,12},{12,10},{14,16},{16,14},{18,20},{2... | collective-permute-start | bytes 3145736 | tf_op jit(solution)/shard_map/ppermute | solution.py:649
  170.3 39.2 %collective-permute-start.10 = (bf16[512,512]{1,0:T(8,128)(2,1)S(1)}, bf16[512,512]{1,0:T(8,128)(2,1)S(1)}, u32[]{:S(2)}, u32[]{:S(2)}) collective-permute-start(bf16[512,512]{1,0:T(8,128)(2,1)S(1)} %get-tuple-element.285), channel_id=1, source_target_pairs={{0,4},{4,8},{6,2},{8,12},{10,6},{12,16},{14,10},{16,20},{18,14},{2... | collective-permute-start | bytes 1572872 | tf_op jit(solution)/shard_map/ppermute | solution.py:655
  174.9 34.6 %collective-permute-start.11 = (bf16[512,512]{1,0:T(8,128)(2,1)S(1)}, bf16[512,512]{1,0:T(8,128)(2,1)}, u32[]{:S(2)}, u32[]{:S(2)}) collective-permute-start(bf16[512,512]{1,0:T(8,128)(2,1)S(1)} %get-tuple-element.284), channel_id=1, source_target_pairs={{2,6},{4,0},{6,10},{8,4},{10,14},{12,8},{14,18},{16,12},{18,22},{2... | collective-permute-start | bytes 1572872 | tf_op jit(solution)/shard_map/ppermute | solution.py:655
  186.9 6.6 %collective-permute-start.12 = (bf16[1024,128]{1,0:T(8,128)(2,1)}, bf16[1024,128]{1,0:T(8,128)(2,1)S(1)}, u32[]{:S(2)}, u32[]{:S(2)}) collective-permute-start(bf16[1024,128]{1,0:T(8,128)(2,1)} %get-tuple-element.122), channel_id=1, source_target_pairs={{0,1},{1,0},{2,3},{3,2},{4,5},{5,4},{6,7},{7,6},{8,9},{9,8},{10,11... | collective-permute-start | bytes 786440 | tf_op jit(solution)/shard_map/ppermute | solution.py:620
  220.5 12.9 %collective-permute-start.13 = (bf16[1024,128]{1,0:T(8,128)(2,1)}, bf16[1024,128]{1,0:T(8,128)(2,1)S(1)}, u32[]{:S(2)}, u32[]{:S(2)}) collective-permute-start(bf16[1024,128]{1,0:T(8,128)(2,1)} %get-tuple-element.124), channel_id=1, source_target_pairs={{0,1},{1,0},{2,3},{3,2},{4,5},{5,4},{6,7},{7,6},{8,9},{9,8},{10,11... | collective-permute-start | bytes 786440 | tf_op jit(solution)/shard_map/ppermute | solution.py:620
  232.5 6.6 %collective-permute-start.14 = (bf16[1024,128]{1,0:T(8,128)(2,1)}, bf16[1024,128]{1,0:T(8,128)(2,1)S(1)}, u32[]{:S(2)}, u32[]{:S(2)}) collective-permute-start(bf16[1024,128]{1,0:T(8,128)(2,1)} %get-tuple-element.126), channel_id=1, source_target_pairs={{0,1},{1,0},{2,3},{3,2},{4,5},{5,4},{6,7},{7,6},{8,9},{9,8},{10,11... | collective-permute-start | bytes 786440 | tf_op jit(solution)/shard_map/ppermute | solution.py:620
  255.7 14.9 %collective-permute-start.15 = (bf16[512,768]{1,0:T(8,128)(2,1)S(1)}, bf16[512,768]{1,0:T(8,128)(2,1)S(1)}, u32[]{:S(2)}, u32[]{:S(2)}) collective-permute-start(bf16[512,768]{1,0:T(8,128)(2,1)S(1)} %fusion.51), channel_id=1, source_target_pairs={{0,1},{1,0},{2,3},{3,2},{4,5},{5,4},{6,7},{7,6},{8,9},{9,8},{10,11... | collective-permute-start | bytes 2359304 | tf_op jit(solution)/shard_map/ppermute | solution.py:620
  265.9 21.6 %collective-permute-start.16 = (bf16[512,768]{1,0:T(8,128)(2,1)S(1)}, bf16[512,768]{1,0:T(8,128)(2,1)S(1)}, u32[]{:S(2)}, u32[]{:S(2)}) collective-permute-start(bf16[512,768]{1,0:T(8,128)(2,1)S(1)} %fusion.54), channel_id=1, source_target_pairs={{0,1},{1,0},{2,3},{3,2},{4,5},{5,4},{6,7},{7,6},{8,9},{9,8},{10,11... | collective-permute-start | bytes 2359304 | tf_op jit(solution)/shard_map/ppermute | solution.py:620
  280.4 43.8 %collective-permute-start.17 = (bf16[512,768]{1,0:T(8,128)(2,1)}, bf16[512,768]{1,0:T(8,128)(2,1)}, u32[]{:S(2)}, u32[]{:S(2)}) collective-permute-start(bf16[512,768]{1,0:T(8,128)(2,1)} %fusion.45), channel_id=1, source_target_pairs={{0,1},{1,0},{2,3},{3,2},{4,5},{5,4},{6,7},{7,6},{8,9},{9,8},{10,11... | collective-permute-start | bytes 2359304 | tf_op jit(solution)/shard_map/ppermute | solution.py:620
  296.1 25.2 %collective-permute-start.18 = (bf16[512,768]{1,0:T(8,128)(2,1)}, bf16[512,768]{1,0:T(8,128)(2,1)}, u32[]{:S(2)}, u32[]{:S(2)}) collective-permute-start(bf16[512,768]{1,0:T(8,128)(2,1)} %fusion.48), channel_id=1, source_target_pairs={{0,1},{1,0},{2,3},{3,2},{4,5},{5,4},{6,7},{7,6},{8,9},{9,8},{10,11... | collective-permute-start | bytes 2359304 | tf_op jit(solution)/shard_map/ppermute | solution.py:620
  328.0 145.2 %copy-start.12 = (f32[512,768]{1,0:T(8,128)}, f32[512,768]{1,0:T(8,128)S(1)}, u32[]{:S(2)}) copy-start(f32[512,768]{1,0:T(8,128)S(1)} %get-tuple-element.240) | copy-start | bytes 4718596
  328.0 145.2 %copy-start.13 = (f32[512,768]{1,0:T(8,128)}, f32[512,768]{1,0:T(8,128)S(1)}, u32[]{:S(2)}) copy-start(f32[512,768]{1,0:T(8,128)S(1)} %get-tuple-element.326) | copy-start | bytes 4718596
  331.5 224.5 %reduce-scatter.6.cloned.1.call-start = ((), (), s32[]{:S(2)}) async-start(), calls=%async_computation.7 | async-start | bytes 2506752 | tf_op jit(solution)/shard_map/reduce_scatter | solution.py:684
  347.4 68.5 %collective-permute-start.19 = (bf16[1024,256]{1,0:T(8,128)(2,1)}, bf16[1024,256]{1,0:T(8,128)(2,1)}, u32[]{:S(2)}, u32[]{:S(2)}) collective-permute-start(bf16[1024,256]{1,0:T(8,128)(2,1)} %get-tuple-element.138), channel_id=1, source_target_pairs={{0,2},{2,0},{4,6},{6,4},{8,10},{10,8},{12,14},{14,12},{16,18},{18,... | collective-permute-start | bytes 1572872 | tf_op jit(solution)/shard_map/ppermute | solution.py:643
  353.1 62.8 %collective-permute-start.20 = (bf16[1024,256]{1,0:T(8,128)(2,1)}, bf16[1024,256]{1,0:T(8,128)(2,1)}, u32[]{:S(2)}, u32[]{:S(2)}) collective-permute-start(bf16[1024,256]{1,0:T(8,128)(2,1)} %get-tuple-element.139), channel_id=1, source_target_pairs={{2,4},{4,2},{6,8},{8,6},{10,12},{12,10},{14,16},{16,14},{18,20},{2... | collective-permute-start | bytes 1572872 | tf_op jit(solution)/shard_map/ppermute | solution.py:649
  354.5 46.9 %collective-permute-start.22 = (bf16[512,256]{1,0:T(8,128)(2,1)}, bf16[512,256]{1,0:T(8,128)(2,1)}, u32[]{:S(2)}, u32[]{:S(2)}) collective-permute-start(bf16[512,256]{1,0:T(8,128)(2,1)} %get-tuple-element.148), channel_id=1, source_target_pairs={{0,4},{4,8},{6,2},{8,12},{10,6},{12,16},{14,10},{16,20},{18,14},{2... | collective-permute-start | bytes 786440 | tf_op jit(solution)/shard_map/ppermute | solution.py:655
  371.2 31.6 %collective-permute-start.21 = (bf16[512,256]{1,0:T(8,128)(2,1)}, bf16[512,256]{1,0:T(8,128)(2,1)}, u32[]{:S(2)}, u32[]{:S(2)}) collective-permute-start(bf16[512,256]{1,0:T(8,128)(2,1)} %get-tuple-element.147), channel_id=1, source_target_pairs={{2,6},{4,0},{6,10},{8,4},{10,14},{12,8},{14,18},{16,12},{18,22},{2... | collective-permute-start | bytes 786440 | tf_op jit(solution)/shard_map/ppermute | solution.py:655
  388.2 26.6 %collective-permute-start.26 = (bf16[512,256]{1,0:T(8,128)(2,1)}, bf16[512,256]{1,0:T(8,128)(2,1)}, u32[]{:S(2)}, u32[]{:S(2)}) collective-permute-start(bf16[512,256]{1,0:T(8,128)(2,1)} %get-tuple-element.153), channel_id=1, source_target_pairs={{0,4},{4,8},{6,2},{8,12},{10,6},{12,16},{14,10},{16,20},{18,14},{2... | collective-permute-start | bytes 786440 | tf_op jit(solution)/shard_map/ppermute | solution.py:655
  401.5 13.4 %collective-permute-start.25 = (bf16[512,256]{1,0:T(8,128)(2,1)}, bf16[512,256]{1,0:T(8,128)(2,1)S(1)}, u32[]{:S(2)}, u32[]{:S(2)}) collective-permute-start(bf16[512,256]{1,0:T(8,128)(2,1)} %get-tuple-element.152), channel_id=1, source_target_pairs={{2,6},{4,0},{6,10},{8,4},{10,14},{12,8},{14,18},{16,12},{18,22},{2... | collective-permute-start | bytes 786440 | tf_op jit(solution)/shard_map/ppermute | solution.py:655
  402.8 49.5 %collective-permute-start.24 = (bf16[1024,256]{1,0:T(8,128)(2,1)}, bf16[1024,256]{1,0:T(8,128)(2,1)S(1)}, u32[]{:S(2)}, u32[]{:S(2)}) collective-permute-start(bf16[1024,256]{1,0:T(8,128)(2,1)} %get-tuple-element.151), channel_id=1, source_target_pairs={{2,4},{4,2},{6,8},{8,6},{10,12},{12,10},{14,16},{16,14},{18,20},{2... | collective-permute-start | bytes 1572872 | tf_op jit(solution)/shard_map/ppermute | solution.py:649
  414.8 41.4 %collective-permute-start.23 = (bf16[1024,256]{1,0:T(8,128)(2,1)}, bf16[1024,256]{1,0:T(8,128)(2,1)}, u32[]{:S(2)}, u32[]{:S(2)}) collective-permute-start(bf16[1024,256]{1,0:T(8,128)(2,1)} %get-tuple-element.150), channel_id=1, source_target_pairs={{0,2},{2,0},{4,6},{6,4},{8,10},{10,8},{12,14},{14,12},{16,18},{18,... | collective-permute-start | bytes 1572872 | tf_op jit(solution)/shard_map/ppermute | solution.py:643
  431.5 31.9 %collective-permute-start.30 = (bf16[512,256]{1,0:T(8,128)(2,1)}, bf16[512,256]{1,0:T(8,128)(2,1)S(1)}, u32[]{:S(2)}, u32[]{:S(2)}) collective-permute-start(bf16[512,256]{1,0:T(8,128)(2,1)} %get-tuple-element.158), channel_id=1, source_target_pairs={{0,4},{4,8},{6,2},{8,12},{10,6},{12,16},{14,10},{16,20},{18,14},{2... | collective-permute-start | bytes 786440 | tf_op jit(solution)/shard_map/ppermute | solution.py:655
  445.3 18.1 %collective-permute-start.29 = (bf16[512,256]{1,0:T(8,128)(2,1)}, bf16[512,256]{1,0:T(8,128)(2,1)S(1)}, u32[]{:S(2)}, u32[]{:S(2)}) collective-permute-start(bf16[512,256]{1,0:T(8,128)(2,1)} %get-tuple-element.157), channel_id=1, source_target_pairs={{2,6},{4,0},{6,10},{8,4},{10,14},{12,8},{14,18},{16,12},{18,22},{2... | collective-permute-start | bytes 786440 | tf_op jit(solution)/shard_map/ppermute | solution.py:655
  446.6 16.9 %collective-permute-start.28 = (bf16[1024,256]{1,0:T(8,128)(2,1)}, bf16[1024,256]{1,0:T(8,128)(2,1)S(1)}, u32[]{:S(2)}, u32[]{:S(2)}) collective-permute-start(bf16[1024,256]{1,0:T(8,128)(2,1)} %get-tuple-element.156), channel_id=1, source_target_pairs={{2,4},{4,2},{6,8},{8,6},{10,12},{12,10},{14,16},{16,14},{18,20},{2... | collective-permute-start | bytes 1572872 | tf_op jit(solution)/shard_map/ppermute | solution.py:649
  452.3 11.2 %collective-permute-start.27 = (bf16[1024,256]{1,0:T(8,128)(2,1)S(1)}, bf16[1024,256]{1,0:T(8,128)(2,1)S(1)}, u32[]{:S(2)}, u32[]{:S(2)}) collective-permute-start(bf16[1024,256]{1,0:T(8,128)(2,1)S(1)} %copy-done.95), channel_id=1, source_target_pairs={{0,2},{2,0},{4,6},{6,4},{8,10},{10,8},{12,14},{14,12},{16,18},{18,... | collective-permute-start | bytes 1572872 | tf_op jit(solution)/shard_map/ppermute | solution.py:643
  472.5 32.7 %collective-permute-start.31 = (bf16[1024,768]{1,0:T(8,128)(2,1)}, bf16[1024,768]{1,0:T(8,128)(2,1)}, u32[]{:S(2)}, u32[]{:S(2)}) collective-permute-start(bf16[1024,768]{1,0:T(8,128)(2,1)} %convolution_convert_fusion.1), channel_id=1, source_target_pairs={{0,1},{1,0},{2,3},{3,2},{4,5},{5,4},{6,7},{7,6},{8,9},{9,8},{10,11... | collective-permute-start | bytes 4718600 | tf_op jit(solution)/shard_map/ppermute | solution.py:620
  484.3 153.8 %reduce-scatter.8.cloned.1.call-start = ((), (), s32[]{:S(2)}) async-start(), calls=%async_computation.8 | async-start | bytes 5222400 | tf_op jit(solution)/shard_map/reduce_scatter | solution.py:684
  562.7 40.2 %copy-start.20 = (f32[48,1536]{1,0:T(8,128)}, f32[48,1536]{1,0:T(8,128)S(1)}, u32[]{:S(2)}) copy-start(f32[48,1536]{1,0:T(8,128)S(1)} %get-tuple-element.222) | copy-start | bytes 884740
  562.7 9.4 %collective-permute-start.33 = (bf16[64,384]{1,0:T(8,128)(2,1)S(1)}, bf16[64,384]{1,0:T(8,128)(2,1)S(1)}, u32[]{:S(2)}, u32[]{:S(2)}) collective-permute-start(bf16[64,384]{1,0:T(8,128)(2,1)S(1)} %get-tuple-element.305), channel_id=1, source_target_pairs={{2,0},{4,2},{6,4},{8,6},{10,8},{12,10},{14,12},{16,14},{18,16},{20... | collective-permute-start | bytes 147464 | tf_op jit(solution)/shard_map/ppermute | solution.py:639
  564.0 8.1 %collective-permute-start.32 = (bf16[64,384]{1,0:T(8,128)(2,1)S(1)}, bf16[64,384]{1,0:T(8,128)(2,1)S(1)}, u32[]{:S(2)}, u32[]{:S(2)}) collective-permute-start(bf16[64,384]{1,0:T(8,128)(2,1)S(1)} %get-tuple-element.304), channel_id=1, source_target_pairs={{0,2},{2,4},{4,6},{6,8},{8,10},{10,12},{12,14},{14,16},{16,18},{18... | collective-permute-start | bytes 147464 | tf_op jit(solution)/shard_map/ppermute | solution.py:639
  572.2 31.5 %copy-start.21 = (f32[1536,48]{0,1:T(8,128)}, f32[1536,48]{0,1:T(8,128)S(1)}, u32[]{:S(2)}) copy-start(f32[1536,48]{0,1:T(8,128)S(1)} %get-tuple-element.218) | copy-start | bytes 884740
  573.2 30.4 %copy-start.40 = (f32[1536,48]{0,1:T(8,128)S(1)}, f32[1536,48]{0,1:T(8,128)}, u32[]{:S(2)}) copy-start(f32[1536,48]{0,1:T(8,128)} %param.47) | copy-start | bytes 884740
  602.2 19.4 %collective-permute-start.34 = (bf16[1024,384]{1,0:T(8,128)(2,1)S(1)}, bf16[1024,384]{1,0:T(8,128)(2,1)S(1)}, u32[]{:S(2)}, u32[]{:S(2)}) collective-permute-start(bf16[1024,384]{1,0:T(8,128)(2,1)S(1)} %convert_element_type.285), channel_id=1, source_target_pairs={{0,1},{1,0},{2,3},{3,2},{4,5},{5,4},{6,7},{7,6},{8,9},{9,8},{10,11... | collective-permute-start | bytes 2359304 | tf_op jit(solution)/shard_map/ppermute | solution.py:620
  (92 other events, 709.7 us)
Sparse Core Ops, SparseCore 0:
  10.9 56.1 all-gather.4
  70.0 40.8 all-gather.6
  113.8 67.3 all-gather.8
  331.6 116.0 reduce-scatter.3
  484.4 68.9 reduce-scatter.5
  557.2 80.8 reduce-scatter.7

commit v6 on v5

--- a/solution.py
+++ b/solution.py
@@ -740,7 +740,6 @@
     )
     w_second = gathered(jnp.concatenate([expand, shrink.T], axis=1).astype(bf16))
     w_combine = w_first[:, 3 * HALF :]
-    w_combine_far = exchange(w_combine)
     cuts = [unitbias.size, chanbias.size, outbias.size, normparams.size]
     parts, at = [], 0
     for size in cuts:
@@ -777,21 +776,26 @@
     kv_bias = jnp.concatenate([jnp.zeros_like(kv_bias), kv_bias], axis=1).reshape(-1)
     both = (proj[:, HALF:] + kv_bias).astype(bf16)
     near = NEAR
+    w_combine_sent, queries = lax.optimization_barrier((w_combine, queries))
+    w_combine_far = exchange(w_combine_sent)
 
     def fetched(lo, hi):
         block = both[:, lo:hi]
         head, tail = block[:near], block[rows - near :]
+        beside = across_chips(block)
+        shared = jnp.where(odd == 1, beside[:near], beside[rows - near :])
         return (
             across_cores(block),
-            across_chips(block),
+            beside,
             chip_along(jnp.where(odd == 1, head, tail), 1),
-            chip_along(jnp.where(odd == 1, tail, head), -1),
+            shared,
         )
 
     early = fetched(0, 256)
+    early = early[:3] + (across_cores(early[3]),)
     both, early = lax.optimization_barrier((both, early))
     late = fetched(256, 256 * PAIRS)
-    pieces = [(both,) + (early if h == 0 else late) for h in range(PAIRS)]
+    pieces = [(both,) + early]
     mixed, attended, attended_far, lse = [], [], [], []
     for h in range(PAIRS):
         q_part = queries
@@ -804,6 +808,9 @@
         lse.append(lse_part)
         attended.append(half)
         attended_far.append(exchange(half))
+        if h == 0:
+            shared, _ = lax.optimization_barrier((late[3], half))
+            pieces += [(both,) + late[:3] + (across_cores(shared),)] * (PAIRS - 1)
     attended = jnp.concatenate(attended, axis=1)
     attended_all = side_by_side(attended, jnp.concatenate(attended_far, axis=1), index)
     w_combine_all = side_by_side(w_combine, w_combine_far, index)

time: 660 us -> 658 us (level)
  waiting for transfers between devices: 150 us -> 127 us
    ppermute x10 -> x8, waiting for transfers between devices: 49.8 us -> 9.01 us  [chip_along(): lax.ppermute(block, 'seq', [(i, j) for i, j in route if 0 <= j < count])]
    ppermute x5 -> x7, starting transfers between devices: 20.8 us -> 50.1 us  [across_cores(): lax.ppermute(block, 'seq', [(i, i ^ 1) for i in range(lax.axis_size('seq'...]
    ppermute x10 -> x8, starting transfers between devices: 57.6 us -> 38.3 us  [chip_along(): lax.ppermute(block, 'seq', [(i, j) for i, j in route if 0 <= j < count])]
    reduce_scatter x3, waiting for transfers between devices: 10.7 us -> 24.9 us  [scattered(): return lax.psum_scatter(whole_sum, 'seq', scatter_dimension=0, tiled=True)]
    ppermute x11, waiting for transfers between devices: 81.9 us -> 92.7 us  [exchange(): return lax.ppermute(part, 'heads', [(0, 1), (1, 0)])]
    all_gather x3, waiting for transfers between devices: 7.15 us -> 0.12 us  [gathered(): return lax.all_gather(shard, 'seq', axis=0, tiled=True)]
    unnamed x223 -> x213, local copies, waits for them, and re-layouts: 19.2 us -> 21.7 us
  transfers between devices with their start and end apart: 41 -> 41, of which waited for: 15 -> 13; matrix products, arithmetic and copies ran while one was open for 19% -> 21% of each run, Pallas kernels for 28% -> 28%
where the time goes in v6:
time: 658 us; the launch traced here: 649 us
  Pallas kernels  183 us (28%)
  waiting for transfers between devices  127 us (19%)
  starting transfers between devices  114 us (17%)
  other arithmetic  81.6 us (12%)
  matrix products  61.5 us (9%)
  local copies, waits for them, and re-layouts  39.1 us (6%)
  blocking collectives  23.3 us (4%)
  between operations  18.8 us (3%)
    pallas_call x4, Pallas kernels, call(): pl.pallas_call(kernel, grid_spec=pltpu.PrefetchScalarGridSpec(num_scalar_...  105 us
    ppermute x11, waiting for transfers between devices, exchange(): return lax.ppermute(part, 'heads', [(0, 1), (1, 0)])  92.7 us
    dot_general x19, matrix products, dot(): lax.dot_general(a, b, (((ca,), (cb,)), ((), ())), preferred_element_type=...  61.5 us
    ppermute x7, starting transfers between devices, across_cores(): lax.ppermute(block, 'seq', [(i, i ^ 1) for i in range(lax.axis_size('seq'...  50.1 us
    pallas_call x3, Pallas kernels, attend_back(): pl.pallas_call(backward_kernel, grid=(ROWS // QT_BACK,), out_shape=(jax.S...  47.1 us
    ppermute x8, starting transfers between devices, chip_along(): lax.ppermute(block, 'seq', [(i, j) for i, j in route if 0 <= j < count])  38.3 us
    pallas_call x3, Pallas kernels, attend(): pl.pallas_call(forward_kernel, grid=(ROWS // QT_AHEAD,), out_shape=(jax.S...  30.8 us
    reduce_scatter x3, waiting for transfers between devices, scattered(): return lax.psum_scatter(whole_sum, 'seq', scatter_dimension=0, tiled=True)  24.9 us
  transfers between devices with their start and end apart: 41, of which 13 were waited for; matrix products, arithmetic and copies ran while one was open for 21% of the time, Pallas kernels for 28%

profile of v6, /device:TPU:0, one launch (start us, length us, event | category | flops | bytes accessed | tf_op | source)
XLA Modules:
  0.0 648.7 jit_solution(16452534254770581715)
XLA Ops:
  12.2 3.0 collective-permute-start
  16.9 23.3 %all-gather = bf16[16,1,552]{2,1,0:T(2,128)(2,1)S(1)} all-gather(bf16[1,1,552]{2,1,0:T(2,128)(2,1)S(1)} %maximum_bitcast_fusion.2), channel_id=1, replica_groups=mesh['seq'=16,'heads'=2] {'seq'}, dimensions={0}, use_global_device_ids=true | all-gather | bytes 18768 | tf_op jit(solution)/shard_map/all_gather | solution.py:680
  48.5 3.0 broadcast_in_dim.196.kseg_ref
  53.9 13.1 %conv_prepare.1 = (bf16[2,4,304,1152]{3,2,1,0:T(8,128)(2,1)}, bf16[2,1024,1088]{2,1,0:T(8,128)(2,1)}, bf16[2,33,272,128]{3,2,1,0:T(8,128)(2,1)}, bf16[2,33,304,1...) custom-call(s32[1]{0:T(128)} %bitcast.1.n_ref, ...), custom_call_target="tpu_custom_call" | custom-call | flops 10000000000 | bytes 15000000 | tf_op jit(solution)/shard_map/conv_prepare/pallas_call | solution.py:137
  67.1 28.2 %conv_forward.1 = (f32[1024,384]{1,0:T(8,128)}, bf16[8,134,64,128]{3,2,1,0:T(8,128)(2,1)}) custom-call(s32[1]{0:T(128)} %bitcast.1.n_ref, bf16[2,8,304,256]{3,2,1,0:T(8,128)(2,1)} %get-tuple-element.113.refs_0_, bf16[2,33,272,128]{3,2,1,0:T(8,128)(2,1)} %get-tuple-element.114.refs_1_.refs_0_, bf16[2,1024,1088]{2,1,0:T(8,128)(2,1)} %get-tuple-element.115.refs_2_.refs_1_, ...), custom_call_target="tpu_custom_call" | custom-call | flops 24999999488 | bytes 15000000 | tf_op jit(solution)/shard_map/conv_forward/pallas_call | solution.py:137
  95.3 5.7 multiply_convert_fusion.2
  103.9 17.2 %collective-permute-done.2 = bf16[1024,384]{1,0:T(8,128)(2,1)} collective-permute-done((bf16[1024,384]{1,0:T(8,128)(2,1)}, bf16[1024,384]{1,0:T(8,128)(2,1)}, u32[]{:S(2)}, u32[]{:S(2)}) %collective-permute-start.2) | collective-permute-done | bytes 786464 | tf_op jit(solution)/shard_map/ppermute | solution.py:620
  127.5 3.7 fusion.25
  136.4 5.1 collective-permute-start.5
  142.3 20.7 %collective-permute-start.6 = (bf16[512,256]{1,0:T(8,128)(2,1)}, bf16[512,256]{1,0:T(8,128)(2,1)}, u32[]{:S(2)}, u32[]{:S(2)}) collective-permute-start(bf16[512,256]{1,0:T(8,128)(2,1)} %slice_select_fusion.2), channel_id=1, source_target_pairs={{0,2},{2,0},{4,6},{6,4},{8,10},{10,8},{12,14},{14,12},{16,18},{18,... | collective-permute-start | bytes 786440 | tf_op jit(solution)/shard_map/ppermute | solution.py:643
  170.3 3.8 collective-permute-start.8
  174.9 4.0 collective-permute-start.10
  179.0 10.2 %attention_forward.3 = (f32[1024,128]{1,0:T(8,128)}, bf16[1024,128]{1,0:T(8,128)(2,1)}, f32[8,1024]{1,0:T(8,128)}) custom-call(s32[3,2]{1,0:T(4,128)} %add_add_fusion.10.range_ref, s32[8,1024]{1,0:T(8,128)} %broadcast_in_dim.195.qseg_ref, s32[4096,128]{1,0:T(8,128)} %broadcast_in_dim.196.kseg_ref, bf16[1024,384]{1,0:T(8,128)(2,1)} %fusion.17.q_ref, ...), custom_call_target="tpu_custom_call" | custom-call | flops 8000000000 | bytes 8000000 | tf_op jit(solution)/shard_map/attention_forward/pallas_call | solution.py:504
  189.3 15.7 %collective-permute-start.11 = (bf16[512,512]{1,0:T(8,128)(2,1)S(1)}, bf16[512,512]{1,0:T(8,128)(2,1)}, u32[]{:S(2)}, u32[]{:S(2)}) collective-permute-start(bf16[512,512]{1,0:T(8,128)(2,1)S(1)} %slice_select_fusion), channel_id=1, source_target_pairs={{0,2},{2,0},{4,6},{6,4},{8,10},{10,8},{12,14},{14,12},{16,18},{18,... | collective-permute-start | bytes 1572872 | tf_op jit(solution)/shard_map/ppermute | solution.py:643
  206.7 6.5 %collective-permute-done.12 = bf16[1024,128]{1,0:T(8,128)(2,1)S(1)} collective-permute-done((bf16[1024,128]{1,0:T(8,128)(2,1)S(1)}, bf16[1024,128]{1,0:T(8,128)(2,1)S(1)}, u32[]{:S(2)}, u32[]{:S(2)}) %collective-permute-start.12) | collective-permute-done | bytes 262176 | tf_op jit(solution)/shard_map/ppermute | solution.py:620
  213.3 10.3 %attention_forward.4 = (f32[1024,128]{1,0:T(8,128)}, bf16[1024,128]{1,0:T(8,128)(2,1)}, f32[8,1024]{1,0:T(8,128)}) custom-call(s32[3,2]{1,0:T(4,128)} %add_add_fusion.10.range_ref, s32[8,1024]{1,0:T(8,128)} %broadcast_in_dim.195.qseg_ref, s32[4096,128]{1,0:T(8,128)} %broadcast_in_dim.196.kseg_ref, bf16[1024,384]{1,0:T(8,128)(2,1)} %fusion.17.q_ref, ...), custom_call_target="tpu_custom_call" | custom-call | flops 8000000000 | bytes 8000000 | tf_op jit(solution)/shard_map/attention_forward/pallas_call | solution.py:504
  225.2 10.4 %attention_forward.5 = (f32[1024,128]{1,0:T(8,128)}, bf16[1024,128]{1,0:T(8,128)(2,1)}, f32[8,1024]{1,0:T(8,128)}) custom-call(s32[3,2]{1,0:T(4,128)} %add_add_fusion.10.range_ref, s32[8,1024]{1,0:T(8,128)} %broadcast_in_dim.195.qseg_ref, s32[4096,128]{1,0:T(8,128)} %broadcast_in_dim.196.kseg_ref, bf16[1024,384]{1,0:T(8,128)(2,1)} %fusion.17.q_ref, ...), custom_call_target="tpu_custom_call" | custom-call | flops 8000000000 | bytes 8000000 | tf_op jit(solution)/shard_map/attention_forward/pallas_call | solution.py:504
  236.5 6.5 %collective-permute-done.14 = bf16[1024,128]{1,0:T(8,128)(2,1)S(1)} collective-permute-done((bf16[1024,128]{1,0:T(8,128)(2,1)}, bf16[1024,128]{1,0:T(8,128)(2,1)S(1)}, u32[]{:S(2)}, u32[]{:S(2)}) %collective-permute-start.14) | collective-permute-done | bytes 262176 | tf_op jit(solution)/shard_map/ppermute | solution.py:620
  250.9 9.7 %multiply_convert_fusion.1 = (bf16[512,1536]{1,0:T(8,128)(2,1)S(1)}, f32[512,1536]{1,0:T(8,128)S(1)}, f32[512,1536]{1,0:T(8,128)S(1)}) fusion(f32[1536]{0:T(1024)S(1)} %reshape.934, bf16[768,3072]{1,0:T(8,128)(2,1)} %all-gather.9.cloned.1.call-done, f32[512,768]{1,0:T(8,128)S(1)} %get-tuple-element.321, f32[768]{0:T(1024)S(1)} %get-tuple-element.199, ...), kind=kOutput, calls=%fused_computation.34 | convolution fusion | flops 1261830144 | bytes 11812864 | tf_op jit(solution)/shard_map/dot_general | solution.py:676
  262.7 8.0 %multiply_convert_fusion = (bf16[512,1536]{1,0:T(8,128)(2,1)S(1)}, f32[512,1536]{1,0:T(8,128)S(1)}, f32[512,1536]{1,0:T(8,128)S(1)}) fusion(f32[1536]{0:T(1024)S(1)} %reshape.934, bf16[768,3072]{1,0:T(8,128)(2,1)S(1)} %copy-done.91, f32[512,768]{1,0:T(8,128)S(1)} %get-tuple-element.318, f32[512]{0:T(512)S(1)} %fusion.93, ...), kind=kOutput, calls=%fused_computation.21 | convolution fusion | flops 1261830144 | bytes 11816960 | tf_op jit(solution)/shard_map/dot_general | solution.py:676
  273.8 9.0 %collective-permute-done.15 = bf16[512,768]{1,0:T(8,128)(2,1)S(1)} collective-permute-done((bf16[512,768]{1,0:T(8,128)(2,1)S(1)}, bf16[512,768]{1,0:T(8,128)(2,1)S(1)}, u32[]{:S(2)}, u32[]{:S(2)}) %collective-permute-start.15) | collective-permute-done | bytes 786464 | tf_op jit(solution)/shard_map/ppermute | solution.py:620
  287.2 3.0 fusion.144
  296.2 3.5 collective-permute-done.16
  314.7 15.7 %collective-permute-done.18 = bf16[512,768]{1,0:T(8,128)(2,1)} collective-permute-done((bf16[512,768]{1,0:T(8,128)(2,1)}, bf16[512,768]{1,0:T(8,128)(2,1)}, u32[]{:S(2)}, u32[]{:S(2)}) %collective-permute-start.18) | collective-permute-done | bytes 786464 | tf_op jit(solution)/shard_map/ppermute | solution.py:620
  330.4 2.9 multiply_reduce_fusion.5
  337.2 3.4 convolution_convert_fusion.2.do_ref
  340.9 15.6 %attention_backward.3 = (bf16[1024,128]{1,0:T(8,128)(2,1)}, f32[1024,256]{1,0:T(8,128)}, bf16[1024,256]{1,0:T(8,128)(2,1)}, bf16[1024,256]{1,0:T(8,128)(2,1)}, b...) custom-call(s32[3,4]{1,0:T(4,128)} %add_add_fusion.11.range_ref, s32[8,1024]{1,0:T(8,128)} %broadcast_in_dim.195.qseg_ref, ...), custom_call_target="tpu_custom_call" | custom-call | flops 8000000000 | bytes 12000000 | tf_op jit(solution)/shard_map/attention_backward/pallas_call | solution.py:587
  358.0 6.7 %collective-permute-start.22 = (bf16[512,256]{1,0:T(8,128)(2,1)}, bf16[512,256]{1,0:T(8,128)(2,1)}, u32[]{:S(2)}, u32[]{:S(2)}) collective-permute-start(bf16[512,256]{1,0:T(8,128)(2,1)} %get-tuple-element.154), channel_id=1, source_target_pairs={{0,4},{4,8},{6,2},{8,12},{10,6},{12,16},{14,10},{16,20},{18,14},{2... | collective-permute-start | bytes 786440 | tf_op jit(solution)/shard_map/ppermute | solution.py:655
  366.0 16.0 %attention_backward.4 = (bf16[1024,128]{1,0:T(8,128)(2,1)}, f32[1024,256]{1,0:T(8,128)}, bf16[1024,256]{1,0:T(8,128)(2,1)}, bf16[1024,256]{1,0:T(8,128)(2,1)}, b...) custom-call(s32[3,4]{1,0:T(4,128)} %add_add_fusion.11.range_ref, s32[8,1024]{1,0:T(8,128)} %broadcast_in_dim.195.qseg_ref, ...), custom_call_target="tpu_custom_call" | custom-call | flops 8000000000 | bytes 12000000 | tf_op jit(solution)/shard_map/attention_backward/pallas_call | solution.py:587
  382.0 5.5 collective-permute-start.26
  393.4 9.0 %collective-permute-done.26 = bf16[512,256]{1,0:T(8,128)(2,1)} collective-permute-done((bf16[512,256]{1,0:T(8,128)(2,1)}, bf16[512,256]{1,0:T(8,128)(2,1)}, u32[]{:S(2)}, u32[]{:S(2)}) %collective-permute-start.26) | collective-permute-done | bytes 262176 | tf_op jit(solution)/shard_map/ppermute | solution.py:655
  405.2 15.6 %attention_backward.5 = (bf16[1024,128]{1,0:T(8,128)(2,1)}, f32[1024,256]{1,0:T(8,128)}, bf16[1024,256]{1,0:T(8,128)(2,1)}, bf16[1024,256]{1,0:T(8,128)(2,1)}, b...) custom-call(s32[3,4]{1,0:T(4,128)} %add_add_fusion.11.range_ref, s32[8,1024]{1,0:T(8,128)} %broadcast_in_dim.195.qseg_ref, ...), custom_call_target="tpu_custom_call" | custom-call | flops 8000000000 | bytes 12000000 | tf_op jit(solution)/shard_map/attention_backward/pallas_call | solution.py:587
  420.8 13.2 %collective-permute-start.30 = (bf16[512,256]{1,0:T(8,128)(2,1)}, bf16[512,256]{1,0:T(8,128)(2,1)S(1)}, u32[]{:S(2)}, u32[]{:S(2)}) collective-permute-start(bf16[512,256]{1,0:T(8,128)(2,1)} %get-tuple-element.164), channel_id=1, source_target_pairs={{0,4},{4,8},{6,2},{8,12},{10,6},{12,16},{14,10},{16,20},{18,14},{2... | collective-permute-start | bytes 786440 | tf_op jit(solution)/shard_map/ppermute | solution.py:655
  438.1 2.9 constant_dynamic-update-slice_fusion.22
  441.0 6.3 collective-permute-start.27
  452.9 5.1 convolution_convert_fusion.1
  460.6 3.0 convolution_convert_fusion.3
  465.9 4.2 convolution_convert_fusion
  471.8 18.9 %collective-permute-done.31 = bf16[1024,768]{1,0:T(8,128)(2,1)} collective-permute-done((bf16[1024,768]{1,0:T(8,128)(2,1)}, bf16[1024,768]{1,0:T(8,128)(2,1)}, u32[]{:S(2)}, u32[]{:S(2)}) %collective-permute-start.31) | collective-permute-done | bytes 1572896 | tf_op jit(solution)/shard_map/ppermute | solution.py:620
  490.7 5.3 multiply_reduce_fusion
  496.3 2.8 fusion.124
  505.0 36.6 %tap_gradient.1 = bf16[16,400,384]{2,1,0:T(8,128)(2,1)} custom-call(s32[1]{0:T(128)} %bitcast.1.n_ref, bf16[2,8,256,304]{3,2,1,0:T(8,128)(2,1)} %get-tuple-element.167.xt_ref, bf16[2,4,304,1152]{3,2,1,0:T(8,128)(2,1)} %get-tuple-element.168.s_ref, bf16[2,33,304,128]{3,2,1,0:T(8,128)(2,1)} %get-tuple-element.169.mask_ref, bf16[1152,384]{1,0:T(8,128)(2,1)} %pad.10.d_ref, ...), custom_call_target="tpu_custom_call" | custom-call | flops 1000000000 | bytes 15000000 | tf_op jit(solution)/shard_map/tap_gradient/pallas_call | solution.py:137
  541.6 5.9 reduce-scatter.6.cloned.1.call-done
  549.9 3.4 pad_maximum_fusion.1
  555.5 3.4 collective-permute-start.32
  560.9 27.3 %conv_back.1 = f32[1024,384]{1,0:T(8,128)} custom-call(s32[1]{0:T(128)} %bitcast.1.n_ref, bf16[1152,384]{1,0:T(8,128)(2,1)} %pad_maximum_fusion.5.d_ref, bf16[2,4,304,1152]{3,2,1,0:T(8,128)(2,1)} %get-tuple-element.168.s_ref, bf16[2,33,272,128]{3,2,1,0:T(8,128)(2,1)} %get-tuple-element.114.refs_1_.refs_0_, ...), custom_call_target="tpu_custom_call" | custom-call | flops 24999999488 | bytes 15000000 | tf_op jit(solution)/shard_map/conv_back/pallas_call | solution.py:137
  592.4 15.4 %collective-permute-done.34 = bf16[1024,384]{1,0:T(8,128)(2,1)S(1)} collective-permute-done((bf16[1024,384]{1,0:T(8,128)(2,1)S(1)}, bf16[1024,384]{1,0:T(8,128)(2,1)S(1)}, u32[]{:S(2)}, u32[]{:S(2)}) %collective-permute-start.34) | collective-permute-done | bytes 786464 | tf_op jit(solution)/shard_map/ppermute | solution.py:620
  613.6 19.0 %reduce-scatter.8.cloned.1.call-done = bf16[1,400,384]{2,1,0:T(8,128)(2,1)} async-done(((bf16[16,400,384]{2,1,0:T(8,128)(2,1)}), bf16[1,400,384]{2,1,0:T(8,128)(2,1)}) %reduce-scatter.8.cloned.1.call-update) | async-done | bytes 307216 | tf_op jit(solution)/shard_map/reduce_scatter | solution.py:684
  (487 shorter events, 143.6 us)
Async XLA Ops:
  7.3 59.9 %all-gather.5.cloned.1.call-start = ((), (), s32[]{:S(2)}) async-start(), calls=%async_computation.3 | async-start | bytes 5013504 | tf_op jit(solution)/shard_map/all_gather | solution.py:680
  9.3 116.6 %all-gather.7.cloned.1.call-start = ((), (), s32[]{:S(2)}) async-start(), calls=%async_computation.4 | async-start | bytes 2506752 | tf_op jit(solution)/shard_map/all_gather | solution.py:680
  10.9 35.9 %collective-permute-start.1 = (bf16[64,384]{1,0:T(8,128)(2,1)S(1)}, bf16[64,384]{1,0:T(8,128)(2,1)S(1)}, u32[]{:S(2)}, u32[]{:S(2)}) collective-permute-start(bf16[64,384]{1,0:T(8,128)(2,1)S(1)} %get-tuple-element.293), channel_id=1, source_target_pairs={{2,0},{4,2},{6,4},{8,6},{10,8},{12,10},{14,12},{16,14},{18,16},{20... | collective-permute-start | bytes 147464 | tf_op jit(solution)/shard_map/ppermute | solution.py:639
  12.2 34.7 %collective-permute-start = (bf16[64,384]{1,0:T(8,128)(2,1)S(1)}, bf16[64,384]{1,0:T(8,128)(2,1)S(1)}, u32[]{:S(2)}, u32[]{:S(2)}) collective-permute-start(bf16[64,384]{1,0:T(8,128)(2,1)S(1)} %get-tuple-element.292), channel_id=1, source_target_pairs={{0,2},{2,4},{4,6},{6,8},{8,10},{10,12},{12,14},{14,16},{16,18},{18... | collective-permute-start | bytes 147464 | tf_op jit(solution)/shard_map/ppermute | solution.py:639
  16.1 234.8 %all-gather.9.cloned.1.call-start = ((), (), s32[]{:S(2)}) async-start(), calls=%async_computation.5 | async-start | bytes 5013504 | tf_op jit(solution)/shard_map/all_gather | solution.py:680
  46.8 48.5 %copy-start.67 = (f32[384]{0:T(512)}, f32[384]{0:T(512)S(1)}, u32[]{:S(2)}) copy-start(f32[384]{0:T(512)S(1)} %add.698) | copy-start | bytes 4612
  101.1 20.1 %collective-permute-start.2 = (bf16[1024,384]{1,0:T(8,128)(2,1)}, bf16[1024,384]{1,0:T(8,128)(2,1)}, u32[]{:S(2)}, u32[]{:S(2)}) collective-permute-start(bf16[1024,384]{1,0:T(8,128)(2,1)} %get-tuple-element.278), channel_id=1, source_target_pairs={{0,1},{1,0},{2,3},{3,2},{4,5},{5,4},{6,7},{7,6},{8,9},{9,8},{10,11... | collective-permute-start | bytes 2359304 | tf_op jit(solution)/shard_map/ppermute | solution.py:620
  103.4 354.6 %reduce-scatter.4.cloned.1.call-start = ((), (), s32[]{:S(2)}) async-start(), calls=%async_computation.6 | async-start | bytes 5013504 | tf_op jit(solution)/shard_map/reduce_scatter | solution.py:684
  133.4 40.7 %copy-start.5 = (bf16[1024,768]{1,0:T(8,128)(2,1)}, bf16[1024,768]{1,0:T(8,128)(2,1)S(1)}, u32[]{:S(2)}) copy-start(bf16[1024,768]{1,0:T(8,128)(2,1)S(1)} %fusion.2.k0) | copy-start | bytes 4718596
  133.4 8.1 %collective-permute-start.4 = (bf16[1024,256]{1,0:T(8,128)(2,1)S(1)}, bf16[1024,256]{1,0:T(8,128)(2,1)S(1)}, u32[]{:S(2)}, u32[]{:S(2)}) collective-permute-start(bf16[1024,256]{1,0:T(8,128)(2,1)S(1)} %slice.343), channel_id=1, source_target_pairs={{2,4},{4,2},{6,8},{8,6},{10,12},{12,10},{14,16},{16,14},{18,20},{2... | collective-permute-start | bytes 1572872 | tf_op jit(solution)/shard_map/ppermute | solution.py:649
  134.5 29.7 %collective-permute-start.3 = (bf16[1024,256]{1,0:T(8,128)(2,1)S(1)}, bf16[1024,256]{1,0:T(8,128)(2,1)}, u32[]{:S(2)}, u32[]{:S(2)}) collective-permute-start(bf16[1024,256]{1,0:T(8,128)(2,1)S(1)} %slice.343), channel_id=1, source_target_pairs={{0,2},{2,0},{4,6},{6,4},{8,10},{10,8},{12,14},{14,12},{16,18},{18,... | collective-permute-start | bytes 1572872 | tf_op jit(solution)/shard_map/ppermute | solution.py:643
  136.4 27.7 %collective-permute-start.5 = (bf16[512,256]{1,0:T(8,128)(2,1)S(1)}, bf16[512,256]{1,0:T(8,128)(2,1)}, u32[]{:S(2)}, u32[]{:S(2)}) collective-permute-start(bf16[512,256]{1,0:T(8,128)(2,1)S(1)} %slice_select_fusion.3), channel_id=1, source_target_pairs={{0,4},{4,8},{6,2},{8,12},{10,6},{12,16},{14,10},{16,20},{18,14},{2... | collective-permute-start | bytes 786440 | tf_op jit(solution)/shard_map/ppermute | solution.py:655
  142.3 22.2 %collective-permute-start.6 = (bf16[512,256]{1,0:T(8,128)(2,1)}, bf16[512,256]{1,0:T(8,128)(2,1)}, u32[]{:S(2)}, u32[]{:S(2)}) collective-permute-start(bf16[512,256]{1,0:T(8,128)(2,1)} %slice_select_fusion.2), channel_id=1, source_target_pairs={{0,2},{2,0},{4,6},{6,4},{8,10},{10,8},{12,14},{14,12},{16,18},{18,... | collective-permute-start | bytes 786440 | tf_op jit(solution)/shard_map/ppermute | solution.py:643
  165.5 23.7 %collective-permute-start.9 = (bf16[1024,512]{1,0:T(8,128)(2,1)}, bf16[1024,512]{1,0:T(8,128)(2,1)S(1)}, u32[]{:S(2)}, u32[]{:S(2)}) collective-permute-start(bf16[1024,512]{1,0:T(8,128)(2,1)} %slice.277), channel_id=1, source_target_pairs={{2,4},{4,2},{6,8},{8,6},{10,12},{12,10},{14,16},{16,14},{18,20},{2... | collective-permute-start | bytes 3145736 | tf_op jit(solution)/shard_map/ppermute | solution.py:649
  168.7 38.0 %collective-permute-start.7 = (bf16[768,384]{1,0:T(8,128)(2,1)S(1)}, bf16[768,384]{1,0:T(8,128)(2,1)}, u32[]{:S(2)}, u32[]{:S(2)}) collective-permute-start(bf16[768,384]{1,0:T(8,128)(2,1)S(1)} %slice.337), channel_id=1, source_target_pairs={{0,1},{1,0},{2,3},{3,2},{4,5},{5,4},{6,7},{7,6},{8,9},{9,8},{10,11... | collective-permute-start | bytes 1769480 | tf_op jit(solution)/shard_map/ppermute | solution.py:620
  170.3 42.9 %collective-permute-start.8 = (bf16[1024,512]{1,0:T(8,128)(2,1)}, bf16[1024,512]{1,0:T(8,128)(2,1)}, u32[]{:S(2)}, u32[]{:S(2)}) collective-permute-start(bf16[1024,512]{1,0:T(8,128)(2,1)} %slice.277), channel_id=1, source_target_pairs={{0,2},{2,0},{4,6},{6,4},{8,10},{10,8},{12,14},{14,12},{16,18},{18,... | collective-permute-start | bytes 3145736 | tf_op jit(solution)/shard_map/ppermute | solution.py:643
  174.9 38.3 %collective-permute-start.10 = (bf16[512,512]{1,0:T(8,128)(2,1)}, bf16[512,512]{1,0:T(8,128)(2,1)}, u32[]{:S(2)}, u32[]{:S(2)}) collective-permute-start(bf16[512,512]{1,0:T(8,128)(2,1)} %slice_select_fusion.1), channel_id=1, source_target_pairs={{0,4},{4,8},{6,2},{8,12},{10,6},{12,16},{14,10},{16,20},{18,14},{2... | collective-permute-start | bytes 1572872 | tf_op jit(solution)/shard_map/ppermute | solution.py:655
  189.3 24.0 %collective-permute-start.11 = (bf16[512,512]{1,0:T(8,128)(2,1)S(1)}, bf16[512,512]{1,0:T(8,128)(2,1)}, u32[]{:S(2)}, u32[]{:S(2)}) collective-permute-start(bf16[512,512]{1,0:T(8,128)(2,1)S(1)} %slice_select_fusion), channel_id=1, source_target_pairs={{0,2},{2,0},{4,6},{6,4},{8,10},{10,8},{12,14},{14,12},{16,18},{18,... | collective-permute-start | bytes 1572872 | tf_op jit(solution)/shard_map/ppermute | solution.py:643
  204.9 8.3 %collective-permute-start.12 = (bf16[1024,128]{1,0:T(8,128)(2,1)S(1)}, bf16[1024,128]{1,0:T(8,128)(2,1)S(1)}, u32[]{:S(2)}, u32[]{:S(2)}) collective-permute-start(bf16[1024,128]{1,0:T(8,128)(2,1)S(1)} %copy-done.49), channel_id=1, source_target_pairs={{0,1},{1,0},{2,3},{3,2},{4,5},{5,4},{6,7},{7,6},{8,9},{9,8},{10,11... | collective-permute-start | bytes 786440 | tf_op jit(solution)/shard_map/ppermute | solution.py:620
  223.5 12.9 %collective-permute-start.13 = (bf16[1024,128]{1,0:T(8,128)(2,1)}, bf16[1024,128]{1,0:T(8,128)(2,1)S(1)}, u32[]{:S(2)}, u32[]{:S(2)}) collective-permute-start(bf16[1024,128]{1,0:T(8,128)(2,1)} %get-tuple-element.130), channel_id=1, source_target_pairs={{0,1},{1,0},{2,3},{3,2},{4,5},{5,4},{6,7},{7,6},{8,9},{9,8},{10,11... | collective-permute-start | bytes 786440 | tf_op jit(solution)/shard_map/ppermute | solution.py:620
  235.6 7.4 %collective-permute-start.14 = (bf16[1024,128]{1,0:T(8,128)(2,1)}, bf16[1024,128]{1,0:T(8,128)(2,1)S(1)}, u32[]{:S(2)}, u32[]{:S(2)}) collective-permute-start(bf16[1024,128]{1,0:T(8,128)(2,1)} %get-tuple-element.132), channel_id=1, source_target_pairs={{0,1},{1,0},{2,3},{3,2},{4,5},{5,4},{6,7},{7,6},{8,9},{9,8},{10,11... | collective-permute-start | bytes 786440 | tf_op jit(solution)/shard_map/ppermute | solution.py:620
  262.2 20.5 %collective-permute-start.15 = (bf16[512,768]{1,0:T(8,128)(2,1)S(1)}, bf16[512,768]{1,0:T(8,128)(2,1)S(1)}, u32[]{:S(2)}, u32[]{:S(2)}) collective-permute-start(bf16[512,768]{1,0:T(8,128)(2,1)S(1)} %fusion.51), channel_id=1, source_target_pairs={{0,1},{1,0},{2,3},{3,2},{4,5},{5,4},{6,7},{7,6},{8,9},{9,8},{10,11... | collective-permute-start | bytes 2359304 | tf_op jit(solution)/shard_map/ppermute | solution.py:620
  272.1 27.5 %collective-permute-start.16 = (bf16[512,768]{1,0:T(8,128)(2,1)S(1)}, bf16[512,768]{1,0:T(8,128)(2,1)S(1)}, u32[]{:S(2)}, u32[]{:S(2)}) collective-permute-start(bf16[512,768]{1,0:T(8,128)(2,1)S(1)} %fusion.54), channel_id=1, source_target_pairs={{0,1},{1,0},{2,3},{3,2},{4,5},{5,4},{6,7},{7,6},{8,9},{9,8},{10,11... | collective-permute-start | bytes 2359304 | tf_op jit(solution)/shard_map/ppermute | solution.py:620
  292.6 40.8 %collective-permute-start.17 = (bf16[512,768]{1,0:T(8,128)(2,1)}, bf16[512,768]{1,0:T(8,128)(2,1)}, u32[]{:S(2)}, u32[]{:S(2)}) collective-permute-start(bf16[512,768]{1,0:T(8,128)(2,1)} %fusion.45), channel_id=1, source_target_pairs={{0,1},{1,0},{2,3},{3,2},{4,5},{5,4},{6,7},{7,6},{8,9},{9,8},{10,11... | collective-permute-start | bytes 2359304 | tf_op jit(solution)/shard_map/ppermute | solution.py:620
  308.3 22.1 %collective-permute-start.18 = (bf16[512,768]{1,0:T(8,128)(2,1)}, bf16[512,768]{1,0:T(8,128)(2,1)}, u32[]{:S(2)}, u32[]{:S(2)}) collective-permute-start(bf16[512,768]{1,0:T(8,128)(2,1)} %fusion.48), channel_id=1, source_target_pairs={{0,1},{1,0},{2,3},{3,2},{4,5},{5,4},{6,7},{7,6},{8,9},{9,8},{10,11... | collective-permute-start | bytes 2359304 | tf_op jit(solution)/shard_map/ppermute | solution.py:620
  337.1 123.4 %copy-start.12 = (f32[512,768]{1,0:T(8,128)}, f32[512,768]{1,0:T(8,128)S(1)}, u32[]{:S(2)}) copy-start(f32[512,768]{1,0:T(8,128)S(1)} %get-tuple-element.246) | copy-start | bytes 4718596
  337.2 123.4 %copy-start.13 = (f32[512,768]{1,0:T(8,128)}, f32[512,768]{1,0:T(8,128)S(1)}, u32[]{:S(2)}) copy-start(f32[512,768]{1,0:T(8,128)S(1)} %get-tuple-element.328) | copy-start | bytes 4718596
  340.6 206.9 %reduce-scatter.6.cloned.1.call-start = ((), (), s32[]{:S(2)}) async-start(), calls=%async_computation.7 | async-start | bytes 2506752 | tf_op jit(solution)/shard_map/reduce_scatter | solution.py:684
  356.5 48.7 %collective-permute-start.19 = (bf16[1024,256]{1,0:T(8,128)(2,1)}, bf16[1024,256]{1,0:T(8,128)(2,1)}, u32[]{:S(2)}, u32[]{:S(2)}) collective-permute-start(bf16[1024,256]{1,0:T(8,128)(2,1)} %get-tuple-element.144), channel_id=1, source_target_pairs={{0,2},{2,0},{4,6},{6,4},{8,10},{10,8},{12,14},{14,12},{16,18},{18,... | collective-permute-start | bytes 1572872 | tf_op jit(solution)/shard_map/ppermute | solution.py:643
  356.5 48.7 %collective-permute-start.20 = (bf16[1024,256]{1,0:T(8,128)(2,1)}, bf16[1024,256]{1,0:T(8,128)(2,1)}, u32[]{:S(2)}, u32[]{:S(2)}) collective-permute-start(bf16[1024,256]{1,0:T(8,128)(2,1)} %get-tuple-element.145), channel_id=1, source_target_pairs={{2,4},{4,2},{6,8},{8,6},{10,12},{12,10},{14,16},{16,14},{18,20},{2... | collective-permute-start | bytes 1572872 | tf_op jit(solution)/shard_map/ppermute | solution.py:649
  358.0 32.3 %collective-permute-start.22 = (bf16[512,256]{1,0:T(8,128)(2,1)}, bf16[512,256]{1,0:T(8,128)(2,1)}, u32[]{:S(2)}, u32[]{:S(2)}) collective-permute-start(bf16[512,256]{1,0:T(8,128)(2,1)} %get-tuple-element.154), channel_id=1, source_target_pairs={{0,4},{4,8},{6,2},{8,12},{10,6},{12,16},{14,10},{16,20},{18,14},{2... | collective-permute-start | bytes 786440 | tf_op jit(solution)/shard_map/ppermute | solution.py:655
  364.7 26.9 %collective-permute-start.21 = (bf16[512,256]{1,0:T(8,128)(2,1)}, bf16[512,256]{1,0:T(8,128)(2,1)}, u32[]{:S(2)}, u32[]{:S(2)}) collective-permute-start(bf16[512,256]{1,0:T(8,128)(2,1)} %get-tuple-element.153), channel_id=1, source_target_pairs={{2,6},{4,0},{6,10},{8,4},{10,14},{12,8},{14,18},{16,12},{18,22},{2... | collective-permute-start | bytes 786440 | tf_op jit(solution)/shard_map/ppermute | solution.py:655
  382.0 20.4 %collective-permute-start.26 = (bf16[512,256]{1,0:T(8,128)(2,1)}, bf16[512,256]{1,0:T(8,128)(2,1)}, u32[]{:S(2)}, u32[]{:S(2)}) collective-permute-start(bf16[512,256]{1,0:T(8,128)(2,1)} %get-tuple-element.159), channel_id=1, source_target_pairs={{0,4},{4,8},{6,2},{8,12},{10,6},{12,16},{14,10},{16,20},{18,14},{2... | collective-permute-start | bytes 786440 | tf_op jit(solution)/shard_map/ppermute | solution.py:655
  390.3 13.9 %collective-permute-start.25 = (bf16[512,256]{1,0:T(8,128)(2,1)}, bf16[512,256]{1,0:T(8,128)(2,1)S(1)}, u32[]{:S(2)}, u32[]{:S(2)}) collective-permute-start(bf16[512,256]{1,0:T(8,128)(2,1)} %get-tuple-element.158), channel_id=1, source_target_pairs={{2,6},{4,0},{6,10},{8,4},{10,14},{12,8},{14,18},{16,12},{18,22},{2... | collective-permute-start | bytes 786440 | tf_op jit(solution)/shard_map/ppermute | solution.py:655
  391.6 49.4 %collective-permute-start.24 = (bf16[1024,256]{1,0:T(8,128)(2,1)}, bf16[1024,256]{1,0:T(8,128)(2,1)S(1)}, u32[]{:S(2)}, u32[]{:S(2)}) collective-permute-start(bf16[1024,256]{1,0:T(8,128)(2,1)} %get-tuple-element.157), channel_id=1, source_target_pairs={{2,4},{4,2},{6,8},{8,6},{10,12},{12,10},{14,16},{16,14},{18,20},{2... | collective-permute-start | bytes 1572872 | tf_op jit(solution)/shard_map/ppermute | solution.py:649
  402.4 44.8 %collective-permute-start.23 = (bf16[1024,256]{1,0:T(8,128)(2,1)}, bf16[1024,256]{1,0:T(8,128)(2,1)}, u32[]{:S(2)}, u32[]{:S(2)}) collective-permute-start(bf16[1024,256]{1,0:T(8,128)(2,1)} %get-tuple-element.156), channel_id=1, source_target_pairs={{0,2},{2,0},{4,6},{6,4},{8,10},{10,8},{12,14},{14,12},{16,18},{18,... | collective-permute-start | bytes 1572872 | tf_op jit(solution)/shard_map/ppermute | solution.py:643
  420.8 28.8 %collective-permute-start.30 = (bf16[512,256]{1,0:T(8,128)(2,1)}, bf16[512,256]{1,0:T(8,128)(2,1)S(1)}, u32[]{:S(2)}, u32[]{:S(2)}) collective-permute-start(bf16[512,256]{1,0:T(8,128)(2,1)} %get-tuple-element.164), channel_id=1, source_target_pairs={{0,4},{4,8},{6,2},{8,12},{10,6},{12,16},{14,10},{16,20},{18,14},{2... | collective-permute-start | bytes 786440 | tf_op jit(solution)/shard_map/ppermute | solution.py:655
  434.0 15.6 %collective-permute-start.29 = (bf16[512,256]{1,0:T(8,128)(2,1)}, bf16[512,256]{1,0:T(8,128)(2,1)S(1)}, u32[]{:S(2)}, u32[]{:S(2)}) collective-permute-start(bf16[512,256]{1,0:T(8,128)(2,1)} %get-tuple-element.163), channel_id=1, source_target_pairs={{2,6},{4,0},{6,10},{8,4},{10,14},{12,8},{14,18},{16,12},{18,22},{2... | collective-permute-start | bytes 786440 | tf_op jit(solution)/shard_map/ppermute | solution.py:655
  435.3 14.4 %collective-permute-start.28 = (bf16[1024,256]{1,0:T(8,128)(2,1)}, bf16[1024,256]{1,0:T(8,128)(2,1)S(1)}, u32[]{:S(2)}, u32[]{:S(2)}) collective-permute-start(bf16[1024,256]{1,0:T(8,128)(2,1)} %get-tuple-element.162), channel_id=1, source_target_pairs={{2,4},{4,2},{6,8},{8,6},{10,12},{12,10},{14,16},{16,14},{18,20},{2... | collective-permute-start | bytes 1572872 | tf_op jit(solution)/shard_map/ppermute | solution.py:649
  441.0 8.7 %collective-permute-start.27 = (bf16[1024,256]{1,0:T(8,128)(2,1)S(1)}, bf16[1024,256]{1,0:T(8,128)(2,1)S(1)}, u32[]{:S(2)}, u32[]{:S(2)}) collective-permute-start(bf16[1024,256]{1,0:T(8,128)(2,1)S(1)} %copy-done.92), channel_id=1, source_target_pairs={{0,2},{2,0},{4,6},{6,4},{8,10},{10,8},{12,14},{14,12},{16,18},{18,... | collective-permute-start | bytes 1572872 | tf_op jit(solution)/shard_map/ppermute | solution.py:643
  459.8 30.8 %collective-permute-start.31 = (bf16[1024,768]{1,0:T(8,128)(2,1)}, bf16[1024,768]{1,0:T(8,128)(2,1)}, u32[]{:S(2)}, u32[]{:S(2)}) collective-permute-start(bf16[1024,768]{1,0:T(8,128)(2,1)} %convolution_convert_fusion.1), channel_id=1, source_target_pairs={{0,1},{1,0},{2,3},{3,2},{4,5},{5,4},{6,7},{7,6},{8,9},{9,8},{10,11... | collective-permute-start | bytes 4718600 | tf_op jit(solution)/shard_map/ppermute | solution.py:620
  471.7 160.9 %reduce-scatter.8.cloned.1.call-start = ((), (), s32[]{:S(2)}) async-start(), calls=%async_computation.8 | async-start | bytes 5222400 | tf_op jit(solution)/shard_map/reduce_scatter | solution.py:684
  554.2 36.7 %copy-start.21 = (f32[48,1536]{1,0:T(8,128)}, f32[48,1536]{1,0:T(8,128)S(1)}, u32[]{:S(2)}) copy-start(f32[48,1536]{1,0:T(8,128)S(1)} %get-tuple-element.228) | copy-start | bytes 884740
  554.2 5.7 collective-permute-start.33
  555.5 4.4 collective-permute-start.32
  559.9 31.8 %copy-start.22 = (f32[1536,48]{0,1:T(8,128)}, f32[1536,48]{0,1:T(8,128)S(1)}, u32[]{:S(2)}) copy-start(f32[1536,48]{0,1:T(8,128)S(1)} %get-tuple-element.224) | copy-start | bytes 884740
  560.9 30.7 %copy-start.43 = (f32[1536,48]{0,1:T(8,128)S(1)}, f32[1536,48]{0,1:T(8,128)}, u32[]{:S(2)}) copy-start(f32[1536,48]{0,1:T(8,128)} %param.47) | copy-start | bytes 884740
  589.9 17.9 %collective-permute-start.34 = (bf16[1024,384]{1,0:T(8,128)(2,1)S(1)}, bf16[1024,384]{1,0:T(8,128)(2,1)S(1)}, u32[]{:S(2)}, u32[]{:S(2)}) collective-permute-start(bf16[1024,384]{1,0:T(8,128)(2,1)S(1)} %convert_element_type.285), channel_id=1, source_target_pairs={{0,1},{1,0},{2,3},{3,2},{4,5},{5,4},{6,7},{7,6},{8,9},{9,8},{10,11... | collective-permute-start | bytes 2359304 | tf_op jit(solution)/shard_map/ppermute | solution.py:620
  (87 other events, 726.1 us)
Sparse Core Ops, SparseCore 0:
  10.9 56.1 all-gather.4
  70.0 40.8 all-gather.6
  113.8 65.4 all-gather.8
  340.7 104.5 reduce-scatter.3
  471.8 75.6 reduce-scatter.5
  551.3 81.1 reduce-scatter.7

commit v7 on v6

--- a/solution.py
+++ b/solution.py
@@ -9,7 +9,7 @@
 
 HEAD = 64
 PAIRS = 3
-CHUNKS = 2
+
 EPSILON = 1e-05
 
 bf16, f32, i32 = jnp.bfloat16, jnp.float32, jnp.int32
@@ -816,8 +816,7 @@
     w_combine_all = side_by_side(w_combine, w_combine_far, index)
     w_expand = w_second[:, :hidden_units]
     w_shrink = w_second[:, hidden_units:]
-    step = rows // CHUNKS
-    cuts_of = [slice(c * step, (c + 1) * step) for c in range(CHUNKS)]
+    cuts_of = [slice(0, rows * 3 // 8), slice(rows * 3 // 8, rows)]
     first_half, second_half = [], []
     for cut in cuts_of:
         branch = dot(attended_all[cut], w_combine_all, 1, 1)
@@ -865,13 +864,14 @@
     d_att = dot(d_branch, w_combine, 1, 0).astype(bf16)
     d_att, second_part = lax.optimization_barrier((d_att, second_part))
     second_sum = scattered(second_part).astype(f32)
+    combine_part = dot(d_branch, attended, 0, 0).astype(bf16)
     dq_parts, kv_parts = [], []
     arrived = {}
     for h in range(PAIRS):
         d_part = d_att
         if h >= 2:
             two = arrived[h - 2][:2]
-            d_part, two = lax.optimization_barrier((d_att, two))
+            d_part, two, combine_part = lax.optimization_barrier((d_att, two, combine_part))
             arrived[h - 2] = two + arrived[h - 2][2:]
         dq_part, own, core, chip, far, beyond = attend_back(
             reach, h, queries, pieces[h], d_part, mixed[h], lse[h]
@@ -902,7 +902,7 @@
     dh1 = dx2 + (dh1_half.astype(f32) + exchange(dh1_half).astype(f32))
     first_part = (
         jnp.concatenate(
-            [dot(h1_half, stacked, 0, 0).astype(bf16), dot(d_branch, attended, 0, 0).astype(bf16)],
+            [dot(h1_half, stacked, 0, 0).astype(bf16), combine_part],
             axis=1,
         )
     )

time: 658 us -> 656 us (level)
    ppermute x4, waiting for transfers between devices: 0.01 us -> 10.9 us  [passed(): return lax.ppermute(block, 'seq', route)]
    ppermute x11, waiting for transfers between devices: 92.7 us -> 84.4 us  [exchange(): return lax.ppermute(part, 'heads', [(0, 1), (1, 0)])]
    unnamed x213 -> x231, local copies, waits for them, and re-layouts: 21.7 us -> 22 us
  transfers between devices with their start and end apart: 41 -> 41, of which waited for: 13 -> 12; matrix products, arithmetic and copies ran while one was open for 21% -> 21% of each run, Pallas kernels for 28% -> 28%
where the time goes in v7:
time: 656 us; the launch traced here: 646 us
  Pallas kernels  184 us (28%)
  waiting for transfers between devices  124 us (19%)
  starting transfers between devices  113 us (17%)
  other arithmetic  80.5 us (12%)
  matrix products  60.9 us (9%)
  local copies, waits for them, and re-layouts  39.3 us (6%)
  blocking collectives  25.2 us (4%)
  between operations  19.2 us (3%)
    pallas_call x4, Pallas kernels, call(): pl.pallas_call(kernel, grid_spec=pltpu.PrefetchScalarGridSpec(num_scalar_...  106 us
    ppermute x11, waiting for transfers between devices, exchange(): return lax.ppermute(part, 'heads', [(0, 1), (1, 0)])  84.4 us
    dot_general x19, matrix products, dot(): lax.dot_general(a, b, (((ca,), (cb,)), ((), ())), preferred_element_type=...  60.9 us
    ppermute x7, starting transfers between devices, across_cores(): lax.ppermute(block, 'seq', [(i, i ^ 1) for i in range(lax.axis_size('seq'...  48.5 us
    pallas_call x3, Pallas kernels, attend_back(): pl.pallas_call(backward_kernel, grid=(ROWS // QT_BACK,), out_shape=(jax.S...  47.3 us
    ppermute x8, starting transfers between devices, chip_along(): lax.ppermute(block, 'seq', [(i, j) for i, j in route if 0 <= j < count])  37.1 us
    pallas_call x3, Pallas kernels, attend(): pl.pallas_call(forward_kernel, grid=(ROWS // QT_AHEAD,), out_shape=(jax.S...  30.9 us
    all_gather x1, blocking collectives, gathered(): return lax.all_gather(shard, 'seq', axis=0, tiled=True)  25.2 us
  transfers between devices with their start and end apart: 41, of which 12 were waited for; matrix products, arithmetic and copies ran while one was open for 21% of the time, Pallas kernels for 28%

profile of v7, /device:TPU:0, one launch (start us, length us, event | category | flops | bytes accessed | tf_op | source)
XLA Modules:
  0.0 646.2 jit_solution(14347170459215024659)
XLA Ops:
  17.2 25.2 %all-gather = bf16[16,1,552]{2,1,0:T(2,128)(2,1)S(1)} all-gather(bf16[1,1,552]{2,1,0:T(2,128)(2,1)S(1)} %maximum_bitcast_fusion.2), channel_id=1, replica_groups=mesh['seq'=16,'heads'=2] {'seq'}, dimensions={0}, use_global_device_ids=true | all-gather | bytes 18768 | tf_op jit(solution)/shard_map/all_gather | solution.py:680
  49.4 2.9 broadcast_in_dim.196.kseg_ref
  54.8 13.1 %conv_prepare.1 = (bf16[2,4,304,1152]{3,2,1,0:T(8,128)(2,1)}, bf16[2,1024,1088]{2,1,0:T(8,128)(2,1)}, bf16[2,33,272,128]{3,2,1,0:T(8,128)(2,1)}, bf16[2,33,304,1...) custom-call(s32[1]{0:T(128)} %bitcast.1.n_ref, ...), custom_call_target="tpu_custom_call" | custom-call | flops 10000000000 | bytes 15000000 | tf_op jit(solution)/shard_map/conv_prepare/pallas_call | solution.py:137
  67.9 28.4 %conv_forward.1 = (f32[1024,384]{1,0:T(8,128)}, bf16[8,134,64,128]{3,2,1,0:T(8,128)(2,1)}) custom-call(s32[1]{0:T(128)} %bitcast.1.n_ref, bf16[2,8,304,256]{3,2,1,0:T(8,128)(2,1)} %get-tuple-element.114.refs_0_, bf16[2,33,272,128]{3,2,1,0:T(8,128)(2,1)} %get-tuple-element.115.refs_1_.refs_0_, bf16[2,1024,1088]{2,1,0:T(8,128)(2,1)} %get-tuple-element.116.refs_2_.refs_1_, ...), custom_call_target="tpu_custom_call" | custom-call | flops 24999999488 | bytes 15000000 | tf_op jit(solution)/shard_map/conv_forward/pallas_call | solution.py:137
  96.4 5.7 multiply_convert_fusion.2
  104.9 17.3 %collective-permute-done.2 = bf16[1024,384]{1,0:T(8,128)(2,1)} collective-permute-done((bf16[1024,384]{1,0:T(8,128)(2,1)}, bf16[1024,384]{1,0:T(8,128)(2,1)}, u32[]{:S(2)}, u32[]{:S(2)}) %collective-permute-start.2) | collective-permute-done | bytes 786464 | tf_op jit(solution)/shard_map/ppermute | solution.py:620
  122.2 2.5 fusion.140
  128.5 3.7 fusion.25
  136.6 5.0 collective-permute-start.5
  142.3 21.2 %collective-permute-start.6 = (bf16[512,256]{1,0:T(8,128)(2,1)}, bf16[512,256]{1,0:T(8,128)(2,1)}, u32[]{:S(2)}, u32[]{:S(2)}) collective-permute-start(bf16[512,256]{1,0:T(8,128)(2,1)} %slice_select_fusion.2), channel_id=1, source_target_pairs={{0,2},{2,0},{4,6},{6,4},{8,10},{10,8},{12,14},{14,12},{16,18},{18,... | collective-permute-start | bytes 786440 | tf_op jit(solution)/shard_map/ppermute | solution.py:643
  170.8 3.8 collective-permute-start.8
  175.4 3.1 collective-permute-start.10
  178.5 10.3 %attention_forward.3 = (f32[1024,128]{1,0:T(8,128)}, bf16[1024,128]{1,0:T(8,128)(2,1)}, f32[8,1024]{1,0:T(8,128)}) custom-call(s32[3,2]{1,0:T(4,128)} %add_add_fusion.10.range_ref, s32[8,1024]{1,0:T(8,128)} %broadcast_in_dim.195.qseg_ref, s32[4096,128]{1,0:T(8,128)} %broadcast_in_dim.196.kseg_ref, bf16[1024,384]{1,0:T(8,128)(2,1)} %fusion.18.q_ref, ...), custom_call_target="tpu_custom_call" | custom-call | flops 8000000000 | bytes 8000000 | tf_op jit(solution)/shard_map/attention_forward/pallas_call | solution.py:504
  188.8 16.7 %collective-permute-start.11 = (bf16[512,512]{1,0:T(8,128)(2,1)S(1)}, bf16[512,512]{1,0:T(8,128)(2,1)}, u32[]{:S(2)}, u32[]{:S(2)}) collective-permute-start(bf16[512,512]{1,0:T(8,128)(2,1)S(1)} %slice_select_fusion), channel_id=1, source_target_pairs={{0,2},{2,0},{4,6},{6,4},{8,10},{10,8},{12,14},{14,12},{16,18},{18,... | collective-permute-start | bytes 1572872 | tf_op jit(solution)/shard_map/ppermute | solution.py:643
  207.1 6.9 %collective-permute-done.12 = bf16[1024,128]{1,0:T(8,128)(2,1)S(1)} collective-permute-done((bf16[1024,128]{1,0:T(8,128)(2,1)}, bf16[1024,128]{1,0:T(8,128)(2,1)S(1)}, u32[]{:S(2)}, u32[]{:S(2)}) %collective-permute-start.12) | collective-permute-done | bytes 262176 | tf_op jit(solution)/shard_map/ppermute | solution.py:620
  214.8 10.2 %attention_forward.4 = (f32[1024,128]{1,0:T(8,128)}, bf16[1024,128]{1,0:T(8,128)(2,1)}, f32[8,1024]{1,0:T(8,128)}) custom-call(s32[3,2]{1,0:T(4,128)} %add_add_fusion.10.range_ref, s32[8,1024]{1,0:T(8,128)} %broadcast_in_dim.195.qseg_ref, s32[4096,128]{1,0:T(8,128)} %broadcast_in_dim.196.kseg_ref, bf16[1024,384]{1,0:T(8,128)(2,1)} %fusion.18.q_ref, ...), custom_call_target="tpu_custom_call" | custom-call | flops 8000000000 | bytes 8000000 | tf_op jit(solution)/shard_map/attention_forward/pallas_call | solution.py:504
  226.6 10.4 %attention_forward.5 = (f32[1024,128]{1,0:T(8,128)}, bf16[1024,128]{1,0:T(8,128)(2,1)}, f32[8,1024]{1,0:T(8,128)}) custom-call(s32[3,2]{1,0:T(4,128)} %add_add_fusion.10.range_ref, s32[8,1024]{1,0:T(8,128)} %broadcast_in_dim.195.qseg_ref, s32[4096,128]{1,0:T(8,128)} %broadcast_in_dim.196.kseg_ref, bf16[1024,384]{1,0:T(8,128)(2,1)} %fusion.18.q_ref, ...), custom_call_target="tpu_custom_call" | custom-call | flops 8000000000 | bytes 8000000 | tf_op jit(solution)/shard_map/attention_forward/pallas_call | solution.py:504
  238.1 6.4 collective-permute-done.14
  252.3 7.7 %multiply_convert_fusion.1 = (bf16[384,1536]{1,0:T(8,128)(2,1)S(1)}, f32[384,1536]{1,0:T(8,128)S(1)}, f32[384,1536]{1,0:T(8,128)S(1)}) fusion(f32[1536]{0:T(1024)S(1)} %reshape.934, bf16[768,3072]{1,0:T(8,128)(2,1)} %all-gather.9.cloned.1.call-done, f32[384,768]{1,0:T(8,128)S(1)} %get-tuple-element.321, f32[768]{0:T(1024)S(1)} %get-tuple-element.201, ...), kind=kOutput, calls=%fused_computation.42 | convolution fusion | flops 946372608 | bytes 9452544 | tf_op jit(solution)/shard_map/dot_general | solution.py:676
  261.8 10.3 %multiply_convert_fusion = (bf16[640,1536]{1,0:T(8,128)(2,1)S(1)}, f32[640,1536]{1,0:T(8,128)S(1)}, f32[640,1536]{1,0:T(8,128)S(1)}) fusion(f32[1536]{0:T(1024)S(1)} %reshape.934, bf16[768,3072]{1,0:T(8,128)(2,1)S(1)} %copy-done.98, f32[640,768]{1,0:T(8,128)S(1)} %get-tuple-element.318, f32[768]{0:T(1024)S(1)} %get-tuple-element.201, ...), kind=kOutput, calls=%fused_computation.7 | convolution fusion | flops 1577287680 | bytes 14180352 | tf_op jit(solution)/shard_map/dot_general | solution.py:676
  283.1 15.5 %collective-permute-done.16 = bf16[640,768]{1,0:T(8,128)(2,1)S(1)} collective-permute-done((bf16[640,768]{1,0:T(8,128)(2,1)S(1)}, bf16[640,768]{1,0:T(8,128)(2,1)S(1)}, u32[]{:S(2)}, u32[]{:S(2)}) %collective-permute-start.16) | collective-permute-done | bytes 983072 | tf_op jit(solution)/shard_map/ppermute | solution.py:620
  304.9 3.5 fusion.149
  310.7 2.7 fusion.46
  318.0 2.7 pad_maximum_fusion
  323.9 7.7 %collective-permute-done.18 = bf16[640,768]{1,0:T(8,128)(2,1)} collective-permute-done((bf16[640,768]{1,0:T(8,128)(2,1)}, bf16[640,768]{1,0:T(8,128)(2,1)}, u32[]{:S(2)}, u32[]{:S(2)}) %collective-permute-start.18) | collective-permute-done | bytes 983072 | tf_op jit(solution)/shard_map/ppermute | solution.py:620
  331.5 2.6 multiply_reduce_fusion.4
  335.2 3.4 convolution_convert_fusion.2.do_ref
  338.9 16.0 %attention_backward.3 = (bf16[1024,128]{1,0:T(8,128)(2,1)}, f32[1024,256]{1,0:T(8,128)}, bf16[1024,256]{1,0:T(8,128)(2,1)}, bf16[1024,256]{1,0:T(8,128)(2,1)}, b...) custom-call(s32[3,4]{1,0:T(4,128)} %add_add_fusion.11.range_ref, s32[8,1024]{1,0:T(8,128)} %broadcast_in_dim.195.qseg_ref, ...), custom_call_target="tpu_custom_call" | custom-call | flops 8000000000 | bytes 12000000 | tf_op jit(solution)/shard_map/attention_backward/pallas_call | solution.py:587
  356.2 6.4 collective-permute-start.22
  364.1 15.7 %attention_backward.4 = (bf16[1024,128]{1,0:T(8,128)(2,1)}, f32[1024,256]{1,0:T(8,128)}, bf16[1024,256]{1,0:T(8,128)(2,1)}, bf16[1024,256]{1,0:T(8,128)(2,1)}, b...) custom-call(s32[3,4]{1,0:T(4,128)} %add_add_fusion.11.range_ref, s32[8,1024]{1,0:T(8,128)} %broadcast_in_dim.195.qseg_ref, ...), custom_call_target="tpu_custom_call" | custom-call | flops 8000000000 | bytes 12000000 | tf_op jit(solution)/shard_map/attention_backward/pallas_call | solution.py:587
  384.4 12.3 %collective-permute-start.26 = (bf16[512,256]{1,0:T(8,128)(2,1)S(1)}, bf16[512,256]{1,0:T(8,128)(2,1)S(1)}, u32[]{:S(2)}, u32[]{:S(2)}) collective-permute-start(bf16[512,256]{1,0:T(8,128)(2,1)S(1)} %copy-done.101), channel_id=1, source_target_pairs={{0,4},{4,8},{6,2},{8,12},{10,6},{12,16},{14,10},{16,20},{18,14},{2... | collective-permute-start | bytes 786440 | tf_op jit(solution)/shard_map/ppermute | solution.py:655
  400.3 8.6 %collective-permute-done.26 = bf16[512,256]{1,0:T(8,128)(2,1)S(1)} collective-permute-done((bf16[512,256]{1,0:T(8,128)(2,1)S(1)}, bf16[512,256]{1,0:T(8,128)(2,1)S(1)}, u32[]{:S(2)}, u32[]{:S(2)}) %collective-permute-start.26) | collective-permute-done | bytes 262176 | tf_op jit(solution)/shard_map/ppermute | solution.py:655
  409.8 15.6 %attention_backward.5 = (bf16[1024,128]{1,0:T(8,128)(2,1)}, f32[1024,256]{1,0:T(8,128)}, bf16[1024,256]{1,0:T(8,128)(2,1)}, bf16[1024,256]{1,0:T(8,128)(2,1)}, b...) custom-call(s32[3,4]{1,0:T(4,128)} %add_add_fusion.11.range_ref, s32[8,1024]{1,0:T(8,128)} %broadcast_in_dim.195.qseg_ref, ...), custom_call_target="tpu_custom_call" | custom-call | flops 8000000000 | bytes 12000000 | tf_op jit(solution)/shard_map/attention_backward/pallas_call | solution.py:587
  426.8 6.5 %collective-permute-start.30 = (bf16[512,256]{1,0:T(8,128)(2,1)}, bf16[512,256]{1,0:T(8,128)(2,1)S(1)}, u32[]{:S(2)}, u32[]{:S(2)}) collective-permute-start(bf16[512,256]{1,0:T(8,128)(2,1)} %get-tuple-element.165), channel_id=1, source_target_pairs={{0,4},{4,8},{6,2},{8,12},{10,6},{12,16},{14,10},{16,20},{18,14},{2... | collective-permute-start | bytes 786440 | tf_op jit(solution)/shard_map/ppermute | solution.py:655
  433.3 4.4 collective-permute-start.27
  447.9 5.1 convolution_convert_fusion.1
  459.9 4.0 convolution_convert_fusion
  465.6 14.8 %collective-permute-done.31 = bf16[1024,768]{1,0:T(8,128)(2,1)} collective-permute-done((bf16[1024,768]{1,0:T(8,128)(2,1)}, bf16[1024,768]{1,0:T(8,128)(2,1)}, u32[]{:S(2)}, u32[]{:S(2)}) %collective-permute-start.31) | collective-permute-done | bytes 1572896 | tf_op jit(solution)/shard_map/ppermute | solution.py:620
  480.4 5.1 multiply_reduce_fusion
  485.9 2.8 fusion.128
  494.6 36.8 %tap_gradient.1 = bf16[16,400,384]{2,1,0:T(8,128)(2,1)} custom-call(s32[1]{0:T(128)} %bitcast.1.n_ref, bf16[2,8,256,304]{3,2,1,0:T(8,128)(2,1)} %get-tuple-element.168.xt_ref, bf16[2,4,304,1152]{3,2,1,0:T(8,128)(2,1)} %get-tuple-element.169.s_ref, bf16[2,33,304,128]{3,2,1,0:T(8,128)(2,1)} %get-tuple-element.170.mask_ref, bf16[1152,384]{1,0:T(8,128)(2,1)} %pad.10.d_ref, ...), custom_call_target="tpu_custom_call" | custom-call | flops 1000000000 | bytes 15000000 | tf_op jit(solution)/shard_map/tap_gradient/pallas_call | solution.py:137
  531.4 9.6 %reduce-scatter.6.cloned.1.call-done = bf16[48,1536]{1,0:T(8,128)(2,1)} async-done(((bf16[768,1536]{1,0:T(8,128)(2,1)}), bf16[48,1536]{1,0:T(8,128)(2,1)}) %reduce-scatter.6.cloned.1.call-update) | async-done | bytes 147472 | tf_op jit(solution)/shard_map/reduce_scatter | solution.py:684
  543.5 3.2 pad_maximum_fusion.1
  547.7 4.0 collective-permute-start.32
  554.0 10.9 %collective-permute-done.33 = bf16[64,384]{1,0:T(8,128)(2,1)S(1)} collective-permute-done((bf16[64,384]{1,0:T(8,128)(2,1)S(1)}, bf16[64,384]{1,0:T(8,128)(2,1)S(1)}, u32[]{:S(2)}, u32[]{:S(2)}) %collective-permute-start.33) | collective-permute-done | bytes 49184 | tf_op jit(solution)/shard_map/ppermute | solution.py:639
  565.9 27.4 %conv_back.1 = f32[1024,384]{1,0:T(8,128)} custom-call(s32[1]{0:T(128)} %bitcast.1.n_ref, bf16[1152,384]{1,0:T(8,128)(2,1)} %pad_maximum_fusion.5.d_ref, bf16[2,4,304,1152]{3,2,1,0:T(8,128)(2,1)} %get-tuple-element.169.s_ref, bf16[2,33,272,128]{3,2,1,0:T(8,128)(2,1)} %get-tuple-element.115.refs_1_.refs_0_, ...), custom_call_target="tpu_custom_call" | custom-call | flops 24999999488 | bytes 15000000 | tf_op jit(solution)/shard_map/conv_back/pallas_call | solution.py:137
  598.0 15.9 %collective-permute-done.34 = bf16[1024,384]{1,0:T(8,128)(2,1)S(1)} collective-permute-done((bf16[1024,384]{1,0:T(8,128)(2,1)S(1)}, bf16[1024,384]{1,0:T(8,128)(2,1)S(1)}, u32[]{:S(2)}, u32[]{:S(2)}) %collective-permute-start.34) | collective-permute-done | bytes 786464 | tf_op jit(solution)/shard_map/ppermute | solution.py:620
  619.8 10.0 %reduce-scatter.8.cloned.1.call-done = bf16[1,400,384]{2,1,0:T(8,128)(2,1)} async-done(((bf16[16,400,384]{2,1,0:T(8,128)(2,1)}), bf16[1,400,384]{2,1,0:T(8,128)(2,1)}) %reduce-scatter.8.cloned.1.call-update) | async-done | bytes 307216 | tf_op jit(solution)/shard_map/reduce_scatter | solution.py:684
  (506 shorter events, 143.3 us)
Async XLA Ops:
  7.3 60.6 %all-gather.5.cloned.1.call-start = ((), (), s32[]{:S(2)}) async-start(), calls=%async_computation.3 | async-start | bytes 5013504 | tf_op jit(solution)/shard_map/all_gather | solution.py:680
  9.3 117.6 %all-gather.7.cloned.1.call-start = ((), (), s32[]{:S(2)}) async-start(), calls=%async_computation.4 | async-start | bytes 2506752 | tf_op jit(solution)/shard_map/all_gather | solution.py:680
  10.9 36.8 %collective-permute-start = (bf16[64,384]{1,0:T(8,128)(2,1)S(1)}, bf16[64,384]{1,0:T(8,128)(2,1)S(1)}, u32[]{:S(2)}, u32[]{:S(2)}) collective-permute-start(bf16[64,384]{1,0:T(8,128)(2,1)S(1)} %get-tuple-element.294), channel_id=1, source_target_pairs={{0,2},{2,4},{4,6},{6,8},{8,10},{10,12},{12,14},{14,16},{16,18},{18... | collective-permute-start | bytes 147464 | tf_op jit(solution)/shard_map/ppermute | solution.py:639
  13.3 34.5 %collective-permute-start.1 = (bf16[64,384]{1,0:T(8,128)(2,1)S(1)}, bf16[64,384]{1,0:T(8,128)(2,1)S(1)}, u32[]{:S(2)}, u32[]{:S(2)}) collective-permute-start(bf16[64,384]{1,0:T(8,128)(2,1)S(1)} %get-tuple-element.295), channel_id=1, source_target_pairs={{2,0},{4,2},{6,4},{8,6},{10,8},{12,10},{14,12},{16,14},{18,16},{20... | collective-permute-start | bytes 147464 | tf_op jit(solution)/shard_map/ppermute | solution.py:639
  15.4 236.9 %all-gather.9.cloned.1.call-start = ((), (), s32[]{:S(2)}) async-start(), calls=%async_computation.5 | async-start | bytes 5013504 | tf_op jit(solution)/shard_map/all_gather | solution.py:680
  47.7 48.6 %copy-start.74 = (f32[384]{0:T(512)}, f32[384]{0:T(512)S(1)}, u32[]{:S(2)}) copy-start(f32[384]{0:T(512)S(1)} %add.708) | copy-start | bytes 4612
  102.1 20.1 %collective-permute-start.2 = (bf16[1024,384]{1,0:T(8,128)(2,1)}, bf16[1024,384]{1,0:T(8,128)(2,1)}, u32[]{:S(2)}, u32[]{:S(2)}) collective-permute-start(bf16[1024,384]{1,0:T(8,128)(2,1)} %get-tuple-element.280), channel_id=1, source_target_pairs={{0,1},{1,0},{2,3},{3,2},{4,5},{5,4},{6,7},{7,6},{8,9},{9,8},{10,11... | collective-permute-start | bytes 2359304 | tf_op jit(solution)/shard_map/ppermute | solution.py:620
  104.4 348.6 %reduce-scatter.4.cloned.1.call-start = ((), (), s32[]{:S(2)}) async-start(), calls=%async_computation.6 | async-start | bytes 5013504 | tf_op jit(solution)/shard_map/reduce_scatter | solution.py:684
  134.4 40.2 %copy-start.4 = (bf16[1024,768]{1,0:T(8,128)(2,1)}, bf16[1024,768]{1,0:T(8,128)(2,1)S(1)}, u32[]{:S(2)}) copy-start(bf16[1024,768]{1,0:T(8,128)(2,1)S(1)} %fusion.6.k0) | copy-start | bytes 4718596
  134.4 7.1 %collective-permute-start.4 = (bf16[1024,256]{1,0:T(8,128)(2,1)S(1)}, bf16[1024,256]{1,0:T(8,128)(2,1)S(1)}, u32[]{:S(2)}, u32[]{:S(2)}) collective-permute-start(bf16[1024,256]{1,0:T(8,128)(2,1)S(1)} %slice.343), channel_id=1, source_target_pairs={{2,4},{4,2},{6,8},{8,6},{10,12},{12,10},{14,16},{16,14},{18,20},{2... | collective-permute-start | bytes 1572872 | tf_op jit(solution)/shard_map/ppermute | solution.py:649
  135.3 29.5 %collective-permute-start.3 = (bf16[1024,256]{1,0:T(8,128)(2,1)S(1)}, bf16[1024,256]{1,0:T(8,128)(2,1)}, u32[]{:S(2)}, u32[]{:S(2)}) collective-permute-start(bf16[1024,256]{1,0:T(8,128)(2,1)S(1)} %slice.343), channel_id=1, source_target_pairs={{0,2},{2,0},{4,6},{6,4},{8,10},{10,8},{12,14},{14,12},{16,18},{18,... | collective-permute-start | bytes 1572872 | tf_op jit(solution)/shard_map/ppermute | solution.py:643
  136.6 28.2 %collective-permute-start.5 = (bf16[512,256]{1,0:T(8,128)(2,1)S(1)}, bf16[512,256]{1,0:T(8,128)(2,1)}, u32[]{:S(2)}, u32[]{:S(2)}) collective-permute-start(bf16[512,256]{1,0:T(8,128)(2,1)S(1)} %slice_select_fusion.3), channel_id=1, source_target_pairs={{0,4},{4,8},{6,2},{8,12},{10,6},{12,16},{14,10},{16,20},{18,14},{2... | collective-permute-start | bytes 786440 | tf_op jit(solution)/shard_map/ppermute | solution.py:655
  142.3 22.7 %collective-permute-start.6 = (bf16[512,256]{1,0:T(8,128)(2,1)}, bf16[512,256]{1,0:T(8,128)(2,1)}, u32[]{:S(2)}, u32[]{:S(2)}) collective-permute-start(bf16[512,256]{1,0:T(8,128)(2,1)} %slice_select_fusion.2), channel_id=1, source_target_pairs={{0,2},{2,0},{4,6},{6,4},{8,10},{10,8},{12,14},{14,12},{16,18},{18,... | collective-permute-start | bytes 786440 | tf_op jit(solution)/shard_map/ppermute | solution.py:643
  166.1 22.7 %collective-permute-start.9 = (bf16[1024,512]{1,0:T(8,128)(2,1)}, bf16[1024,512]{1,0:T(8,128)(2,1)S(1)}, u32[]{:S(2)}, u32[]{:S(2)}) collective-permute-start(bf16[1024,512]{1,0:T(8,128)(2,1)} %slice.277), channel_id=1, source_target_pairs={{2,4},{4,2},{6,8},{8,6},{10,12},{12,10},{14,16},{16,14},{18,20},{2... | collective-permute-start | bytes 3145736 | tf_op jit(solution)/shard_map/ppermute | solution.py:649
  169.3 37.9 %collective-permute-start.7 = (bf16[768,384]{1,0:T(8,128)(2,1)S(1)}, bf16[768,384]{1,0:T(8,128)(2,1)}, u32[]{:S(2)}, u32[]{:S(2)}) collective-permute-start(bf16[768,384]{1,0:T(8,128)(2,1)S(1)} %slice.337), channel_id=1, source_target_pairs={{0,1},{1,0},{2,3},{3,2},{4,5},{5,4},{6,7},{7,6},{8,9},{9,8},{10,11... | collective-permute-start | bytes 1769480 | tf_op jit(solution)/shard_map/ppermute | solution.py:620
  170.8 43.2 %collective-permute-start.8 = (bf16[1024,512]{1,0:T(8,128)(2,1)}, bf16[1024,512]{1,0:T(8,128)(2,1)}, u32[]{:S(2)}, u32[]{:S(2)}) collective-permute-start(bf16[1024,512]{1,0:T(8,128)(2,1)} %slice.277), channel_id=1, source_target_pairs={{0,2},{2,0},{4,6},{6,4},{8,10},{10,8},{12,14},{14,12},{16,18},{18,... | collective-permute-start | bytes 3145736 | tf_op jit(solution)/shard_map/ppermute | solution.py:643
  175.4 38.6 %collective-permute-start.10 = (bf16[512,512]{1,0:T(8,128)(2,1)}, bf16[512,512]{1,0:T(8,128)(2,1)S(1)}, u32[]{:S(2)}, u32[]{:S(2)}) collective-permute-start(bf16[512,512]{1,0:T(8,128)(2,1)} %slice_select_fusion.1), channel_id=1, source_target_pairs={{0,4},{4,8},{6,2},{8,12},{10,6},{12,16},{14,10},{16,20},{18,14},{2... | collective-permute-start | bytes 1572872 | tf_op jit(solution)/shard_map/ppermute | solution.py:655
  188.8 25.2 %collective-permute-start.11 = (bf16[512,512]{1,0:T(8,128)(2,1)S(1)}, bf16[512,512]{1,0:T(8,128)(2,1)}, u32[]{:S(2)}, u32[]{:S(2)}) collective-permute-start(bf16[512,512]{1,0:T(8,128)(2,1)S(1)} %slice_select_fusion), channel_id=1, source_target_pairs={{0,2},{2,0},{4,6},{6,4},{8,10},{10,8},{12,14},{14,12},{16,18},{18,... | collective-permute-start | bytes 1572872 | tf_op jit(solution)/shard_map/ppermute | solution.py:643
  205.5 8.5 %collective-permute-start.12 = (bf16[1024,128]{1,0:T(8,128)(2,1)}, bf16[1024,128]{1,0:T(8,128)(2,1)S(1)}, u32[]{:S(2)}, u32[]{:S(2)}) collective-permute-start(bf16[1024,128]{1,0:T(8,128)(2,1)} %get-tuple-element.127), channel_id=1, source_target_pairs={{0,1},{1,0},{2,3},{3,2},{4,5},{5,4},{6,7},{7,6},{8,9},{9,8},{10,11... | collective-permute-start | bytes 786440 | tf_op jit(solution)/shard_map/ppermute | solution.py:620
  225.0 12.9 %collective-permute-start.13 = (bf16[1024,128]{1,0:T(8,128)(2,1)}, bf16[1024,128]{1,0:T(8,128)(2,1)S(1)}, u32[]{:S(2)}, u32[]{:S(2)}) collective-permute-start(bf16[1024,128]{1,0:T(8,128)(2,1)} %get-tuple-element.131), channel_id=1, source_target_pairs={{0,1},{1,0},{2,3},{3,2},{4,5},{5,4},{6,7},{7,6},{8,9},{9,8},{10,11... | collective-permute-start | bytes 786440 | tf_op jit(solution)/shard_map/ppermute | solution.py:620
  237.0 7.5 %collective-permute-start.14 = (bf16[1024,128]{1,0:T(8,128)(2,1)}, bf16[1024,128]{1,0:T(8,128)(2,1)S(1)}, u32[]{:S(2)}, u32[]{:S(2)}) collective-permute-start(bf16[1024,128]{1,0:T(8,128)(2,1)} %get-tuple-element.133), channel_id=1, source_target_pairs={{0,1},{1,0},{2,3},{3,2},{4,5},{5,4},{6,7},{7,6},{8,9},{9,8},{10,11... | collective-permute-start | bytes 786440 | tf_op jit(solution)/shard_map/ppermute | solution.py:620
  261.2 14.1 %collective-permute-start.15 = (bf16[384,768]{1,0:T(8,128)(2,1)S(1)}, bf16[384,768]{1,0:T(8,128)(2,1)S(1)}, u32[]{:S(2)}, u32[]{:S(2)}) collective-permute-start(bf16[384,768]{1,0:T(8,128)(2,1)S(1)} %fusion.55), channel_id=1, source_target_pairs={{0,1},{1,0},{2,3},{3,2},{4,5},{5,4},{6,7},{7,6},{8,9},{9,8},{10,11... | collective-permute-start | bytes 1769480 | tf_op jit(solution)/shard_map/ppermute | solution.py:620
  273.8 24.8 %collective-permute-start.16 = (bf16[640,768]{1,0:T(8,128)(2,1)S(1)}, bf16[640,768]{1,0:T(8,128)(2,1)S(1)}, u32[]{:S(2)}, u32[]{:S(2)}) collective-permute-start(bf16[640,768]{1,0:T(8,128)(2,1)S(1)} %fusion.49), channel_id=1, source_target_pairs={{0,1},{1,0},{2,3},{3,2},{4,5},{5,4},{6,7},{7,6},{8,9},{9,8},{10,11... | collective-permute-start | bytes 2949128 | tf_op jit(solution)/shard_map/ppermute | solution.py:620
  278.2 38.3 %copy-start.6 = (f32[384,768]{1,0:T(8,128)}, f32[384,768]{1,0:T(8,128)S(1)}, u32[]{:S(2)}) copy-start(f32[384,768]{1,0:T(8,128)S(1)} %get-tuple-element.271) | copy-start | bytes 3538948
  282.1 38.7 %collective-permute-start.17 = (bf16[384,768]{1,0:T(8,128)(2,1)}, bf16[384,768]{1,0:T(8,128)(2,1)}, u32[]{:S(2)}, u32[]{:S(2)}) collective-permute-start(bf16[384,768]{1,0:T(8,128)(2,1)} %fusion.52), channel_id=1, source_target_pairs={{0,1},{1,0},{2,3},{3,2},{4,5},{5,4},{6,7},{7,6},{8,9},{9,8},{10,11... | collective-permute-start | bytes 1769480 | tf_op jit(solution)/shard_map/ppermute | solution.py:620
  313.3 18.2 %collective-permute-start.18 = (bf16[640,768]{1,0:T(8,128)(2,1)}, bf16[640,768]{1,0:T(8,128)(2,1)}, u32[]{:S(2)}, u32[]{:S(2)}) collective-permute-start(bf16[640,768]{1,0:T(8,128)(2,1)} %fusion.46), channel_id=1, source_target_pairs={{0,1},{1,0},{2,3},{3,2},{4,5},{5,4},{6,7},{7,6},{8,9},{9,8},{10,11... | collective-permute-start | bytes 2949128 | tf_op jit(solution)/shard_map/ppermute | solution.py:620
  323.9 58.0 %copy-start.14 = (f32[384,768]{1,0:T(8,128)}, f32[384,768]{1,0:T(8,128)S(1)}, u32[]{:S(2)}) copy-start(f32[384,768]{1,0:T(8,128)S(1)} %get-tuple-element.250) | copy-start | bytes 3538948
  335.1 46.7 %copy-start.8 = (f32[640,768]{1,0:T(8,128)}, f32[640,768]{1,0:T(8,128)S(1)}, u32[]{:S(2)}) copy-start(f32[640,768]{1,0:T(8,128)S(1)} %get-tuple-element.248) | copy-start | bytes 5898244
  338.6 202.5 %reduce-scatter.6.cloned.1.call-start = ((), (), s32[]{:S(2)}) async-start(), calls=%async_computation.7 | async-start | bytes 2506752 | tf_op jit(solution)/shard_map/reduce_scatter | solution.py:684
  354.9 29.5 %collective-permute-start.21 = (bf16[512,256]{1,0:T(8,128)(2,1)}, bf16[512,256]{1,0:T(8,128)(2,1)S(1)}, u32[]{:S(2)}, u32[]{:S(2)}) collective-permute-start(bf16[512,256]{1,0:T(8,128)(2,1)} %get-tuple-element.154), channel_id=1, source_target_pairs={{2,6},{4,0},{6,10},{8,4},{10,14},{12,8},{14,18},{16,12},{18,22},{2... | collective-permute-start | bytes 786440 | tf_op jit(solution)/shard_map/ppermute | solution.py:655
  356.2 40.5 %collective-permute-start.22 = (bf16[512,256]{1,0:T(8,128)(2,1)}, bf16[512,256]{1,0:T(8,128)(2,1)S(1)}, u32[]{:S(2)}, u32[]{:S(2)}) collective-permute-start(bf16[512,256]{1,0:T(8,128)(2,1)} %get-tuple-element.155), channel_id=1, source_target_pairs={{0,4},{4,8},{6,2},{8,12},{10,6},{12,16},{14,10},{16,20},{18,14},{2... | collective-permute-start | bytes 786440 | tf_op jit(solution)/shard_map/ppermute | solution.py:655
  362.6 46.5 %collective-permute-start.19 = (bf16[1024,256]{1,0:T(8,128)(2,1)}, bf16[1024,256]{1,0:T(8,128)(2,1)S(1)}, u32[]{:S(2)}, u32[]{:S(2)}) collective-permute-start(bf16[1024,256]{1,0:T(8,128)(2,1)} %get-tuple-element.145), channel_id=1, source_target_pairs={{0,2},{2,0},{4,6},{6,4},{8,10},{10,8},{12,14},{14,12},{16,18},{18,... | collective-permute-start | bytes 1572872 | tf_op jit(solution)/shard_map/ppermute | solution.py:643
  362.6 46.4 %collective-permute-start.20 = (bf16[1024,256]{1,0:T(8,128)(2,1)}, bf16[1024,256]{1,0:T(8,128)(2,1)}, u32[]{:S(2)}, u32[]{:S(2)}) collective-permute-start(bf16[1024,256]{1,0:T(8,128)(2,1)} %get-tuple-element.146), channel_id=1, source_target_pairs={{2,4},{4,2},{6,8},{8,6},{10,12},{12,10},{14,16},{16,14},{18,20},{2... | collective-permute-start | bytes 1572872 | tf_op jit(solution)/shard_map/ppermute | solution.py:649
  379.8 19.9 %collective-permute-start.25 = (bf16[512,256]{1,0:T(8,128)(2,1)}, bf16[512,256]{1,0:T(8,128)(2,1)S(1)}, u32[]{:S(2)}, u32[]{:S(2)}) collective-permute-start(bf16[512,256]{1,0:T(8,128)(2,1)} %get-tuple-element.159), channel_id=1, source_target_pairs={{2,6},{4,0},{6,10},{8,4},{10,14},{12,8},{14,18},{16,12},{18,22},{2... | collective-permute-start | bytes 786440 | tf_op jit(solution)/shard_map/ppermute | solution.py:655
  384.4 24.5 %collective-permute-start.26 = (bf16[512,256]{1,0:T(8,128)(2,1)S(1)}, bf16[512,256]{1,0:T(8,128)(2,1)S(1)}, u32[]{:S(2)}, u32[]{:S(2)}) collective-permute-start(bf16[512,256]{1,0:T(8,128)(2,1)S(1)} %copy-done.101), channel_id=1, source_target_pairs={{0,4},{4,8},{6,2},{8,12},{10,6},{12,16},{14,10},{16,20},{18,14},{2... | collective-permute-start | bytes 786440 | tf_op jit(solution)/shard_map/ppermute | solution.py:655
  397.4 44.4 %collective-permute-start.23 = (bf16[1024,256]{1,0:T(8,128)(2,1)}, bf16[1024,256]{1,0:T(8,128)(2,1)S(1)}, u32[]{:S(2)}, u32[]{:S(2)}) collective-permute-start(bf16[1024,256]{1,0:T(8,128)(2,1)} %get-tuple-element.157), channel_id=1, source_target_pairs={{0,2},{2,0},{4,6},{6,4},{8,10},{10,8},{12,14},{14,12},{16,18},{18,... | collective-permute-start | bytes 1572872 | tf_op jit(solution)/shard_map/ppermute | solution.py:643
  399.6 42.9 %collective-permute-start.24 = (bf16[1024,256]{1,0:T(8,128)(2,1)}, bf16[1024,256]{1,0:T(8,128)(2,1)S(1)}, u32[]{:S(2)}, u32[]{:S(2)}) collective-permute-start(bf16[1024,256]{1,0:T(8,128)(2,1)} %get-tuple-element.158), channel_id=1, source_target_pairs={{2,4},{4,2},{6,8},{8,6},{10,12},{12,10},{14,16},{16,14},{18,20},{2... | collective-permute-start | bytes 1572872 | tf_op jit(solution)/shard_map/ppermute | solution.py:649
  425.5 20.2 %collective-permute-start.29 = (bf16[512,256]{1,0:T(8,128)(2,1)}, bf16[512,256]{1,0:T(8,128)(2,1)S(1)}, u32[]{:S(2)}, u32[]{:S(2)}) collective-permute-start(bf16[512,256]{1,0:T(8,128)(2,1)} %get-tuple-element.164), channel_id=1, source_target_pairs={{2,6},{4,0},{6,10},{8,4},{10,14},{12,8},{14,18},{16,12},{18,22},{2... | collective-permute-start | bytes 786440 | tf_op jit(solution)/shard_map/ppermute | solution.py:655
  426.8 18.9 %collective-permute-start.30 = (bf16[512,256]{1,0:T(8,128)(2,1)}, bf16[512,256]{1,0:T(8,128)(2,1)S(1)}, u32[]{:S(2)}, u32[]{:S(2)}) collective-permute-start(bf16[512,256]{1,0:T(8,128)(2,1)} %get-tuple-element.165), channel_id=1, source_target_pairs={{0,4},{4,8},{6,2},{8,12},{10,6},{12,16},{14,10},{16,20},{18,14},{2... | collective-permute-start | bytes 786440 | tf_op jit(solution)/shard_map/ppermute | solution.py:655
  433.3 12.5 %collective-permute-start.27 = (bf16[1024,256]{1,0:T(8,128)(2,1)}, bf16[1024,256]{1,0:T(8,128)(2,1)S(1)}, u32[]{:S(2)}, u32[]{:S(2)}) collective-permute-start(bf16[1024,256]{1,0:T(8,128)(2,1)} %get-tuple-element.162), channel_id=1, source_target_pairs={{0,2},{2,0},{4,6},{6,4},{8,10},{10,8},{12,14},{14,12},{16,18},{18,... | collective-permute-start | bytes 1572872 | tf_op jit(solution)/shard_map/ppermute | solution.py:643
  441.8 4.0 collective-permute-start.28
  454.9 25.5 %collective-permute-start.31 = (bf16[1024,768]{1,0:T(8,128)(2,1)}, bf16[1024,768]{1,0:T(8,128)(2,1)}, u32[]{:S(2)}, u32[]{:S(2)}) collective-permute-start(bf16[1024,768]{1,0:T(8,128)(2,1)} %convolution_convert_fusion.1), channel_id=1, source_target_pairs={{0,1},{1,0},{2,3},{3,2},{4,5},{5,4},{6,7},{7,6},{8,9},{9,8},{10,11... | collective-permute-start | bytes 4718600 | tf_op jit(solution)/shard_map/ppermute | solution.py:620
  465.5 164.2 %reduce-scatter.8.cloned.1.call-start = ((), (), s32[]{:S(2)}) async-start(), calls=%async_computation.8 | async-start | bytes 5222400 | tf_op jit(solution)/shard_map/reduce_scatter | solution.py:684
  547.7 48.8 %copy-start.22 = (f32[1536,48]{0,1:T(8,128)}, f32[1536,48]{0,1:T(8,128)S(1)}, u32[]{:S(2)}) copy-start(f32[1536,48]{0,1:T(8,128)S(1)} %get-tuple-element.226) | copy-start | bytes 884740
  547.7 6.3 collective-permute-start.32
  551.8 13.1 %collective-permute-start.33 = (bf16[64,384]{1,0:T(8,128)(2,1)S(1)}, bf16[64,384]{1,0:T(8,128)(2,1)S(1)}, u32[]{:S(2)}, u32[]{:S(2)}) collective-permute-start(bf16[64,384]{1,0:T(8,128)(2,1)S(1)} %get-tuple-element.309), channel_id=1, source_target_pairs={{2,0},{4,2},{6,4},{8,6},{10,8},{12,10},{14,12},{16,14},{18,16},{20... | collective-permute-start | bytes 147464 | tf_op jit(solution)/shard_map/ppermute | solution.py:639
  554.0 43.2 %copy-start.23 = (f32[48,1536]{1,0:T(8,128)}, f32[48,1536]{1,0:T(8,128)S(1)}, u32[]{:S(2)}) copy-start(f32[48,1536]{1,0:T(8,128)S(1)} %get-tuple-element.230) | copy-start | bytes 884740
  595.0 18.9 %collective-permute-start.34 = (bf16[1024,384]{1,0:T(8,128)(2,1)S(1)}, bf16[1024,384]{1,0:T(8,128)(2,1)S(1)}, u32[]{:S(2)}, u32[]{:S(2)}) collective-permute-start(bf16[1024,384]{1,0:T(8,128)(2,1)S(1)} %convert_element_type.286), channel_id=1, source_target_pairs={{0,1},{1,0},{2,3},{3,2},{4,5},{5,4},{6,7},{7,6},{8,9},{9,8},{10,11... | collective-permute-start | bytes 2359304 | tf_op jit(solution)/shard_map/ppermute | solution.py:620
  (96 other events, 973.4 us)
Sparse Core Ops, SparseCore 0:
  11.0 56.2 all-gather.4
  70.2 40.8 all-gather.6
  113.9 65.6 all-gather.8
  338.7 100.1 reduce-scatter.3
  465.6 75.3 reduce-scatter.5
  544.9 84.8 reduce-scatter.7
